TPU v7x, 128 devices: a whole 4x4x4 slice. The times are simulated.
128 devices in a mesh: slab: 16 (over z, y), angle: 8 (over x, core).
Axes of the slice: x: 4, y: 4, z: 4, core: 2. Of those that a mesh axis runs over, the one named last changes fastest.
Arguments:
- volume0: float32 [128, 512, 128], P('slab'), may hold values from -6 to 6
- weights: bfloat16 [16, 8, 3, 512, 4096], P('slab', 'angle'), as said below
- tile_block: int32 [16, 8, 3], P('slab', 'angle'), may hold values from 0 to 15, as said below
- tile_count: int32 [16, 8], P('slab', 'angle'), may hold values from 1 to 3, as said below
- owner: int32 [8, 16], P('angle'), may hold values from 0 to 15, as said below
- sino: bfloat16 [8, 16, 512, 128], P('angle', 'slab'), may hold values from -4 to 12
- weight_z: bfloat16 [128, 512, 128], P('slab'), may hold values from 0.25 to 2
- weight_y: bfloat16 [128, 512, 128], P('slab'), may hold values from 0.25 to 2
- weight_x: bfloat16 [128, 512, 128], P('slab'), may hold values from 0.25 to 2
Outputs:
- volume: float32 [128, 512, 128], P('slab', None, 'angle')
- residual: float32 [8, 16, 512, 128], P('angle', 'slab')
Inputs may be any that keep to these rules, and one draw needn't show every extreme that they name: `tile_block`: slot 0 of slab s names owner[a, s]. Slot t of slab s names owner[a, (s + d) % 16] for a distance d in 0 to 2 that differs between the slots of one slab; for a live slot, s + d stays below 16. So a live tile's block is held by its own slab or by one of the 2 slabs above it, and the 3 slots of one slab name different ray blocks. Slots t with t >= tile_count[s, a] are unused; the count 3 is reached on some device. `owner`: each row names every ray block of its angle group once. `weights`: entries are positive.
All inputs are finite; a program needn't handle non-finite values.
Results may differ from a plain program's by a relative error of at most 0.013.
Values may be sent and summed in bfloat16 or wider, within the bound.
A program may use at most 128 MiB of HBM per device.

v0:
```python
import functools

import jax
import jax.numpy as jnp
from jax import lax
from jax.experimental import pallas as pl
from jax.experimental.pallas import tpu as pltpu
from jax.sharding import PartitionSpec as P

ITERS = 3


SMOOTH_EPS = 0.01
SMOOTH_RATE = 0.15

MESH_ID = pl.DeviceIdType.MESH


def from_behind(value, axis, steps):
    count = lax.axis_size(axis)
    first, last = (max(0, -steps), min(count, count - steps))
    return lax.ppermute(value, axis, [(source, source + steps) for source in range(first, last)])


def limiter(difference):
    return difference / jnp.sqrt(difference * difference + SMOOTH_EPS)


def _where_am_i():
    slab = lax.axis_index("slab")
    here = lax.axis_index("angle")
    chip = here // 2
    core = here % 2
    partner = here + 1 - 2 * core
    return slab, here, chip, core, partner


def _greet(slab, chip, core, partner, n_chip):
    barrier = pltpu.get_barrier_semaphore()
    pl.semaphore_signal(barrier, 1, device_id=(slab, partner), device_id_type=MESH_ID)
    for d in range(1, n_chip):
        peer = ((chip + d) % n_chip) * 2 + core
        pl.semaphore_signal(barrier, 1, device_id=(slab, peer), device_id_type=MESH_ID)
    pl.semaphore_wait(barrier, n_chip)


def _scatter_kernel(n_chip, part_ref, out_ref, got_pair, got_ring, chip_sum,
                    send_a, recv_a, send_b, recv_b):
    slab, here, chip, core, partner = _where_am_i()
    _greet(slab, chip, core, partner, n_chip)
    pair = []
    for k in range(n_chip):
        copy = pltpu.make_async_remote_copy(
            src_ref=part_ref.at[2 * k + 1 - core],
            dst_ref=got_pair.at[k],
            send_sem=send_a.at[k],
            recv_sem=recv_a.at[k],
            device_id=(slab, partner),
            device_id_type=MESH_ID,
        )
        copy.start()
        pair.append(copy)
    for copy in pair:
        copy.wait()
    for k in range(n_chip):
        chip_sum[k] = part_ref[2 * k + core] + got_pair[k]
    ring = []
    for d in range(1, n_chip):
        dest = (chip + d) % n_chip
        copy = pltpu.make_async_remote_copy(
            src_ref=chip_sum.at[dest],
            dst_ref=got_ring.at[d],
            send_sem=send_b.at[d],
            recv_sem=recv_b.at[d],
            device_id=(slab, 2 * dest + core),
            device_id_type=MESH_ID,
        )
        copy.start()
        ring.append(copy)
    for copy in ring:
        copy.wait()
    total = chip_sum[chip]
    for d in range(1, n_chip):
        total = total + got_ring[d]
    out_ref[...] = total


def scatter_angle(part):
    blocks, rows, cols = part.shape
    n_chip = blocks // 2
    return pl.pallas_call(
        functools.partial(_scatter_kernel, n_chip),
        out_shape=jax.ShapeDtypeStruct((rows, cols), jnp.float32),
        in_specs=[pl.BlockSpec(memory_space=pltpu.VMEM)],
        out_specs=pl.BlockSpec(memory_space=pltpu.VMEM),
        scratch_shapes=[
            pltpu.VMEM((n_chip, rows, cols), jnp.float32),
            pltpu.VMEM((n_chip, rows, cols), jnp.float32),
            pltpu.VMEM((n_chip, rows, cols), jnp.float32),
            pltpu.SemaphoreType.DMA((n_chip,)),
            pltpu.SemaphoreType.DMA((n_chip,)),
            pltpu.SemaphoreType.DMA((n_chip,)),
            pltpu.SemaphoreType.DMA((n_chip,)),
        ],
        compiler_params=pltpu.CompilerParams(collective_id=0, has_side_effects=True),
        cost_estimate=pl.CostEstimate(
            flops=2 * blocks * rows * cols, bytes_accessed=4 * 3 * blocks * rows * cols,
            transcendentals=0,
        ),
    )(part)


def _gather_kernel(n_chip, own_ref, out_ref, held, send_a, recv_a, send_b, recv_b, local_sem):
    slab, here, chip, core, partner = _where_am_i()
    _greet(slab, chip, core, partner, n_chip)
    mine = pltpu.make_async_copy(own_ref, held.at[here], local_sem.at[0])
    mine.start()
    ring = []
    for d in range(1, n_chip):
        dest = (chip + d) % n_chip
        copy = pltpu.make_async_remote_copy(
            src_ref=own_ref,
            dst_ref=held.at[here],
            send_sem=send_a.at[d],
            recv_sem=recv_a.at[d],
            device_id=(slab, 2 * dest + core),
            device_id_type=MESH_ID,
        )
        copy.start()
        ring.append(copy)
    mine.wait()
    for copy in ring:
        copy.wait()
    pair = []
    for k in range(n_chip):
        copy = pltpu.make_async_remote_copy(
            src_ref=held.at[2 * k + core],
            dst_ref=held.at[2 * k + core],
            send_sem=send_b.at[k],
            recv_sem=recv_b.at[k],
            device_id=(slab, partner),
            device_id_type=MESH_ID,
        )
        copy.start()
        pair.append(copy)
    for copy in pair:
        copy.wait()
    out_ref[...] = held[...]


def gather_angle(own, groups):
    rows, cols = own.shape
    n_chip = groups // 2
    return pl.pallas_call(
        functools.partial(_gather_kernel, n_chip),
        out_shape=jax.ShapeDtypeStruct((groups, rows, cols), own.dtype),
        in_specs=[pl.BlockSpec(memory_space=pltpu.VMEM)],
        out_specs=pl.BlockSpec(memory_space=pltpu.VMEM),
        scratch_shapes=[
            pltpu.VMEM((groups, rows, cols), own.dtype),
            pltpu.SemaphoreType.DMA((n_chip,)),
            pltpu.SemaphoreType.DMA((n_chip,)),
            pltpu.SemaphoreType.DMA((n_chip,)),
            pltpu.SemaphoreType.DMA((n_chip,)),
            pltpu.SemaphoreType.DMA((1,)),
        ],
        compiler_params=pltpu.CompilerParams(collective_id=1, has_side_effects=True),
        cost_estimate=pl.CostEstimate(
            flops=0, bytes_accessed=2 * 2 * groups * rows * cols, transcendentals=0,
        ),
    )(own)


def smooth_share(
    volume,
    weight_z,
    weight_y,
    weight_x,
    lower_rim,
    left_rim,
    z_first,
    z_total,
    x_first,
    x_total,
):
    upper_halo = from_behind(volume[:, 0], "slab", -1)
    lower_halo = from_behind(volume[:, -1], "slab", 1)
    right_halo = from_behind(volume[0], "angle", -1)
    left_halo = from_behind(volume[-1], "angle", 1)
    upper = jnp.concatenate([volume[:, 1:], upper_halo[:, None]], axis=1)
    inside = (z_first + lax.broadcasted_iota(jnp.int32, volume.shape, 1) + 1 < z_total).astype(
        jnp.float32
    )
    face_flux = weight_z * limiter(upper - volume) * inside
    lower_flux = lower_rim * limiter(volume[:, 0] - lower_halo)
    previous = jnp.concatenate([lower_flux[:, None], face_flux[:, :-1]], axis=1)
    change = face_flux - previous
    following = jnp.concatenate([volume[:, :, 1:], jnp.zeros_like(volume[:, :, :1])], axis=2)
    inside = (lax.broadcasted_iota(jnp.int32, volume.shape, 2) < volume.shape[2] - 1).astype(
        jnp.float32
    )
    face_flux = weight_y * limiter(following - volume) * inside
    previous = jnp.concatenate([jnp.zeros_like(face_flux[:, :, :1]), face_flux[:, :, :-1]], axis=2)
    change = change + face_flux - previous
    following = jnp.concatenate([volume[1:], right_halo[None]], axis=0)
    inside = (x_first + lax.broadcasted_iota(jnp.int32, volume.shape, 0) + 1 < x_total).astype(
        jnp.float32
    )
    face_flux = weight_x * limiter(following - volume) * inside
    lower_flux = left_rim * limiter(volume[0] - left_halo)
    previous = jnp.concatenate([lower_flux[None], face_flux[:-1]], axis=0)
    change = change + face_flux - previous
    return volume + SMOOTH_RATE * change


def shards(volume0, weights, tile_block, tile_count, owner, sino, weight_z, weight_y, weight_x):
    tiles = weights[0, 0]
    slot_count, ray_count, voxels = tiles.shape
    slab_depth, height, column_count = volume0.shape
    blocks = tile_block[0, 0]
    live_count = tile_count[0, 0]
    owner_row = owner[0]
    live_slots = jnp.arange(slot_count, dtype=jnp.int32) < live_count
    select = (owner_row[None, :] == blocks[:, None]) & live_slots[:, None]
    slab_pos = lax.axis_index("slab")
    holder_ids = jnp.arange(owner_row.shape[0], dtype=jnp.int32)
    target = jnp.sum(jnp.where(select, holder_ids[None, :], 0), axis=1)
    distance_ids = jnp.arange(slot_count, dtype=jnp.int32)
    relative = ((target - slab_pos)[:, None] == distance_ids[None, :]) & live_slots[:, None]
    relative_float = relative.astype(jnp.float32)
    relative_half = relative.astype(jnp.bfloat16)
    flat_tiles = tiles.reshape(slot_count * ray_count, voxels)
    ray_local = jnp.dot(
        flat_tiles, jnp.ones((voxels,), jnp.bfloat16), preferred_element_type=jnp.float32
    )
    ray_sends = jnp.einsum("td,tr->dr", relative_float, ray_local.reshape(slot_count, ray_count))
    ray_total = ray_sends[0]
    for distance in range(1, slot_count):
        ray_total = ray_total + from_behind(ray_sends[distance], "slab", distance)
    live_rows = jnp.repeat(live_slots, ray_count).astype(jnp.bfloat16)
    voxel_local = jnp.dot(live_rows, flat_tiles, preferred_element_type=jnp.float32)
    voxel_total = lax.psum(voxel_local, "angle")
    ray_scale = 1.0 / ray_total
    voxel_scale = (1.0 / voxel_total).reshape(1, slab_depth, height)
    lower_all = from_behind(weight_z[slab_depth - 1], "slab", 1)
    z_first = slab_pos * slab_depth
    z_total = slab_depth * lax.axis_size("slab")
    groups = lax.axis_size("angle")
    share_width = column_count // groups
    angle_pos = lax.axis_index("angle")
    share_first = angle_pos * share_width

    def share_of(array):
        part = lax.dynamic_slice_in_dim(array, share_first, share_width, array.ndim - 1)
        return jnp.moveaxis(part, -1, 0).astype(jnp.float32)

    measured = sino[0, 0].astype(jnp.float32)
    volume = share_of(volume0)
    local_z = share_of(weight_z)
    local_y = share_of(weight_y)
    local_x = share_of(weight_x)
    lower_rim = share_of(lower_all)
    left_index = jnp.maximum(share_first - 1, 0)
    left_rim = lax.dynamic_index_in_dim(weight_x, left_index, 2, keepdims=False).astype(
        jnp.float32
    ) * (angle_pos > 0).astype(jnp.float32)
    gathered = None
    residual = jnp.zeros((ray_count, column_count), jnp.float32)
    for iteration in range(ITERS):
        if gathered is None:
            flat_volume = volume0.astype(jnp.bfloat16).reshape(voxels, column_count)
            products = jnp.einsum(
                "trv,vn->trn", tiles, flat_volume, preferred_element_type=jnp.float32
            ).astype(jnp.bfloat16)
        else:
            products = jnp.einsum(
                "trv,nv->trn", tiles, gathered, preferred_element_type=jnp.float32
            ).astype(jnp.bfloat16)
        sends = jnp.einsum(
            "td,trn->drn", relative_half, products, preferred_element_type=jnp.float32
        )
        sends_half = sends.astype(jnp.bfloat16)
        projected = sends[0]
        for distance in range(1, slot_count):
            arrived = from_behind(sends_half[distance], "slab", distance)
            projected = projected + arrived.astype(jnp.float32)
        residual = (measured - projected) * ray_scale[:, None]
        residual_half = residual.astype(jnp.bfloat16)
        nearby = [residual_half] + [
            from_behind(residual_half, "slab", -distance) for distance in range(1, slot_count)
        ]
        picked = jnp.einsum(
            "td,drn->trn", relative_half, jnp.stack(nearby), preferred_element_type=jnp.float32
        ).astype(jnp.bfloat16)
        back_t = jnp.einsum("trn,trv->nv", picked, tiles, preferred_element_type=jnp.float32)
        back_own = scatter_angle(back_t.reshape(groups, share_width, voxels))
        volume = volume + voxel_scale * back_own.reshape(share_width, slab_depth, height)
        volume = smooth_share(
            volume,
            local_z,
            local_y,
            local_x,
            lower_rim,
            left_rim,
            z_first,
            z_total,
            share_first,
            column_count,
        )
        if iteration + 1 < ITERS:
            own_half = volume.astype(jnp.bfloat16).reshape(share_width, voxels)
            gathered = gather_angle(own_half, groups).reshape(column_count, voxels)
    volume_out = jnp.moveaxis(volume, 0, -1)
    return (volume_out, residual[None, None])


def solution(mesh):
    in_specs = (
        P("slab", None, None),
        P("slab", "angle", None, None, None),
        P("slab", "angle", None),
        P("slab", "angle"),
        P("angle", None),
        P("angle", "slab", None, None),
        P("slab", None, None),
        P("slab", None, None),
        P("slab", None, None),
    )
    out_specs = (P("slab", None, "angle"), P("angle", "slab", None, None))
    return jax.shard_map(shards, mesh=mesh, in_specs=in_specs, out_specs=out_specs, check_vma=False)
```

profile of v0, /device:TPU:33, one launch (start us, length us, event | category | flops | bytes accessed | tf_op | source)
XLA Modules:
  0.0 338.7 jit_solution(12699068190305155740)
XLA Ops:
  2.4 7.9 %fusion.10 = bf16[1,3,512]{2,0,1:T(2,128)(2,1)S(1)} fusion(bf16[1,1,3,512,4096]{4,3,2,1,0:T(8,128)(2,1)} %param.10), kind=kOutput, calls=%fused_computation.10 | convolution fusion | flops 12582912 | bytes 12585984 | tf_op jit(solution)/shard_map/dot_general | solution.py:233
  11.1 4.8 %collective-permute-start.3 = (f32[512]{0:T(512)}, f32[512]{0:T(512)}, u32[]{:S(2)}, u32[]{:S(2)}) collective-permute-start(f32[512]{0:T(512)} %bitcast.16), channel_id=1, source_target_pairs={{0,16},{8,24},{16,32},{24,40},{32,48},{40,56},{48,64},{56,72},{64,... | collective-permute-start | bytes 6152 | tf_op jit(solution)/shard_map/ppermute | solution.py:22
  16.0 2.3 collective-permute-start.2
  19.1 2.6 collective-permute-start.7
  21.8 6.5 %fusion.23 = bf16[3,512,128]{2,1,0:T(8,128)(2,1)S(1)} fusion(bf16[4096,128,1]{1,0,2:T(8,128)(2,1)S(1)} %bitcast.311, bf16[1,1,3,512,4096]{4,3,2,1,0:T(8,128)(2,1)} %param.10), kind=kOutput, calls=%fused_computation.20 | convolution fusion | flops 1610809344 | bytes 14024704 | tf_op jit(solution)/shard_map/trv,vn->trn/dot_general | solution.py:272
  28.3 1.6 fusion.113
  30.4 6.0 %collective-permute-start.1 = (bf16[512,128]{1,0:T(8,128)(2,1)S(1)}, bf16[512,128]{1,0:T(8,128)(2,1)}, u32[]{:S(2)}, u32[]{:S(2)}) collective-permute-start(bf16[512,128]{1,0:T(8,128)(2,1)S(1)} %bitcast.322), channel_id=1, source_target_pairs={{0,16},{8,24},{16,32},{24,40},{32,48},{40,56},{48,64},{56,72},{64,... | collective-permute-start | bytes 393224 | tf_op jit(solution)/shard_map/ppermute | solution.py:22
  36.5 1.9 collective-permute-start
  38.5 2.6 constant_dynamic-slice_fusion.3
  41.1 1.9 constant_dynamic-slice_fusion.4
  43.1 6.5 %fusion.114 = f32[1,4096]{1,0:T(1,128)S(1)} fusion(pred[1536,1]{0,1:T(4,128)(4,1)S(1)} %bitcast.331, bf16[1536,4096]{1,0:T(8,128)(2,1)} %bitcast.299), kind=kOutput, calls=%fused_computation.173 | convolution fusion | flops 12582912 | bytes 12600832 | tf_op jit(solution)/shard_map/dot_general | solution.py:241
  49.6 22.7 %psum.7 = f32[4096]{0:T(1024)} all-reduce(f32[4096]{0:T(1024)S(1)} %bitcast.330), channel_id=1, replica_groups=mesh['slab'=16,'angle'=8] {'angle'}, use_global_device_ids=true, to_apply=%region_0.1 | all-reduce | flops 4096 | bytes 32768 | tf_op jit(solution)/shard_map/psum | solution.py:242
  73.0 1.3 constant_dynamic-slice_fusion
  74.4 3.2 constant_dynamic-slice_fusion.1
  77.6 1.4 slice.178
  79.7 1.1 fusion.47
  80.8 4.1 %collective-permute-start.5 = (bf16[512,128]{1,0:T(8,128)(2,1)S(1)}, bf16[512,128]{1,0:T(8,128)(2,1)S(1)}, u32[]{:S(2)}, u32[]{:S(2)}) collective-permute-start(bf16[512,128]{1,0:T(8,128)(2,1)S(1)} %fusion.47), channel_id=1, source_target_pairs={{16,0},{24,8},{32,16},{40,24},{48,32},{56,40},{64,48},{72,56},{80,... | collective-permute-start | bytes 393224 | tf_op jit(solution)/shard_map/ppermute | solution.py:22
  85.0 3.4 %collective-permute-start.4 = (bf16[512,128]{1,0:T(8,128)(2,1)S(1)}, bf16[512,128]{1,0:T(8,128)(2,1)S(1)}, u32[]{:S(2)}, u32[]{:S(2)}) collective-permute-start(bf16[512,128]{1,0:T(8,128)(2,1)S(1)} %fusion.47), channel_id=1, source_target_pairs={{8,0},{16,8},{24,16},{32,24},{40,32},{48,40},{56,48},{64,56},{72,6... | collective-permute-start | bytes 393224 | tf_op jit(solution)/shard_map/ppermute | solution.py:22
  88.5 1.6 copy.205
  90.1 1.6 copy.199
  92.3 1.6 copy.204
  93.9 1.6 copy.203
  96.9 7.7 %fusion.14.part_ref = f32[8,16,4096]{2,1,0:T(8,128)} fusion(bf16[8,16,512,3]{2,1,0,3:T(8,128)(2,1)S(1)} %bitcast.308, bf16[1,1,3,512,4096]{4,3,2,1,0:T(8,128)(2,1)} %param.10), kind=kOutput, calls=%fused_computation.14 | convolution fusion | flops 1610612736 | bytes 15073280 | tf_op jit(solution)/shard_map/trn,trv->nv/dot_general | solution.py:295
  104.6 24.6 %shard_map.104 = f32[16,4096]{1,0:T(8,128)} custom-call(f32[8,16,4096]{2,1,0:T(8,128)} %fusion.14.part_ref), custom_call_target="tpu_custom_call" | custom-call | flops 1048576 | bytes 6291456 | tf_op jit(solution)/shard_map/pallas_call | solution.py:91
  129.2 1.1 copy.208
  130.4 2.2 collective-permute-start.10
  132.8 2.1 collective-permute-start.9
  135.0 2.5 collective-permute-start.6
  137.5 2.8 collective-permute-start.8
  140.3 4.5 %collective-permute-done.8 = f32[16,512]{1,0:T(8,128)S(1)} collective-permute-done((f32[16,512]{1,0:T(8,128)S(1)}, f32[16,512]{1,0:T(8,128)S(1)}, u32[]{:S(2)}, u32[]{:S(2)}) %collective-permute-start.8) | collective-permute-done | bytes 32800 | tf_op jit(solution)/shard_map/ppermute | solution.py:22
  146.8 14.9 %shard_map.105 = bf16[8,16,4096]{2,1,0:T(8,128)(2,1)} custom-call(bf16[16,4096]{1,0:T(8,128)(2,1)} %bitcast.317), custom_call_target="tpu_custom_call" | custom-call | bytes 2097152 | tf_op jit(solution)/shard_map/pallas_call | solution.py:154
  161.7 9.2 %fusion.35 = bf16[3,512,128]{1,2,0:T(8,128)(2,1)S(1)} fusion(bf16[128,4096,1]{1,0,2:T(8,128)(2,1)} %bitcast.300, bf16[1,1,3,512,4096]{4,3,2,1,0:T(8,128)(2,1)} %param.10), kind=kOutput, calls=%fused_computation.26 | convolution fusion | flops 1610809344 | bytes 14024704 | tf_op jit(solution)/shard_map/trv,nv->trn/dot_general | solution.py:276
  171.9 1.9 collective-permute-start.11
  173.8 3.3 collective-permute-start.12
  177.1 3.7 %collective-permute-done.11 = bf16[512,128]{1,0:T(8,128)(2,1)S(1)} collective-permute-done((bf16[512,128]{1,0:T(8,128)(2,1)S(1)}, bf16[512,128]{1,0:T(8,128)(2,1)S(1)}, u32[]{:S(2)}, u32[]{:S(2)}) %collective-permute-start.11) | collective-permute-done | bytes 131104 | tf_op jit(solution)/shard_map/ppermute | solution.py:22
  180.9 2.3 collective-permute-done.12
  183.3 1.9 collective-permute-start.14
  185.2 4.4 %collective-permute-start.13 = (bf16[512,128]{1,0:T(8,128)(2,1)S(1)}, bf16[512,128]{1,0:T(8,128)(2,1)S(1)}, u32[]{:S(2)}, u32[]{:S(2)}) collective-permute-start(bf16[512,128]{1,0:T(8,128)(2,1)S(1)} %fusion.49), channel_id=1, source_target_pairs={{8,0},{16,8},{24,16},{32,24},{40,32},{48,40},{56,48},{64,56},{72,6... | collective-permute-start | bytes 393224 | tf_op jit(solution)/shard_map/ppermute | solution.py:22
  190.5 3.5 %collective-permute-done.13 = bf16[512,128]{1,0:T(8,128)(2,1)S(1)} collective-permute-done((bf16[512,128]{1,0:T(8,128)(2,1)S(1)}, bf16[512,128]{1,0:T(8,128)(2,1)S(1)}, u32[]{:S(2)}, u32[]{:S(2)}) %collective-permute-start.13) | collective-permute-done | bytes 131104 | tf_op jit(solution)/shard_map/ppermute | solution.py:22
  194.8 7.7 %fusion.17.part_ref = f32[8,16,4096]{2,1,0:T(8,128)} fusion(bf16[8,16,512,3]{2,1,0,3:T(8,128)(2,1)S(1)} %bitcast.309, bf16[1,1,3,512,4096]{4,3,2,1,0:T(8,128)(2,1)} %param.10), kind=kOutput, calls=%fused_computation.15 | convolution fusion | flops 1610612736 | bytes 15073280 | tf_op jit(solution)/shard_map/trn,trv->nv/dot_general | solution.py:295
  202.5 21.8 %shard_map.106 = f32[16,4096]{1,0:T(8,128)} custom-call(f32[8,16,4096]{2,1,0:T(8,128)} %fusion.17.part_ref), custom_call_target="tpu_custom_call" | custom-call | flops 1048576 | bytes 6291456 | tf_op jit(solution)/shard_map/pallas_call | solution.py:91
  224.3 1.1 copy.210
  225.8 2.2 collective-permute-start.18
  228.0 2.1 collective-permute-start.17
  230.2 2.8 collective-permute-start.16
  233.0 4.6 %collective-permute-start.15 = (f32[16,512]{1,0:T(8,128)S(1)}, f32[16,512]{1,0:T(8,128)S(1)}, u32[]{:S(2)}, u32[]{:S(2)}) collective-permute-start(f32[16,512]{1,0:T(8,128)S(1)} %get-tuple-element.24), channel_id=1, source_target_pairs={{8,0},{16,8},{24,16},{32,24},{40,32},{48,40},{56,48},{64,56},{72,6... | collective-permute-start | bytes 98312 | tf_op jit(solution)/shard_map/ppermute | solution.py:22
  240.2 15.1 %shard_map.107 = bf16[8,16,4096]{2,1,0:T(8,128)(2,1)} custom-call(bf16[16,4096]{1,0:T(8,128)(2,1)} %bitcast.318), custom_call_target="tpu_custom_call" | custom-call | bytes 2097152 | tf_op jit(solution)/shard_map/pallas_call | solution.py:154
  255.2 9.2 %fusion.38 = bf16[3,512,128]{1,2,0:T(8,128)(2,1)S(1)} fusion(bf16[128,4096,1]{1,0,2:T(8,128)(2,1)} %bitcast.301, bf16[1,1,3,512,4096]{4,3,2,1,0:T(8,128)(2,1)} %param.10), kind=kOutput, calls=%fused_computation.27 | convolution fusion | flops 1610809344 | bytes 14024704 | tf_op jit(solution)/shard_map/trv,nv->trn/dot_general | solution.py:276
  265.4 2.5 collective-permute-start.19
  267.9 6.0 %collective-permute-start.20 = (bf16[512,128]{1,0:T(8,128)(2,1)S(1)}, bf16[512,128]{1,0:T(8,128)(2,1)S(1)}, u32[]{:S(2)}, u32[]{:S(2)}) collective-permute-start(bf16[512,128]{1,0:T(8,128)(2,1)S(1)} %get-tuple-element.13), channel_id=1, source_target_pairs={{0,16},{8,24},{16,32},{24,40},{32,48},{40,56},{48,64},{56,72},{64,... | collective-permute-start | bytes 393224 | tf_op jit(solution)/shard_map/ppermute | solution.py:22
  274.0 1.2 collective-permute-done.19
  275.2 3.7 %collective-permute-done.20 = bf16[512,128]{1,0:T(8,128)(2,1)S(1)} collective-permute-done((bf16[512,128]{1,0:T(8,128)(2,1)S(1)}, bf16[512,128]{1,0:T(8,128)(2,1)S(1)}, u32[]{:S(2)}, u32[]{:S(2)}) %collective-permute-start.20) | collective-permute-done | bytes 131104 | tf_op jit(solution)/shard_map/ppermute | solution.py:22
  279.8 3.7 %collective-permute-start.22 = (bf16[512,128]{1,0:T(8,128)(2,1)S(1)}, bf16[512,128]{1,0:T(8,128)(2,1)S(1)}, u32[]{:S(2)}, u32[]{:S(2)}) collective-permute-start(bf16[512,128]{1,0:T(8,128)(2,1)S(1)} %get-tuple-element.9), channel_id=1, source_target_pairs={{16,0},{24,8},{32,16},{40,24},{48,32},{56,40},{64,48},{72,56},{80,... | collective-permute-start | bytes 393224 | tf_op jit(solution)/shard_map/ppermute | solution.py:22
  283.4 2.2 collective-permute-start.21
  285.6 1.4 collective-permute-done.22
  287.0 2.2 collective-permute-done.21
  290.0 7.7 %fusion.20.part_ref = f32[8,16,4096]{2,1,0:T(8,128)} fusion(bf16[8,16,512,3]{2,1,0,3:T(8,128)(2,1)S(1)} %bitcast.310, bf16[1,1,3,512,4096]{4,3,2,1,0:T(8,128)(2,1)} %param.10), kind=kOutput, calls=%fused_computation.16 | convolution fusion | flops 1610612736 | bytes 15073280 | tf_op jit(solution)/shard_map/trn,trv->nv/dot_general | solution.py:295
  297.7 22.9 %shard_map.108 = f32[16,4096]{1,0:T(8,128)} custom-call(f32[8,16,4096]{2,1,0:T(8,128)} %fusion.20.part_ref), custom_call_target="tpu_custom_call" | custom-call | flops 1048576 | bytes 6291456 | tf_op jit(solution)/shard_map/pallas_call | solution.py:91
  320.5 1.1 copy.211
  322.4 2.2 collective-permute-start.26
  324.8 1.9 collective-permute-start.24
  326.7 5.5 %collective-permute-start.23 = (f32[16,512]{1,0:T(8,128)S(1)}, f32[16,512]{1,0:T(8,128)S(1)}, u32[]{:S(2)}, u32[]{:S(2)}) collective-permute-start(f32[16,512]{1,0:T(8,128)S(1)} %get-tuple-element.17), channel_id=1, source_target_pairs={{8,0},{16,8},{24,16},{32,24},{40,32},{48,40},{56,48},{64,56},{72,6... | collective-permute-start | bytes 98312 | tf_op jit(solution)/shard_map/ppermute | solution.py:22
  332.2 2.7 collective-permute-start.25
  335.8 1.5 collective-permute-done.25
  (126 shorter events, 20.3 us)
Async XLA Ops:
  0.6 17.7 %slice-start = ((bf16[8,512,128]{2,1,0:T(8,128)(2,1)}), bf16[1,512,128]{2,1,0:T(8,128)(2,1)S(1)}, s32[]{:S(2)}) async-start(bf16[8,512,128]{2,1,0:T(8,128)(2,1)} %param.15), calls=%async_computation | async-start | bytes 262144 | tf_op jit(solution)/shard_map/slice | solution.py:245
  0.6 21.0 %copy-start = (f32[8,512,128]{2,1,0:T(8,128)S(1)}, f32[8,512,128]{2,1,0:T(8,128)}, u32[]{:S(2)}) copy-start(f32[8,512,128]{2,1,0:T(8,128)} %param.9) | copy-start | bytes 6291460
  2.4 25.9 %copy-start.4 = (pred[3,3]{1,0:T(4,128)(4,1)}, pred[3,3]{1,0:T(4,128)(4,1)S(1)}, u32[]{:S(2)}) copy-start(pred[3,3]{1,0:T(4,128)(4,1)S(1)} %fusion.93) | copy-start | bytes 31
  11.1 67.9 %collective-permute-start.3 = (f32[512]{0:T(512)}, f32[512]{0:T(512)}, u32[]{:S(2)}, u32[]{:S(2)}) collective-permute-start(f32[512]{0:T(512)} %bitcast.16), channel_id=1, source_target_pairs={{0,16},{8,24},{16,32},{24,40},{32,48},{40,56},{48,64},{56,72},{64,... | collective-permute-start | bytes 6152 | tf_op jit(solution)/shard_map/ppermute | solution.py:22
  16.0 63.1 %collective-permute-start.2 = (f32[512]{0:T(512)}, f32[512]{0:T(512)}, u32[]{:S(2)}, u32[]{:S(2)}) collective-permute-start(f32[512]{0:T(512)} %bitcast.15), channel_id=1, source_target_pairs={{0,8},{8,16},{16,24},{24,32},{32,40},{40,48},{48,56},{56,64},{64,7... | collective-permute-start | bytes 6152 | tf_op jit(solution)/shard_map/ppermute | solution.py:22
  19.1 121.3 %collective-permute-start.7 = (bf16[512,128]{0,1:T(8,128)(2,1)}, bf16[512,128]{0,1:T(8,128)(2,1)}, u32[]{:S(2)}, u32[]{:S(2)}) collective-permute-start(bf16[512,128]{0,1:T(8,128)(2,1)} %bitcast.27), channel_id=1, source_target_pairs={{0,8},{8,16},{16,24},{24,32},{32,40},{40,48},{48,56},{56,64},{64,7... | collective-permute-start | bytes 393224 | tf_op jit(solution)/shard_map/ppermute | solution.py:22
  30.4 49.3 %collective-permute-start.1 = (bf16[512,128]{1,0:T(8,128)(2,1)S(1)}, bf16[512,128]{1,0:T(8,128)(2,1)}, u32[]{:S(2)}, u32[]{:S(2)}) collective-permute-start(bf16[512,128]{1,0:T(8,128)(2,1)S(1)} %bitcast.322), channel_id=1, source_target_pairs={{0,16},{8,24},{16,32},{24,40},{32,48},{40,56},{48,64},{56,72},{64,... | collective-permute-start | bytes 393224 | tf_op jit(solution)/shard_map/ppermute | solution.py:22
  36.5 43.2 %collective-permute-start = (bf16[512,128]{1,0:T(8,128)(2,1)S(1)}, bf16[512,128]{1,0:T(8,128)(2,1)}, u32[]{:S(2)}, u32[]{:S(2)}) collective-permute-start(bf16[512,128]{1,0:T(8,128)(2,1)S(1)} %bitcast.323), channel_id=1, source_target_pairs={{0,8},{8,16},{16,24},{24,32},{32,40},{40,48},{48,56},{56,64},{64,7... | collective-permute-start | bytes 393224 | tf_op jit(solution)/shard_map/ppermute | solution.py:22
  38.5 34.5 %copy-start.2 = (bf16[8,512,128]{2,1,0:T(8,128)(2,1)S(1)}, bf16[8,512,128]{2,1,0:T(8,128)(2,1)}, u32[]{:S(2)}) copy-start(bf16[8,512,128]{2,1,0:T(8,128)(2,1)} %param.17) | copy-start | bytes 3145732
  43.1 36.6 %copy-start.3 = (bf16[1,1,512,128]{3,2,1,0:T(8,128)(2,1)S(1)}, bf16[1,1,512,128]{3,2,1,0:T(8,128)(2,1)}, u32[]{:S(2)}) copy-start(bf16[1,1,512,128]{3,2,1,0:T(8,128)(2,1)} %param.14) | copy-start | bytes 393220
  43.1 48.6 %copy-start.1 = (f32[8,512,16]{2,1,0:T(8,128)S(1)}, f32[8,512,16]{2,1,0:T(8,128)}, u32[]{:S(2)}) copy-start(f32[8,512,16]{2,1,0:T(8,128)} %constant_dynamic-slice_fusion.4) | copy-start | bytes 786436
  77.6 68.0 %copy-start.6 = (pred[16]{0:T(512)(128)(4,1)}, pred[16]{0:T(512)(128)(4,1)S(1)}, u32[]{:S(2)}) copy-start(pred[16]{0:T(512)(128)(4,1)S(1)} %add_compare_fusion) | copy-start | bytes 52
  80.8 14.6 %collective-permute-start.5 = (bf16[512,128]{1,0:T(8,128)(2,1)S(1)}, bf16[512,128]{1,0:T(8,128)(2,1)S(1)}, u32[]{:S(2)}, u32[]{:S(2)}) collective-permute-start(bf16[512,128]{1,0:T(8,128)(2,1)S(1)} %fusion.47), channel_id=1, source_target_pairs={{16,0},{24,8},{32,16},{40,24},{48,32},{56,40},{64,48},{72,56},{80,... | collective-permute-start | bytes 393224 | tf_op jit(solution)/shard_map/ppermute | solution.py:22
  85.0 10.5 %collective-permute-start.4 = (bf16[512,128]{1,0:T(8,128)(2,1)S(1)}, bf16[512,128]{1,0:T(8,128)(2,1)S(1)}, u32[]{:S(2)}, u32[]{:S(2)}) collective-permute-start(bf16[512,128]{1,0:T(8,128)(2,1)S(1)} %fusion.47), channel_id=1, source_target_pairs={{8,0},{16,8},{24,16},{32,24},{40,32},{48,40},{56,48},{64,56},{72,6... | collective-permute-start | bytes 393224 | tf_op jit(solution)/shard_map/ppermute | solution.py:22
  129.2 42.0 %copy-start.5 = (pred[3,3]{1,0:T(4,128)(4,1)S(1)}, pred[3,3]{1,0:T(4,128)(4,1)}, u32[]{:S(2)}) copy-start(pred[3,3]{1,0:T(4,128)(4,1)} %copy-done.4) | copy-start | bytes 31
  130.4 9.9 %collective-permute-start.10 = (f32[8,512]{1,0:T(8,128)S(1)}, f32[8,512]{1,0:T(8,128)S(1)}, u32[]{:S(2)}, u32[]{:S(2)}) collective-permute-start(f32[8,512]{1,0:T(8,128)S(1)} %get-tuple-element.33), channel_id=1, source_target_pairs={{0,1},{1,2},{2,3},{3,4},{4,5},{5,6},{6,7},{8,9},{9,10},{10,11},{11... | collective-permute-start | bytes 49160 | tf_op jit(solution)/shard_map/ppermute | solution.py:22
  132.8 12.8 %collective-permute-start.9 = (f32[8,512]{1,0:T(8,128)S(1)}, f32[8,512]{1,0:T(8,128)S(1)}, u32[]{:S(2)}, u32[]{:S(2)}) collective-permute-start(f32[8,512]{1,0:T(8,128)S(1)} %get-tuple-element.34), channel_id=1, source_target_pairs={{1,0},{2,1},{3,2},{4,3},{5,4},{6,5},{7,6},{9,8},{10,9},{11,10},{12... | collective-permute-start | bytes 49160 | tf_op jit(solution)/shard_map/ppermute | solution.py:22
  135.0 10.6 %collective-permute-start.6 = (f32[16,512]{1,0:T(8,128)S(1)}, f32[16,512]{1,0:T(8,128)S(1)}, u32[]{:S(2)}, u32[]{:S(2)}) collective-permute-start(f32[16,512]{1,0:T(8,128)S(1)} %bitcast.333), channel_id=1, source_target_pairs={{8,0},{16,8},{24,16},{32,24},{40,32},{48,40},{56,48},{64,56},{72,6... | collective-permute-start | bytes 98312 | tf_op jit(solution)/shard_map/ppermute | solution.py:22
  137.5 7.3 %collective-permute-start.8 = (f32[16,512]{1,0:T(8,128)S(1)}, f32[16,512]{1,0:T(8,128)S(1)}, u32[]{:S(2)}, u32[]{:S(2)}) collective-permute-start(f32[16,512]{1,0:T(8,128)S(1)} %bitcast.334), channel_id=1, source_target_pairs={{0,8},{8,16},{16,24},{24,32},{32,40},{40,48},{48,56},{56,64},{64,7... | collective-permute-start | bytes 98312 | tf_op jit(solution)/shard_map/ppermute | solution.py:22
  171.9 66.8 %copy-start.7 = (pred[16]{0:T(512)(128)(4,1)S(1)}, pred[16]{0:T(512)(128)(4,1)}, u32[]{:S(2)}) copy-start(pred[16]{0:T(512)(128)(4,1)} %copy-done.6) | copy-start | bytes 52
  171.9 9.0 %collective-permute-start.11 = (bf16[512,128]{1,0:T(8,128)(2,1)S(1)}, bf16[512,128]{1,0:T(8,128)(2,1)S(1)}, u32[]{:S(2)}, u32[]{:S(2)}) collective-permute-start(bf16[512,128]{1,0:T(8,128)(2,1)S(1)} %get-tuple-element.14), channel_id=1, source_target_pairs={{0,8},{8,16},{16,24},{24,32},{32,40},{40,48},{48,56},{56,64},{64,7... | collective-permute-start | bytes 393224 | tf_op jit(solution)/shard_map/ppermute | solution.py:22
  173.8 9.3 %collective-permute-start.12 = (bf16[512,128]{1,0:T(8,128)(2,1)S(1)}, bf16[512,128]{1,0:T(8,128)(2,1)S(1)}, u32[]{:S(2)}, u32[]{:S(2)}) collective-permute-start(bf16[512,128]{1,0:T(8,128)(2,1)S(1)} %get-tuple-element.15), channel_id=1, source_target_pairs={{0,16},{8,24},{16,32},{24,40},{32,48},{40,56},{48,64},{56,72},{64,... | collective-permute-start | bytes 393224 | tf_op jit(solution)/shard_map/ppermute | solution.py:22
  183.3 7.2 %collective-permute-start.14 = (bf16[512,128]{1,0:T(8,128)(2,1)S(1)}, bf16[512,128]{1,0:T(8,128)(2,1)S(1)}, u32[]{:S(2)}, u32[]{:S(2)}) collective-permute-start(bf16[512,128]{1,0:T(8,128)(2,1)S(1)} %fusion.49), channel_id=1, source_target_pairs={{16,0},{24,8},{32,16},{40,24},{48,32},{56,40},{64,48},{72,56},{80,... | collective-permute-start | bytes 393224 | tf_op jit(solution)/shard_map/ppermute | solution.py:22
  185.2 8.8 %collective-permute-start.13 = (bf16[512,128]{1,0:T(8,128)(2,1)S(1)}, bf16[512,128]{1,0:T(8,128)(2,1)S(1)}, u32[]{:S(2)}, u32[]{:S(2)}) collective-permute-start(bf16[512,128]{1,0:T(8,128)(2,1)S(1)} %fusion.49), channel_id=1, source_target_pairs={{8,0},{16,8},{24,16},{32,24},{40,32},{48,40},{56,48},{64,56},{72,6... | collective-permute-start | bytes 393224 | tf_op jit(solution)/shard_map/ppermute | solution.py:22
  225.8 11.8 %collective-permute-start.18 = (f32[8,512]{1,0:T(8,128)S(1)}, f32[8,512]{1,0:T(8,128)S(1)}, u32[]{:S(2)}, u32[]{:S(2)}) collective-permute-start(f32[8,512]{1,0:T(8,128)S(1)} %get-tuple-element.21), channel_id=1, source_target_pairs={{0,1},{1,2},{2,3},{3,4},{4,5},{5,6},{6,7},{8,9},{9,10},{10,11},{11... | collective-permute-start | bytes 49160 | tf_op jit(solution)/shard_map/ppermute | solution.py:22
  228.0 10.7 %collective-permute-start.17 = (f32[8,512]{1,0:T(8,128)S(1)}, f32[8,512]{1,0:T(8,128)S(1)}, u32[]{:S(2)}, u32[]{:S(2)}) collective-permute-start(f32[8,512]{1,0:T(8,128)S(1)} %get-tuple-element.22), channel_id=1, source_target_pairs={{1,0},{2,1},{3,2},{4,3},{5,4},{6,5},{7,6},{9,8},{10,9},{11,10},{12... | collective-permute-start | bytes 49160 | tf_op jit(solution)/shard_map/ppermute | solution.py:22
  230.2 7.4 %collective-permute-start.16 = (f32[16,512]{1,0:T(8,128)S(1)}, f32[16,512]{1,0:T(8,128)S(1)}, u32[]{:S(2)}, u32[]{:S(2)}) collective-permute-start(f32[16,512]{1,0:T(8,128)S(1)} %get-tuple-element.23), channel_id=1, source_target_pairs={{0,8},{8,16},{16,24},{24,32},{32,40},{40,48},{48,56},{56,64},{64,7... | collective-permute-start | bytes 98312 | tf_op jit(solution)/shard_map/ppermute | solution.py:22
  233.0 5.7 %collective-permute-start.15 = (f32[16,512]{1,0:T(8,128)S(1)}, f32[16,512]{1,0:T(8,128)S(1)}, u32[]{:S(2)}, u32[]{:S(2)}) collective-permute-start(f32[16,512]{1,0:T(8,128)S(1)} %get-tuple-element.24), channel_id=1, source_target_pairs={{8,0},{16,8},{24,16},{32,24},{40,32},{48,40},{56,48},{64,56},{72,6... | collective-permute-start | bytes 98312 | tf_op jit(solution)/shard_map/ppermute | solution.py:22
  265.4 9.8 %collective-permute-start.19 = (bf16[512,128]{1,0:T(8,128)(2,1)S(1)}, bf16[512,128]{1,0:T(8,128)(2,1)S(1)}, u32[]{:S(2)}, u32[]{:S(2)}) collective-permute-start(bf16[512,128]{1,0:T(8,128)(2,1)S(1)} %get-tuple-element.12), channel_id=1, source_target_pairs={{0,8},{8,16},{16,24},{24,32},{32,40},{40,48},{48,56},{56,64},{64,7... | collective-permute-start | bytes 393224 | tf_op jit(solution)/shard_map/ppermute | solution.py:22
  267.9 11.0 %collective-permute-start.20 = (bf16[512,128]{1,0:T(8,128)(2,1)S(1)}, bf16[512,128]{1,0:T(8,128)(2,1)S(1)}, u32[]{:S(2)}, u32[]{:S(2)}) collective-permute-start(bf16[512,128]{1,0:T(8,128)(2,1)S(1)} %get-tuple-element.13), channel_id=1, source_target_pairs={{0,16},{8,24},{16,32},{24,40},{32,48},{40,56},{48,64},{56,72},{64,... | collective-permute-start | bytes 393224 | tf_op jit(solution)/shard_map/ppermute | solution.py:22
  279.8 7.2 %collective-permute-start.22 = (bf16[512,128]{1,0:T(8,128)(2,1)S(1)}, bf16[512,128]{1,0:T(8,128)(2,1)S(1)}, u32[]{:S(2)}, u32[]{:S(2)}) collective-permute-start(bf16[512,128]{1,0:T(8,128)(2,1)S(1)} %get-tuple-element.9), channel_id=1, source_target_pairs={{16,0},{24,8},{32,16},{40,24},{48,32},{56,40},{64,48},{72,56},{80,... | collective-permute-start | bytes 393224 | tf_op jit(solution)/shard_map/ppermute | solution.py:22
  283.4 5.7 %collective-permute-start.21 = (bf16[512,128]{1,0:T(8,128)(2,1)S(1)}, bf16[512,128]{1,0:T(8,128)(2,1)S(1)}, u32[]{:S(2)}, u32[]{:S(2)}) collective-permute-start(bf16[512,128]{1,0:T(8,128)(2,1)S(1)} %get-tuple-element.9), channel_id=1, source_target_pairs={{8,0},{16,8},{24,16},{32,24},{40,32},{48,40},{56,48},{64,56},{72,6... | collective-permute-start | bytes 393224 | tf_op jit(solution)/shard_map/ppermute | solution.py:22
  322.4 12.5 %collective-permute-start.26 = (f32[8,512]{1,0:T(8,128)S(1)}, f32[8,512]{1,0:T(8,128)S(1)}, u32[]{:S(2)}, u32[]{:S(2)}) collective-permute-start(f32[8,512]{1,0:T(8,128)S(1)} %bitcast.339), channel_id=1, source_target_pairs={{0,1},{1,2},{2,3},{3,4},{4,5},{5,6},{6,7},{8,9},{9,10},{10,11},{11... | collective-permute-start | bytes 49160 | tf_op jit(solution)/shard_map/ppermute | solution.py:22
  324.8 10.1 %collective-permute-start.24 = (f32[16,512]{1,0:T(8,128)S(1)}, f32[16,512]{1,0:T(8,128)S(1)}, u32[]{:S(2)}, u32[]{:S(2)}) collective-permute-start(f32[16,512]{1,0:T(8,128)S(1)} %get-tuple-element.16), channel_id=1, source_target_pairs={{0,8},{8,16},{16,24},{24,32},{32,40},{40,48},{48,56},{56,64},{64,7... | collective-permute-start | bytes 98312 | tf_op jit(solution)/shard_map/ppermute | solution.py:22
  326.7 9.0 %collective-permute-start.23 = (f32[16,512]{1,0:T(8,128)S(1)}, f32[16,512]{1,0:T(8,128)S(1)}, u32[]{:S(2)}, u32[]{:S(2)}) collective-permute-start(f32[16,512]{1,0:T(8,128)S(1)} %get-tuple-element.17), channel_id=1, source_target_pairs={{8,0},{16,8},{24,16},{32,24},{40,32},{48,40},{56,48},{64,56},{72,6... | collective-permute-start | bytes 98312 | tf_op jit(solution)/shard_map/ppermute | solution.py:22
  332.2 5.1 %collective-permute-start.25 = (f32[8,512]{1,0:T(8,128)S(1)}, f32[8,512]{1,0:T(8,128)S(1)}, u32[]{:S(2)}, u32[]{:S(2)}) collective-permute-start(f32[8,512]{1,0:T(8,128)S(1)} %slice_bitcast_fusion.10), channel_id=1, source_target_pairs={{1,0},{2,1},{3,2},{4,3},{5,4},{6,5},{7,6},{9,8},{10,9},{11,10},{12... | collective-permute-start | bytes 49160 | tf_op jit(solution)/shard_map/ppermute | solution.py:22
where the time goes:
time: 340 us; the launch traced here: 339 us
  Pallas kernels  99.2 us (29%)
  starting transfers between devices  84.8 us (25%)
  matrix products  67.1 us (20%)
  local copies, waits for them, and re-layouts  26.9 us (8%)
  waiting for transfers between devices  25.1 us (7%)
  blocking collectives  22.7 us (7%)
  other arithmetic  10.3 us (3%)
    ppermute x27, starting transfers between devices, from_behind(): lax.ppermute(value, axis, [(source, source + steps) for source in range(f...  84.8 us
    pallas_call x3, Pallas kernels, scatter_angle(): pl.pallas_call(functools.partial(_scatter_kernel, n_chip), out_shape=jax....  69.2 us
    pallas_call x2, Pallas kernels, gather_angle(): pl.pallas_call(functools.partial(_gather_kernel, n_chip), out_shape=jax.S...  30 us
    ppermute x27, waiting for transfers between devices, from_behind(): lax.ppermute(value, axis, [(source, source + steps) for source in range(f...  25.1 us
    dot_general x3, matrix products, shards(): jnp.einsum('trn,trv->nv', picked, tiles, preferred_element_type=jnp.float32)  23.1 us
    psum x1, blocking collectives, shards(): voxel_total = lax.psum(voxel_local, 'angle')  22.7 us
    dot_general x2, matrix products, shards(): jnp.einsum('trv,nv->trn', tiles, gathered, preferred_element_type=jnp.flo...  18.4 us
    unnamed x33, local copies, waits for them, and re-layouts  11.9 us
  transfers between devices with their start and end apart: 27, of which 11 were waited for; matrix products, arithmetic and copies ran while one was open for 15% of the time, Pallas kernels for 7%

commit v1 on v0

--- a/solution.py
+++ b/solution.py
@@ -44,14 +44,14 @@
     pl.semaphore_wait(barrier, n_chip)
 
 
-def _scatter_kernel(n_chip, part_ref, out_ref, got_pair, got_ring, chip_sum,
+def _scatter_kernel(n_chip, part_ref, half_ref, out_ref, got_pair, got_ring, chip_sum,
                     send_a, recv_a, send_b, recv_b):
     slab, here, chip, core, partner = _where_am_i()
     _greet(slab, chip, core, partner, n_chip)
     pair = []
     for k in range(n_chip):
         copy = pltpu.make_async_remote_copy(
-            src_ref=part_ref.at[2 * k + 1 - core],
+            src_ref=half_ref.at[2 * k + 1 - core],
             dst_ref=got_pair.at[k],
             send_sem=send_a.at[k],
             recv_sem=recv_a.at[k],
@@ -62,8 +62,11 @@
         pair.append(copy)
     for copy in pair:
         copy.wait()
-    for k in range(n_chip):
-        chip_sum[k] = part_ref[2 * k + core] + got_pair[k]
+    for d in range(1, n_chip):
+        dest = (chip + d) % n_chip
+        chip_sum[dest] = (
+            part_ref[2 * dest + core] + got_pair[dest].astype(jnp.float32)
+        ).astype(chip_sum.dtype)
     ring = []
     for d in range(1, n_chip):
         dest = (chip + d) % n_chip
@@ -77,26 +80,27 @@
         )
         copy.start()
         ring.append(copy)
+    total = part_ref[here] + got_pair[chip].astype(jnp.float32)
     for copy in ring:
         copy.wait()
-    total = chip_sum[chip]
-    for d in range(1, n_chip):
-        total = total + got_ring[d]
+    for d in range(1, n_chip):
+        total = total + got_ring[d].astype(jnp.float32)
     out_ref[...] = total
 
 
 def scatter_angle(part):
     blocks, rows, cols = part.shape
     n_chip = blocks // 2
+    link = part.dtype
     return pl.pallas_call(
         functools.partial(_scatter_kernel, n_chip),
         out_shape=jax.ShapeDtypeStruct((rows, cols), jnp.float32),
-        in_specs=[pl.BlockSpec(memory_space=pltpu.VMEM)],
+        in_specs=[pl.BlockSpec(memory_space=pltpu.VMEM)] * 2,
         out_specs=pl.BlockSpec(memory_space=pltpu.VMEM),
         scratch_shapes=[
-            pltpu.VMEM((n_chip, rows, cols), jnp.float32),
-            pltpu.VMEM((n_chip, rows, cols), jnp.float32),
-            pltpu.VMEM((n_chip, rows, cols), jnp.float32),
+            pltpu.VMEM((n_chip, rows, cols), link),
+            pltpu.VMEM((n_chip, rows, cols), link),
+            pltpu.VMEM((n_chip, rows, cols), link),
             pltpu.SemaphoreType.DMA((n_chip,)),
             pltpu.SemaphoreType.DMA((n_chip,)),
             pltpu.SemaphoreType.DMA((n_chip,)),
@@ -105,6 +109,53 @@
         compiler_params=pltpu.CompilerParams(collective_id=0, has_side_effects=True),
         cost_estimate=pl.CostEstimate(
             flops=2 * blocks * rows * cols, bytes_accessed=4 * 3 * blocks * rows * cols,
+            transcendentals=0,
+        ),
+    )(part, part.astype(link))
+
+
+def _sum_kernel(groups, part_ref, out_ref, got, send_sem, recv_sem):
+    slab = lax.axis_index("slab")
+    here = lax.axis_index("angle")
+    barrier = pltpu.get_barrier_semaphore()
+    for d in range(1, groups):
+        peer = (here + d) % groups
+        pl.semaphore_signal(barrier, 1, device_id=(slab, peer), device_id_type=MESH_ID)
+    pl.semaphore_wait(barrier, groups - 1)
+    copies = []
+    for d in range(1, groups):
+        copy = pltpu.make_async_remote_copy(
+            src_ref=part_ref,
+            dst_ref=got.at[d],
+            send_sem=send_sem.at[d],
+            recv_sem=recv_sem.at[d],
+            device_id=(slab, (here + d) % groups),
+            device_id_type=MESH_ID,
+        )
+        copy.start()
+        copies.append(copy)
+    total = part_ref[...]
+    for copy in copies:
+        copy.wait()
+    for d in range(1, groups):
+        total = total + got[d]
+    out_ref[...] = total
+
+
+def sum_angle(part, groups):
+    return pl.pallas_call(
+        functools.partial(_sum_kernel, groups),
+        out_shape=jax.ShapeDtypeStruct(part.shape, part.dtype),
+        in_specs=[pl.BlockSpec(memory_space=pltpu.VMEM)],
+        out_specs=pl.BlockSpec(memory_space=pltpu.VMEM),
+        scratch_shapes=[
+            pltpu.VMEM((groups,) + part.shape, part.dtype),
+            pltpu.SemaphoreType.DMA((groups,)),
+            pltpu.SemaphoreType.DMA((groups,)),
+        ],
+        compiler_params=pltpu.CompilerParams(collective_id=2, has_side_effects=True),
+        cost_estimate=pl.CostEstimate(
+            flops=groups * part.size, bytes_accessed=4 * 2 * groups * part.size,
             transcendentals=0,
         ),
     )(part)
@@ -239,7 +290,7 @@
         ray_total = ray_total + from_behind(ray_sends[distance], "slab", distance)
     live_rows = jnp.repeat(live_slots, ray_count).astype(jnp.bfloat16)
     voxel_local = jnp.dot(live_rows, flat_tiles, preferred_element_type=jnp.float32)
-    voxel_total = lax.psum(voxel_local, "angle")
+    voxel_total = sum_angle(voxel_local.reshape(slab_depth, height), lax.axis_size("angle"))
     ray_scale = 1.0 / ray_total
     voxel_scale = (1.0 / voxel_total).reshape(1, slab_depth, height)
     lower_all = from_behind(weight_z[slab_depth - 1], "slab", 1)

time: 340 us -> 328 us (0.965)
  blocking collectives: 22.7 us -> 0 us
  Pallas kernels: 99.2 us -> 107 us
    psum x1 -> x0, blocking collectives: 22.7 us -> none  [shards(): voxel_total = lax.psum(voxel_local, 'angle')]
    pallas_call x0 -> x1, Pallas kernels: none -> 9.38 us  [sum_angle(): pl.pallas_call(functools.partial(_sum_kernel, groups), out_shape=jax.Shap...]
    unnamed x33 -> x31, local copies, waits for them, and re-layouts: 11.9 us -> 11.8 us
  transfers between devices with their start and end apart: 27 -> 27, of which waited for: 11 -> 11; matrix products, arithmetic and copies ran while one was open for 15% -> 15% of each run, Pallas kernels for 7% -> 9%
where the time goes in v1:
time: 328 us; the launch traced here: 326 us
  Pallas kernels  107 us (33%)
  starting transfers between devices  85.1 us (26%)
  matrix products  67 us (20%)
  local copies, waits for them, and re-layouts  28.1 us (9%)
  waiting for transfers between devices  25.6 us (8%)
  other arithmetic  10.3 us (3%)
    ppermute x27, starting transfers between devices, from_behind(): lax.ppermute(value, axis, [(source, source + steps) for source in range(f...  85.1 us
    pallas_call x3, Pallas kernels, scatter_angle(): pl.pallas_call(functools.partial(_scatter_kernel, n_chip), out_shape=jax....  67.3 us
    pallas_call x2, Pallas kernels, gather_angle(): pl.pallas_call(functools.partial(_gather_kernel, n_chip), out_shape=jax.S...  30.8 us
    ppermute x27, waiting for transfers between devices, from_behind(): lax.ppermute(value, axis, [(source, source + steps) for source in range(f...  25.6 us
    dot_general x3, matrix products, shards(): jnp.einsum('trn,trv->nv', picked, tiles, preferred_element_type=jnp.float32)  23.2 us
    dot_general x2, matrix products, shards(): jnp.einsum('trv,nv->trn', tiles, gathered, preferred_element_type=jnp.flo...  18.4 us
    unnamed x31, local copies, waits for them, and re-layouts  11.8 us
    pallas_call x1, Pallas kernels, sum_angle(): pl.pallas_call(functools.partial(_sum_kernel, groups), out_shape=jax.Shap...  9.38 us
  transfers between devices with their start and end apart: 27, of which 11 were waited for; matrix products, arithmetic and copies ran while one was open for 15% of the time, Pallas kernels for 9%

profile of v1, /device:TPU:33, one launch (start us, length us, event | category | flops | bytes accessed | tf_op | source)
XLA Modules:
  0.0 326.1 jit_solution(6584211792165095381)
XLA Ops:
  2.4 7.9 %fusion.13 = bf16[1,3,512]{2,0,1:T(2,128)(2,1)S(1)} fusion(bf16[1,1,3,512,4096]{4,3,2,1,0:T(8,128)(2,1)} %param.10), kind=kOutput, calls=%fused_computation.13 | convolution fusion | flops 12582912 | bytes 12585984 | tf_op jit(solution)/shard_map/dot_general | solution.py:284
  11.1 4.8 %collective-permute-start.3 = (f32[512]{0:T(512)}, f32[512]{0:T(512)}, u32[]{:S(2)}, u32[]{:S(2)}) collective-permute-start(f32[512]{0:T(512)} %bitcast.17), channel_id=1, source_target_pairs={{0,16},{8,24},{16,32},{24,40},{32,48},{40,56},{48,64},{56,72},{64,... | collective-permute-start | bytes 6152 | tf_op jit(solution)/shard_map/ppermute | solution.py:22
  16.0 2.3 collective-permute-start.2
  19.1 2.6 collective-permute-start.7
  21.8 6.5 %fusion.26 = bf16[3,512,128]{2,1,0:T(8,128)(2,1)S(1)} fusion(bf16[4096,128,1]{1,0,2:T(8,128)(2,1)S(1)} %bitcast.313, bf16[1,1,3,512,4096]{4,3,2,1,0:T(8,128)(2,1)} %param.10), kind=kOutput, calls=%fused_computation.23 | convolution fusion | flops 1610809344 | bytes 14024704 | tf_op jit(solution)/shard_map/trv,vn->trn/dot_general | solution.py:323
  28.3 1.6 fusion.116
  30.4 6.0 %collective-permute-start.1 = (bf16[512,128]{1,0:T(8,128)(2,1)S(1)}, bf16[512,128]{1,0:T(8,128)(2,1)}, u32[]{:S(2)}, u32[]{:S(2)}) collective-permute-start(bf16[512,128]{1,0:T(8,128)(2,1)S(1)} %bitcast.324), channel_id=1, source_target_pairs={{0,16},{8,24},{16,32},{24,40},{32,48},{40,56},{48,64},{56,72},{64,... | collective-permute-start | bytes 393224 | tf_op jit(solution)/shard_map/ppermute | solution.py:22
  36.5 1.9 collective-permute-start
  38.4 2.6 constant_dynamic-slice_fusion.3
  41.0 1.9 constant_dynamic-slice_fusion.4
  43.7 6.3 %fusion = f32[1,8,512]{2,0,1:T(1,128)S(1)} fusion(pred[1536,1,1]{0,1,2:T(4,128)(4,1)} %reshape.68, bf16[192,8,8,512]{3,2,1,0:T(8,128)(2,1)} %bitcast.301), kind=kOutput, calls=%fused_computation | convolution fusion | flops 12582912 | bytes 12600832 | tf_op jit(solution)/shard_map/dot_general | solution.py:292
  50.6 9.4 %shard_map.104 = f32[8,512]{1,0:T(8,128)} custom-call(f32[8,512]{1,0:T(8,128)} %bitcast.332), custom_call_target="tpu_custom_call" | custom-call | flops 32768 | bytes 262144 | tf_op jit(solution)/shard_map/pallas_call | solution.py:146
  60.7 1.3 constant_dynamic-slice_fusion
  62.1 3.2 constant_dynamic-slice_fusion.1
  65.3 1.4 slice.178
  67.4 1.1 fusion.50
  68.5 4.4 %collective-permute-start.5 = (bf16[512,128]{1,0:T(8,128)(2,1)S(1)}, bf16[512,128]{1,0:T(8,128)(2,1)S(1)}, u32[]{:S(2)}, u32[]{:S(2)}) collective-permute-start(bf16[512,128]{1,0:T(8,128)(2,1)S(1)} %fusion.50), channel_id=1, source_target_pairs={{16,0},{24,8},{32,16},{40,24},{48,32},{56,40},{64,48},{72,56},{80,... | collective-permute-start | bytes 393224 | tf_op jit(solution)/shard_map/ppermute | solution.py:22
  72.9 3.4 %collective-permute-start.4 = (bf16[512,128]{1,0:T(8,128)(2,1)S(1)}, bf16[512,128]{1,0:T(8,128)(2,1)S(1)}, u32[]{:S(2)}, u32[]{:S(2)}) collective-permute-start(bf16[512,128]{1,0:T(8,128)(2,1)S(1)} %fusion.50), channel_id=1, source_target_pairs={{8,0},{16,8},{24,16},{32,24},{40,32},{48,40},{56,48},{64,56},{72,6... | collective-permute-start | bytes 393224 | tf_op jit(solution)/shard_map/ppermute | solution.py:22
  76.4 1.6 copy.207
  78.0 1.6 copy.201
  80.2 1.6 copy.206
  81.8 1.6 copy.205
  83.5 1.1 fusion.35
  84.8 7.7 %fusion.17.part_ref.half_ref = f32[8,16,4096]{2,1,0:T(8,128)} fusion(bf16[8,16,512,3]{2,1,0,3:T(8,128)(2,1)S(1)} %bitcast.310, bf16[1,1,3,512,4096]{4,3,2,1,0:T(8,128)(2,1)} %param.10), kind=kOutput, calls=%fused_computation.17 | convolution fusion | flops 1610612736 | bytes 15073280 | tf_op jit(solution)/shard_map/trn,trv->nv/dot_general | solution.py:346
  92.5 21.4 %shard_map.105 = f32[16,4096]{1,0:T(8,128)} custom-call(f32[8,16,4096]{2,1,0:T(8,128)} %fusion.17.part_ref.half_ref, f32[8,16,4096]{2,1,0:T(8,128)} %fusion.17.part_ref.half_ref), custom_call_target="tpu_custom_call" | custom-call | flops 1048576 | bytes 6291456 | tf_op jit(solution)/shard_map/pallas_call | solution.py:95
  114.0 1.1 copy.210
  115.2 2.2 collective-permute-start.10
  117.6 2.1 collective-permute-start.9
  119.8 3.2 collective-permute-start.6
  123.0 2.1 collective-permute-start.8
  125.1 5.1 %collective-permute-done.8 = f32[16,512]{1,0:T(8,128)S(1)} collective-permute-done((f32[16,512]{1,0:T(8,128)S(1)}, f32[16,512]{1,0:T(8,128)S(1)}, u32[]{:S(2)}, u32[]{:S(2)}) %collective-permute-start.8) | collective-permute-done | bytes 32800 | tf_op jit(solution)/shard_map/ppermute | solution.py:22
  132.3 15.8 %shard_map.106 = bf16[8,16,4096]{2,1,0:T(8,128)(2,1)} custom-call(bf16[16,4096]{1,0:T(8,128)(2,1)} %bitcast.319), custom_call_target="tpu_custom_call" | custom-call | bytes 2097152 | tf_op jit(solution)/shard_map/pallas_call | solution.py:205
  148.1 9.2 %fusion.38 = bf16[3,512,128]{1,2,0:T(8,128)(2,1)S(1)} fusion(bf16[128,4096,1]{1,0,2:T(8,128)(2,1)} %bitcast.302, bf16[1,1,3,512,4096]{4,3,2,1,0:T(8,128)(2,1)} %param.10), kind=kOutput, calls=%fused_computation.29 | convolution fusion | flops 1610809344 | bytes 14024704 | tf_op jit(solution)/shard_map/trv,nv->trn/dot_general | solution.py:327
  158.3 1.9 collective-permute-start.11
  160.2 2.7 collective-permute-start.12
  162.9 4.4 %collective-permute-done.11 = bf16[512,128]{1,0:T(8,128)(2,1)S(1)} collective-permute-done((bf16[512,128]{1,0:T(8,128)(2,1)S(1)}, bf16[512,128]{1,0:T(8,128)(2,1)S(1)}, u32[]{:S(2)}, u32[]{:S(2)}) %collective-permute-start.11) | collective-permute-done | bytes 131104 | tf_op jit(solution)/shard_map/ppermute | solution.py:22
  167.2 2.3 collective-permute-done.12
  169.6 1.9 collective-permute-start.14
  171.6 4.4 %collective-permute-start.13 = (bf16[512,128]{1,0:T(8,128)(2,1)S(1)}, bf16[512,128]{1,0:T(8,128)(2,1)S(1)}, u32[]{:S(2)}, u32[]{:S(2)}) collective-permute-start(bf16[512,128]{1,0:T(8,128)(2,1)S(1)} %fusion.52), channel_id=1, source_target_pairs={{8,0},{16,8},{24,16},{32,24},{40,32},{48,40},{56,48},{64,56},{72,6... | collective-permute-start | bytes 393224 | tf_op jit(solution)/shard_map/ppermute | solution.py:22
  176.9 3.5 %collective-permute-done.13 = bf16[512,128]{1,0:T(8,128)(2,1)S(1)} collective-permute-done((bf16[512,128]{1,0:T(8,128)(2,1)S(1)}, bf16[512,128]{1,0:T(8,128)(2,1)S(1)}, u32[]{:S(2)}, u32[]{:S(2)}) %collective-permute-start.13) | collective-permute-done | bytes 131104 | tf_op jit(solution)/shard_map/ppermute | solution.py:22
  181.2 7.7 %fusion.20.part_ref.half_ref = f32[8,16,4096]{2,1,0:T(8,128)} fusion(bf16[8,16,512,3]{2,1,0,3:T(8,128)(2,1)S(1)} %bitcast.311, bf16[1,1,3,512,4096]{4,3,2,1,0:T(8,128)(2,1)} %param.10), kind=kOutput, calls=%fused_computation.18 | convolution fusion | flops 1610612736 | bytes 15073280 | tf_op jit(solution)/shard_map/trn,trv->nv/dot_general | solution.py:346
  188.9 22.4 %shard_map.107 = f32[16,4096]{1,0:T(8,128)} custom-call(f32[8,16,4096]{2,1,0:T(8,128)} %fusion.20.part_ref.half_ref, f32[8,16,4096]{2,1,0:T(8,128)} %fusion.20.part_ref.half_ref), custom_call_target="tpu_custom_call" | custom-call | flops 1048576 | bytes 6291456 | tf_op jit(solution)/shard_map/pallas_call | solution.py:95
  211.3 1.1 copy.212
  212.8 2.2 collective-permute-start.18
  215.0 2.1 collective-permute-start.17
  217.2 2.8 collective-permute-start.16
  219.9 4.6 %collective-permute-start.15 = (f32[16,512]{1,0:T(8,128)S(1)}, f32[16,512]{1,0:T(8,128)S(1)}, u32[]{:S(2)}, u32[]{:S(2)}) collective-permute-start(f32[16,512]{1,0:T(8,128)S(1)} %get-tuple-element.24), channel_id=1, source_target_pairs={{8,0},{16,8},{24,16},{32,24},{40,32},{48,40},{56,48},{64,56},{72,6... | collective-permute-start | bytes 98312 | tf_op jit(solution)/shard_map/ppermute | solution.py:22
  227.1 15.0 %shard_map.108 = bf16[8,16,4096]{2,1,0:T(8,128)(2,1)} custom-call(bf16[16,4096]{1,0:T(8,128)(2,1)} %bitcast.320), custom_call_target="tpu_custom_call" | custom-call | bytes 2097152 | tf_op jit(solution)/shard_map/pallas_call | solution.py:205
  242.1 9.2 %fusion.41 = bf16[3,512,128]{1,2,0:T(8,128)(2,1)S(1)} fusion(bf16[128,4096,1]{1,0,2:T(8,128)(2,1)} %bitcast.303, bf16[1,1,3,512,4096]{4,3,2,1,0:T(8,128)(2,1)} %param.10), kind=kOutput, calls=%fused_computation.30 | convolution fusion | flops 1610809344 | bytes 14024704 | tf_op jit(solution)/shard_map/trv,nv->trn/dot_general | solution.py:327
  252.3 2.9 collective-permute-start.19
  255.2 6.4 %collective-permute-start.20 = (bf16[512,128]{1,0:T(8,128)(2,1)S(1)}, bf16[512,128]{1,0:T(8,128)(2,1)S(1)}, u32[]{:S(2)}, u32[]{:S(2)}) collective-permute-start(bf16[512,128]{1,0:T(8,128)(2,1)S(1)} %get-tuple-element.13), channel_id=1, source_target_pairs={{0,16},{8,24},{16,32},{24,40},{32,48},{40,56},{48,64},{56,72},{64,... | collective-permute-start | bytes 393224 | tf_op jit(solution)/shard_map/ppermute | solution.py:22
  262.1 3.7 %collective-permute-done.20 = bf16[512,128]{1,0:T(8,128)(2,1)S(1)} collective-permute-done((bf16[512,128]{1,0:T(8,128)(2,1)S(1)}, bf16[512,128]{1,0:T(8,128)(2,1)S(1)}, u32[]{:S(2)}, u32[]{:S(2)}) %collective-permute-start.20) | collective-permute-done | bytes 131104 | tf_op jit(solution)/shard_map/ppermute | solution.py:22
  266.6 3.7 %collective-permute-start.22 = (bf16[512,128]{1,0:T(8,128)(2,1)S(1)}, bf16[512,128]{1,0:T(8,128)(2,1)S(1)}, u32[]{:S(2)}, u32[]{:S(2)}) collective-permute-start(bf16[512,128]{1,0:T(8,128)(2,1)S(1)} %get-tuple-element.9), channel_id=1, source_target_pairs={{16,0},{24,8},{32,16},{40,24},{48,32},{56,40},{64,48},{72,56},{80,... | collective-permute-start | bytes 393224 | tf_op jit(solution)/shard_map/ppermute | solution.py:22
  270.3 2.2 collective-permute-start.21
  272.5 1.4 collective-permute-done.22
  273.9 2.2 collective-permute-done.21
  276.8 7.7 %fusion.23.part_ref.half_ref = f32[8,16,4096]{2,1,0:T(8,128)} fusion(bf16[8,16,512,3]{2,1,0,3:T(8,128)(2,1)S(1)} %bitcast.312, bf16[1,1,3,512,4096]{4,3,2,1,0:T(8,128)(2,1)} %param.10), kind=kOutput, calls=%fused_computation.19 | convolution fusion | flops 1610612736 | bytes 15073280 | tf_op jit(solution)/shard_map/trn,trv->nv/dot_general | solution.py:346
  284.5 23.5 %shard_map.109 = f32[16,4096]{1,0:T(8,128)} custom-call(f32[8,16,4096]{2,1,0:T(8,128)} %fusion.23.part_ref.half_ref, f32[8,16,4096]{2,1,0:T(8,128)} %fusion.23.part_ref.half_ref), custom_call_target="tpu_custom_call" | custom-call | flops 1048576 | bytes 6291456 | tf_op jit(solution)/shard_map/pallas_call | solution.py:95
  308.0 1.1 copy.213
  309.8 2.2 collective-permute-start.26
  312.2 2.4 collective-permute-start.24
  314.6 5.0 %collective-permute-start.23 = (f32[16,512]{1,0:T(8,128)S(1)}, f32[16,512]{1,0:T(8,128)S(1)}, u32[]{:S(2)}, u32[]{:S(2)}) collective-permute-start(f32[16,512]{1,0:T(8,128)S(1)} %get-tuple-element.17), channel_id=1, source_target_pairs={{8,0},{16,8},{24,16},{32,24},{40,32},{48,40},{56,48},{64,56},{72,6... | collective-permute-start | bytes 98312 | tf_op jit(solution)/shard_map/ppermute | solution.py:22
  319.6 2.7 collective-permute-start.25
  323.2 1.5 collective-permute-done.25
  (126 shorter events, 20.9 us)
Async XLA Ops:
  0.6 17.6 %slice-start = ((bf16[8,512,128]{2,1,0:T(8,128)(2,1)}), bf16[1,512,128]{2,1,0:T(8,128)(2,1)S(1)}, s32[]{:S(2)}) async-start(bf16[8,512,128]{2,1,0:T(8,128)(2,1)} %param.15), calls=%async_computation | async-start | bytes 262144 | tf_op jit(solution)/shard_map/slice | solution.py:296
  0.6 21.0 %copy-start = (f32[8,512,128]{2,1,0:T(8,128)S(1)}, f32[8,512,128]{2,1,0:T(8,128)}, u32[]{:S(2)}) copy-start(f32[8,512,128]{2,1,0:T(8,128)} %param.9) | copy-start | bytes 6291460
  2.4 25.9 %copy-start.4 = (pred[3,3]{1,0:T(4,128)(4,1)}, pred[3,3]{1,0:T(4,128)(4,1)S(1)}, u32[]{:S(2)}) copy-start(pred[3,3]{1,0:T(4,128)(4,1)S(1)} %fusion.96) | copy-start | bytes 31
  11.1 55.6 %collective-permute-start.3 = (f32[512]{0:T(512)}, f32[512]{0:T(512)}, u32[]{:S(2)}, u32[]{:S(2)}) collective-permute-start(f32[512]{0:T(512)} %bitcast.17), channel_id=1, source_target_pairs={{0,16},{8,24},{16,32},{24,40},{32,48},{40,56},{48,64},{56,72},{64,... | collective-permute-start | bytes 6152 | tf_op jit(solution)/shard_map/ppermute | solution.py:22
  16.0 50.8 %collective-permute-start.2 = (f32[512]{0:T(512)}, f32[512]{0:T(512)}, u32[]{:S(2)}, u32[]{:S(2)}) collective-permute-start(f32[512]{0:T(512)} %bitcast.16), channel_id=1, source_target_pairs={{0,8},{8,16},{16,24},{24,32},{32,40},{40,48},{48,56},{56,64},{64,7... | collective-permute-start | bytes 6152 | tf_op jit(solution)/shard_map/ppermute | solution.py:22
  19.1 106.1 %collective-permute-start.7 = (bf16[512,128]{0,1:T(8,128)(2,1)}, bf16[512,128]{0,1:T(8,128)(2,1)}, u32[]{:S(2)}, u32[]{:S(2)}) collective-permute-start(bf16[512,128]{0,1:T(8,128)(2,1)} %bitcast.28), channel_id=1, source_target_pairs={{0,8},{8,16},{16,24},{24,32},{32,40},{40,48},{48,56},{56,64},{64,7... | collective-permute-start | bytes 393224 | tf_op jit(solution)/shard_map/ppermute | solution.py:22
  28.3 32.4 %copy-start.2 = (bf16[8,512,128]{2,1,0:T(8,128)(2,1)S(1)}, bf16[8,512,128]{2,1,0:T(8,128)(2,1)}, u32[]{:S(2)}) copy-start(bf16[8,512,128]{2,1,0:T(8,128)(2,1)} %param.17) | copy-start | bytes 3145732
  30.4 37.0 %collective-permute-start.1 = (bf16[512,128]{1,0:T(8,128)(2,1)S(1)}, bf16[512,128]{1,0:T(8,128)(2,1)}, u32[]{:S(2)}, u32[]{:S(2)}) collective-permute-start(bf16[512,128]{1,0:T(8,128)(2,1)S(1)} %bitcast.324), channel_id=1, source_target_pairs={{0,16},{8,24},{16,32},{24,40},{32,48},{40,56},{48,64},{56,72},{64,... | collective-permute-start | bytes 393224 | tf_op jit(solution)/shard_map/ppermute | solution.py:22
  36.5 30.9 %collective-permute-start = (bf16[512,128]{1,0:T(8,128)(2,1)S(1)}, bf16[512,128]{1,0:T(8,128)(2,1)}, u32[]{:S(2)}, u32[]{:S(2)}) collective-permute-start(bf16[512,128]{1,0:T(8,128)(2,1)S(1)} %bitcast.325), channel_id=1, source_target_pairs={{0,8},{8,16},{16,24},{24,32},{32,40},{40,48},{48,56},{56,64},{64,7... | collective-permute-start | bytes 393224 | tf_op jit(solution)/shard_map/ppermute | solution.py:22
  38.4 29.0 %copy-start.3 = (bf16[1,1,512,128]{3,2,1,0:T(8,128)(2,1)S(1)}, bf16[1,1,512,128]{3,2,1,0:T(8,128)(2,1)}, u32[]{:S(2)}) copy-start(bf16[1,1,512,128]{3,2,1,0:T(8,128)(2,1)} %param.14) | copy-start | bytes 393220
  43.0 36.6 %copy-start.1 = (f32[8,512,16]{2,1,0:T(8,128)S(1)}, f32[8,512,16]{2,1,0:T(8,128)}, u32[]{:S(2)}) copy-start(f32[8,512,16]{2,1,0:T(8,128)} %constant_dynamic-slice_fusion.4) | copy-start | bytes 786436
  65.3 160.4 %copy-start.6 = (pred[16]{0:T(512)(128)(4,1)}, pred[16]{0:T(512)(128)(4,1)S(1)}, u32[]{:S(2)}) copy-start(pred[16]{0:T(512)(128)(4,1)S(1)} %add_compare_fusion) | copy-start | bytes 52
  68.5 14.8 %collective-permute-start.5 = (bf16[512,128]{1,0:T(8,128)(2,1)S(1)}, bf16[512,128]{1,0:T(8,128)(2,1)S(1)}, u32[]{:S(2)}, u32[]{:S(2)}) collective-permute-start(bf16[512,128]{1,0:T(8,128)(2,1)S(1)} %fusion.50), channel_id=1, source_target_pairs={{16,0},{24,8},{32,16},{40,24},{48,32},{56,40},{64,48},{72,56},{80,... | collective-permute-start | bytes 393224 | tf_op jit(solution)/shard_map/ppermute | solution.py:22
  72.9 10.5 %collective-permute-start.4 = (bf16[512,128]{1,0:T(8,128)(2,1)S(1)}, bf16[512,128]{1,0:T(8,128)(2,1)S(1)}, u32[]{:S(2)}, u32[]{:S(2)}) collective-permute-start(bf16[512,128]{1,0:T(8,128)(2,1)S(1)} %fusion.50), channel_id=1, source_target_pairs={{8,0},{16,8},{24,16},{32,24},{40,32},{48,40},{56,48},{64,56},{72,6... | collective-permute-start | bytes 393224 | tf_op jit(solution)/shard_map/ppermute | solution.py:22
  114.0 43.6 %copy-start.5 = (pred[3,3]{1,0:T(4,128)(4,1)S(1)}, pred[3,3]{1,0:T(4,128)(4,1)}, u32[]{:S(2)}) copy-start(pred[3,3]{1,0:T(4,128)(4,1)} %copy-done.4) | copy-start | bytes 31
  115.2 9.9 %collective-permute-start.10 = (f32[8,512]{1,0:T(8,128)S(1)}, f32[8,512]{1,0:T(8,128)S(1)}, u32[]{:S(2)}, u32[]{:S(2)}) collective-permute-start(f32[8,512]{1,0:T(8,128)S(1)} %get-tuple-element.33), channel_id=1, source_target_pairs={{0,1},{1,2},{2,3},{3,4},{4,5},{5,6},{6,7},{8,9},{9,10},{10,11},{11... | collective-permute-start | bytes 49160 | tf_op jit(solution)/shard_map/ppermute | solution.py:22
  117.6 13.5 %collective-permute-start.9 = (f32[8,512]{1,0:T(8,128)S(1)}, f32[8,512]{1,0:T(8,128)S(1)}, u32[]{:S(2)}, u32[]{:S(2)}) collective-permute-start(f32[8,512]{1,0:T(8,128)S(1)} %get-tuple-element.34), channel_id=1, source_target_pairs={{1,0},{2,1},{3,2},{4,3},{5,4},{6,5},{7,6},{9,8},{10,9},{11,10},{12... | collective-permute-start | bytes 49160 | tf_op jit(solution)/shard_map/ppermute | solution.py:22
  119.8 11.2 %collective-permute-start.6 = (f32[16,512]{1,0:T(8,128)S(1)}, f32[16,512]{1,0:T(8,128)S(1)}, u32[]{:S(2)}, u32[]{:S(2)}) collective-permute-start(f32[16,512]{1,0:T(8,128)S(1)} %bitcast.334), channel_id=1, source_target_pairs={{8,0},{16,8},{24,16},{32,24},{40,32},{48,40},{56,48},{64,56},{72,6... | collective-permute-start | bytes 98312 | tf_op jit(solution)/shard_map/ppermute | solution.py:22
  123.0 7.3 %collective-permute-start.8 = (f32[16,512]{1,0:T(8,128)S(1)}, f32[16,512]{1,0:T(8,128)S(1)}, u32[]{:S(2)}, u32[]{:S(2)}) collective-permute-start(f32[16,512]{1,0:T(8,128)S(1)} %bitcast.335), channel_id=1, source_target_pairs={{0,8},{8,16},{16,24},{24,32},{32,40},{40,48},{48,56},{56,64},{64,7... | collective-permute-start | bytes 98312 | tf_op jit(solution)/shard_map/ppermute | solution.py:22
  158.3 9.0 %collective-permute-start.11 = (bf16[512,128]{1,0:T(8,128)(2,1)S(1)}, bf16[512,128]{1,0:T(8,128)(2,1)S(1)}, u32[]{:S(2)}, u32[]{:S(2)}) collective-permute-start(bf16[512,128]{1,0:T(8,128)(2,1)S(1)} %get-tuple-element.14), channel_id=1, source_target_pairs={{0,8},{8,16},{16,24},{24,32},{32,40},{40,48},{48,56},{56,64},{64,7... | collective-permute-start | bytes 393224 | tf_op jit(solution)/shard_map/ppermute | solution.py:22
  160.2 9.3 %collective-permute-start.12 = (bf16[512,128]{1,0:T(8,128)(2,1)S(1)}, bf16[512,128]{1,0:T(8,128)(2,1)S(1)}, u32[]{:S(2)}, u32[]{:S(2)}) collective-permute-start(bf16[512,128]{1,0:T(8,128)(2,1)S(1)} %get-tuple-element.15), channel_id=1, source_target_pairs={{0,16},{8,24},{16,32},{24,40},{32,48},{40,56},{48,64},{56,72},{64,... | collective-permute-start | bytes 393224 | tf_op jit(solution)/shard_map/ppermute | solution.py:22
  169.6 7.2 %collective-permute-start.14 = (bf16[512,128]{1,0:T(8,128)(2,1)S(1)}, bf16[512,128]{1,0:T(8,128)(2,1)S(1)}, u32[]{:S(2)}, u32[]{:S(2)}) collective-permute-start(bf16[512,128]{1,0:T(8,128)(2,1)S(1)} %fusion.52), channel_id=1, source_target_pairs={{16,0},{24,8},{32,16},{40,24},{48,32},{56,40},{64,48},{72,56},{80,... | collective-permute-start | bytes 393224 | tf_op jit(solution)/shard_map/ppermute | solution.py:22
  171.6 8.8 %collective-permute-start.13 = (bf16[512,128]{1,0:T(8,128)(2,1)S(1)}, bf16[512,128]{1,0:T(8,128)(2,1)S(1)}, u32[]{:S(2)}, u32[]{:S(2)}) collective-permute-start(bf16[512,128]{1,0:T(8,128)(2,1)S(1)} %fusion.52), channel_id=1, source_target_pairs={{8,0},{16,8},{24,16},{32,24},{40,32},{48,40},{56,48},{64,56},{72,6... | collective-permute-start | bytes 393224 | tf_op jit(solution)/shard_map/ppermute | solution.py:22
  212.8 11.8 %collective-permute-start.18 = (f32[8,512]{1,0:T(8,128)S(1)}, f32[8,512]{1,0:T(8,128)S(1)}, u32[]{:S(2)}, u32[]{:S(2)}) collective-permute-start(f32[8,512]{1,0:T(8,128)S(1)} %get-tuple-element.21), channel_id=1, source_target_pairs={{0,1},{1,2},{2,3},{3,4},{4,5},{5,6},{6,7},{8,9},{9,10},{10,11},{11... | collective-permute-start | bytes 49160 | tf_op jit(solution)/shard_map/ppermute | solution.py:22
  215.0 10.7 %collective-permute-start.17 = (f32[8,512]{1,0:T(8,128)S(1)}, f32[8,512]{1,0:T(8,128)S(1)}, u32[]{:S(2)}, u32[]{:S(2)}) collective-permute-start(f32[8,512]{1,0:T(8,128)S(1)} %get-tuple-element.22), channel_id=1, source_target_pairs={{1,0},{2,1},{3,2},{4,3},{5,4},{6,5},{7,6},{9,8},{10,9},{11,10},{12... | collective-permute-start | bytes 49160 | tf_op jit(solution)/shard_map/ppermute | solution.py:22
  217.2 7.4 %collective-permute-start.16 = (f32[16,512]{1,0:T(8,128)S(1)}, f32[16,512]{1,0:T(8,128)S(1)}, u32[]{:S(2)}, u32[]{:S(2)}) collective-permute-start(f32[16,512]{1,0:T(8,128)S(1)} %get-tuple-element.23), channel_id=1, source_target_pairs={{0,8},{8,16},{16,24},{24,32},{32,40},{40,48},{48,56},{56,64},{64,7... | collective-permute-start | bytes 98312 | tf_op jit(solution)/shard_map/ppermute | solution.py:22
  219.9 5.7 %collective-permute-start.15 = (f32[16,512]{1,0:T(8,128)S(1)}, f32[16,512]{1,0:T(8,128)S(1)}, u32[]{:S(2)}, u32[]{:S(2)}) collective-permute-start(f32[16,512]{1,0:T(8,128)S(1)} %get-tuple-element.24), channel_id=1, source_target_pairs={{8,0},{16,8},{24,16},{32,24},{40,32},{48,40},{56,48},{64,56},{72,6... | collective-permute-start | bytes 98312 | tf_op jit(solution)/shard_map/ppermute | solution.py:22
  252.3 9.8 %collective-permute-start.19 = (bf16[512,128]{1,0:T(8,128)(2,1)S(1)}, bf16[512,128]{1,0:T(8,128)(2,1)S(1)}, u32[]{:S(2)}, u32[]{:S(2)}) collective-permute-start(bf16[512,128]{1,0:T(8,128)(2,1)S(1)} %get-tuple-element.12), channel_id=1, source_target_pairs={{0,8},{8,16},{16,24},{24,32},{32,40},{40,48},{48,56},{56,64},{64,7... | collective-permute-start | bytes 393224 | tf_op jit(solution)/shard_map/ppermute | solution.py:22
  255.2 10.6 %collective-permute-start.20 = (bf16[512,128]{1,0:T(8,128)(2,1)S(1)}, bf16[512,128]{1,0:T(8,128)(2,1)S(1)}, u32[]{:S(2)}, u32[]{:S(2)}) collective-permute-start(bf16[512,128]{1,0:T(8,128)(2,1)S(1)} %get-tuple-element.13), channel_id=1, source_target_pairs={{0,16},{8,24},{16,32},{24,40},{32,48},{40,56},{48,64},{56,72},{64,... | collective-permute-start | bytes 393224 | tf_op jit(solution)/shard_map/ppermute | solution.py:22
  266.6 7.2 %collective-permute-start.22 = (bf16[512,128]{1,0:T(8,128)(2,1)S(1)}, bf16[512,128]{1,0:T(8,128)(2,1)S(1)}, u32[]{:S(2)}, u32[]{:S(2)}) collective-permute-start(bf16[512,128]{1,0:T(8,128)(2,1)S(1)} %get-tuple-element.9), channel_id=1, source_target_pairs={{16,0},{24,8},{32,16},{40,24},{48,32},{56,40},{64,48},{72,56},{80,... | collective-permute-start | bytes 393224 | tf_op jit(solution)/shard_map/ppermute | solution.py:22
  270.3 5.7 %collective-permute-start.21 = (bf16[512,128]{1,0:T(8,128)(2,1)S(1)}, bf16[512,128]{1,0:T(8,128)(2,1)S(1)}, u32[]{:S(2)}, u32[]{:S(2)}) collective-permute-start(bf16[512,128]{1,0:T(8,128)(2,1)S(1)} %get-tuple-element.9), channel_id=1, source_target_pairs={{8,0},{16,8},{24,16},{32,24},{40,32},{48,40},{56,48},{64,56},{72,6... | collective-permute-start | bytes 393224 | tf_op jit(solution)/shard_map/ppermute | solution.py:22
  276.5 48.2 %copy-start.7 = (pred[16]{0:T(512)(128)(4,1)S(1)}, pred[16]{0:T(512)(128)(4,1)}, u32[]{:S(2)}) copy-start(pred[16]{0:T(512)(128)(4,1)} %copy-done.6) | copy-start | bytes 52
  309.8 12.5 %collective-permute-start.26 = (f32[8,512]{1,0:T(8,128)S(1)}, f32[8,512]{1,0:T(8,128)S(1)}, u32[]{:S(2)}, u32[]{:S(2)}) collective-permute-start(f32[8,512]{1,0:T(8,128)S(1)} %bitcast.340), channel_id=1, source_target_pairs={{0,1},{1,2},{2,3},{3,4},{4,5},{5,6},{6,7},{8,9},{9,10},{10,11},{11... | collective-permute-start | bytes 49160 | tf_op jit(solution)/shard_map/ppermute | solution.py:22
  312.2 10.1 %collective-permute-start.24 = (f32[16,512]{1,0:T(8,128)S(1)}, f32[16,512]{1,0:T(8,128)S(1)}, u32[]{:S(2)}, u32[]{:S(2)}) collective-permute-start(f32[16,512]{1,0:T(8,128)S(1)} %get-tuple-element.16), channel_id=1, source_target_pairs={{0,8},{8,16},{16,24},{24,32},{32,40},{40,48},{48,56},{56,64},{64,7... | collective-permute-start | bytes 98312 | tf_op jit(solution)/shard_map/ppermute | solution.py:22
  314.6 8.6 %collective-permute-start.23 = (f32[16,512]{1,0:T(8,128)S(1)}, f32[16,512]{1,0:T(8,128)S(1)}, u32[]{:S(2)}, u32[]{:S(2)}) collective-permute-start(f32[16,512]{1,0:T(8,128)S(1)} %get-tuple-element.17), channel_id=1, source_target_pairs={{8,0},{16,8},{24,16},{32,24},{40,32},{48,40},{56,48},{64,56},{72,6... | collective-permute-start | bytes 98312 | tf_op jit(solution)/shard_map/ppermute | solution.py:22
  319.6 5.1 %collective-permute-start.25 = (f32[8,512]{1,0:T(8,128)S(1)}, f32[8,512]{1,0:T(8,128)S(1)}, u32[]{:S(2)}, u32[]{:S(2)}) collective-permute-start(f32[8,512]{1,0:T(8,128)S(1)} %slice_bitcast_fusion.10), channel_id=1, source_target_pairs={{1,0},{2,1},{3,2},{4,3},{5,4},{6,5},{7,6},{9,8},{10,9},{11,10},{12... | collective-permute-start | bytes 49160 | tf_op jit(solution)/shard_map/ppermute | solution.py:22

commit v2 on v1

--- a/solution.py
+++ b/solution.py
@@ -159,6 +159,53 @@
             transcendentals=0,
         ),
     )(part)
+
+
+def _slab_kernel(shifts, send_ref, out_ref, got, send_sem, recv_sem):
+    slab = lax.axis_index("slab")
+    here = lax.axis_index("angle")
+    count = lax.axis_size("slab")
+    barrier = pltpu.get_barrier_semaphore()
+    for shift in shifts:
+        sender = (slab - shift + count) % count
+        pl.semaphore_signal(barrier, 1, device_id=(sender, here), device_id_type=MESH_ID)
+    pl.semaphore_wait(barrier, len(shifts))
+    copies = []
+    for i, shift in enumerate(shifts):
+        copy = pltpu.make_async_remote_copy(
+            src_ref=send_ref.at[i if send_ref.shape[0] > 1 else 0],
+            dst_ref=got.at[i],
+            send_sem=send_sem.at[i],
+            recv_sem=recv_sem.at[i],
+            device_id=((slab + shift + count) % count, here),
+            device_id_type=MESH_ID,
+        )
+        copy.start()
+        copies.append(copy)
+    for copy in copies:
+        copy.wait()
+    out_ref[...] = got[...]
+
+
+def exchange_slab(send, shifts, collective_id):
+    rows, cols = send.shape[1:]
+    moves = len(shifts)
+    return pl.pallas_call(
+        functools.partial(_slab_kernel, shifts),
+        out_shape=jax.ShapeDtypeStruct((moves, rows, cols), send.dtype),
+        in_specs=[pl.BlockSpec(memory_space=pltpu.VMEM)],
+        out_specs=pl.BlockSpec(memory_space=pltpu.VMEM),
+        scratch_shapes=[
+            pltpu.VMEM((moves, rows, cols), send.dtype),
+            pltpu.SemaphoreType.DMA((moves,)),
+            pltpu.SemaphoreType.DMA((moves,)),
+        ],
+        compiler_params=pltpu.CompilerParams(collective_id=collective_id, has_side_effects=True),
+        cost_estimate=pl.CostEstimate(
+            flops=0, bytes_accessed=4 * moves * rows * cols * send.dtype.itemsize,
+            transcendentals=0,
+        ),
+    )(send)
 
 
 def _gather_kernel(n_chip, own_ref, out_ref, held, send_a, recv_a, send_b, recv_b, local_sem):
@@ -331,17 +378,17 @@
             "td,trn->drn", relative_half, products, preferred_element_type=jnp.float32
         )
         sends_half = sends.astype(jnp.bfloat16)
+        shifts = tuple(range(1, slot_count))
+        arrived = exchange_slab(sends_half[1:], shifts, 3)
         projected = sends[0]
         for distance in range(1, slot_count):
-            arrived = from_behind(sends_half[distance], "slab", distance)
-            projected = projected + arrived.astype(jnp.float32)
+            projected = projected + arrived[distance - 1].astype(jnp.float32)
         residual = (measured - projected) * ray_scale[:, None]
         residual_half = residual.astype(jnp.bfloat16)
-        nearby = [residual_half] + [
-            from_behind(residual_half, "slab", -distance) for distance in range(1, slot_count)
-        ]
+        returned = exchange_slab(residual_half[None], tuple(-s for s in shifts), 4)
+        nearby = jnp.concatenate([residual_half[None], returned], axis=0)
         picked = jnp.einsum(
-            "td,drn->trn", relative_half, jnp.stack(nearby), preferred_element_type=jnp.float32
+            "td,drn->trn", relative_half, nearby, preferred_element_type=jnp.float32
         ).astype(jnp.bfloat16)
         back_t = jnp.einsum("trn,trv->nv", picked, tiles, preferred_element_type=jnp.float32)
         back_own = scatter_angle(back_t.reshape(groups, share_width, voxels))

time: 328 us -> 346 us (1.055)
  Pallas kernels: 107 us -> 168 us
  starting transfers between devices: 85.1 us -> 48.6 us
  waiting for transfers between devices: 25.6 us -> 6.72 us
  other arithmetic: 10.3 us -> 21.5 us
    pallas_call x0 -> x6, Pallas kernels: none -> 59 us  [exchange_slab(): pl.pallas_call(functools.partial(_slab_kernel, shifts), out_shape=jax.Sha...]
    ppermute x27 -> x15, starting transfers between devices: 85.1 us -> 48.6 us  [from_behind(): lax.ppermute(value, axis, [(source, source + steps) for source in range(f...]
    ppermute x27 -> x15, waiting for transfers between devices: 25.6 us -> 6.72 us  [from_behind(): lax.ppermute(value, axis, [(source, source + steps) for source in range(f...]
    convert_element_type x2 -> x3, other arithmetic: 1.23 us -> 5.28 us  [shards(): residual_half = residual.astype(jnp.bfloat16)]
    unnamed x31 -> x40, local copies, waits for them, and re-layouts: 11.8 us -> 14.6 us
  transfers between devices with their start and end apart: 27 -> 15, of which waited for: 11 -> 2; matrix products, arithmetic and copies ran while one was open for 15% -> 16% of each run, Pallas kernels for 9% -> 15%
where the time goes in v2:
time: 346 us; the launch traced here: 345 us
  Pallas kernels  168 us (49%)
  matrix products  68.2 us (20%)
  starting transfers between devices  48.6 us (14%)
  local copies, waits for them, and re-layouts  29.6 us (9%)
  other arithmetic  21.5 us (6%)
  waiting for transfers between devices  6.72 us (2%)
    pallas_call x3, Pallas kernels, scatter_angle(): pl.pallas_call(functools.partial(_scatter_kernel, n_chip), out_shape=jax....  69.1 us
    pallas_call x6, Pallas kernels, exchange_slab(): pl.pallas_call(functools.partial(_slab_kernel, shifts), out_shape=jax.Sha...  59 us
    ppermute x15, starting transfers between devices, from_behind(): lax.ppermute(value, axis, [(source, source + steps) for source in range(f...  48.6 us
    pallas_call x2, Pallas kernels, gather_angle(): pl.pallas_call(functools.partial(_gather_kernel, n_chip), out_shape=jax.S...  30.4 us
    dot_general x3, matrix products, shards(): jnp.einsum('trn,trv->nv', picked, tiles, preferred_element_type=jnp.float32)  23.2 us
    dot_general x2, matrix products, shards(): jnp.einsum('trv,nv->trn', tiles, gathered, preferred_element_type=jnp.flo...  18.4 us
    unnamed x40, local copies, waits for them, and re-layouts  14.6 us
    pallas_call x1, Pallas kernels, sum_angle(): pl.pallas_call(functools.partial(_sum_kernel, groups), out_shape=jax.Shap...  9.04 us
  transfers between devices with their start and end apart: 15, of which 2 were waited for; matrix products, arithmetic and copies ran while one was open for 16% of the time, Pallas kernels for 15%

profile of v2, /device:TPU:33, one launch (start us, length us, event | category | flops | bytes accessed | tf_op | source)
XLA Modules:
  0.0 344.7 jit_solution(7726997306185252391)
XLA Ops:
  1.5 1.0 select_reduce_fusion
  2.6 7.9 %fusion.13 = bf16[1,3,512]{2,0,1:T(2,128)(2,1)S(1)} fusion(bf16[1,1,3,512,4096]{4,3,2,1,0:T(8,128)(2,1)} %param.10), kind=kOutput, calls=%fused_computation.13 | convolution fusion | flops 12582912 | bytes 12585984 | tf_op jit(solution)/shard_map/dot_general | solution.py:331
  11.3 4.8 %collective-permute-start.1 = (f32[512]{0:T(512)}, f32[512]{0:T(512)}, u32[]{:S(2)}, u32[]{:S(2)}) collective-permute-start(f32[512]{0:T(512)} %bitcast.16), channel_id=1, source_target_pairs={{0,16},{8,24},{16,32},{24,40},{32,48},{40,56},{48,64},{56,72},{64,... | collective-permute-start | bytes 6152 | tf_op jit(solution)/shard_map/ppermute | solution.py:22
  16.1 2.3 collective-permute-start
  18.5 0.8 copy.160
  19.2 2.8 collective-permute-start.3
  23.7 1.2 convert_element_type.174
  24.9 1.4 constant_dynamic-slice_fusion.3
  26.2 2.0 constant_dynamic-slice_fusion.4
  28.3 5.6 %fusion = f32[1,8,512]{2,0,1:T(1,128)S(1)} fusion(pred[1536,1,1]{0,1,2:T(4,128)(4,1)S(1)} %reshape.134, bf16[192,8,8,512]{3,2,1,0:T(8,128)(2,1)} %bitcast.266), kind=kOutput, calls=%fused_computation | convolution fusion | flops 12582912 | bytes 12600832 | tf_op jit(solution)/shard_map/dot_general | solution.py:339
  34.5 9.0 %shard_map.104 = f32[8,512]{1,0:T(8,128)} custom-call(f32[8,512]{1,0:T(8,128)} %bitcast.285), custom_call_target="tpu_custom_call" | custom-call | flops 32768 | bytes 262144 | tf_op jit(solution)/shard_map/pallas_call | solution.py:146
  44.3 8.4 %fusion.26 = bf16[3,512,128]{2,1,0:T(8,128)(2,1)S(1)} fusion(bf16[4096,128,1]{1,0,2:T(8,128)(2,1)} %bitcast.278, bf16[1,1,3,512,4096]{4,3,2,1,0:T(8,128)(2,1)} %param.10), kind=kOutput, calls=%fused_computation.23 | convolution fusion | flops 1610809344 | bytes 14024704 | tf_op jit(solution)/shard_map/trv,vn->trn/dot_general | solution.py:370
  52.7 1.5 fusion.47
  54.3 1.3 constant_dynamic-slice_fusion
  55.6 3.3 constant_dynamic-slice_fusion.1
  59.4 1.5 slice.191
  60.9 2.2 copy.164
  63.8 12.9 %shard_map.105 = bf16[2,512,128]{2,1,0:T(8,128)(2,1)} custom-call(bf16[2,512,128]{2,1,0:T(8,128)(2,1)} %copy.239.send_ref), custom_call_target="tpu_custom_call" | custom-call | bytes 1048576 | tf_op jit(solution)/shard_map/pallas_call | solution.py:193
  76.8 1.6 copy.158
  79.0 1.6 copy.163
  80.6 1.6 copy.162
  82.9 1.8 fusion.53.send_ref
  84.7 7.0 %shard_map.106 = bf16[2,512,128]{2,1,0:T(8,128)(2,1)} custom-call(bf16[1,512,128]{2,1,0:T(8,128)(2,1)} %fusion.53.send_ref), custom_call_target="tpu_custom_call" | custom-call | bytes 1048576 | tf_op jit(solution)/shard_map/pallas_call | solution.py:193
  91.6 1.0 pad_maximum_fusion
  92.7 1.0 fusion.35
  94.0 7.7 %fusion.17.part_ref.half_ref = f32[8,16,4096]{2,1,0:T(8,128)} fusion(bf16[8,16,512,3]{2,1,0,3:T(8,128)(2,1)S(1)} %bitcast.275, bf16[1,1,3,512,4096]{4,3,2,1,0:T(8,128)(2,1)} %param.10), kind=kOutput, calls=%fused_computation.17 | convolution fusion | flops 1610612736 | bytes 15073280 | tf_op jit(solution)/shard_map/trn,trv->nv/dot_general | solution.py:393
  101.8 23.4 %shard_map.107 = f32[16,4096]{1,0:T(8,128)} custom-call(f32[8,16,4096]{2,1,0:T(8,128)} %fusion.17.part_ref.half_ref, f32[8,16,4096]{2,1,0:T(8,128)} %fusion.17.part_ref.half_ref), custom_call_target="tpu_custom_call" | custom-call | flops 1048576 | bytes 6291456 | tf_op jit(solution)/shard_map/pallas_call | solution.py:95
  125.2 1.1 copy.173
  126.4 2.4 collective-permute-start.6
  129.1 2.1 collective-permute-start.5
  131.2 6.2 %collective-permute-start.2 = (f32[16,512]{1,0:T(8,128)S(1)}, f32[16,512]{1,0:T(8,128)S(1)}, u32[]{:S(2)}, u32[]{:S(2)}) collective-permute-start(f32[16,512]{1,0:T(8,128)S(1)} %bitcast.289), channel_id=1, source_target_pairs={{8,0},{16,8},{24,16},{32,24},{40,32},{48,40},{56,48},{64,56},{72,6... | collective-permute-start | bytes 98312 | tf_op jit(solution)/shard_map/ppermute | solution.py:22
  137.4 1.9 collective-permute-start.4
  139.8 4.9 %collective-permute-done.4 = f32[16,512]{1,0:T(8,128)S(1)} collective-permute-done((f32[16,512]{1,0:T(8,128)S(1)}, f32[16,512]{1,0:T(8,128)S(1)}, u32[]{:S(2)}, u32[]{:S(2)}) %collective-permute-start.4) | collective-permute-done | bytes 32800 | tf_op jit(solution)/shard_map/ppermute | solution.py:22
  146.4 15.8 %shard_map.108 = bf16[8,16,4096]{2,1,0:T(8,128)(2,1)} custom-call(bf16[16,4096]{1,0:T(8,128)(2,1)} %bitcast.283), custom_call_target="tpu_custom_call" | custom-call | bytes 2097152 | tf_op jit(solution)/shard_map/pallas_call | solution.py:252
  162.2 9.2 %fusion.38 = bf16[3,512,128]{1,2,0:T(8,128)(2,1)S(1)} fusion(bf16[128,4096,1]{1,0,2:T(8,128)(2,1)} %bitcast.267, bf16[1,1,3,512,4096]{4,3,2,1,0:T(8,128)(2,1)} %param.10), kind=kOutput, calls=%fused_computation.29 | convolution fusion | flops 1610809344 | bytes 14024704 | tf_op jit(solution)/shard_map/trv,nv->trn/dot_general | solution.py:374
  173.4 11.9 %shard_map.109 = bf16[2,512,128]{2,1,0:T(8,128)(2,1)} custom-call(bf16[2,512,128]{2,1,0:T(8,128)(2,1)} %copy.238.send_ref), custom_call_target="tpu_custom_call" | custom-call | bytes 1048576 | tf_op jit(solution)/shard_map/pallas_call | solution.py:193
  185.3 1.8 fusion.55.send_ref
  187.1 7.0 %shard_map.110 = bf16[2,512,128]{2,1,0:T(8,128)(2,1)} custom-call(bf16[1,512,128]{2,1,0:T(8,128)(2,1)} %fusion.55.send_ref), custom_call_target="tpu_custom_call" | custom-call | bytes 1048576 | tf_op jit(solution)/shard_map/pallas_call | solution.py:193
  194.1 1.0 pad_maximum_fusion.1
  195.8 7.7 %fusion.20.part_ref.half_ref = f32[8,16,4096]{2,1,0:T(8,128)} fusion(bf16[8,16,512,3]{2,1,0,3:T(8,128)(2,1)S(1)} %bitcast.276, bf16[1,1,3,512,4096]{4,3,2,1,0:T(8,128)(2,1)} %param.10), kind=kOutput, calls=%fused_computation.18 | convolution fusion | flops 1610612736 | bytes 15073280 | tf_op jit(solution)/shard_map/trn,trv->nv/dot_general | solution.py:393
  203.6 22.8 %shard_map.111 = f32[16,4096]{1,0:T(8,128)} custom-call(f32[8,16,4096]{2,1,0:T(8,128)} %fusion.20.part_ref.half_ref, f32[8,16,4096]{2,1,0:T(8,128)} %fusion.20.part_ref.half_ref), custom_call_target="tpu_custom_call" | custom-call | flops 1048576 | bytes 6291456 | tf_op jit(solution)/shard_map/pallas_call | solution.py:95
  226.4 1.1 copy.175
  228.0 2.2 collective-permute-start.10
  230.2 2.1 collective-permute-start.9
  232.3 4.0 %collective-permute-start.8 = (f32[16,512]{1,0:T(8,128)S(1)}, f32[16,512]{1,0:T(8,128)S(1)}, u32[]{:S(2)}, u32[]{:S(2)}) collective-permute-start(f32[16,512]{1,0:T(8,128)S(1)} %get-tuple-element.11), channel_id=1, source_target_pairs={{0,8},{8,16},{16,24},{24,32},{32,40},{40,48},{48,56},{56,64},{64,7... | collective-permute-start | bytes 98312 | tf_op jit(solution)/shard_map/ppermute | solution.py:22
  236.4 4.7 %collective-permute-start.7 = (f32[16,512]{1,0:T(8,128)S(1)}, f32[16,512]{1,0:T(8,128)S(1)}, u32[]{:S(2)}, u32[]{:S(2)}) collective-permute-start(f32[16,512]{1,0:T(8,128)S(1)} %get-tuple-element.12), channel_id=1, source_target_pairs={{8,0},{16,8},{24,16},{32,24},{40,32},{48,40},{56,48},{64,56},{72,6... | collective-permute-start | bytes 98312 | tf_op jit(solution)/shard_map/ppermute | solution.py:22
  241.1 0.7 fusion.91
  243.4 14.6 %shard_map.112 = bf16[8,16,4096]{2,1,0:T(8,128)(2,1)} custom-call(bf16[16,4096]{1,0:T(8,128)(2,1)} %bitcast.284), custom_call_target="tpu_custom_call" | custom-call | bytes 2097152 | tf_op jit(solution)/shard_map/pallas_call | solution.py:252
  258.0 9.2 %fusion.41 = bf16[3,512,128]{1,2,0:T(8,128)(2,1)S(1)} fusion(bf16[128,4096,1]{1,0,2:T(8,128)(2,1)} %bitcast.268, bf16[1,1,3,512,4096]{4,3,2,1,0:T(8,128)(2,1)} %param.10), kind=kOutput, calls=%fused_computation.30 | convolution fusion | flops 1610809344 | bytes 14024704 | tf_op jit(solution)/shard_map/trv,nv->trn/dot_general | solution.py:374
  269.3 13.3 %shard_map.113 = bf16[2,512,128]{2,1,0:T(8,128)(2,1)} custom-call(bf16[2,512,128]{2,1,0:T(8,128)(2,1)} %copy.237.send_ref), custom_call_target="tpu_custom_call" | custom-call | bytes 1048576 | tf_op jit(solution)/shard_map/pallas_call | solution.py:193
  282.6 1.8 fusion.57.send_ref
  284.4 1.8 fusion.58
  286.2 7.0 %shard_map.114 = bf16[2,512,128]{2,1,0:T(8,128)(2,1)} custom-call(bf16[1,512,128]{2,1,0:T(8,128)(2,1)} %fusion.57.send_ref), custom_call_target="tpu_custom_call" | custom-call | bytes 1048576 | tf_op jit(solution)/shard_map/pallas_call | solution.py:193
  293.2 1.0 pad_maximum_fusion.2
  294.9 7.7 %fusion.23.part_ref.half_ref = f32[8,16,4096]{2,1,0:T(8,128)} fusion(bf16[8,16,512,3]{2,1,0,3:T(8,128)(2,1)S(1)} %bitcast.277, bf16[1,1,3,512,4096]{4,3,2,1,0:T(8,128)(2,1)} %param.10), kind=kOutput, calls=%fused_computation.19 | convolution fusion | flops 1610612736 | bytes 15073280 | tf_op jit(solution)/shard_map/trn,trv->nv/dot_general | solution.py:393
  302.7 22.8 %shard_map.115 = f32[16,4096]{1,0:T(8,128)} custom-call(f32[8,16,4096]{2,1,0:T(8,128)} %fusion.23.part_ref.half_ref, f32[8,16,4096]{2,1,0:T(8,128)} %fusion.23.part_ref.half_ref), custom_call_target="tpu_custom_call" | custom-call | flops 1048576 | bytes 6291456 | tf_op jit(solution)/shard_map/pallas_call | solution.py:95
  325.5 1.1 copy.176
  327.3 2.2 collective-permute-start.14
  329.7 4.4 %collective-permute-start.12 = (f32[16,512]{1,0:T(8,128)S(1)}, f32[16,512]{1,0:T(8,128)S(1)}, u32[]{:S(2)}, u32[]{:S(2)}) collective-permute-start(f32[16,512]{1,0:T(8,128)S(1)} %get-tuple-element.4), channel_id=1, source_target_pairs={{0,8},{8,16},{16,24},{24,32},{32,40},{40,48},{48,56},{56,64},{64,7... | collective-permute-start | bytes 98312 | tf_op jit(solution)/shard_map/ppermute | solution.py:22
  334.1 4.0 %collective-permute-start.11 = (f32[16,512]{1,0:T(8,128)S(1)}, f32[16,512]{1,0:T(8,128)S(1)}, u32[]{:S(2)}, u32[]{:S(2)}) collective-permute-start(f32[16,512]{1,0:T(8,128)S(1)} %get-tuple-element.5), channel_id=1, source_target_pairs={{8,0},{16,8},{24,16},{32,24},{40,32},{48,40},{56,48},{64,56},{72,6... | collective-permute-start | bytes 98312 | tf_op jit(solution)/shard_map/ppermute | solution.py:22
  338.2 2.4 collective-permute-start.13
  340.6 0.7 fusion.92
  341.5 1.7 collective-permute-done.13
  343.8 0.9 fusion.88
  (119 shorter events, 18.1 us)
Async XLA Ops:
  0.6 17.8 %slice-start.1 = ((bf16[8,512,128]{2,1,0:T(8,128)(2,1)}), bf16[1,512,128]{2,1,0:T(8,128)(2,1)S(1)}, s32[]{:S(2)}) async-start(bf16[8,512,128]{2,1,0:T(8,128)(2,1)} %param.15), calls=%async_computation.1 | async-start | bytes 262144 | tf_op jit(solution)/shard_map/slice | solution.py:343
  0.6 24.2 %copy-start.4 = (bf16[8,512,128]{2,1,0:T(8,128)(2,1)S(1)}, bf16[8,512,128]{2,1,0:T(8,128)(2,1)}, u32[]{:S(2)}) copy-start(bf16[8,512,128]{2,1,0:T(8,128)(2,1)} %param.15) | copy-start | bytes 3145732
  0.7 23.1 %copy-start = (f32[8,512,128]{2,1,0:T(8,128)S(1)}, f32[8,512,128]{2,1,0:T(8,128)}, u32[]{:S(2)}) copy-start(f32[8,512,128]{2,1,0:T(8,128)} %param.9) | copy-start | bytes 6291460
  2.6 50.1 %copy-start.7 = (pred[3,3]{1,0:T(4,128)(4,1)}, pred[3,3]{1,0:T(4,128)(4,1)S(1)}, u32[]{:S(2)}) copy-start(pred[3,3]{1,0:T(4,128)(4,1)S(1)} %fusion.100) | copy-start | bytes 31
  11.3 70.9 %collective-permute-start.1 = (f32[512]{0:T(512)}, f32[512]{0:T(512)}, u32[]{:S(2)}, u32[]{:S(2)}) collective-permute-start(f32[512]{0:T(512)} %bitcast.16), channel_id=1, source_target_pairs={{0,16},{8,24},{16,32},{24,40},{32,48},{40,56},{48,64},{56,72},{64,... | collective-permute-start | bytes 6152 | tf_op jit(solution)/shard_map/ppermute | solution.py:22
  16.1 66.0 %collective-permute-start = (f32[512]{0:T(512)}, f32[512]{0:T(512)}, u32[]{:S(2)}, u32[]{:S(2)}) collective-permute-start(f32[512]{0:T(512)} %bitcast.15), channel_id=1, source_target_pairs={{0,8},{8,16},{16,24},{24,32},{32,40},{40,48},{48,56},{56,64},{64,7... | collective-permute-start | bytes 6152 | tf_op jit(solution)/shard_map/ppermute | solution.py:22
  19.2 125.5 %collective-permute-start.3 = (bf16[512,128]{0,1:T(8,128)(2,1)}, bf16[512,128]{0,1:T(8,128)(2,1)}, u32[]{:S(2)}, u32[]{:S(2)}) collective-permute-start(bf16[512,128]{0,1:T(8,128)(2,1)} %bitcast.24), channel_id=1, source_target_pairs={{0,8},{8,16},{16,24},{24,32},{32,40},{40,48},{48,56},{56,64},{64,7... | collective-permute-start | bytes 393224 | tf_op jit(solution)/shard_map/ppermute | solution.py:22
  28.3 26.0 %copy-start.2 = (bf16[8,512,128]{2,1,0:T(8,128)(2,1)S(1)}, bf16[8,512,128]{2,1,0:T(8,128)(2,1)}, u32[]{:S(2)}) copy-start(bf16[8,512,128]{2,1,0:T(8,128)(2,1)} %param.17) | copy-start | bytes 3145732
  44.3 34.1 %copy-start.1 = (f32[8,512,16]{2,1,0:T(8,128)S(1)}, f32[8,512,16]{2,1,0:T(8,128)}, u32[]{:S(2)}) copy-start(f32[8,512,16]{2,1,0:T(8,128)} %constant_dynamic-slice_fusion.4) | copy-start | bytes 786436
  44.3 38.6 %copy-start.3 = (bf16[1,1,512,128]{3,2,1,0:T(8,128)(2,1)S(1)}, bf16[1,1,512,128]{3,2,1,0:T(8,128)(2,1)}, u32[]{:S(2)}) copy-start(bf16[1,1,512,128]{3,2,1,0:T(8,128)(2,1)} %param.14) | copy-start | bytes 393220
  54.3 28.6 %slice-start = ((f32[3,512,128]{2,0,1:T(4,128)}), f32[1,512,128]{2,0,1:T(1,128)S(1)}, s32[]{:S(2)}) async-start(f32[3,512,128]{2,0,1:T(4,128)} %fusion.47), calls=%async_computation | async-start | bytes 524288 | tf_op jit(solution)/shard_map/slice | solution.py:383
  92.7 46.7 %copy-start.5 = (bf16[8,512,1]{1,0,2:T(8,128)(2,1)S(1)}, bf16[8,512,1]{1,0,2:T(8,128)(2,1)}, u32[]{:S(2)}) copy-start(bf16[8,512,1]{1,0,2:T(8,128)(2,1)} %copy.164) | copy-start | bytes 24580
  92.7 46.8 %copy-start.9 = (pred[16]{0:T(512)(128)(4,1)S(1)}, pred[16]{0:T(512)(128)(4,1)}, u32[]{:S(2)}) copy-start(pred[16]{0:T(512)(128)(4,1)} %add_compare_fusion) | copy-start | bytes 52
  92.7 46.8 %copy-start.10 = (pred[8]{0:T(512)(128)(4,1)S(1)}, pred[8]{0:T(512)(128)(4,1)}, u32[]{:S(2)}) copy-start(pred[8]{0:T(512)(128)(4,1)} %add_compare_fusion.1) | copy-start | bytes 28
  92.7 46.8 %copy-start.11 = (pred[512]{0:T(512)(128)(4,1)S(1)}, pred[512]{0:T(512)(128)(4,1)}, u32[]{:S(2)}) copy-start(pred[512]{0:T(512)(128)(4,1)} %iota_compare_fusion) | copy-start | bytes 1540
  125.2 46.5 %copy-start.8 = (pred[3,3]{1,0:T(4,128)(4,1)S(1)}, pred[3,3]{1,0:T(4,128)(4,1)}, u32[]{:S(2)}) copy-start(pred[3,3]{1,0:T(4,128)(4,1)} %copy-done.7) | copy-start | bytes 31
  126.4 12.9 %collective-permute-start.6 = (f32[8,512]{1,0:T(8,128)S(1)}, f32[8,512]{1,0:T(8,128)S(1)}, u32[]{:S(2)}, u32[]{:S(2)}) collective-permute-start(f32[8,512]{1,0:T(8,128)S(1)} %get-tuple-element.21), channel_id=1, source_target_pairs={{0,1},{1,2},{2,3},{3,4},{4,5},{5,6},{6,7},{8,9},{9,10},{10,11},{11... | collective-permute-start | bytes 49160 | tf_op jit(solution)/shard_map/ppermute | solution.py:22
  129.1 10.4 %collective-permute-start.5 = (f32[8,512]{1,0:T(8,128)S(1)}, f32[8,512]{1,0:T(8,128)S(1)}, u32[]{:S(2)}, u32[]{:S(2)}) collective-permute-start(f32[8,512]{1,0:T(8,128)S(1)} %get-tuple-element.22), channel_id=1, source_target_pairs={{1,0},{2,1},{3,2},{4,3},{5,4},{6,5},{7,6},{9,8},{10,9},{11,10},{12... | collective-permute-start | bytes 49160 | tf_op jit(solution)/shard_map/ppermute | solution.py:22
  131.2 8.2 %collective-permute-start.2 = (f32[16,512]{1,0:T(8,128)S(1)}, f32[16,512]{1,0:T(8,128)S(1)}, u32[]{:S(2)}, u32[]{:S(2)}) collective-permute-start(f32[16,512]{1,0:T(8,128)S(1)} %bitcast.289), channel_id=1, source_target_pairs={{8,0},{16,8},{24,16},{32,24},{40,32},{48,40},{56,48},{64,56},{72,6... | collective-permute-start | bytes 98312 | tf_op jit(solution)/shard_map/ppermute | solution.py:22
  137.4 7.3 %collective-permute-start.4 = (f32[16,512]{1,0:T(8,128)S(1)}, f32[16,512]{1,0:T(8,128)S(1)}, u32[]{:S(2)}, u32[]{:S(2)}) collective-permute-start(f32[16,512]{1,0:T(8,128)S(1)} %bitcast.286), channel_id=1, source_target_pairs={{0,8},{8,16},{16,24},{24,32},{32,40},{40,48},{48,56},{56,64},{64,7... | collective-permute-start | bytes 98312 | tf_op jit(solution)/shard_map/ppermute | solution.py:22
  195.1 46.8 %copy-start.6 = (f32[512]{0:T(512)S(1)}, f32[512]{0:T(512)}, u32[]{:S(2)}) copy-start(f32[512]{0:T(512)} %fusion.109) | copy-start | bytes 6148
  228.0 13.1 %collective-permute-start.10 = (f32[8,512]{1,0:T(8,128)S(1)}, f32[8,512]{1,0:T(8,128)S(1)}, u32[]{:S(2)}, u32[]{:S(2)}) collective-permute-start(f32[8,512]{1,0:T(8,128)S(1)} %get-tuple-element.9), channel_id=1, source_target_pairs={{0,1},{1,2},{2,3},{3,4},{4,5},{5,6},{6,7},{8,9},{9,10},{10,11},{11... | collective-permute-start | bytes 49160 | tf_op jit(solution)/shard_map/ppermute | solution.py:22
  230.2 11.7 %collective-permute-start.9 = (f32[8,512]{1,0:T(8,128)S(1)}, f32[8,512]{1,0:T(8,128)S(1)}, u32[]{:S(2)}, u32[]{:S(2)}) collective-permute-start(f32[8,512]{1,0:T(8,128)S(1)} %get-tuple-element.10), channel_id=1, source_target_pairs={{1,0},{2,1},{3,2},{4,3},{5,4},{6,5},{7,6},{9,8},{10,9},{11,10},{12... | collective-permute-start | bytes 49160 | tf_op jit(solution)/shard_map/ppermute | solution.py:22
  232.3 8.7 %collective-permute-start.8 = (f32[16,512]{1,0:T(8,128)S(1)}, f32[16,512]{1,0:T(8,128)S(1)}, u32[]{:S(2)}, u32[]{:S(2)}) collective-permute-start(f32[16,512]{1,0:T(8,128)S(1)} %get-tuple-element.11), channel_id=1, source_target_pairs={{0,8},{8,16},{16,24},{24,32},{32,40},{40,48},{48,56},{56,64},{64,7... | collective-permute-start | bytes 98312 | tf_op jit(solution)/shard_map/ppermute | solution.py:22
  236.4 5.5 %collective-permute-start.7 = (f32[16,512]{1,0:T(8,128)S(1)}, f32[16,512]{1,0:T(8,128)S(1)}, u32[]{:S(2)}, u32[]{:S(2)}) collective-permute-start(f32[16,512]{1,0:T(8,128)S(1)} %get-tuple-element.12), channel_id=1, source_target_pairs={{8,0},{16,8},{24,16},{32,24},{40,32},{48,40},{56,48},{64,56},{72,6... | collective-permute-start | bytes 98312 | tf_op jit(solution)/shard_map/ppermute | solution.py:22
  327.3 13.3 %collective-permute-start.14 = (f32[8,512]{1,0:T(8,128)S(1)}, f32[8,512]{1,0:T(8,128)S(1)}, u32[]{:S(2)}, u32[]{:S(2)}) collective-permute-start(f32[8,512]{1,0:T(8,128)S(1)} %bitcast.293), channel_id=1, source_target_pairs={{0,1},{1,2},{2,3},{3,4},{4,5},{5,6},{6,7},{8,9},{9,10},{10,11},{11... | collective-permute-start | bytes 49160 | tf_op jit(solution)/shard_map/ppermute | solution.py:22
  329.7 10.9 %collective-permute-start.12 = (f32[16,512]{1,0:T(8,128)S(1)}, f32[16,512]{1,0:T(8,128)S(1)}, u32[]{:S(2)}, u32[]{:S(2)}) collective-permute-start(f32[16,512]{1,0:T(8,128)S(1)} %get-tuple-element.4), channel_id=1, source_target_pairs={{0,8},{8,16},{16,24},{24,32},{32,40},{40,48},{48,56},{56,64},{64,7... | collective-permute-start | bytes 98312 | tf_op jit(solution)/shard_map/ppermute | solution.py:22
  334.1 7.3 %collective-permute-start.11 = (f32[16,512]{1,0:T(8,128)S(1)}, f32[16,512]{1,0:T(8,128)S(1)}, u32[]{:S(2)}, u32[]{:S(2)}) collective-permute-start(f32[16,512]{1,0:T(8,128)S(1)} %get-tuple-element.5), channel_id=1, source_target_pairs={{8,0},{16,8},{24,16},{32,24},{40,32},{48,40},{56,48},{64,56},{72,6... | collective-permute-start | bytes 98312 | tf_op jit(solution)/shard_map/ppermute | solution.py:22
  338.2 5.1 %collective-permute-start.13 = (f32[8,512]{1,0:T(8,128)S(1)}, f32[8,512]{1,0:T(8,128)S(1)}, u32[]{:S(2)}, u32[]{:S(2)}) collective-permute-start(f32[8,512]{1,0:T(8,128)S(1)} %slice_bitcast_fusion.4), channel_id=1, source_target_pairs={{1,0},{2,1},{3,2},{4,3},{5,4},{6,5},{7,6},{9,8},{10,9},{11,10},{12... | collective-permute-start | bytes 49160 | tf_op jit(solution)/shard_map/ppermute | solution.py:22

commit v3 on v1

--- a/solution.py
+++ b/solution.py
@@ -280,19 +280,25 @@
     relative = ((target - slab_pos)[:, None] == distance_ids[None, :]) & live_slots[:, None]
     relative_float = relative.astype(jnp.float32)
     relative_half = relative.astype(jnp.bfloat16)
-    flat_tiles = tiles.reshape(slot_count * ray_count, voxels)
-    ray_local = jnp.dot(
-        flat_tiles, jnp.ones((voxels,), jnp.bfloat16), preferred_element_type=jnp.float32
-    )
-    ray_sends = jnp.einsum("td,tr->dr", relative_float, ray_local.reshape(slot_count, ray_count))
+    first_volume = jnp.concatenate(
+        [
+            volume0.astype(jnp.bfloat16).reshape(voxels, column_count),
+            jnp.ones((voxels, 1), jnp.bfloat16),
+        ],
+        axis=1,
+    )
+    first_products = jnp.einsum(
+        "trv,vn->trn", tiles, first_volume, preferred_element_type=jnp.float32
+    )
+    ray_local = first_products[:, :, column_count]
+    ray_sends = jnp.einsum("td,tr->dr", relative_float, ray_local)
     ray_total = ray_sends[0]
     for distance in range(1, slot_count):
         ray_total = ray_total + from_behind(ray_sends[distance], "slab", distance)
-    live_rows = jnp.repeat(live_slots, ray_count).astype(jnp.bfloat16)
-    voxel_local = jnp.dot(live_rows, flat_tiles, preferred_element_type=jnp.float32)
-    voxel_total = sum_angle(voxel_local.reshape(slab_depth, height), lax.axis_size("angle"))
     ray_scale = 1.0 / ray_total
-    voxel_scale = (1.0 / voxel_total).reshape(1, slab_depth, height)
+    live_column = jnp.broadcast_to(
+        live_slots.astype(jnp.bfloat16)[:, None, None], (slot_count, ray_count, 1)
+    )
     lower_all = from_behind(weight_z[slab_depth - 1], "slab", 1)
     z_first = slab_pos * slab_depth
     z_total = slab_depth * lax.axis_size("slab")
@@ -319,10 +325,7 @@
     residual = jnp.zeros((ray_count, column_count), jnp.float32)
     for iteration in range(ITERS):
         if gathered is None:
-            flat_volume = volume0.astype(jnp.bfloat16).reshape(voxels, column_count)
-            products = jnp.einsum(
-                "trv,vn->trn", tiles, flat_volume, preferred_element_type=jnp.float32
-            ).astype(jnp.bfloat16)
+            products = first_products[:, :, :column_count].astype(jnp.bfloat16)
         else:
             products = jnp.einsum(
                 "trv,nv->trn", tiles, gathered, preferred_element_type=jnp.float32
@@ -343,7 +346,19 @@
         picked = jnp.einsum(
             "td,drn->trn", relative_half, jnp.stack(nearby), preferred_element_type=jnp.float32
         ).astype(jnp.bfloat16)
-        back_t = jnp.einsum("trn,trv->nv", picked, tiles, preferred_element_type=jnp.float32)
+        if iteration == 0:
+            picked_ext = jnp.concatenate([picked, live_column], axis=2)
+            back_ext = jnp.einsum(
+                "trn,trv->nv", picked_ext, tiles, preferred_element_type=jnp.float32
+            )
+            back_t = back_ext[:column_count]
+            voxel_local = back_ext[column_count]
+            voxel_total = sum_angle(voxel_local.reshape(slab_depth, height), groups)
+            voxel_scale = (1.0 / voxel_total).reshape(1, slab_depth, height)
+        else:
+            back_t = jnp.einsum(
+                "trn,trv->nv", picked, tiles, preferred_element_type=jnp.float32
+            )
         back_own = scatter_angle(back_t.reshape(groups, share_width, voxels))
         volume = volume + voxel_scale * back_own.reshape(share_width, slab_depth, height)
         volume = smooth_share(

time: 328 us -> 328 us (level)
  matrix products: 67 us -> 54.8 us
  waiting for transfers between devices: 25.6 us -> 32.8 us
  starting transfers between devices: 85.1 us -> 79.5 us
  local copies, waits for them, and re-layouts: 28.1 us -> 33.3 us
  other arithmetic: 10.3 us -> 14.8 us
    dot_general x3 -> x2, matrix products: 23.2 us -> 15.4 us  [shards(): jnp.einsum('trn,trv->nv', picked, tiles, preferred_element_type=jnp.float32)]
    ppermute x27, waiting for transfers between devices: 25.6 us -> 32.8 us  [from_behind(): lax.ppermute(value, axis, [(source, source + steps) for source in range(f...]
    ppermute x27, starting transfers between devices: 85.1 us -> 79.5 us  [from_behind(): lax.ppermute(value, axis, [(source, source + steps) for source in range(f...]
    dot_general x4 -> x3, matrix products: 20.9 us -> 15.9 us  [the longest x1 9.27 us: shards(): jnp.einsum('trv,vn->trn', tiles, first_volume, preferred_element_type=jnp...]
    unnamed x31 -> x29, local copies, waits for them, and re-layouts: 11.8 us -> 13.6 us
  transfers between devices with their start and end apart: 27 -> 27, of which waited for: 11 -> 10; matrix products, arithmetic and copies ran while one was open for 15% -> 12% of each run, Pallas kernels for 9% -> 10%
where the time goes in v3:
time: 328 us; the launch traced here: 325 us
  Pallas kernels  108 us (33%)
  starting transfers between devices  79.5 us (24%)
  matrix products  54.8 us (17%)
  local copies, waits for them, and re-layouts  33.3 us (10%)
  waiting for transfers between devices  32.8 us (10%)
  other arithmetic  14.8 us (5%)
    ppermute x27, starting transfers between devices, from_behind(): lax.ppermute(value, axis, [(source, source + steps) for source in range(f...  79.5 us
    pallas_call x3, Pallas kernels, scatter_angle(): pl.pallas_call(functools.partial(_scatter_kernel, n_chip), out_shape=jax....  68.1 us
    ppermute x27, waiting for transfers between devices, from_behind(): lax.ppermute(value, axis, [(source, source + steps) for source in range(f...  32.8 us
    pallas_call x2, Pallas kernels, gather_angle(): pl.pallas_call(functools.partial(_gather_kernel, n_chip), out_shape=jax.S...  30 us
    dot_general x2, matrix products, shards(): jnp.einsum('trv,nv->trn', tiles, gathered, preferred_element_type=jnp.flo...  18.4 us
    dot_general x2, matrix products, shards(): jnp.einsum('trn,trv->nv', picked, tiles, preferred_element_type=jnp.float32)  15.4 us
    unnamed x29, local copies, waits for them, and re-layouts  13.6 us
    pallas_call x1, Pallas kernels, sum_angle(): pl.pallas_call(functools.partial(_sum_kernel, groups), out_shape=jax.Shap...  9.89 us
  transfers between devices with their start and end apart: 27, of which 10 were waited for; matrix products, arithmetic and copies ran while one was open for 12% of the time, Pallas kernels for 10%

profile of v3, /device:TPU:33, one launch (start us, length us, event | category | flops | bytes accessed | tf_op | source)
XLA Modules:
  0.0 325.4 jit_solution(16417702245592392012)
XLA Ops:
  2.7 1.9 convert_element_type.137
  4.7 1.3 copy.238
  6.0 9.3 %fusion.21 = bf16[3,512,129]{1,2,0:T(8,128)(2,1)S(1)} fusion(bf16[1,1,3,512,4096]{4,3,2,1,0:T(8,128)(2,1)} %param.10, bf16[4096,128]{0,1:T(8,128)(2,1)} %copy.238), kind=kOutput, calls=%fused_computation.15 | convolution fusion | flops 1623195648 | bytes 14027776 | tf_op jit(solution)/shard_map/trv,vn->trn/dot_general | solution.py:290
  16.1 3.2 collective-permute-start.2
  19.3 4.5 %collective-permute-start.3 = (f32[512]{0:T(512)S(1)}, f32[512]{0:T(512)}, u32[]{:S(2)}, u32[]{:S(2)}) collective-permute-start(f32[512]{0:T(512)S(1)} %bitcast.326), channel_id=1, source_target_pairs={{0,16},{8,24},{16,32},{24,40},{32,48},{40,56},{48,64},{56,72},{64,... | collective-permute-start | bytes 6152 | tf_op jit(solution)/shard_map/ppermute | solution.py:22
  24.9 2.6 fusion.115
  28.7 2.6 collective-permute-start
  32.0 4.8 %collective-permute-start.1 = (bf16[512,128]{1,0:T(8,128)(2,1)}, bf16[512,128]{1,0:T(8,128)(2,1)}, u32[]{:S(2)}, u32[]{:S(2)}) collective-permute-start(bf16[512,128]{1,0:T(8,128)(2,1)} %bitcast.276), channel_id=1, source_target_pairs={{0,16},{8,24},{16,32},{24,40},{32,48},{40,56},{48,64},{56,72},{64,... | collective-permute-start | bytes 393224 | tf_op jit(solution)/shard_map/ppermute | solution.py:22
  38.5 2.9 collective-permute-start.7
  41.4 2.0 constant_dynamic-slice_fusion.4
  43.3 1.6 constant_dynamic-slice_fusion.3
  44.9 1.3 constant_dynamic-slice_fusion
  46.3 2.8 constant_dynamic-slice_fusion.1
  49.6 1.4 slice.196
  52.3 1.1 fusion.47
  53.4 4.5 %collective-permute-start.4 = (bf16[512,128]{1,0:T(8,128)(2,1)S(1)}, bf16[512,128]{1,0:T(8,128)(2,1)S(1)}, u32[]{:S(2)}, u32[]{:S(2)}) collective-permute-start(bf16[512,128]{1,0:T(8,128)(2,1)S(1)} %fusion.47), channel_id=1, source_target_pairs={{8,0},{16,8},{24,16},{32,24},{40,32},{48,40},{56,48},{64,56},{72,6... | collective-permute-start | bytes 393224 | tf_op jit(solution)/shard_map/ppermute | solution.py:22
  57.9 2.1 collective-permute-start.5
  60.6 2.9 copy.245
  63.5 1.6 copy.252
  65.1 1.6 copy.250
  69.5 6.5 %fusion.12 = f32[129,4096]{1,0:T(8,128)S(1)} fusion(bf16[1,1,3,512,4096]{4,3,2,1,0:T(8,128)(2,1)} %param.10, bf16[3,512,1]{1,2,0:T(2,128)(2,1)S(1)} %broadcast_in_dim.68, bf16[3,512,128]{1,2,0:T(8,128)(2,1)S(1)} %copy.193), kind=kOutput, calls=%fused_computation.12 | convolution fusion | flops 1623988224 | bytes 15092736 | tf_op jit(solution)/shard_map/trn,trv->nv/dot_general | solution.py:351
  76.6 1.5 slice.204
  78.1 9.9 %shard_map.104 = f32[8,512]{1,0:T(8,128)} custom-call(f32[8,512]{1,0:T(8,128)} %reshape_squeeze.3.part_ref), custom_call_target="tpu_custom_call" | custom-call | flops 32768 | bytes 262144 | tf_op jit(solution)/shard_map/pallas_call | solution.py:146
  88.7 21.2 %shard_map.105 = f32[16,4096]{1,0:T(8,128)} custom-call(f32[8,16,4096]{2,1,0:T(8,128)} %bitcast.288, f32[8,16,4096]{2,1,0:T(8,128)} %bitcast.289), custom_call_target="tpu_custom_call" | custom-call | flops 1048576 | bytes 6291456 | tf_op jit(solution)/shard_map/pallas_call | solution.py:95
  109.9 1.1 copy.254
  111.1 2.2 collective-permute-start.10
  113.5 2.5 collective-permute-start.8
  116.0 4.9 %collective-permute-start.6 = (f32[16,512]{1,0:T(8,128)S(1)}, f32[16,512]{1,0:T(8,128)S(1)}, u32[]{:S(2)}, u32[]{:S(2)}) collective-permute-start(f32[16,512]{1,0:T(8,128)S(1)} %bitcast.317), channel_id=1, source_target_pairs={{8,0},{16,8},{24,16},{32,24},{40,32},{48,40},{56,48},{64,56},{72,6... | collective-permute-start | bytes 98312 | tf_op jit(solution)/shard_map/ppermute | solution.py:22
  120.9 2.7 collective-permute-start.9
  124.5 1.5 collective-permute-done.9
  127.8 14.7 %shard_map.106 = bf16[8,16,4096]{2,1,0:T(8,128)(2,1)} custom-call(bf16[16,4096]{1,0:T(8,128)(2,1)} %bitcast.306), custom_call_target="tpu_custom_call" | custom-call | bytes 2097152 | tf_op jit(solution)/shard_map/pallas_call | solution.py:205
  142.6 9.2 %fusion.35 = bf16[3,512,128]{1,2,0:T(8,128)(2,1)S(1)} fusion(bf16[128,4096,1]{1,0,2:T(8,128)(2,1)} %bitcast.291, bf16[1,1,3,512,4096]{4,3,2,1,0:T(8,128)(2,1)} %param.10), kind=kOutput, calls=%fused_computation.24 | convolution fusion | flops 1610809344 | bytes 14024704 | tf_op jit(solution)/shard_map/trv,nv->trn/dot_general | solution.py:330
  152.7 1.9 collective-permute-start.11
  154.7 3.9 %collective-permute-start.12 = (bf16[512,128]{1,0:T(8,128)(2,1)S(1)}, bf16[512,128]{1,0:T(8,128)(2,1)S(1)}, u32[]{:S(2)}, u32[]{:S(2)}) collective-permute-start(bf16[512,128]{1,0:T(8,128)(2,1)S(1)} %get-tuple-element.15), channel_id=1, source_target_pairs={{0,16},{8,24},{16,32},{24,40},{32,48},{40,56},{48,64},{56,72},{64,... | collective-permute-start | bytes 393224 | tf_op jit(solution)/shard_map/ppermute | solution.py:22
  158.5 3.2 collective-permute-done.11
  161.7 2.3 collective-permute-done.12
  164.1 4.2 %collective-permute-start.13 = (bf16[512,128]{1,0:T(8,128)(2,1)S(1)}, bf16[512,128]{1,0:T(8,128)(2,1)S(1)}, u32[]{:S(2)}, u32[]{:S(2)}) collective-permute-start(bf16[512,128]{1,0:T(8,128)(2,1)S(1)} %fusion.49), channel_id=1, source_target_pairs={{8,0},{16,8},{24,16},{32,24},{40,32},{48,40},{56,48},{64,56},{72,6... | collective-permute-start | bytes 393224 | tf_op jit(solution)/shard_map/ppermute | solution.py:22
  168.3 2.1 collective-permute-start.14
  170.5 5.0 %collective-permute-done.14 = bf16[512,128]{1,0:T(8,128)(2,1)S(1)} collective-permute-done((bf16[512,128]{1,0:T(8,128)(2,1)S(1)}, bf16[512,128]{1,0:T(8,128)(2,1)S(1)}, u32[]{:S(2)}, u32[]{:S(2)}) %collective-permute-start.14) | collective-permute-done | bytes 131104 | tf_op jit(solution)/shard_map/ppermute | solution.py:22
  176.4 7.7 %fusion.15.part_ref.half_ref = f32[8,16,4096]{2,1,0:T(8,128)} fusion(bf16[8,16,512,3]{2,1,0,3:T(8,128)(2,1)S(1)} %bitcast.299, bf16[1,1,3,512,4096]{4,3,2,1,0:T(8,128)(2,1)} %param.10), kind=kOutput, calls=%fused_computation.13 | convolution fusion | flops 1610612736 | bytes 15073280 | tf_op jit(solution)/shard_map/trn,trv->nv/dot_general | solution.py:359
  184.1 23.5 %shard_map.107 = f32[16,4096]{1,0:T(8,128)} custom-call(f32[8,16,4096]{2,1,0:T(8,128)} %fusion.15.part_ref.half_ref, f32[8,16,4096]{2,1,0:T(8,128)} %fusion.15.part_ref.half_ref), custom_call_target="tpu_custom_call" | custom-call | flops 1048576 | bytes 6291456 | tf_op jit(solution)/shard_map/pallas_call | solution.py:95
  207.6 1.1 copy.256
  208.9 2.2 collective-permute-start.18
  211.3 3.1 collective-permute-start.15
  214.4 2.4 collective-permute-start.17
  216.9 2.2 collective-permute-start.16
  219.8 4.2 %collective-permute-done.16 = f32[16,512]{1,0:T(8,128)S(1)} collective-permute-done((f32[16,512]{1,0:T(8,128)S(1)}, f32[16,512]{1,0:T(8,128)S(1)}, u32[]{:S(2)}, u32[]{:S(2)}) %collective-permute-start.16) | collective-permute-done | bytes 32800 | tf_op jit(solution)/shard_map/ppermute | solution.py:22
  225.9 15.2 %shard_map.108 = bf16[8,16,4096]{2,1,0:T(8,128)(2,1)} custom-call(bf16[16,4096]{1,0:T(8,128)(2,1)} %bitcast.307), custom_call_target="tpu_custom_call" | custom-call | bytes 2097152 | tf_op jit(solution)/shard_map/pallas_call | solution.py:205
  241.1 9.2 %fusion.32 = bf16[3,512,128]{1,2,0:T(8,128)(2,1)S(1)} fusion(bf16[128,4096,1]{1,0,2:T(8,128)(2,1)} %bitcast.292, bf16[1,1,3,512,4096]{4,3,2,1,0:T(8,128)(2,1)} %param.10), kind=kOutput, calls=%fused_computation.23 | convolution fusion | flops 1610809344 | bytes 14024704 | tf_op jit(solution)/shard_map/trv,nv->trn/dot_general | solution.py:330
  251.3 1.9 collective-permute-start.19
  253.2 2.7 collective-permute-start.20
  255.9 4.4 %collective-permute-done.19 = bf16[512,128]{1,0:T(8,128)(2,1)S(1)} collective-permute-done((bf16[512,128]{1,0:T(8,128)(2,1)S(1)}, bf16[512,128]{1,0:T(8,128)(2,1)S(1)}, u32[]{:S(2)}, u32[]{:S(2)}) %collective-permute-start.19) | collective-permute-done | bytes 131104 | tf_op jit(solution)/shard_map/ppermute | solution.py:22
  260.3 2.3 collective-permute-done.20
  263.4 4.2 %collective-permute-start.21 = (bf16[512,128]{1,0:T(8,128)(2,1)S(1)}, bf16[512,128]{1,0:T(8,128)(2,1)S(1)}, u32[]{:S(2)}, u32[]{:S(2)}) collective-permute-start(bf16[512,128]{1,0:T(8,128)(2,1)S(1)} %get-tuple-element.9), channel_id=1, source_target_pairs={{8,0},{16,8},{24,16},{32,24},{40,32},{48,40},{56,48},{64,56},{72,6... | collective-permute-start | bytes 393224 | tf_op jit(solution)/shard_map/ppermute | solution.py:22
  267.6 2.2 collective-permute-start.22
  269.8 5.0 %collective-permute-done.22 = bf16[512,128]{1,0:T(8,128)(2,1)S(1)} collective-permute-done((bf16[512,128]{1,0:T(8,128)(2,1)S(1)}, bf16[512,128]{1,0:T(8,128)(2,1)S(1)}, u32[]{:S(2)}, u32[]{:S(2)}) %collective-permute-start.22) | collective-permute-done | bytes 131104 | tf_op jit(solution)/shard_map/ppermute | solution.py:22
  275.6 7.7 %fusion.18.part_ref.half_ref = f32[8,16,4096]{2,1,0:T(8,128)} fusion(bf16[8,16,512,3]{2,1,0,3:T(8,128)(2,1)S(1)} %bitcast.300, bf16[1,1,3,512,4096]{4,3,2,1,0:T(8,128)(2,1)} %param.10), kind=kOutput, calls=%fused_computation.14 | convolution fusion | flops 1610612736 | bytes 15073280 | tf_op jit(solution)/shard_map/trn,trv->nv/dot_general | solution.py:359
  283.3 23.5 %shard_map.109 = f32[16,4096]{1,0:T(8,128)} custom-call(f32[8,16,4096]{2,1,0:T(8,128)} %fusion.18.part_ref.half_ref, f32[8,16,4096]{2,1,0:T(8,128)} %fusion.18.part_ref.half_ref), custom_call_target="tpu_custom_call" | custom-call | flops 1048576 | bytes 6291456 | tf_op jit(solution)/shard_map/pallas_call | solution.py:95
  306.8 1.1 copy.257
  308.6 2.2 collective-permute-start.26
  311.0 2.1 collective-permute-start.25
  313.1 3.1 collective-permute-start.23
  316.3 2.2 collective-permute-start.24
  318.9 4.6 %collective-permute-done.24 = f32[16,512]{1,0:T(8,128)S(1)} collective-permute-done((f32[16,512]{1,0:T(8,128)S(1)}, f32[16,512]{1,0:T(8,128)S(1)}, u32[]{:S(2)}, u32[]{:S(2)}) %collective-permute-start.24) | collective-permute-done | bytes 32800 | tf_op jit(solution)/shard_map/ppermute | solution.py:22
  (126 shorter events, 26.7 us)
Async XLA Ops:
  2.7 38.6 %copy-start = (f32[8,512,128]{2,1,0:T(8,128)S(1)}, f32[8,512,128]{2,1,0:T(8,128)}, u32[]{:S(2)}) copy-start(f32[8,512,128]{2,1,0:T(8,128)} %param.9) | copy-start | bytes 6291460
  6.0 38.9 %copy-start.1 = (bf16[8,512,128]{2,1,0:T(8,128)(2,1)S(1)}, bf16[8,512,128]{2,1,0:T(8,128)(2,1)}, u32[]{:S(2)}) copy-start(bf16[8,512,128]{2,1,0:T(8,128)(2,1)} %param.17) | copy-start | bytes 3145732
  16.1 35.0 %collective-permute-start.2 = (f32[512]{0:T(512)}, f32[512]{0:T(512)S(1)}, u32[]{:S(2)}, u32[]{:S(2)}) collective-permute-start(f32[512]{0:T(512)} %bitcast.13), channel_id=1, source_target_pairs={{0,8},{8,16},{16,24},{24,32},{32,40},{40,48},{48,56},{56,64},{64,7... | collective-permute-start | bytes 6152 | tf_op jit(solution)/shard_map/ppermute | solution.py:22
  19.3 31.8 %collective-permute-start.3 = (f32[512]{0:T(512)S(1)}, f32[512]{0:T(512)}, u32[]{:S(2)}, u32[]{:S(2)}) collective-permute-start(f32[512]{0:T(512)S(1)} %bitcast.326), channel_id=1, source_target_pairs={{0,16},{8,24},{16,32},{24,40},{32,48},{40,56},{48,64},{56,72},{64,... | collective-permute-start | bytes 6152 | tf_op jit(solution)/shard_map/ppermute | solution.py:22
  24.9 27.4 %copy-start.2 = (bf16[1,1,512,128]{3,2,1,0:T(8,128)(2,1)S(1)}, bf16[1,1,512,128]{3,2,1,0:T(8,128)(2,1)}, u32[]{:S(2)}) copy-start(bf16[1,1,512,128]{3,2,1,0:T(8,128)(2,1)} %param.14) | copy-start | bytes 393220
  28.7 23.6 %collective-permute-start = (bf16[512,128]{1,0:T(8,128)(2,1)}, bf16[512,128]{1,0:T(8,128)(2,1)}, u32[]{:S(2)}, u32[]{:S(2)}) collective-permute-start(bf16[512,128]{1,0:T(8,128)(2,1)} %bitcast.277), channel_id=1, source_target_pairs={{0,8},{8,16},{16,24},{24,32},{32,40},{40,48},{48,56},{56,64},{64,7... | collective-permute-start | bytes 393224 | tf_op jit(solution)/shard_map/ppermute | solution.py:22
  32.0 20.4 %collective-permute-start.1 = (bf16[512,128]{1,0:T(8,128)(2,1)}, bf16[512,128]{1,0:T(8,128)(2,1)}, u32[]{:S(2)}, u32[]{:S(2)}) collective-permute-start(bf16[512,128]{1,0:T(8,128)(2,1)} %bitcast.276), channel_id=1, source_target_pairs={{0,16},{8,24},{16,32},{24,40},{32,48},{40,56},{48,64},{56,72},{64,... | collective-permute-start | bytes 393224 | tf_op jit(solution)/shard_map/ppermute | solution.py:22
  38.5 85.2 %collective-permute-start.7 = (bf16[512,128]{0,1:T(8,128)(2,1)}, bf16[512,128]{0,1:T(8,128)(2,1)}, u32[]{:S(2)}, u32[]{:S(2)}) collective-permute-start(bf16[512,128]{0,1:T(8,128)(2,1)} %bitcast.22), channel_id=1, source_target_pairs={{0,8},{8,16},{16,24},{24,32},{32,40},{40,48},{48,56},{56,64},{64,7... | collective-permute-start | bytes 393224 | tf_op jit(solution)/shard_map/ppermute | solution.py:22
  51.1 0.6 copy-start.6
  53.4 14.5 %collective-permute-start.4 = (bf16[512,128]{1,0:T(8,128)(2,1)S(1)}, bf16[512,128]{1,0:T(8,128)(2,1)S(1)}, u32[]{:S(2)}, u32[]{:S(2)}) collective-permute-start(bf16[512,128]{1,0:T(8,128)(2,1)S(1)} %fusion.47), channel_id=1, source_target_pairs={{8,0},{16,8},{24,16},{32,24},{40,32},{48,40},{56,48},{64,56},{72,6... | collective-permute-start | bytes 393224 | tf_op jit(solution)/shard_map/ppermute | solution.py:22
  57.9 10.0 %collective-permute-start.5 = (bf16[512,128]{1,0:T(8,128)(2,1)S(1)}, bf16[512,128]{1,0:T(8,128)(2,1)S(1)}, u32[]{:S(2)}, u32[]{:S(2)}) collective-permute-start(bf16[512,128]{1,0:T(8,128)(2,1)S(1)} %fusion.47), channel_id=1, source_target_pairs={{16,0},{24,8},{32,16},{40,24},{48,32},{56,40},{64,48},{72,56},{80,... | collective-permute-start | bytes 393224 | tf_op jit(solution)/shard_map/ppermute | solution.py:22
  68.5 42.5 %copy-start.3 = (f32[8,512,16]{1,0,2:T(8,128)S(1)}, f32[8,512,16]{1,0,2:T(8,128)}, u32[]{:S(2)}) copy-start(f32[8,512,16]{1,0,2:T(8,128)} %copy.245) | copy-start | bytes 786436
  111.1 12.6 %collective-permute-start.10 = (f32[8,512]{1,0:T(8,128)S(1)}, f32[8,512]{1,0:T(8,128)S(1)}, u32[]{:S(2)}, u32[]{:S(2)}) collective-permute-start(f32[8,512]{1,0:T(8,128)S(1)} %get-tuple-element.33), channel_id=1, source_target_pairs={{0,1},{1,2},{2,3},{3,4},{4,5},{5,6},{6,7},{8,9},{9,10},{10,11},{11... | collective-permute-start | bytes 49160 | tf_op jit(solution)/shard_map/ppermute | solution.py:22
  113.5 10.2 %collective-permute-start.8 = (f32[16,512]{1,0:T(8,128)S(1)}, f32[16,512]{1,0:T(8,128)S(1)}, u32[]{:S(2)}, u32[]{:S(2)}) collective-permute-start(f32[16,512]{1,0:T(8,128)S(1)} %bitcast.318), channel_id=1, source_target_pairs={{0,8},{8,16},{16,24},{24,32},{32,40},{40,48},{48,56},{56,64},{64,7... | collective-permute-start | bytes 98312 | tf_op jit(solution)/shard_map/ppermute | solution.py:22
  116.0 8.5 %collective-permute-start.6 = (f32[16,512]{1,0:T(8,128)S(1)}, f32[16,512]{1,0:T(8,128)S(1)}, u32[]{:S(2)}, u32[]{:S(2)}) collective-permute-start(f32[16,512]{1,0:T(8,128)S(1)} %bitcast.317), channel_id=1, source_target_pairs={{8,0},{16,8},{24,16},{32,24},{40,32},{48,40},{56,48},{64,56},{72,6... | collective-permute-start | bytes 98312 | tf_op jit(solution)/shard_map/ppermute | solution.py:22
  120.9 5.1 %collective-permute-start.9 = (f32[8,512]{1,0:T(8,128)S(1)}, f32[8,512]{1,0:T(8,128)S(1)}, u32[]{:S(2)}, u32[]{:S(2)}) collective-permute-start(f32[8,512]{1,0:T(8,128)S(1)} %get-tuple-element.34), channel_id=1, source_target_pairs={{1,0},{2,1},{3,2},{4,3},{5,4},{6,5},{7,6},{9,8},{10,9},{11,10},{12... | collective-permute-start | bytes 49160 | tf_op jit(solution)/shard_map/ppermute | solution.py:22
  152.7 9.0 %collective-permute-start.11 = (bf16[512,128]{1,0:T(8,128)(2,1)S(1)}, bf16[512,128]{1,0:T(8,128)(2,1)S(1)}, u32[]{:S(2)}, u32[]{:S(2)}) collective-permute-start(bf16[512,128]{1,0:T(8,128)(2,1)S(1)} %get-tuple-element.14), channel_id=1, source_target_pairs={{0,8},{8,16},{16,24},{24,32},{32,40},{40,48},{48,56},{56,64},{64,7... | collective-permute-start | bytes 393224 | tf_op jit(solution)/shard_map/ppermute | solution.py:22
  154.7 9.3 %collective-permute-start.12 = (bf16[512,128]{1,0:T(8,128)(2,1)S(1)}, bf16[512,128]{1,0:T(8,128)(2,1)S(1)}, u32[]{:S(2)}, u32[]{:S(2)}) collective-permute-start(bf16[512,128]{1,0:T(8,128)(2,1)S(1)} %get-tuple-element.15), channel_id=1, source_target_pairs={{0,16},{8,24},{16,32},{24,40},{32,48},{40,56},{48,64},{56,72},{64,... | collective-permute-start | bytes 393224 | tf_op jit(solution)/shard_map/ppermute | solution.py:22
  164.1 6.4 %collective-permute-start.13 = (bf16[512,128]{1,0:T(8,128)(2,1)S(1)}, bf16[512,128]{1,0:T(8,128)(2,1)S(1)}, u32[]{:S(2)}, u32[]{:S(2)}) collective-permute-start(bf16[512,128]{1,0:T(8,128)(2,1)S(1)} %fusion.49), channel_id=1, source_target_pairs={{8,0},{16,8},{24,16},{32,24},{40,32},{48,40},{56,48},{64,56},{72,6... | collective-permute-start | bytes 393224 | tf_op jit(solution)/shard_map/ppermute | solution.py:22
  168.3 7.2 %collective-permute-start.14 = (bf16[512,128]{1,0:T(8,128)(2,1)S(1)}, bf16[512,128]{1,0:T(8,128)(2,1)S(1)}, u32[]{:S(2)}, u32[]{:S(2)}) collective-permute-start(bf16[512,128]{1,0:T(8,128)(2,1)S(1)} %fusion.49), channel_id=1, source_target_pairs={{16,0},{24,8},{32,16},{40,24},{48,32},{56,40},{64,48},{72,56},{80,... | collective-permute-start | bytes 393224 | tf_op jit(solution)/shard_map/ppermute | solution.py:22
  175.6 43.9 %copy-start.4 = (pred[16]{0:T(512)(128)(4,1)S(1)}, pred[16]{0:T(512)(128)(4,1)}, u32[]{:S(2)}) copy-start(pred[16]{0:T(512)(128)(4,1)} %add_compare_fusion) | copy-start | bytes 52
  175.6 43.9 %copy-start.5 = (pred[8]{0:T(512)(128)(4,1)S(1)}, pred[8]{0:T(512)(128)(4,1)}, u32[]{:S(2)}) copy-start(pred[8]{0:T(512)(128)(4,1)} %add_compare_fusion.1) | copy-start | bytes 28
  208.9 10.1 %collective-permute-start.18 = (f32[8,512]{1,0:T(8,128)S(1)}, f32[8,512]{1,0:T(8,128)S(1)}, u32[]{:S(2)}, u32[]{:S(2)}) collective-permute-start(f32[8,512]{1,0:T(8,128)S(1)} %get-tuple-element.21), channel_id=1, source_target_pairs={{0,1},{1,2},{2,3},{3,4},{4,5},{5,6},{6,7},{8,9},{9,10},{10,11},{11... | collective-permute-start | bytes 49160 | tf_op jit(solution)/shard_map/ppermute | solution.py:22
  211.3 7.8 %collective-permute-start.15 = (f32[16,512]{1,0:T(8,128)S(1)}, f32[16,512]{1,0:T(8,128)S(1)}, u32[]{:S(2)}, u32[]{:S(2)}) collective-permute-start(f32[16,512]{1,0:T(8,128)S(1)} %get-tuple-element.24), channel_id=1, source_target_pairs={{8,0},{16,8},{24,16},{32,24},{40,32},{48,40},{56,48},{64,56},{72,6... | collective-permute-start | bytes 98312 | tf_op jit(solution)/shard_map/ppermute | solution.py:22
  214.4 5.1 %collective-permute-start.17 = (f32[8,512]{1,0:T(8,128)S(1)}, f32[8,512]{1,0:T(8,128)S(1)}, u32[]{:S(2)}, u32[]{:S(2)}) collective-permute-start(f32[8,512]{1,0:T(8,128)S(1)} %get-tuple-element.22), channel_id=1, source_target_pairs={{1,0},{2,1},{3,2},{4,3},{5,4},{6,5},{7,6},{9,8},{10,9},{11,10},{12... | collective-permute-start | bytes 49160 | tf_op jit(solution)/shard_map/ppermute | solution.py:22
  216.9 7.1 %collective-permute-start.16 = (f32[16,512]{1,0:T(8,128)S(1)}, f32[16,512]{1,0:T(8,128)S(1)}, u32[]{:S(2)}, u32[]{:S(2)}) collective-permute-start(f32[16,512]{1,0:T(8,128)S(1)} %get-tuple-element.23), channel_id=1, source_target_pairs={{0,8},{8,16},{16,24},{24,32},{32,40},{40,48},{48,56},{56,64},{64,7... | collective-permute-start | bytes 98312 | tf_op jit(solution)/shard_map/ppermute | solution.py:22
  251.3 9.0 %collective-permute-start.19 = (bf16[512,128]{1,0:T(8,128)(2,1)S(1)}, bf16[512,128]{1,0:T(8,128)(2,1)S(1)}, u32[]{:S(2)}, u32[]{:S(2)}) collective-permute-start(bf16[512,128]{1,0:T(8,128)(2,1)S(1)} %get-tuple-element.12), channel_id=1, source_target_pairs={{0,8},{8,16},{16,24},{24,32},{32,40},{40,48},{48,56},{56,64},{64,7... | collective-permute-start | bytes 393224 | tf_op jit(solution)/shard_map/ppermute | solution.py:22
  253.2 9.3 %collective-permute-start.20 = (bf16[512,128]{1,0:T(8,128)(2,1)S(1)}, bf16[512,128]{1,0:T(8,128)(2,1)S(1)}, u32[]{:S(2)}, u32[]{:S(2)}) collective-permute-start(bf16[512,128]{1,0:T(8,128)(2,1)S(1)} %get-tuple-element.13), channel_id=1, source_target_pairs={{0,16},{8,24},{16,32},{24,40},{32,48},{40,56},{48,64},{56,72},{64,... | collective-permute-start | bytes 393224 | tf_op jit(solution)/shard_map/ppermute | solution.py:22
  263.4 6.4 %collective-permute-start.21 = (bf16[512,128]{1,0:T(8,128)(2,1)S(1)}, bf16[512,128]{1,0:T(8,128)(2,1)S(1)}, u32[]{:S(2)}, u32[]{:S(2)}) collective-permute-start(bf16[512,128]{1,0:T(8,128)(2,1)S(1)} %get-tuple-element.9), channel_id=1, source_target_pairs={{8,0},{16,8},{24,16},{32,24},{40,32},{48,40},{56,48},{64,56},{72,6... | collective-permute-start | bytes 393224 | tf_op jit(solution)/shard_map/ppermute | solution.py:22
  267.6 7.2 %collective-permute-start.22 = (bf16[512,128]{1,0:T(8,128)(2,1)S(1)}, bf16[512,128]{1,0:T(8,128)(2,1)S(1)}, u32[]{:S(2)}, u32[]{:S(2)}) collective-permute-start(bf16[512,128]{1,0:T(8,128)(2,1)S(1)} %get-tuple-element.9), channel_id=1, source_target_pairs={{16,0},{24,8},{32,16},{40,24},{48,32},{56,40},{64,48},{72,56},{80,... | collective-permute-start | bytes 393224 | tf_op jit(solution)/shard_map/ppermute | solution.py:22
  308.6 9.8 %collective-permute-start.26 = (f32[8,512]{1,0:T(8,128)S(1)}, f32[8,512]{1,0:T(8,128)S(1)}, u32[]{:S(2)}, u32[]{:S(2)}) collective-permute-start(f32[8,512]{1,0:T(8,128)S(1)} %bitcast.324), channel_id=1, source_target_pairs={{0,1},{1,2},{2,3},{3,4},{4,5},{5,6},{6,7},{8,9},{9,10},{10,11},{11... | collective-permute-start | bytes 49160 | tf_op jit(solution)/shard_map/ppermute | solution.py:22
  311.0 7.5 %collective-permute-start.25 = (f32[8,512]{1,0:T(8,128)S(1)}, f32[8,512]{1,0:T(8,128)S(1)}, u32[]{:S(2)}, u32[]{:S(2)}) collective-permute-start(f32[8,512]{1,0:T(8,128)S(1)} %slice_bitcast_fusion.10), channel_id=1, source_target_pairs={{1,0},{2,1},{3,2},{4,3},{5,4},{6,5},{7,6},{9,8},{10,9},{11,10},{12... | collective-permute-start | bytes 49160 | tf_op jit(solution)/shard_map/ppermute | solution.py:22
  313.1 5.3 %collective-permute-start.23 = (f32[16,512]{1,0:T(8,128)S(1)}, f32[16,512]{1,0:T(8,128)S(1)}, u32[]{:S(2)}, u32[]{:S(2)}) collective-permute-start(f32[16,512]{1,0:T(8,128)S(1)} %get-tuple-element.17), channel_id=1, source_target_pairs={{8,0},{16,8},{24,16},{32,24},{40,32},{48,40},{56,48},{64,56},{72,6... | collective-permute-start | bytes 98312 | tf_op jit(solution)/shard_map/ppermute | solution.py:22
  316.3 7.3 %collective-permute-start.24 = (f32[16,512]{1,0:T(8,128)S(1)}, f32[16,512]{1,0:T(8,128)S(1)}, u32[]{:S(2)}, u32[]{:S(2)}) collective-permute-start(f32[16,512]{1,0:T(8,128)S(1)} %get-tuple-element.16), channel_id=1, source_target_pairs={{0,8},{8,16},{16,24},{24,32},{32,40},{40,48},{48,56},{56,64},{64,7... | collective-permute-start | bytes 98312 | tf_op jit(solution)/shard_map/ppermute | solution.py:22

commit v4 on v1

--- a/solution.py
+++ b/solution.py
@@ -48,30 +48,29 @@
                     send_a, recv_a, send_b, recv_b):
     slab, here, chip, core, partner = _where_am_i()
     _greet(slab, chip, core, partner, n_chip)
+    order = list(range(1, n_chip)) + [0]
     pair = []
-    for k in range(n_chip):
-        copy = pltpu.make_async_remote_copy(
-            src_ref=half_ref.at[2 * k + 1 - core],
-            dst_ref=got_pair.at[k],
-            send_sem=send_a.at[k],
-            recv_sem=recv_a.at[k],
+    for i, d in enumerate(order):
+        dest = (chip + d) % n_chip
+        copy = pltpu.make_async_remote_copy(
+            src_ref=half_ref.at[2 * dest + 1 - core],
+            dst_ref=got_pair.at[i],
+            send_sem=send_a.at[i],
+            recv_sem=recv_a.at[i],
             device_id=(slab, partner),
             device_id_type=MESH_ID,
         )
         copy.start()
         pair.append(copy)
-    for copy in pair:
-        copy.wait()
-    for d in range(1, n_chip):
+    ring = []
+    for i, d in enumerate(order[:-1]):
         dest = (chip + d) % n_chip
-        chip_sum[dest] = (
-            part_ref[2 * dest + core] + got_pair[dest].astype(jnp.float32)
+        pair[i].wait_recv()
+        chip_sum[i] = (
+            part_ref[2 * dest + core] + got_pair[i].astype(jnp.float32)
         ).astype(chip_sum.dtype)
-    ring = []
-    for d in range(1, n_chip):
-        dest = (chip + d) % n_chip
-        copy = pltpu.make_async_remote_copy(
-            src_ref=chip_sum.at[dest],
+        copy = pltpu.make_async_remote_copy(
+            src_ref=chip_sum.at[i],
             dst_ref=got_ring.at[d],
             send_sem=send_b.at[d],
             recv_sem=recv_b.at[d],
@@ -80,7 +79,10 @@
         )
         copy.start()
         ring.append(copy)
-    total = part_ref[here] + got_pair[chip].astype(jnp.float32)
+    pair[-1].wait_recv()
+    total = part_ref[here] + got_pair[n_chip - 1].astype(jnp.float32)
+    for copy in pair:
+        copy.wait_send()
     for copy in ring:
         copy.wait()
     for d in range(1, n_chip):
@@ -166,7 +168,18 @@
     _greet(slab, chip, core, partner, n_chip)
     mine = pltpu.make_async_copy(own_ref, held.at[here], local_sem.at[0])
     mine.start()
-    ring = []
+    pair = [
+        pltpu.make_async_remote_copy(
+            src_ref=own_ref,
+            dst_ref=held.at[here],
+            send_sem=send_b.at[0],
+            recv_sem=recv_b.at[0],
+            device_id=(slab, partner),
+            device_id_type=MESH_ID,
+        )
+    ]
+    pair[0].start()
+    ring = [None]
     for d in range(1, n_chip):
         dest = (chip + d) % n_chip
         copy = pltpu.make_async_remote_copy(
@@ -179,21 +192,22 @@
         )
         copy.start()
         ring.append(copy)
+    for d in range(1, n_chip):
+        ring[d].wait_recv()
+        block = 2 * ((chip - d + n_chip) % n_chip) + core
+        copy = pltpu.make_async_remote_copy(
+            src_ref=held.at[block],
+            dst_ref=held.at[block],
+            send_sem=send_b.at[d],
+            recv_sem=recv_b.at[d],
+            device_id=(slab, partner),
+            device_id_type=MESH_ID,
+        )
+        copy.start()
+        pair.append(copy)
     mine.wait()
-    for copy in ring:
-        copy.wait()
-    pair = []
-    for k in range(n_chip):
-        copy = pltpu.make_async_remote_copy(
-            src_ref=held.at[2 * k + core],
-            dst_ref=held.at[2 * k + core],
-            send_sem=send_b.at[k],
-            recv_sem=recv_b.at[k],
-            device_id=(slab, partner),
-            device_id_type=MESH_ID,
-        )
-        copy.start()
-        pair.append(copy)
+    for d in range(1, n_chip):
+        ring[d].wait_send()
     for copy in pair:
         copy.wait()
     out_ref[...] = held[...]

time: 328 us -> 322 us (0.982)
  Pallas kernels: 107 us -> 101 us
    pallas_call x3, Pallas kernels: 67.3 us -> 61.9 us  [scatter_angle(): pl.pallas_call(functools.partial(_scatter_kernel, n_chip), out_shape=jax....]
  transfers between devices with their start and end apart: 27 -> 27, of which waited for: 11 -> 11; matrix products, arithmetic and copies ran while one was open for 15% -> 16% of each run, Pallas kernels for 9% -> 9%
where the time goes in v4:
time: 322 us; the launch traced here: 320 us
  Pallas kernels  101 us (31%)
  starting transfers between devices  85.3 us (26%)
  matrix products  67 us (21%)
  local copies, waits for them, and re-layouts  28.1 us (9%)
  waiting for transfers between devices  25.3 us (8%)
  other arithmetic  10.3 us (3%)
    ppermute x27, starting transfers between devices, from_behind(): lax.ppermute(value, axis, [(source, source + steps) for source in range(f...  85.3 us
    pallas_call x3, Pallas kernels, scatter_angle(): pl.pallas_call(functools.partial(_scatter_kernel, n_chip), out_shape=jax....  61.9 us
    pallas_call x2, Pallas kernels, gather_angle(): pl.pallas_call(functools.partial(_gather_kernel, n_chip), out_shape=jax.S...  29.9 us
    ppermute x27, waiting for transfers between devices, from_behind(): lax.ppermute(value, axis, [(source, source + steps) for source in range(f...  25.3 us
    dot_general x3, matrix products, shards(): jnp.einsum('trn,trv->nv', picked, tiles, preferred_element_type=jnp.float32)  23.2 us
    dot_general x2, matrix products, shards(): jnp.einsum('trv,nv->trn', tiles, gathered, preferred_element_type=jnp.flo...  18.4 us
    unnamed x31, local copies, waits for them, and re-layouts  11.8 us
    pallas_call x1, Pallas kernels, sum_angle(): pl.pallas_call(functools.partial(_sum_kernel, groups), out_shape=jax.Shap...  9.38 us
  transfers between devices with their start and end apart: 27, of which 11 were waited for; matrix products, arithmetic and copies ran while one was open for 16% of the time, Pallas kernels for 9%

profile of v4, /device:TPU:33, one launch (start us, length us, event | category | flops | bytes accessed | tf_op | source)
XLA Modules:
  0.0 319.8 jit_solution(7829698110741982114)
XLA Ops:
  2.4 7.9 %fusion.13 = bf16[1,3,512]{2,0,1:T(2,128)(2,1)S(1)} fusion(bf16[1,1,3,512,4096]{4,3,2,1,0:T(8,128)(2,1)} %param.10), kind=kOutput, calls=%fused_computation.13 | convolution fusion | flops 12582912 | bytes 12585984 | tf_op jit(solution)/shard_map/dot_general | solution.py:298
  11.1 4.8 %collective-permute-start.3 = (f32[512]{0:T(512)}, f32[512]{0:T(512)}, u32[]{:S(2)}, u32[]{:S(2)}) collective-permute-start(f32[512]{0:T(512)} %bitcast.17), channel_id=1, source_target_pairs={{0,16},{8,24},{16,32},{24,40},{32,48},{40,56},{48,64},{56,72},{64,... | collective-permute-start | bytes 6152 | tf_op jit(solution)/shard_map/ppermute | solution.py:22
  16.0 2.3 collective-permute-start.2
  19.1 2.6 collective-permute-start.7
  21.8 6.5 %fusion.26 = bf16[3,512,128]{2,1,0:T(8,128)(2,1)S(1)} fusion(bf16[4096,128,1]{1,0,2:T(8,128)(2,1)S(1)} %bitcast.313, bf16[1,1,3,512,4096]{4,3,2,1,0:T(8,128)(2,1)} %param.10), kind=kOutput, calls=%fused_computation.23 | convolution fusion | flops 1610809344 | bytes 14024704 | tf_op jit(solution)/shard_map/trv,vn->trn/dot_general | solution.py:337
  28.3 1.6 fusion.116
  30.4 6.0 %collective-permute-start.1 = (bf16[512,128]{1,0:T(8,128)(2,1)S(1)}, bf16[512,128]{1,0:T(8,128)(2,1)}, u32[]{:S(2)}, u32[]{:S(2)}) collective-permute-start(bf16[512,128]{1,0:T(8,128)(2,1)S(1)} %bitcast.324), channel_id=1, source_target_pairs={{0,16},{8,24},{16,32},{24,40},{32,48},{40,56},{48,64},{56,72},{64,... | collective-permute-start | bytes 393224 | tf_op jit(solution)/shard_map/ppermute | solution.py:22
  36.5 1.9 collective-permute-start
  38.4 2.6 constant_dynamic-slice_fusion.3
  41.0 1.9 constant_dynamic-slice_fusion.4
  43.7 6.3 %fusion = f32[1,8,512]{2,0,1:T(1,128)S(1)} fusion(pred[1536,1,1]{0,1,2:T(4,128)(4,1)} %reshape.68, bf16[192,8,8,512]{3,2,1,0:T(8,128)(2,1)} %bitcast.301), kind=kOutput, calls=%fused_computation | convolution fusion | flops 12582912 | bytes 12600832 | tf_op jit(solution)/shard_map/dot_general | solution.py:306
  50.6 9.4 %shard_map.104 = f32[8,512]{1,0:T(8,128)} custom-call(f32[8,512]{1,0:T(8,128)} %bitcast.332), custom_call_target="tpu_custom_call" | custom-call | flops 32768 | bytes 262144 | tf_op jit(solution)/shard_map/pallas_call | solution.py:148
  60.7 1.3 constant_dynamic-slice_fusion
  62.1 3.2 %constant_dynamic-slice_fusion.1 = (bf16[8,512,16]{2,1,0:T(8,128)(2,1)}, bf16[8,512,16]{2,1,0:T(8,128)(2,1)}) fusion(bf16[8,512,128]{2,1,0:T(8,128)(2,1)S(1)} %copy-done.2, s32[]{:T(128)S(6)} %select_n.7, bf16[8,512,128]{2,1,0:T(8,128)(2,1)} %param.16), kind=kLoop, calls=%fused_computation.157 | loop fusion | bytes 524292 | tf_op jit(solution)/shard_map/dynamic_slice | solution.py:319
  65.3 1.4 slice.178
  67.4 1.1 fusion.50
  68.5 4.4 %collective-permute-start.5 = (bf16[512,128]{1,0:T(8,128)(2,1)S(1)}, bf16[512,128]{1,0:T(8,128)(2,1)S(1)}, u32[]{:S(2)}, u32[]{:S(2)}) collective-permute-start(bf16[512,128]{1,0:T(8,128)(2,1)S(1)} %fusion.50), channel_id=1, source_target_pairs={{16,0},{24,8},{32,16},{40,24},{48,32},{56,40},{64,48},{72,56},{80,... | collective-permute-start | bytes 393224 | tf_op jit(solution)/shard_map/ppermute | solution.py:22
  72.9 3.4 %collective-permute-start.4 = (bf16[512,128]{1,0:T(8,128)(2,1)S(1)}, bf16[512,128]{1,0:T(8,128)(2,1)S(1)}, u32[]{:S(2)}, u32[]{:S(2)}) collective-permute-start(bf16[512,128]{1,0:T(8,128)(2,1)S(1)} %fusion.50), channel_id=1, source_target_pairs={{8,0},{16,8},{24,16},{32,24},{40,32},{48,40},{56,48},{64,56},{72,6... | collective-permute-start | bytes 393224 | tf_op jit(solution)/shard_map/ppermute | solution.py:22
  76.4 1.6 copy.207
  78.0 1.6 copy.201
  80.2 1.6 copy.206
  81.8 1.6 copy.205
  83.5 1.1 fusion.35
  84.8 7.7 %fusion.17.part_ref.half_ref = f32[8,16,4096]{2,1,0:T(8,128)} fusion(bf16[8,16,512,3]{2,1,0,3:T(8,128)(2,1)S(1)} %bitcast.310, bf16[1,1,3,512,4096]{4,3,2,1,0:T(8,128)(2,1)} %param.10), kind=kOutput, calls=%fused_computation.17 | convolution fusion | flops 1610612736 | bytes 15073280 | tf_op jit(solution)/shard_map/trn,trv->nv/dot_general | solution.py:360
  92.5 20.0 %shard_map.105 = f32[16,4096]{1,0:T(8,128)} custom-call(f32[8,16,4096]{2,1,0:T(8,128)} %fusion.17.part_ref.half_ref, f32[8,16,4096]{2,1,0:T(8,128)} %fusion.17.part_ref.half_ref), custom_call_target="tpu_custom_call" | custom-call | flops 1048576 | bytes 6291456 | tf_op jit(solution)/shard_map/pallas_call | solution.py:97
  112.6 1.1 copy.210
  113.8 2.6 collective-permute-start.10
  116.6 1.9 collective-permute-start.9
  118.6 3.2 %collective-permute-start.6 = (f32[16,512]{1,0:T(8,128)S(1)}, f32[16,512]{1,0:T(8,128)S(1)}, u32[]{:S(2)}, u32[]{:S(2)}) collective-permute-start(f32[16,512]{1,0:T(8,128)S(1)} %bitcast.334), channel_id=1, source_target_pairs={{8,0},{16,8},{24,16},{32,24},{40,32},{48,40},{56,48},{64,56},{72,6... | collective-permute-start | bytes 98312 | tf_op jit(solution)/shard_map/ppermute | solution.py:22
  121.8 2.1 collective-permute-start.8
  123.9 5.1 %collective-permute-done.8 = f32[16,512]{1,0:T(8,128)S(1)} collective-permute-done((f32[16,512]{1,0:T(8,128)S(1)}, f32[16,512]{1,0:T(8,128)S(1)}, u32[]{:S(2)}, u32[]{:S(2)}) %collective-permute-start.8) | collective-permute-done | bytes 32800 | tf_op jit(solution)/shard_map/ppermute | solution.py:22
  131.1 15.5 %shard_map.106 = bf16[8,16,4096]{2,1,0:T(8,128)(2,1)} custom-call(bf16[16,4096]{1,0:T(8,128)(2,1)} %bitcast.319), custom_call_target="tpu_custom_call" | custom-call | bytes 2097152 | tf_op jit(solution)/shard_map/pallas_call | solution.py:219
  146.5 9.2 %fusion.38 = bf16[3,512,128]{1,2,0:T(8,128)(2,1)S(1)} fusion(bf16[128,4096,1]{1,0,2:T(8,128)(2,1)} %bitcast.302, bf16[1,1,3,512,4096]{4,3,2,1,0:T(8,128)(2,1)} %param.10), kind=kOutput, calls=%fused_computation.29 | convolution fusion | flops 1610809344 | bytes 14024704 | tf_op jit(solution)/shard_map/trv,nv->trn/dot_general | solution.py:341
  156.7 1.9 collective-permute-start.11
  158.6 2.7 collective-permute-start.12
  161.3 4.4 %collective-permute-done.11 = bf16[512,128]{1,0:T(8,128)(2,1)S(1)} collective-permute-done((bf16[512,128]{1,0:T(8,128)(2,1)S(1)}, bf16[512,128]{1,0:T(8,128)(2,1)S(1)}, u32[]{:S(2)}, u32[]{:S(2)}) %collective-permute-start.11) | collective-permute-done | bytes 131104 | tf_op jit(solution)/shard_map/ppermute | solution.py:22
  165.7 2.3 collective-permute-done.12
  168.1 1.9 collective-permute-start.14
  170.0 4.4 %collective-permute-start.13 = (bf16[512,128]{1,0:T(8,128)(2,1)S(1)}, bf16[512,128]{1,0:T(8,128)(2,1)S(1)}, u32[]{:S(2)}, u32[]{:S(2)}) collective-permute-start(bf16[512,128]{1,0:T(8,128)(2,1)S(1)} %fusion.52), channel_id=1, source_target_pairs={{8,0},{16,8},{24,16},{32,24},{40,32},{48,40},{56,48},{64,56},{72,6... | collective-permute-start | bytes 393224 | tf_op jit(solution)/shard_map/ppermute | solution.py:22
  175.3 3.5 %collective-permute-done.13 = bf16[512,128]{1,0:T(8,128)(2,1)S(1)} collective-permute-done((bf16[512,128]{1,0:T(8,128)(2,1)S(1)}, bf16[512,128]{1,0:T(8,128)(2,1)S(1)}, u32[]{:S(2)}, u32[]{:S(2)}) %collective-permute-start.13) | collective-permute-done | bytes 131104 | tf_op jit(solution)/shard_map/ppermute | solution.py:22
  179.6 7.7 %fusion.20.part_ref.half_ref = f32[8,16,4096]{2,1,0:T(8,128)} fusion(bf16[8,16,512,3]{2,1,0,3:T(8,128)(2,1)S(1)} %bitcast.311, bf16[1,1,3,512,4096]{4,3,2,1,0:T(8,128)(2,1)} %param.10), kind=kOutput, calls=%fused_computation.18 | convolution fusion | flops 1610612736 | bytes 15073280 | tf_op jit(solution)/shard_map/trn,trv->nv/dot_general | solution.py:360
  187.3 20.4 %shard_map.107 = f32[16,4096]{1,0:T(8,128)} custom-call(f32[8,16,4096]{2,1,0:T(8,128)} %fusion.20.part_ref.half_ref, f32[8,16,4096]{2,1,0:T(8,128)} %fusion.20.part_ref.half_ref), custom_call_target="tpu_custom_call" | custom-call | flops 1048576 | bytes 6291456 | tf_op jit(solution)/shard_map/pallas_call | solution.py:97
  207.7 1.1 copy.212
  209.3 2.2 collective-permute-start.18
  211.5 2.1 collective-permute-start.17
  213.6 2.8 collective-permute-start.16
  216.4 4.6 %collective-permute-start.15 = (f32[16,512]{1,0:T(8,128)S(1)}, f32[16,512]{1,0:T(8,128)S(1)}, u32[]{:S(2)}, u32[]{:S(2)}) collective-permute-start(f32[16,512]{1,0:T(8,128)S(1)} %get-tuple-element.24), channel_id=1, source_target_pairs={{8,0},{16,8},{24,16},{32,24},{40,32},{48,40},{56,48},{64,56},{72,6... | collective-permute-start | bytes 98312 | tf_op jit(solution)/shard_map/ppermute | solution.py:22
  223.6 14.4 %shard_map.108 = bf16[8,16,4096]{2,1,0:T(8,128)(2,1)} custom-call(bf16[16,4096]{1,0:T(8,128)(2,1)} %bitcast.320), custom_call_target="tpu_custom_call" | custom-call | bytes 2097152 | tf_op jit(solution)/shard_map/pallas_call | solution.py:219
  238.0 9.2 %fusion.41 = bf16[3,512,128]{1,2,0:T(8,128)(2,1)S(1)} fusion(bf16[128,4096,1]{1,0,2:T(8,128)(2,1)} %bitcast.303, bf16[1,1,3,512,4096]{4,3,2,1,0:T(8,128)(2,1)} %param.10), kind=kOutput, calls=%fused_computation.30 | convolution fusion | flops 1610809344 | bytes 14024704 | tf_op jit(solution)/shard_map/trv,nv->trn/dot_general | solution.py:341
  248.2 3.5 %collective-permute-start.19 = (bf16[512,128]{1,0:T(8,128)(2,1)S(1)}, bf16[512,128]{1,0:T(8,128)(2,1)S(1)}, u32[]{:S(2)}, u32[]{:S(2)}) collective-permute-start(bf16[512,128]{1,0:T(8,128)(2,1)S(1)} %get-tuple-element.12), channel_id=1, source_target_pairs={{0,8},{8,16},{16,24},{24,32},{32,40},{40,48},{48,56},{56,64},{64,7... | collective-permute-start | bytes 393224 | tf_op jit(solution)/shard_map/ppermute | solution.py:22
  251.7 5.8 %collective-permute-start.20 = (bf16[512,128]{1,0:T(8,128)(2,1)S(1)}, bf16[512,128]{1,0:T(8,128)(2,1)S(1)}, u32[]{:S(2)}, u32[]{:S(2)}) collective-permute-start(bf16[512,128]{1,0:T(8,128)(2,1)S(1)} %get-tuple-element.13), channel_id=1, source_target_pairs={{0,16},{8,24},{16,32},{24,40},{32,48},{40,56},{48,64},{56,72},{64,... | collective-permute-start | bytes 393224 | tf_op jit(solution)/shard_map/ppermute | solution.py:22
  258.0 3.7 %collective-permute-done.20 = bf16[512,128]{1,0:T(8,128)(2,1)S(1)} collective-permute-done((bf16[512,128]{1,0:T(8,128)(2,1)S(1)}, bf16[512,128]{1,0:T(8,128)(2,1)S(1)}, u32[]{:S(2)}, u32[]{:S(2)}) %collective-permute-start.20) | collective-permute-done | bytes 131104 | tf_op jit(solution)/shard_map/ppermute | solution.py:22
  262.5 3.7 %collective-permute-start.22 = (bf16[512,128]{1,0:T(8,128)(2,1)S(1)}, bf16[512,128]{1,0:T(8,128)(2,1)S(1)}, u32[]{:S(2)}, u32[]{:S(2)}) collective-permute-start(bf16[512,128]{1,0:T(8,128)(2,1)S(1)} %get-tuple-element.9), channel_id=1, source_target_pairs={{16,0},{24,8},{32,16},{40,24},{48,32},{56,40},{64,48},{72,56},{80,... | collective-permute-start | bytes 393224 | tf_op jit(solution)/shard_map/ppermute | solution.py:22
  266.2 2.2 collective-permute-start.21
  268.4 1.4 collective-permute-done.22
  269.7 2.2 collective-permute-done.21
  272.7 7.7 %fusion.23.part_ref.half_ref = f32[8,16,4096]{2,1,0:T(8,128)} fusion(bf16[8,16,512,3]{2,1,0,3:T(8,128)(2,1)S(1)} %bitcast.312, bf16[1,1,3,512,4096]{4,3,2,1,0:T(8,128)(2,1)} %param.10), kind=kOutput, calls=%fused_computation.19 | convolution fusion | flops 1610612736 | bytes 15073280 | tf_op jit(solution)/shard_map/trn,trv->nv/dot_general | solution.py:360
  280.4 21.5 %shard_map.109 = f32[16,4096]{1,0:T(8,128)} custom-call(f32[8,16,4096]{2,1,0:T(8,128)} %fusion.23.part_ref.half_ref, f32[8,16,4096]{2,1,0:T(8,128)} %fusion.23.part_ref.half_ref), custom_call_target="tpu_custom_call" | custom-call | flops 1048576 | bytes 6291456 | tf_op jit(solution)/shard_map/pallas_call | solution.py:97
  301.9 1.1 copy.213
  303.7 1.9 collective-permute-start.26
  305.9 3.2 %collective-permute-start.24 = (f32[16,512]{1,0:T(8,128)S(1)}, f32[16,512]{1,0:T(8,128)S(1)}, u32[]{:S(2)}, u32[]{:S(2)}) collective-permute-start(f32[16,512]{1,0:T(8,128)S(1)} %get-tuple-element.16), channel_id=1, source_target_pairs={{0,8},{8,16},{16,24},{24,32},{32,40},{40,48},{48,56},{56,64},{64,7... | collective-permute-start | bytes 98312 | tf_op jit(solution)/shard_map/ppermute | solution.py:22
  309.1 4.2 %collective-permute-start.23 = (f32[16,512]{1,0:T(8,128)S(1)}, f32[16,512]{1,0:T(8,128)S(1)}, u32[]{:S(2)}, u32[]{:S(2)}) collective-permute-start(f32[16,512]{1,0:T(8,128)S(1)} %get-tuple-element.17), channel_id=1, source_target_pairs={{8,0},{16,8},{24,16},{32,24},{40,32},{48,40},{56,48},{64,56},{72,6... | collective-permute-start | bytes 98312 | tf_op jit(solution)/shard_map/ppermute | solution.py:22
  313.3 3.0 collective-permute-start.25
  317.1 1.2 collective-permute-done.25
  (126 shorter events, 20.9 us)
Async XLA Ops:
  0.6 17.6 %slice-start = ((bf16[8,512,128]{2,1,0:T(8,128)(2,1)}), bf16[1,512,128]{2,1,0:T(8,128)(2,1)S(1)}, s32[]{:S(2)}) async-start(bf16[8,512,128]{2,1,0:T(8,128)(2,1)} %param.15), calls=%async_computation | async-start | bytes 262144 | tf_op jit(solution)/shard_map/slice | solution.py:310
  0.6 21.0 %copy-start = (f32[8,512,128]{2,1,0:T(8,128)S(1)}, f32[8,512,128]{2,1,0:T(8,128)}, u32[]{:S(2)}) copy-start(f32[8,512,128]{2,1,0:T(8,128)} %param.9) | copy-start | bytes 6291460
  2.4 25.9 %copy-start.4 = (pred[3,3]{1,0:T(4,128)(4,1)}, pred[3,3]{1,0:T(4,128)(4,1)S(1)}, u32[]{:S(2)}) copy-start(pred[3,3]{1,0:T(4,128)(4,1)S(1)} %fusion.96) | copy-start | bytes 31
  11.1 55.6 %collective-permute-start.3 = (f32[512]{0:T(512)}, f32[512]{0:T(512)}, u32[]{:S(2)}, u32[]{:S(2)}) collective-permute-start(f32[512]{0:T(512)} %bitcast.17), channel_id=1, source_target_pairs={{0,16},{8,24},{16,32},{24,40},{32,48},{40,56},{48,64},{56,72},{64,... | collective-permute-start | bytes 6152 | tf_op jit(solution)/shard_map/ppermute | solution.py:22
  16.0 50.8 %collective-permute-start.2 = (f32[512]{0:T(512)}, f32[512]{0:T(512)}, u32[]{:S(2)}, u32[]{:S(2)}) collective-permute-start(f32[512]{0:T(512)} %bitcast.16), channel_id=1, source_target_pairs={{0,8},{8,16},{16,24},{24,32},{32,40},{40,48},{48,56},{56,64},{64,7... | collective-permute-start | bytes 6152 | tf_op jit(solution)/shard_map/ppermute | solution.py:22
  19.1 104.9 %collective-permute-start.7 = (bf16[512,128]{0,1:T(8,128)(2,1)}, bf16[512,128]{0,1:T(8,128)(2,1)}, u32[]{:S(2)}, u32[]{:S(2)}) collective-permute-start(bf16[512,128]{0,1:T(8,128)(2,1)} %bitcast.28), channel_id=1, source_target_pairs={{0,8},{8,16},{16,24},{24,32},{32,40},{40,48},{48,56},{56,64},{64,7... | collective-permute-start | bytes 393224 | tf_op jit(solution)/shard_map/ppermute | solution.py:22
  28.3 32.4 %copy-start.2 = (bf16[8,512,128]{2,1,0:T(8,128)(2,1)S(1)}, bf16[8,512,128]{2,1,0:T(8,128)(2,1)}, u32[]{:S(2)}) copy-start(bf16[8,512,128]{2,1,0:T(8,128)(2,1)} %param.17) | copy-start | bytes 3145732
  30.4 37.0 %collective-permute-start.1 = (bf16[512,128]{1,0:T(8,128)(2,1)S(1)}, bf16[512,128]{1,0:T(8,128)(2,1)}, u32[]{:S(2)}, u32[]{:S(2)}) collective-permute-start(bf16[512,128]{1,0:T(8,128)(2,1)S(1)} %bitcast.324), channel_id=1, source_target_pairs={{0,16},{8,24},{16,32},{24,40},{32,48},{40,56},{48,64},{56,72},{64,... | collective-permute-start | bytes 393224 | tf_op jit(solution)/shard_map/ppermute | solution.py:22
  36.5 30.9 %collective-permute-start = (bf16[512,128]{1,0:T(8,128)(2,1)S(1)}, bf16[512,128]{1,0:T(8,128)(2,1)}, u32[]{:S(2)}, u32[]{:S(2)}) collective-permute-start(bf16[512,128]{1,0:T(8,128)(2,1)S(1)} %bitcast.325), channel_id=1, source_target_pairs={{0,8},{8,16},{16,24},{24,32},{32,40},{40,48},{48,56},{56,64},{64,7... | collective-permute-start | bytes 393224 | tf_op jit(solution)/shard_map/ppermute | solution.py:22
  38.4 29.0 %copy-start.3 = (bf16[1,1,512,128]{3,2,1,0:T(8,128)(2,1)S(1)}, bf16[1,1,512,128]{3,2,1,0:T(8,128)(2,1)}, u32[]{:S(2)}) copy-start(bf16[1,1,512,128]{3,2,1,0:T(8,128)(2,1)} %param.14) | copy-start | bytes 393220
  43.0 36.6 %copy-start.1 = (f32[8,512,16]{2,1,0:T(8,128)S(1)}, f32[8,512,16]{2,1,0:T(8,128)}, u32[]{:S(2)}) copy-start(f32[8,512,16]{2,1,0:T(8,128)} %constant_dynamic-slice_fusion.4) | copy-start | bytes 786436
  65.3 156.8 %copy-start.6 = (pred[16]{0:T(512)(128)(4,1)}, pred[16]{0:T(512)(128)(4,1)S(1)}, u32[]{:S(2)}) copy-start(pred[16]{0:T(512)(128)(4,1)S(1)} %add_compare_fusion) | copy-start | bytes 52
  68.5 14.8 %collective-permute-start.5 = (bf16[512,128]{1,0:T(8,128)(2,1)S(1)}, bf16[512,128]{1,0:T(8,128)(2,1)S(1)}, u32[]{:S(2)}, u32[]{:S(2)}) collective-permute-start(bf16[512,128]{1,0:T(8,128)(2,1)S(1)} %fusion.50), channel_id=1, source_target_pairs={{16,0},{24,8},{32,16},{40,24},{48,32},{56,40},{64,48},{72,56},{80,... | collective-permute-start | bytes 393224 | tf_op jit(solution)/shard_map/ppermute | solution.py:22
  72.9 10.5 %collective-permute-start.4 = (bf16[512,128]{1,0:T(8,128)(2,1)S(1)}, bf16[512,128]{1,0:T(8,128)(2,1)S(1)}, u32[]{:S(2)}, u32[]{:S(2)}) collective-permute-start(bf16[512,128]{1,0:T(8,128)(2,1)S(1)} %fusion.50), channel_id=1, source_target_pairs={{8,0},{16,8},{24,16},{32,24},{40,32},{48,40},{56,48},{64,56},{72,6... | collective-permute-start | bytes 393224 | tf_op jit(solution)/shard_map/ppermute | solution.py:22
  112.6 43.5 %copy-start.5 = (pred[3,3]{1,0:T(4,128)(4,1)S(1)}, pred[3,3]{1,0:T(4,128)(4,1)}, u32[]{:S(2)}) copy-start(pred[3,3]{1,0:T(4,128)(4,1)} %copy-done.4) | copy-start | bytes 31
  113.8 10.1 %collective-permute-start.10 = (f32[8,512]{1,0:T(8,128)S(1)}, f32[8,512]{1,0:T(8,128)S(1)}, u32[]{:S(2)}, u32[]{:S(2)}) collective-permute-start(f32[8,512]{1,0:T(8,128)S(1)} %get-tuple-element.33), channel_id=1, source_target_pairs={{0,1},{1,2},{2,3},{3,4},{4,5},{5,6},{6,7},{8,9},{9,10},{10,11},{11... | collective-permute-start | bytes 49160 | tf_op jit(solution)/shard_map/ppermute | solution.py:22
  116.6 13.2 %collective-permute-start.9 = (f32[8,512]{1,0:T(8,128)S(1)}, f32[8,512]{1,0:T(8,128)S(1)}, u32[]{:S(2)}, u32[]{:S(2)}) collective-permute-start(f32[8,512]{1,0:T(8,128)S(1)} %get-tuple-element.34), channel_id=1, source_target_pairs={{1,0},{2,1},{3,2},{4,3},{5,4},{6,5},{7,6},{9,8},{10,9},{11,10},{12... | collective-permute-start | bytes 49160 | tf_op jit(solution)/shard_map/ppermute | solution.py:22
  118.6 11.2 %collective-permute-start.6 = (f32[16,512]{1,0:T(8,128)S(1)}, f32[16,512]{1,0:T(8,128)S(1)}, u32[]{:S(2)}, u32[]{:S(2)}) collective-permute-start(f32[16,512]{1,0:T(8,128)S(1)} %bitcast.334), channel_id=1, source_target_pairs={{8,0},{16,8},{24,16},{32,24},{40,32},{48,40},{56,48},{64,56},{72,6... | collective-permute-start | bytes 98312 | tf_op jit(solution)/shard_map/ppermute | solution.py:22
  121.8 7.2 %collective-permute-start.8 = (f32[16,512]{1,0:T(8,128)S(1)}, f32[16,512]{1,0:T(8,128)S(1)}, u32[]{:S(2)}, u32[]{:S(2)}) collective-permute-start(f32[16,512]{1,0:T(8,128)S(1)} %bitcast.335), channel_id=1, source_target_pairs={{0,8},{8,16},{16,24},{24,32},{32,40},{40,48},{48,56},{56,64},{64,7... | collective-permute-start | bytes 98312 | tf_op jit(solution)/shard_map/ppermute | solution.py:22
  156.7 9.0 %collective-permute-start.11 = (bf16[512,128]{1,0:T(8,128)(2,1)S(1)}, bf16[512,128]{1,0:T(8,128)(2,1)S(1)}, u32[]{:S(2)}, u32[]{:S(2)}) collective-permute-start(bf16[512,128]{1,0:T(8,128)(2,1)S(1)} %get-tuple-element.14), channel_id=1, source_target_pairs={{0,8},{8,16},{16,24},{24,32},{32,40},{40,48},{48,56},{56,64},{64,7... | collective-permute-start | bytes 393224 | tf_op jit(solution)/shard_map/ppermute | solution.py:22
  158.6 9.3 %collective-permute-start.12 = (bf16[512,128]{1,0:T(8,128)(2,1)S(1)}, bf16[512,128]{1,0:T(8,128)(2,1)S(1)}, u32[]{:S(2)}, u32[]{:S(2)}) collective-permute-start(bf16[512,128]{1,0:T(8,128)(2,1)S(1)} %get-tuple-element.15), channel_id=1, source_target_pairs={{0,16},{8,24},{16,32},{24,40},{32,48},{40,56},{48,64},{56,72},{64,... | collective-permute-start | bytes 393224 | tf_op jit(solution)/shard_map/ppermute | solution.py:22
  168.1 7.2 %collective-permute-start.14 = (bf16[512,128]{1,0:T(8,128)(2,1)S(1)}, bf16[512,128]{1,0:T(8,128)(2,1)S(1)}, u32[]{:S(2)}, u32[]{:S(2)}) collective-permute-start(bf16[512,128]{1,0:T(8,128)(2,1)S(1)} %fusion.52), channel_id=1, source_target_pairs={{16,0},{24,8},{32,16},{40,24},{48,32},{56,40},{64,48},{72,56},{80,... | collective-permute-start | bytes 393224 | tf_op jit(solution)/shard_map/ppermute | solution.py:22
  170.0 8.8 %collective-permute-start.13 = (bf16[512,128]{1,0:T(8,128)(2,1)S(1)}, bf16[512,128]{1,0:T(8,128)(2,1)S(1)}, u32[]{:S(2)}, u32[]{:S(2)}) collective-permute-start(bf16[512,128]{1,0:T(8,128)(2,1)S(1)} %fusion.52), channel_id=1, source_target_pairs={{8,0},{16,8},{24,16},{32,24},{40,32},{48,40},{56,48},{64,56},{72,6... | collective-permute-start | bytes 393224 | tf_op jit(solution)/shard_map/ppermute | solution.py:22
  209.3 11.8 %collective-permute-start.18 = (f32[8,512]{1,0:T(8,128)S(1)}, f32[8,512]{1,0:T(8,128)S(1)}, u32[]{:S(2)}, u32[]{:S(2)}) collective-permute-start(f32[8,512]{1,0:T(8,128)S(1)} %get-tuple-element.21), channel_id=1, source_target_pairs={{0,1},{1,2},{2,3},{3,4},{4,5},{5,6},{6,7},{8,9},{9,10},{10,11},{11... | collective-permute-start | bytes 49160 | tf_op jit(solution)/shard_map/ppermute | solution.py:22
  211.5 10.7 %collective-permute-start.17 = (f32[8,512]{1,0:T(8,128)S(1)}, f32[8,512]{1,0:T(8,128)S(1)}, u32[]{:S(2)}, u32[]{:S(2)}) collective-permute-start(f32[8,512]{1,0:T(8,128)S(1)} %get-tuple-element.22), channel_id=1, source_target_pairs={{1,0},{2,1},{3,2},{4,3},{5,4},{6,5},{7,6},{9,8},{10,9},{11,10},{12... | collective-permute-start | bytes 49160 | tf_op jit(solution)/shard_map/ppermute | solution.py:22
  213.6 7.4 %collective-permute-start.16 = (f32[16,512]{1,0:T(8,128)S(1)}, f32[16,512]{1,0:T(8,128)S(1)}, u32[]{:S(2)}, u32[]{:S(2)}) collective-permute-start(f32[16,512]{1,0:T(8,128)S(1)} %get-tuple-element.23), channel_id=1, source_target_pairs={{0,8},{8,16},{16,24},{24,32},{32,40},{40,48},{48,56},{56,64},{64,7... | collective-permute-start | bytes 98312 | tf_op jit(solution)/shard_map/ppermute | solution.py:22
  216.4 5.7 %collective-permute-start.15 = (f32[16,512]{1,0:T(8,128)S(1)}, f32[16,512]{1,0:T(8,128)S(1)}, u32[]{:S(2)}, u32[]{:S(2)}) collective-permute-start(f32[16,512]{1,0:T(8,128)S(1)} %get-tuple-element.24), channel_id=1, source_target_pairs={{8,0},{16,8},{24,16},{32,24},{40,32},{48,40},{56,48},{64,56},{72,6... | collective-permute-start | bytes 98312 | tf_op jit(solution)/shard_map/ppermute | solution.py:22
  248.2 9.8 %collective-permute-start.19 = (bf16[512,128]{1,0:T(8,128)(2,1)S(1)}, bf16[512,128]{1,0:T(8,128)(2,1)S(1)}, u32[]{:S(2)}, u32[]{:S(2)}) collective-permute-start(bf16[512,128]{1,0:T(8,128)(2,1)S(1)} %get-tuple-element.12), channel_id=1, source_target_pairs={{0,8},{8,16},{16,24},{24,32},{32,40},{40,48},{48,56},{56,64},{64,7... | collective-permute-start | bytes 393224 | tf_op jit(solution)/shard_map/ppermute | solution.py:22
  251.7 10.0 %collective-permute-start.20 = (bf16[512,128]{1,0:T(8,128)(2,1)S(1)}, bf16[512,128]{1,0:T(8,128)(2,1)S(1)}, u32[]{:S(2)}, u32[]{:S(2)}) collective-permute-start(bf16[512,128]{1,0:T(8,128)(2,1)S(1)} %get-tuple-element.13), channel_id=1, source_target_pairs={{0,16},{8,24},{16,32},{24,40},{32,48},{40,56},{48,64},{56,72},{64,... | collective-permute-start | bytes 393224 | tf_op jit(solution)/shard_map/ppermute | solution.py:22
  262.5 7.2 %collective-permute-start.22 = (bf16[512,128]{1,0:T(8,128)(2,1)S(1)}, bf16[512,128]{1,0:T(8,128)(2,1)S(1)}, u32[]{:S(2)}, u32[]{:S(2)}) collective-permute-start(bf16[512,128]{1,0:T(8,128)(2,1)S(1)} %get-tuple-element.9), channel_id=1, source_target_pairs={{16,0},{24,8},{32,16},{40,24},{48,32},{56,40},{64,48},{72,56},{80,... | collective-permute-start | bytes 393224 | tf_op jit(solution)/shard_map/ppermute | solution.py:22
  266.2 5.7 %collective-permute-start.21 = (bf16[512,128]{1,0:T(8,128)(2,1)S(1)}, bf16[512,128]{1,0:T(8,128)(2,1)S(1)}, u32[]{:S(2)}, u32[]{:S(2)}) collective-permute-start(bf16[512,128]{1,0:T(8,128)(2,1)S(1)} %get-tuple-element.9), channel_id=1, source_target_pairs={{8,0},{16,8},{24,16},{32,24},{40,32},{48,40},{56,48},{64,56},{72,6... | collective-permute-start | bytes 393224 | tf_op jit(solution)/shard_map/ppermute | solution.py:22
  272.4 45.9 %copy-start.7 = (pred[16]{0:T(512)(128)(4,1)S(1)}, pred[16]{0:T(512)(128)(4,1)}, u32[]{:S(2)}) copy-start(pred[16]{0:T(512)(128)(4,1)} %copy-done.6) | copy-start | bytes 52
  303.7 12.5 %collective-permute-start.26 = (f32[8,512]{1,0:T(8,128)S(1)}, f32[8,512]{1,0:T(8,128)S(1)}, u32[]{:S(2)}, u32[]{:S(2)}) collective-permute-start(f32[8,512]{1,0:T(8,128)S(1)} %bitcast.340), channel_id=1, source_target_pairs={{0,1},{1,2},{2,3},{3,4},{4,5},{5,6},{6,7},{8,9},{9,10},{10,11},{11... | collective-permute-start | bytes 49160 | tf_op jit(solution)/shard_map/ppermute | solution.py:22
  305.9 10.4 %collective-permute-start.24 = (f32[16,512]{1,0:T(8,128)S(1)}, f32[16,512]{1,0:T(8,128)S(1)}, u32[]{:S(2)}, u32[]{:S(2)}) collective-permute-start(f32[16,512]{1,0:T(8,128)S(1)} %get-tuple-element.16), channel_id=1, source_target_pairs={{0,8},{8,16},{16,24},{24,32},{32,40},{40,48},{48,56},{56,64},{64,7... | collective-permute-start | bytes 98312 | tf_op jit(solution)/shard_map/ppermute | solution.py:22
  309.1 8.0 %collective-permute-start.23 = (f32[16,512]{1,0:T(8,128)S(1)}, f32[16,512]{1,0:T(8,128)S(1)}, u32[]{:S(2)}, u32[]{:S(2)}) collective-permute-start(f32[16,512]{1,0:T(8,128)S(1)} %get-tuple-element.17), channel_id=1, source_target_pairs={{8,0},{16,8},{24,16},{32,24},{40,32},{48,40},{56,48},{64,56},{72,6... | collective-permute-start | bytes 98312 | tf_op jit(solution)/shard_map/ppermute | solution.py:22
  313.3 5.1 %collective-permute-start.25 = (f32[8,512]{1,0:T(8,128)S(1)}, f32[8,512]{1,0:T(8,128)S(1)}, u32[]{:S(2)}, u32[]{:S(2)}) collective-permute-start(f32[8,512]{1,0:T(8,128)S(1)} %slice_bitcast_fusion.10), channel_id=1, source_target_pairs={{1,0},{2,1},{3,2},{4,3},{5,4},{6,5},{7,6},{9,8},{10,9},{11,10},{12... | collective-permute-start | bytes 49160 | tf_op jit(solution)/shard_map/ppermute | solution.py:22

commit v5 on v4

--- a/solution.py
+++ b/solution.py
@@ -293,7 +293,7 @@
     distance_ids = jnp.arange(slot_count, dtype=jnp.int32)
     relative = ((target - slab_pos)[:, None] == distance_ids[None, :]) & live_slots[:, None]
     relative_float = relative.astype(jnp.float32)
-    relative_half = relative.astype(jnp.bfloat16)
+    far_relative = relative[1:, 1:].astype(jnp.bfloat16)
     flat_tiles = tiles.reshape(slot_count * ray_count, voxels)
     ray_local = jnp.dot(
         flat_tiles, jnp.ones((voxels,), jnp.bfloat16), preferred_element_type=jnp.float32
@@ -334,30 +334,46 @@
     for iteration in range(ITERS):
         if gathered is None:
             flat_volume = volume0.astype(jnp.bfloat16).reshape(voxels, column_count)
-            products = jnp.einsum(
-                "trv,vn->trn", tiles, flat_volume, preferred_element_type=jnp.float32
+            far_products = jnp.einsum(
+                "trv,vn->trn", tiles[1:], flat_volume, preferred_element_type=jnp.float32
             ).astype(jnp.bfloat16)
         else:
-            products = jnp.einsum(
-                "trv,nv->trn", tiles, gathered, preferred_element_type=jnp.float32
+            far_products = jnp.einsum(
+                "trv,nv->trn", tiles[1:], gathered, preferred_element_type=jnp.float32
             ).astype(jnp.bfloat16)
-        sends = jnp.einsum(
-            "td,trn->drn", relative_half, products, preferred_element_type=jnp.float32
-        )
-        sends_half = sends.astype(jnp.bfloat16)
-        projected = sends[0]
+        sends_half = jnp.einsum(
+            "td,trn->drn", far_relative, far_products, preferred_element_type=jnp.float32
+        ).astype(jnp.bfloat16)
+        arrived = [
+            from_behind(sends_half[distance - 1], "slab", distance)
+            for distance in range(1, slot_count)
+        ]
+        if gathered is None:
+            near_products = jnp.einsum(
+                "rv,vn->rn", tiles[0], flat_volume, preferred_element_type=jnp.float32
+            )
+        else:
+            near_products = jnp.einsum(
+                "rv,nv->rn", tiles[0], gathered, preferred_element_type=jnp.float32
+            )
+        near_products = lax.optimization_barrier(near_products.astype(jnp.bfloat16))
+        projected = near_products.astype(jnp.float32)
         for distance in range(1, slot_count):
-            arrived = from_behind(sends_half[distance], "slab", distance)
-            projected = projected + arrived.astype(jnp.float32)
+            projected = projected + arrived[distance - 1].astype(jnp.float32)
         residual = (measured - projected) * ray_scale[:, None]
         residual_half = residual.astype(jnp.bfloat16)
-        nearby = [residual_half] + [
+        nearby = [
             from_behind(residual_half, "slab", -distance) for distance in range(1, slot_count)
         ]
+        near_back = lax.optimization_barrier(
+            jnp.einsum("rn,rv->nv", residual_half, tiles[0], preferred_element_type=jnp.float32)
+        )
         picked = jnp.einsum(
-            "td,drn->trn", relative_half, jnp.stack(nearby), preferred_element_type=jnp.float32
+            "td,drn->trn", far_relative, jnp.stack(nearby), preferred_element_type=jnp.float32
         ).astype(jnp.bfloat16)
-        back_t = jnp.einsum("trn,trv->nv", picked, tiles, preferred_element_type=jnp.float32)
+        back_t = near_back + jnp.einsum(
+            "trn,trv->nv", picked, tiles[1:], preferred_element_type=jnp.float32
+        )
         back_own = scatter_angle(back_t.reshape(groups, share_width, voxels))
         volume = volume + voxel_scale * back_own.reshape(share_width, slab_depth, height)
         volume = smooth_share(

time: 322 us -> 319 us (level)
  waiting for transfers between devices: 25.3 us -> 13.8 us
  matrix products: 67 us -> 74.7 us
    ppermute x27, waiting for transfers between devices: 25.3 us -> 13.8 us  [from_behind(): lax.ppermute(value, axis, [(source, source + steps) for source in range(f...]
    dot_general x12 -> x18, matrix products: 52.6 us -> 61.1 us  [the longest x3 18 us: shards(): jnp.einsum('trn,trv->nv', picked, tiles[1:], preferred_element_type=jnp.f...]
    unnamed x31 -> x73, local copies, waits for them, and re-layouts: 11.8 us -> 13.7 us
  transfers between devices with their start and end apart: 27 -> 27, of which waited for: 11 -> 9; matrix products, arithmetic and copies ran while one was open for 16% -> 20% of each run, Pallas kernels for 9% -> 9%
where the time goes in v5:
time: 319 us; the launch traced here: 317 us
  Pallas kernels  102 us (32%)
  starting transfers between devices  87 us (27%)
  matrix products  74.7 us (23%)
  local copies, waits for them, and re-layouts  24.9 us (8%)
  waiting for transfers between devices  13.8 us (4%)
  other arithmetic  12.3 us (4%)
    ppermute x27, starting transfers between devices, from_behind(): lax.ppermute(value, axis, [(source, source + steps) for source in range(f...  87 us
    pallas_call x3, Pallas kernels, scatter_angle(): pl.pallas_call(functools.partial(_scatter_kernel, n_chip), out_shape=jax....  62.1 us
    pallas_call x2, Pallas kernels, gather_angle(): pl.pallas_call(functools.partial(_gather_kernel, n_chip), out_shape=jax.S...  29.9 us
    dot_general x3, matrix products, shards(): jnp.einsum('trn,trv->nv', picked, tiles[1:], preferred_element_type=jnp.f...  18 us
    ppermute x27, waiting for transfers between devices, from_behind(): lax.ppermute(value, axis, [(source, source + steps) for source in range(f...  13.8 us
    unnamed x73, local copies, waits for them, and re-layouts  13.7 us
    dot_general x2, matrix products, shards(): jnp.einsum('trv,nv->trn', tiles[1:], gathered, preferred_element_type=jnp...  13.4 us
    pallas_call x1, Pallas kernels, sum_angle(): pl.pallas_call(functools.partial(_sum_kernel, groups), out_shape=jax.Shap...  9.63 us
  transfers between devices with their start and end apart: 27, of which 9 were waited for; matrix products, arithmetic and copies ran while one was open for 20% of the time, Pallas kernels for 9%

profile of v5, /device:TPU:33, one launch (start us, length us, event | category | flops | bytes accessed | tf_op | source)
XLA Modules:
  0.0 317.1 jit_solution(5221907451804472247)
XLA Ops:
  2.4 7.9 %fusion.3 = bf16[1,3,512]{2,0,1:T(2,128)(2,1)S(1)} fusion(bf16[1,1,3,512,4096]{4,3,2,1,0:T(8,128)(2,1)} %param.10), kind=kOutput, calls=%fused_computation.3 | convolution fusion | flops 12582912 | bytes 12585984 | tf_op jit(solution)/shard_map/dot_general | solution.py:298
  11.0 4.8 %collective-permute-start.3 = (f32[512]{0:T(512)}, f32[512]{0:T(512)}, u32[]{:S(2)}, u32[]{:S(2)}) collective-permute-start(f32[512]{0:T(512)} %bitcast.19), channel_id=1, source_target_pairs={{0,16},{8,24},{16,32},{24,40},{32,48},{40,56},{48,64},{56,72},{64,... | collective-permute-start | bytes 6152 | tf_op jit(solution)/shard_map/ppermute | solution.py:22
  15.8 2.3 collective-permute-start.2
  18.9 2.6 collective-permute-start.7
  22.7 5.7 %fusion.15 = bf16[2,512,128]{2,1,0:T(8,128)(2,1)S(1)} fusion(bf16[4096,128,1]{1,0,2:T(8,128)(2,1)S(1)} %bitcast.308, bf16[1,1,3,512,4096]{4,3,2,1,0:T(8,128)(2,1)} %param.10), kind=kOutput, calls=%fused_computation.15 | convolution fusion | flops 1073741824 | bytes 9699328 | tf_op jit(solution)/shard_map/trv,vn->trn/dot_general | solution.py:337
  29.6 3.8 %collective-permute-start = (bf16[512,128]{1,0:T(8,128)(2,1)}, bf16[512,128]{1,0:T(8,128)(2,1)S(1)}, u32[]{:S(2)}, u32[]{:S(2)}) collective-permute-start(bf16[512,128]{1,0:T(8,128)(2,1)} %get-tuple-element.29), channel_id=1, source_target_pairs={{0,8},{8,16},{16,24},{24,32},{32,40},{40,48},{48,56},{56,64},{64,7... | collective-permute-start | bytes 393224 | tf_op jit(solution)/shard_map/ppermute | solution.py:22
  33.5 4.5 %collective-permute-start.1 = (bf16[512,128]{1,0:T(8,128)(2,1)}, bf16[512,128]{1,0:T(8,128)(2,1)S(1)}, u32[]{:S(2)}, u32[]{:S(2)}) collective-permute-start(bf16[512,128]{1,0:T(8,128)(2,1)} %get-tuple-element.30), channel_id=1, source_target_pairs={{0,16},{8,24},{16,32},{24,40},{32,48},{40,56},{48,64},{56,72},{64,... | collective-permute-start | bytes 393224 | tf_op jit(solution)/shard_map/ppermute | solution.py:22
  39.7 1.3 constant_dynamic-slice_fusion.3
  41.1 1.9 constant_dynamic-slice_fusion.4
  43.1 5.6 %fusion = f32[1,8,512]{2,0,1:T(1,128)S(1)} fusion(pred[1536,1,1]{0,1,2:T(4,128)(4,1)S(1)} %reshape.77, bf16[192,8,8,512]{3,2,1,0:T(8,128)(2,1)} %bitcast.295), kind=kOutput, calls=%fused_computation | convolution fusion | flops 12582912 | bytes 12600832 | tf_op jit(solution)/shard_map/dot_general | solution.py:306
  49.4 9.6 %shard_map.104 = f32[8,512]{1,0:T(8,128)} custom-call(f32[8,512]{1,0:T(8,128)} %bitcast.326), custom_call_target="tpu_custom_call" | custom-call | flops 32768 | bytes 262144 | tf_op jit(solution)/shard_map/pallas_call | solution.py:148
  59.8 4.4 %fusion.65 = bf16[512,128]{1,0:T(8,128)(2,1)} fusion(bf16[4096,128]{1,0:T(8,128)(2,1)} %bitcast.309, bf16[1,1,3,512,4096]{4,3,2,1,0:T(8,128)(2,1)} %param.10), kind=kOutput, calls=%fused_computation.49 | convolution fusion | flops 536936448 | bytes 5373952 | tf_op jit(solution)/shard_map/rv,vn->rn/dot_general | solution.py:352
  64.2 1.4 constant_dynamic-slice_fusion
  65.6 2.0 constant_dynamic-slice_fusion.1
  68.0 2.2 copy.99
  70.2 1.6 copy.93
  72.4 1.6 copy.98
  74.0 1.6 copy.97
  77.4 3.2 collective-permute-start.5
  80.6 3.4 %collective-permute-start.4 = (bf16[512,128]{1,0:T(8,128)(2,1)S(1)}, bf16[512,128]{1,0:T(8,128)(2,1)S(1)}, u32[]{:S(2)}, u32[]{:S(2)}) collective-permute-start(bf16[512,128]{1,0:T(8,128)(2,1)S(1)} %fusion.81), channel_id=1, source_target_pairs={{8,0},{16,8},{24,16},{32,24},{40,32},{48,40},{56,48},{64,56},{72,6... | collective-permute-start | bytes 393224 | tf_op jit(solution)/shard_map/ppermute | solution.py:22
  84.0 2.9 fusion.43
  86.9 1.5 collective-permute-done.4
  88.5 1.3 fusion.125
  90.0 6.0 %fusion.32 = f32[128,4096]{1,0:T(8,128)} fusion(f32[128,4096]{1,0:T(8,128)S(1)} %fusion.43, bf16[1,1,3,512,4096]{4,3,2,1,0:T(8,128)(2,1)} %param.10, bf16[2,512,128]{1,2,0:T(8,128)(2,1)S(1)} %copy.82), kind=kOutput, calls=%fused_computation.22 | convolution fusion | flops 1074266112 | bytes 12845056 | tf_op jit(solution)/shard_map/trn,trv->nv/dot_general | solution.py:374
  96.0 20.3 %shard_map.105 = f32[16,4096]{1,0:T(8,128)} custom-call(f32[8,16,4096]{2,1,0:T(8,128)} %bitcast.296, f32[8,16,4096]{2,1,0:T(8,128)} %bitcast.297), custom_call_target="tpu_custom_call" | custom-call | flops 1048576 | bytes 6291456 | tf_op jit(solution)/shard_map/pallas_call | solution.py:97
  116.3 1.1 copy.102
  117.5 2.6 collective-permute-start.10
  120.3 1.9 collective-permute-start.9
  122.3 5.5 %collective-permute-start.6 = (f32[16,512]{1,0:T(8,128)S(1)}, f32[16,512]{1,0:T(8,128)S(1)}, u32[]{:S(2)}, u32[]{:S(2)}) collective-permute-start(f32[16,512]{1,0:T(8,128)S(1)} %bitcast.328), channel_id=1, source_target_pairs={{8,0},{16,8},{24,16},{32,24},{40,32},{48,40},{56,48},{64,56},{72,6... | collective-permute-start | bytes 98312 | tf_op jit(solution)/shard_map/ppermute | solution.py:22
  127.8 1.9 collective-permute-start.8
  129.8 5.2 %collective-permute-done.8 = f32[16,512]{1,0:T(8,128)S(1)} collective-permute-done((f32[16,512]{1,0:T(8,128)S(1)}, f32[16,512]{1,0:T(8,128)S(1)}, u32[]{:S(2)}, u32[]{:S(2)}) %collective-permute-start.8) | collective-permute-done | bytes 32800 | tf_op jit(solution)/shard_map/ppermute | solution.py:22
  137.1 15.5 %shard_map.106 = bf16[8,16,4096]{2,1,0:T(8,128)(2,1)} custom-call(bf16[16,4096]{1,0:T(8,128)(2,1)} %bitcast.318), custom_call_target="tpu_custom_call" | custom-call | bytes 2097152 | tf_op jit(solution)/shard_map/pallas_call | solution.py:219
  152.6 6.7 %fusion.59 = bf16[128,2,512]{2,0,1:T(8,128)(2,1)S(1)} fusion(bf16[128,4096,1]{1,0,2:T(8,128)(2,1)} %bitcast.313, bf16[1,1,3,512,4096]{4,3,2,1,0:T(8,128)(2,1)} %param.10), kind=kOutput, calls=%fused_computation.47 | convolution fusion | flops 1073872896 | bytes 9699328 | tf_op jit(solution)/shard_map/trv,nv->trn/dot_general | solution.py:341
  160.1 1.9 collective-permute-start.11
  162.0 2.7 collective-permute-start.12
  164.7 3.4 %fusion.77 = bf16[512,128]{1,0:T(8,128)(2,1)S(1)} fusion(bf16[128,4096]{1,0:T(8,128)(2,1)S(1)} %bitcast.314, bf16[1,1,3,512,4096]{4,3,2,1,0:T(8,128)(2,1)} %param.10), kind=kOutput, calls=%fused_computation.53 | convolution fusion | flops 536936448 | bytes 5373952 | tf_op jit(solution)/shard_map/rv,nv->rn/dot_general | solution.py:356
  169.1 2.3 collective-permute-done.12
  171.5 1.9 collective-permute-start.14
  173.4 4.8 %collective-permute-start.13 = (bf16[512,128]{1,0:T(8,128)(2,1)S(1)}, bf16[512,128]{1,0:T(8,128)(2,1)S(1)}, u32[]{:S(2)}, u32[]{:S(2)}) collective-permute-start(bf16[512,128]{1,0:T(8,128)(2,1)S(1)} %fusion.83), channel_id=1, source_target_pairs={{8,0},{16,8},{24,16},{32,24},{40,32},{48,40},{56,48},{64,56},{72,6... | collective-permute-start | bytes 393224 | tf_op jit(solution)/shard_map/ppermute | solution.py:22
  178.2 2.9 fusion.39
  181.1 1.1 collective-permute-done.13
  183.1 6.0 %fusion.29 = f32[128,4096]{1,0:T(8,128)} fusion(f32[128,4096]{1,0:T(8,128)S(1)} %fusion.39, bf16[1,1,3,512,4096]{4,3,2,1,0:T(8,128)(2,1)} %param.10, bf16[2,512,128]{1,2,0:T(8,128)(2,1)S(1)} %copy.86), kind=kOutput, calls=%fused_computation.21 | convolution fusion | flops 1074266112 | bytes 12845056 | tf_op jit(solution)/shard_map/trn,trv->nv/dot_general | solution.py:374
  189.1 20.4 %shard_map.107 = f32[16,4096]{1,0:T(8,128)} custom-call(f32[8,16,4096]{2,1,0:T(8,128)} %bitcast.298, f32[8,16,4096]{2,1,0:T(8,128)} %bitcast.299), custom_call_target="tpu_custom_call" | custom-call | flops 1048576 | bytes 6291456 | tf_op jit(solution)/shard_map/pallas_call | solution.py:97
  209.4 1.1 copy.104
  211.0 2.2 collective-permute-start.18
  213.2 2.1 collective-permute-start.17
  215.3 2.8 collective-permute-start.16
  218.1 4.6 %collective-permute-start.15 = (f32[16,512]{1,0:T(8,128)S(1)}, f32[16,512]{1,0:T(8,128)S(1)}, u32[]{:S(2)}, u32[]{:S(2)}) collective-permute-start(f32[16,512]{1,0:T(8,128)S(1)} %get-tuple-element.16), channel_id=1, source_target_pairs={{8,0},{16,8},{24,16},{32,24},{40,32},{48,40},{56,48},{64,56},{72,6... | collective-permute-start | bytes 98312 | tf_op jit(solution)/shard_map/ppermute | solution.py:22
  225.3 14.4 %shard_map.108 = bf16[8,16,4096]{2,1,0:T(8,128)(2,1)} custom-call(bf16[16,4096]{1,0:T(8,128)(2,1)} %bitcast.319), custom_call_target="tpu_custom_call" | custom-call | bytes 2097152 | tf_op jit(solution)/shard_map/pallas_call | solution.py:219
  239.8 6.7 %fusion.62 = bf16[128,2,512]{2,0,1:T(8,128)(2,1)S(1)} fusion(bf16[128,4096,1]{1,0,2:T(8,128)(2,1)} %bitcast.315, bf16[1,1,3,512,4096]{4,3,2,1,0:T(8,128)(2,1)} %param.10), kind=kOutput, calls=%fused_computation.48 | convolution fusion | flops 1073872896 | bytes 9699328 | tf_op jit(solution)/shard_map/trv,nv->trn/dot_general | solution.py:341
  247.2 3.5 %collective-permute-start.19 = (bf16[512,128]{1,0:T(8,128)(2,1)S(1)}, bf16[512,128]{1,0:T(8,128)(2,1)S(1)}, u32[]{:S(2)}, u32[]{:S(2)}) collective-permute-start(bf16[512,128]{1,0:T(8,128)(2,1)S(1)} %get-tuple-element.11), channel_id=1, source_target_pairs={{0,8},{8,16},{16,24},{24,32},{32,40},{40,48},{48,56},{56,64},{64,7... | collective-permute-start | bytes 393224 | tf_op jit(solution)/shard_map/ppermute | solution.py:22
  250.8 5.8 %collective-permute-start.20 = (bf16[512,128]{1,0:T(8,128)(2,1)S(1)}, bf16[512,128]{1,0:T(8,128)(2,1)S(1)}, u32[]{:S(2)}, u32[]{:S(2)}) collective-permute-start(bf16[512,128]{1,0:T(8,128)(2,1)S(1)} %get-tuple-element.12), channel_id=1, source_target_pairs={{0,16},{8,24},{16,32},{24,40},{32,48},{40,56},{48,64},{56,72},{64,... | collective-permute-start | bytes 393224 | tf_op jit(solution)/shard_map/ppermute | solution.py:22
  256.6 3.4 %fusion.74 = bf16[512,128]{1,0:T(8,128)(2,1)S(1)} fusion(bf16[128,4096]{1,0:T(8,128)(2,1)S(1)} %bitcast.316, bf16[1,1,3,512,4096]{4,3,2,1,0:T(8,128)(2,1)} %param.10), kind=kOutput, calls=%fused_computation.52 | convolution fusion | flops 536936448 | bytes 5373952 | tf_op jit(solution)/shard_map/rv,nv->rn/dot_general | solution.py:356
  261.6 3.7 %collective-permute-start.22 = (bf16[512,128]{1,0:T(8,128)(2,1)S(1)}, bf16[512,128]{1,0:T(8,128)(2,1)S(1)}, u32[]{:S(2)}, u32[]{:S(2)}) collective-permute-start(bf16[512,128]{1,0:T(8,128)(2,1)S(1)} %get-tuple-element.5), channel_id=1, source_target_pairs={{16,0},{24,8},{32,16},{40,24},{48,32},{56,40},{64,48},{72,56},{80,... | collective-permute-start | bytes 393224 | tf_op jit(solution)/shard_map/ppermute | solution.py:22
  265.3 2.2 collective-permute-start.21
  267.5 2.9 fusion.35
  271.8 6.0 %fusion.26 = f32[128,4096]{1,0:T(8,128)} fusion(f32[128,4096]{1,0:T(8,128)S(1)} %fusion.35, bf16[1,1,3,512,4096]{4,3,2,1,0:T(8,128)(2,1)} %param.10, bf16[2,512,128]{1,2,0:T(8,128)(2,1)S(1)} %copy.90), kind=kOutput, calls=%fused_computation.20 | convolution fusion | flops 1074266112 | bytes 12845056 | tf_op jit(solution)/shard_map/trn,trv->nv/dot_general | solution.py:374
  277.8 21.5 %shard_map.109 = f32[16,4096]{1,0:T(8,128)} custom-call(f32[8,16,4096]{2,1,0:T(8,128)} %bitcast.300, f32[8,16,4096]{2,1,0:T(8,128)} %bitcast.301), custom_call_target="tpu_custom_call" | custom-call | flops 1048576 | bytes 6291456 | tf_op jit(solution)/shard_map/pallas_call | solution.py:97
  299.3 1.1 copy.105
  301.1 1.9 collective-permute-start.26
  303.2 3.3 %collective-permute-start.24 = (f32[16,512]{1,0:T(8,128)S(1)}, f32[16,512]{1,0:T(8,128)S(1)}, u32[]{:S(2)}, u32[]{:S(2)}) collective-permute-start(f32[16,512]{1,0:T(8,128)S(1)} %get-tuple-element.6), channel_id=1, source_target_pairs={{0,8},{8,16},{16,24},{24,32},{32,40},{40,48},{48,56},{56,64},{64,7... | collective-permute-start | bytes 98312 | tf_op jit(solution)/shard_map/ppermute | solution.py:22
  306.5 4.1 %collective-permute-start.23 = (f32[16,512]{1,0:T(8,128)S(1)}, f32[16,512]{1,0:T(8,128)S(1)}, u32[]{:S(2)}, u32[]{:S(2)}) collective-permute-start(f32[16,512]{1,0:T(8,128)S(1)} %get-tuple-element.7), channel_id=1, source_target_pairs={{8,0},{16,8},{24,16},{32,24},{40,32},{48,40},{56,48},{64,56},{72,6... | collective-permute-start | bytes 98312 | tf_op jit(solution)/shard_map/ppermute | solution.py:22
  310.6 3.0 collective-permute-start.25
  314.5 1.2 collective-permute-done.25
  (172 shorter events, 25.5 us)
Async XLA Ops:
  0.6 17.5 %slice-start = ((bf16[8,512,128]{2,1,0:T(8,128)(2,1)}), bf16[1,512,128]{2,1,0:T(8,128)(2,1)S(1)}, s32[]{:S(2)}) async-start(bf16[8,512,128]{2,1,0:T(8,128)(2,1)} %param.15), calls=%async_computation | async-start | bytes 262144 | tf_op jit(solution)/shard_map/slice | solution.py:310
  0.6 20.9 %copy-start = (f32[8,512,128]{2,1,0:T(8,128)S(1)}, f32[8,512,128]{2,1,0:T(8,128)}, u32[]{:S(2)}) copy-start(f32[8,512,128]{2,1,0:T(8,128)} %param.9) | copy-start | bytes 6291460
  2.3 26.0 %copy-start.24 = (pred[3,3]{0,1:T(4,128)(4,1)}, pred[3,3]{0,1:T(4,128)(4,1)S(1)}, u32[]{:S(2)}) copy-start(pred[3,3]{0,1:T(4,128)(4,1)S(1)} %fusion.139) | copy-start | bytes 31
  11.0 64.6 %collective-permute-start.3 = (f32[512]{0:T(512)}, f32[512]{0:T(512)}, u32[]{:S(2)}, u32[]{:S(2)}) collective-permute-start(f32[512]{0:T(512)} %bitcast.19), channel_id=1, source_target_pairs={{0,16},{8,24},{16,32},{24,40},{32,48},{40,56},{48,64},{56,72},{64,... | collective-permute-start | bytes 6152 | tf_op jit(solution)/shard_map/ppermute | solution.py:22
  15.8 59.8 %collective-permute-start.2 = (f32[512]{0:T(512)}, f32[512]{0:T(512)}, u32[]{:S(2)}, u32[]{:S(2)}) collective-permute-start(f32[512]{0:T(512)} %bitcast.18), channel_id=1, source_target_pairs={{0,8},{8,16},{16,24},{24,32},{32,40},{40,48},{48,56},{56,64},{64,7... | collective-permute-start | bytes 6152 | tf_op jit(solution)/shard_map/ppermute | solution.py:22
  18.9 110.9 %collective-permute-start.7 = (bf16[512,128]{0,1:T(8,128)(2,1)}, bf16[512,128]{0,1:T(8,128)(2,1)}, u32[]{:S(2)}, u32[]{:S(2)}) collective-permute-start(bf16[512,128]{0,1:T(8,128)(2,1)} %bitcast.26), channel_id=1, source_target_pairs={{0,8},{8,16},{16,24},{24,32},{32,40},{40,48},{48,56},{56,64},{64,7... | collective-permute-start | bytes 393224 | tf_op jit(solution)/shard_map/ppermute | solution.py:22
  21.7 1.0 copy-start.6
  21.7 18.0 %copy-start.3 = (bf16[8,512,128]{2,1,0:T(8,128)(2,1)S(1)}, bf16[8,512,128]{2,1,0:T(8,128)(2,1)}, u32[]{:S(2)}) copy-start(bf16[8,512,128]{2,1,0:T(8,128)(2,1)} %param.15) | copy-start | bytes 3145732
  29.6 46.7 %collective-permute-start = (bf16[512,128]{1,0:T(8,128)(2,1)}, bf16[512,128]{1,0:T(8,128)(2,1)S(1)}, u32[]{:S(2)}, u32[]{:S(2)}) collective-permute-start(bf16[512,128]{1,0:T(8,128)(2,1)} %get-tuple-element.29), channel_id=1, source_target_pairs={{0,8},{8,16},{16,24},{24,32},{32,40},{40,48},{48,56},{56,64},{64,7... | collective-permute-start | bytes 393224 | tf_op jit(solution)/shard_map/ppermute | solution.py:22
  33.5 42.9 %collective-permute-start.1 = (bf16[512,128]{1,0:T(8,128)(2,1)}, bf16[512,128]{1,0:T(8,128)(2,1)S(1)}, u32[]{:S(2)}, u32[]{:S(2)}) collective-permute-start(bf16[512,128]{1,0:T(8,128)(2,1)} %get-tuple-element.30), channel_id=1, source_target_pairs={{0,16},{8,24},{16,32},{24,40},{32,48},{40,56},{48,64},{56,72},{64,... | collective-permute-start | bytes 393224 | tf_op jit(solution)/shard_map/ppermute | solution.py:22
  43.1 21.1 %copy-start.2 = (bf16[8,512,128]{2,1,0:T(8,128)(2,1)S(1)}, bf16[8,512,128]{2,1,0:T(8,128)(2,1)}, u32[]{:S(2)}) copy-start(bf16[8,512,128]{2,1,0:T(8,128)(2,1)} %param.17) | copy-start | bytes 3145732
  48.8 23.0 %copy-start.1 = (f32[8,512,16]{2,1,0:T(8,128)S(1)}, f32[8,512,16]{2,1,0:T(8,128)}, u32[]{:S(2)}) copy-start(f32[8,512,16]{2,1,0:T(8,128)} %constant_dynamic-slice_fusion.4) | copy-start | bytes 786436
  59.0 6.6 %copy-start.5 = (bf16[8,512,128]{2,1,0:T(8,128)(2,1)S(1)}, bf16[8,512,128]{2,1,0:T(8,128)(2,1)}, u32[]{:S(2)}) copy-start(bf16[8,512,128]{2,1,0:T(8,128)(2,1)} %param.16) | copy-start | bytes 3145732
  64.2 12.1 %copy-start.4 = (bf16[1,1,512,128]{3,2,1,0:T(8,128)(2,1)S(1)}, bf16[1,1,512,128]{3,2,1,0:T(8,128)(2,1)}, u32[]{:S(2)}) copy-start(bf16[1,1,512,128]{3,2,1,0:T(8,128)(2,1)} %param.14) | copy-start | bytes 393220
  76.3 12.1 %copy-start.12 = (f32[512]{0:T(512)}, f32[512]{0:T(512)S(1)}, u32[]{:S(2)}) copy-start(f32[512]{0:T(512)S(1)} %add_divide_fusion) | copy-start | bytes 6148
  77.4 9.5 %collective-permute-start.5 = (bf16[512,128]{1,0:T(8,128)(2,1)S(1)}, bf16[512,128]{1,0:T(8,128)(2,1)S(1)}, u32[]{:S(2)}, u32[]{:S(2)}) collective-permute-start(bf16[512,128]{1,0:T(8,128)(2,1)S(1)} %fusion.81), channel_id=1, source_target_pairs={{16,0},{24,8},{32,16},{40,24},{48,32},{56,40},{64,48},{72,56},{80,... | collective-permute-start | bytes 393224 | tf_op jit(solution)/shard_map/ppermute | solution.py:22
  80.6 7.9 %collective-permute-start.4 = (bf16[512,128]{1,0:T(8,128)(2,1)S(1)}, bf16[512,128]{1,0:T(8,128)(2,1)S(1)}, u32[]{:S(2)}, u32[]{:S(2)}) collective-permute-start(bf16[512,128]{1,0:T(8,128)(2,1)S(1)} %fusion.81), channel_id=1, source_target_pairs={{8,0},{16,8},{24,16},{32,24},{40,32},{48,40},{56,48},{64,56},{72,6... | collective-permute-start | bytes 393224 | tf_op jit(solution)/shard_map/ppermute | solution.py:22
  90.0 39.8 %copy-start.9 = (bf16[8,512,1]{1,0,2:T(8,128)(2,1)S(1)}, bf16[8,512,1]{1,0,2:T(8,128)(2,1)}, u32[]{:S(2)}) copy-start(bf16[8,512,1]{1,0,2:T(8,128)(2,1)} %copy.99) | copy-start | bytes 24580
  90.0 45.9 %copy-start.17 = (pred[16]{0:T(512)(128)(4,1)S(1)}, pred[16]{0:T(512)(128)(4,1)}, u32[]{:S(2)}) copy-start(pred[16]{0:T(512)(128)(4,1)} %add_compare_fusion) | copy-start | bytes 52
  90.0 45.9 %copy-start.20 = (pred[8]{0:T(512)(128)(4,1)S(1)}, pred[8]{0:T(512)(128)(4,1)}, u32[]{:S(2)}) copy-start(pred[8]{0:T(512)(128)(4,1)} %add_compare_fusion.1) | copy-start | bytes 28
  90.0 45.9 %copy-start.23 = (pred[512]{0:T(512)(128)(4,1)S(1)}, pred[512]{0:T(512)(128)(4,1)}, u32[]{:S(2)}) copy-start(pred[512]{0:T(512)(128)(4,1)} %iota_compare_fusion) | copy-start | bytes 1540
  117.5 12.3 %collective-permute-start.10 = (f32[8,512]{1,0:T(8,128)S(1)}, f32[8,512]{1,0:T(8,128)S(1)}, u32[]{:S(2)}, u32[]{:S(2)}) collective-permute-start(f32[8,512]{1,0:T(8,128)S(1)} %get-tuple-element.27), channel_id=1, source_target_pairs={{0,1},{1,2},{2,3},{3,4},{4,5},{5,6},{6,7},{8,9},{9,10},{10,11},{11... | collective-permute-start | bytes 49160 | tf_op jit(solution)/shard_map/ppermute | solution.py:22
  120.3 15.5 %collective-permute-start.9 = (f32[8,512]{1,0:T(8,128)S(1)}, f32[8,512]{1,0:T(8,128)S(1)}, u32[]{:S(2)}, u32[]{:S(2)}) collective-permute-start(f32[8,512]{1,0:T(8,128)S(1)} %get-tuple-element.28), channel_id=1, source_target_pairs={{1,0},{2,1},{3,2},{4,3},{5,4},{6,5},{7,6},{9,8},{10,9},{11,10},{12... | collective-permute-start | bytes 49160 | tf_op jit(solution)/shard_map/ppermute | solution.py:22
  122.3 13.6 %collective-permute-start.6 = (f32[16,512]{1,0:T(8,128)S(1)}, f32[16,512]{1,0:T(8,128)S(1)}, u32[]{:S(2)}, u32[]{:S(2)}) collective-permute-start(f32[16,512]{1,0:T(8,128)S(1)} %bitcast.328), channel_id=1, source_target_pairs={{8,0},{16,8},{24,16},{32,24},{40,32},{48,40},{56,48},{64,56},{72,6... | collective-permute-start | bytes 98312 | tf_op jit(solution)/shard_map/ppermute | solution.py:22
  127.8 7.2 %collective-permute-start.8 = (f32[16,512]{1,0:T(8,128)S(1)}, f32[16,512]{1,0:T(8,128)S(1)}, u32[]{:S(2)}, u32[]{:S(2)}) collective-permute-start(f32[16,512]{1,0:T(8,128)S(1)} %bitcast.329), channel_id=1, source_target_pairs={{0,8},{8,16},{16,24},{24,32},{32,40},{40,48},{48,56},{56,64},{64,7... | collective-permute-start | bytes 98312 | tf_op jit(solution)/shard_map/ppermute | solution.py:22
  136.2 23.3 %copy-start.25 = (pred[3,3]{0,1:T(4,128)(4,1)S(1)}, pred[3,3]{0,1:T(4,128)(4,1)}, u32[]{:S(2)}) copy-start(pred[3,3]{0,1:T(4,128)(4,1)} %copy-done.24) | copy-start | bytes 31
  152.6 12.1 %copy-start.7 = (bf16[8,16,4096]{2,1,0:T(8,128)(2,1)S(1)}, bf16[8,16,4096]{2,1,0:T(8,128)(2,1)}, u32[]{:S(2)}) copy-start(bf16[8,16,4096]{2,1,0:T(8,128)(2,1)} %shard_map.106) | copy-start | bytes 3145732
  152.6 18.7 %copy-start.13 = (f32[512]{0:T(512)S(1)}, f32[512]{0:T(512)}, u32[]{:S(2)}) copy-start(f32[512]{0:T(512)} %copy-done.12) | copy-start | bytes 6148
  159.5 22.7 %copy-start.26 = (pred[3,3]{0,1:T(4,128)(4,1)S(1)}, pred[3,3]{0,1:T(4,128)(4,1)}, u32[]{:S(2)}) copy-start(pred[3,3]{0,1:T(4,128)(4,1)} %copy-done.24) | copy-start | bytes 31
  160.1 9.0 %collective-permute-start.11 = (bf16[512,128]{1,0:T(8,128)(2,1)S(1)}, bf16[512,128]{1,0:T(8,128)(2,1)S(1)}, u32[]{:S(2)}, u32[]{:S(2)}) collective-permute-start(bf16[512,128]{1,0:T(8,128)(2,1)S(1)} %get-tuple-element.20), channel_id=1, source_target_pairs={{0,8},{8,16},{16,24},{24,32},{32,40},{40,48},{48,56},{56,64},{64,7... | collective-permute-start | bytes 393224 | tf_op jit(solution)/shard_map/ppermute | solution.py:22
  162.0 9.3 %collective-permute-start.12 = (bf16[512,128]{1,0:T(8,128)(2,1)S(1)}, bf16[512,128]{1,0:T(8,128)(2,1)S(1)}, u32[]{:S(2)}, u32[]{:S(2)}) collective-permute-start(bf16[512,128]{1,0:T(8,128)(2,1)S(1)} %get-tuple-element.21), channel_id=1, source_target_pairs={{0,16},{8,24},{16,32},{24,40},{32,48},{40,56},{48,64},{56,72},{64,... | collective-permute-start | bytes 393224 | tf_op jit(solution)/shard_map/ppermute | solution.py:22
  171.5 9.6 %collective-permute-start.14 = (bf16[512,128]{1,0:T(8,128)(2,1)S(1)}, bf16[512,128]{1,0:T(8,128)(2,1)S(1)}, u32[]{:S(2)}, u32[]{:S(2)}) collective-permute-start(bf16[512,128]{1,0:T(8,128)(2,1)S(1)} %fusion.83), channel_id=1, source_target_pairs={{16,0},{24,8},{32,16},{40,24},{48,32},{56,40},{64,48},{72,56},{80,... | collective-permute-start | bytes 393224 | tf_op jit(solution)/shard_map/ppermute | solution.py:22
  173.4 8.8 %collective-permute-start.13 = (bf16[512,128]{1,0:T(8,128)(2,1)S(1)}, bf16[512,128]{1,0:T(8,128)(2,1)S(1)}, u32[]{:S(2)}, u32[]{:S(2)}) collective-permute-start(bf16[512,128]{1,0:T(8,128)(2,1)S(1)} %fusion.83), channel_id=1, source_target_pairs={{8,0},{16,8},{24,16},{32,24},{40,32},{48,40},{56,48},{64,56},{72,6... | collective-permute-start | bytes 393224 | tf_op jit(solution)/shard_map/ppermute | solution.py:22
  183.0 39.7 %copy-start.10 = (bf16[8,512,1]{1,0,2:T(8,128)(2,1)S(1)}, bf16[8,512,1]{1,0,2:T(8,128)(2,1)}, u32[]{:S(2)}) copy-start(bf16[8,512,1]{1,0,2:T(8,128)(2,1)} %copy.99) | copy-start | bytes 24580
  183.0 40.8 %copy-start.15 = (f32[512]{0:T(512)S(1)}, f32[512]{0:T(512)}, u32[]{:S(2)}) copy-start(f32[512]{0:T(512)} %fusion.140) | copy-start | bytes 6148
  183.0 40.8 %copy-start.18 = (pred[16]{0:T(512)(128)(4,1)S(1)}, pred[16]{0:T(512)(128)(4,1)}, u32[]{:S(2)}) copy-start(pred[16]{0:T(512)(128)(4,1)} %add_compare_fusion) | copy-start | bytes 52
  183.0 40.8 %copy-start.21 = (pred[8]{0:T(512)(128)(4,1)S(1)}, pred[8]{0:T(512)(128)(4,1)}, u32[]{:S(2)}) copy-start(pred[8]{0:T(512)(128)(4,1)} %add_compare_fusion.1) | copy-start | bytes 28
  211.0 11.8 %collective-permute-start.18 = (f32[8,512]{1,0:T(8,128)S(1)}, f32[8,512]{1,0:T(8,128)S(1)}, u32[]{:S(2)}, u32[]{:S(2)}) collective-permute-start(f32[8,512]{1,0:T(8,128)S(1)} %get-tuple-element.13), channel_id=1, source_target_pairs={{0,1},{1,2},{2,3},{3,4},{4,5},{5,6},{6,7},{8,9},{9,10},{10,11},{11... | collective-permute-start | bytes 49160 | tf_op jit(solution)/shard_map/ppermute | solution.py:22
  213.2 10.7 %collective-permute-start.17 = (f32[8,512]{1,0:T(8,128)S(1)}, f32[8,512]{1,0:T(8,128)S(1)}, u32[]{:S(2)}, u32[]{:S(2)}) collective-permute-start(f32[8,512]{1,0:T(8,128)S(1)} %get-tuple-element.14), channel_id=1, source_target_pairs={{1,0},{2,1},{3,2},{4,3},{5,4},{6,5},{7,6},{9,8},{10,9},{11,10},{12... | collective-permute-start | bytes 49160 | tf_op jit(solution)/shard_map/ppermute | solution.py:22
  215.3 7.5 %collective-permute-start.16 = (f32[16,512]{1,0:T(8,128)S(1)}, f32[16,512]{1,0:T(8,128)S(1)}, u32[]{:S(2)}, u32[]{:S(2)}) collective-permute-start(f32[16,512]{1,0:T(8,128)S(1)} %get-tuple-element.15), channel_id=1, source_target_pairs={{0,8},{8,16},{16,24},{24,32},{32,40},{40,48},{48,56},{56,64},{64,7... | collective-permute-start | bytes 98312 | tf_op jit(solution)/shard_map/ppermute | solution.py:22
  218.1 5.7 %collective-permute-start.15 = (f32[16,512]{1,0:T(8,128)S(1)}, f32[16,512]{1,0:T(8,128)S(1)}, u32[]{:S(2)}, u32[]{:S(2)}) collective-permute-start(f32[16,512]{1,0:T(8,128)S(1)} %get-tuple-element.16), channel_id=1, source_target_pairs={{8,0},{16,8},{24,16},{32,24},{40,32},{48,40},{56,48},{64,56},{72,6... | collective-permute-start | bytes 98312 | tf_op jit(solution)/shard_map/ppermute | solution.py:22
  224.2 22.5 %copy-start.27 = (pred[3,3]{0,1:T(4,128)(4,1)S(1)}, pred[3,3]{0,1:T(4,128)(4,1)}, u32[]{:S(2)}) copy-start(pred[3,3]{0,1:T(4,128)(4,1)} %copy-done.24) | copy-start | bytes 31
  239.8 16.8 %copy-start.8 = (bf16[8,16,4096]{2,1,0:T(8,128)(2,1)S(1)}, bf16[8,16,4096]{2,1,0:T(8,128)(2,1)}, u32[]{:S(2)}) copy-start(bf16[8,16,4096]{2,1,0:T(8,128)(2,1)} %shard_map.108) | copy-start | bytes 3145732
  239.8 21.0 %copy-start.14 = (f32[512]{0:T(512)S(1)}, f32[512]{0:T(512)}, u32[]{:S(2)}) copy-start(f32[512]{0:T(512)} %copy-done.12) | copy-start | bytes 6148
  246.7 24.4 %copy-start.28 = (pred[3,3]{0,1:T(4,128)(4,1)S(1)}, pred[3,3]{0,1:T(4,128)(4,1)}, u32[]{:S(2)}) copy-start(pred[3,3]{0,1:T(4,128)(4,1)} %copy-done.24) | copy-start | bytes 31
  247.2 12.8 %collective-permute-start.19 = (bf16[512,128]{1,0:T(8,128)(2,1)S(1)}, bf16[512,128]{1,0:T(8,128)(2,1)S(1)}, u32[]{:S(2)}, u32[]{:S(2)}) collective-permute-start(bf16[512,128]{1,0:T(8,128)(2,1)S(1)} %get-tuple-element.11), channel_id=1, source_target_pairs={{0,8},{8,16},{16,24},{24,32},{32,40},{40,48},{48,56},{56,64},{64,7... | collective-permute-start | bytes 393224 | tf_op jit(solution)/shard_map/ppermute | solution.py:22
  250.8 10.0 %collective-permute-start.20 = (bf16[512,128]{1,0:T(8,128)(2,1)S(1)}, bf16[512,128]{1,0:T(8,128)(2,1)S(1)}, u32[]{:S(2)}, u32[]{:S(2)}) collective-permute-start(bf16[512,128]{1,0:T(8,128)(2,1)S(1)} %get-tuple-element.12), channel_id=1, source_target_pairs={{0,16},{8,24},{16,32},{24,40},{32,48},{40,56},{48,64},{56,72},{64,... | collective-permute-start | bytes 393224 | tf_op jit(solution)/shard_map/ppermute | solution.py:22
  261.6 8.8 %collective-permute-start.22 = (bf16[512,128]{1,0:T(8,128)(2,1)S(1)}, bf16[512,128]{1,0:T(8,128)(2,1)S(1)}, u32[]{:S(2)}, u32[]{:S(2)}) collective-permute-start(bf16[512,128]{1,0:T(8,128)(2,1)S(1)} %get-tuple-element.5), channel_id=1, source_target_pairs={{16,0},{24,8},{32,16},{40,24},{48,32},{56,40},{64,48},{72,56},{80,... | collective-permute-start | bytes 393224 | tf_op jit(solution)/shard_map/ppermute | solution.py:22
  265.3 5.7 %collective-permute-start.21 = (bf16[512,128]{1,0:T(8,128)(2,1)S(1)}, bf16[512,128]{1,0:T(8,128)(2,1)S(1)}, u32[]{:S(2)}, u32[]{:S(2)}) collective-permute-start(bf16[512,128]{1,0:T(8,128)(2,1)S(1)} %get-tuple-element.5), channel_id=1, source_target_pairs={{8,0},{16,8},{24,16},{32,24},{40,32},{48,40},{56,48},{64,56},{72,6... | collective-permute-start | bytes 393224 | tf_op jit(solution)/shard_map/ppermute | solution.py:22
  271.8 41.8 %copy-start.11 = (bf16[8,512,1]{1,0,2:T(8,128)(2,1)S(1)}, bf16[8,512,1]{1,0,2:T(8,128)(2,1)}, u32[]{:S(2)}) copy-start(bf16[8,512,1]{1,0,2:T(8,128)(2,1)} %copy.99) | copy-start | bytes 24580
  271.8 43.9 %copy-start.16 = (f32[512]{0:T(512)S(1)}, f32[512]{0:T(512)}, u32[]{:S(2)}) copy-start(f32[512]{0:T(512)} %fusion.140) | copy-start | bytes 6148
  271.8 43.9 %copy-start.19 = (pred[16]{0:T(512)(128)(4,1)S(1)}, pred[16]{0:T(512)(128)(4,1)}, u32[]{:S(2)}) copy-start(pred[16]{0:T(512)(128)(4,1)} %add_compare_fusion) | copy-start | bytes 52
  271.8 43.9 %copy-start.22 = (pred[8]{0:T(512)(128)(4,1)S(1)}, pred[8]{0:T(512)(128)(4,1)}, u32[]{:S(2)}) copy-start(pred[8]{0:T(512)(128)(4,1)} %add_compare_fusion.1) | copy-start | bytes 28
  301.1 12.5 %collective-permute-start.26 = (f32[8,512]{1,0:T(8,128)S(1)}, f32[8,512]{1,0:T(8,128)S(1)}, u32[]{:S(2)}, u32[]{:S(2)}) collective-permute-start(f32[8,512]{1,0:T(8,128)S(1)} %bitcast.334), channel_id=1, source_target_pairs={{0,1},{1,2},{2,3},{3,4},{4,5},{5,6},{6,7},{8,9},{9,10},{10,11},{11... | collective-permute-start | bytes 49160 | tf_op jit(solution)/shard_map/ppermute | solution.py:22
  303.2 10.4 %collective-permute-start.24 = (f32[16,512]{1,0:T(8,128)S(1)}, f32[16,512]{1,0:T(8,128)S(1)}, u32[]{:S(2)}, u32[]{:S(2)}) collective-permute-start(f32[16,512]{1,0:T(8,128)S(1)} %get-tuple-element.6), channel_id=1, source_target_pairs={{0,8},{8,16},{16,24},{24,32},{32,40},{40,48},{48,56},{56,64},{64,7... | collective-permute-start | bytes 98312 | tf_op jit(solution)/shard_map/ppermute | solution.py:22
  306.5 7.9 %collective-permute-start.23 = (f32[16,512]{1,0:T(8,128)S(1)}, f32[16,512]{1,0:T(8,128)S(1)}, u32[]{:S(2)}, u32[]{:S(2)}) collective-permute-start(f32[16,512]{1,0:T(8,128)S(1)} %get-tuple-element.7), channel_id=1, source_target_pairs={{8,0},{16,8},{24,16},{32,24},{40,32},{48,40},{56,48},{64,56},{72,6... | collective-permute-start | bytes 98312 | tf_op jit(solution)/shard_map/ppermute | solution.py:22
  310.6 5.1 %collective-permute-start.25 = (f32[8,512]{1,0:T(8,128)S(1)}, f32[8,512]{1,0:T(8,128)S(1)}, u32[]{:S(2)}, u32[]{:S(2)}) collective-permute-start(f32[8,512]{1,0:T(8,128)S(1)} %slice_bitcast_fusion.10), channel_id=1, source_target_pairs={{1,0},{2,1},{3,2},{4,3},{5,4},{6,5},{7,6},{9,8},{10,9},{11,10},{12... | collective-permute-start | bytes 49160 | tf_op jit(solution)/shard_map/ppermute | solution.py:22

commit v6 on v5

--- a/solution.py
+++ b/solution.py
@@ -234,6 +234,60 @@
             flops=0, bytes_accessed=2 * 2 * groups * rows * cols, transcendentals=0,
         ),
     )(own)
+
+
+def _project_kernel(w_ref, v_ref, o_ref):
+    o_ref[...] = jnp.dot(w_ref[...], v_ref[...], preferred_element_type=jnp.float32).astype(
+        o_ref.dtype
+    )
+
+
+def project(tiles, volume, first, count, rows=256):
+    ray_count, voxels = tiles.shape[1:]
+    columns = volume.shape[1]
+    return pl.pallas_call(
+        _project_kernel,
+        grid=(count, ray_count // rows),
+        in_specs=[
+            pl.BlockSpec((None, rows, voxels), lambda t, r: (t + first, r, 0)),
+            pl.BlockSpec((voxels, columns), lambda t, r: (0, 0)),
+        ],
+        out_specs=pl.BlockSpec((None, rows, columns), lambda t, r: (t, r, 0)),
+        out_shape=jax.ShapeDtypeStruct((count, ray_count, columns), jnp.bfloat16),
+        cost_estimate=pl.CostEstimate(
+            flops=2 * count * ray_count * voxels * columns,
+            bytes_accessed=2 * (count * ray_count * voxels + voxels * columns),
+            transcendentals=0,
+        ),
+    )(tiles, volume)
+
+
+def _back_kernel(p_ref, w_ref, o_ref):
+    @pl.when((pl.program_id(0) == 0) & (pl.program_id(1) == 0))
+    def _():
+        o_ref[...] = jnp.zeros_like(o_ref)
+
+    o_ref[...] += jnp.dot(p_ref[...], w_ref[...], preferred_element_type=jnp.float32)
+
+
+def back_project(picked_t, tiles, first, rows=256):
+    count, columns, ray_count = picked_t.shape
+    voxels = tiles.shape[2]
+    return pl.pallas_call(
+        _back_kernel,
+        grid=(count, ray_count // rows),
+        in_specs=[
+            pl.BlockSpec((None, columns, rows), lambda t, r: (t, 0, r)),
+            pl.BlockSpec((None, rows, voxels), lambda t, r: (t + first, r, 0)),
+        ],
+        out_specs=pl.BlockSpec((columns, voxels), lambda t, r: (0, 0)),
+        out_shape=jax.ShapeDtypeStruct((columns, voxels), jnp.float32),
+        cost_estimate=pl.CostEstimate(
+            flops=2 * count * ray_count * voxels * columns,
+            bytes_accessed=2 * count * ray_count * voxels + 4 * columns * voxels,
+            transcendentals=0,
+        ),
+    )(picked_t, tiles)
 
 
 def smooth_share(
@@ -334,13 +388,9 @@
     for iteration in range(ITERS):
         if gathered is None:
             flat_volume = volume0.astype(jnp.bfloat16).reshape(voxels, column_count)
-            far_products = jnp.einsum(
-                "trv,vn->trn", tiles[1:], flat_volume, preferred_element_type=jnp.float32
-            ).astype(jnp.bfloat16)
         else:
-            far_products = jnp.einsum(
-                "trv,nv->trn", tiles[1:], gathered, preferred_element_type=jnp.float32
-            ).astype(jnp.bfloat16)
+            flat_volume = gathered.T
+        far_products = project(tiles, flat_volume, 1, slot_count - 1)
         sends_half = jnp.einsum(
             "td,trn->drn", far_relative, far_products, preferred_element_type=jnp.float32
         ).astype(jnp.bfloat16)
@@ -348,15 +398,7 @@
             from_behind(sends_half[distance - 1], "slab", distance)
             for distance in range(1, slot_count)
         ]
-        if gathered is None:
-            near_products = jnp.einsum(
-                "rv,vn->rn", tiles[0], flat_volume, preferred_element_type=jnp.float32
-            )
-        else:
-            near_products = jnp.einsum(
-                "rv,nv->rn", tiles[0], gathered, preferred_element_type=jnp.float32
-            )
-        near_products = lax.optimization_barrier(near_products.astype(jnp.bfloat16))
+        near_products = project(tiles, flat_volume, 0, 1)[0]
         projected = near_products.astype(jnp.float32)
         for distance in range(1, slot_count):
             projected = projected + arrived[distance - 1].astype(jnp.float32)
@@ -365,15 +407,11 @@
         nearby = [
             from_behind(residual_half, "slab", -distance) for distance in range(1, slot_count)
         ]
-        near_back = lax.optimization_barrier(
-            jnp.einsum("rn,rv->nv", residual_half, tiles[0], preferred_element_type=jnp.float32)
-        )
-        picked = jnp.einsum(
-            "td,drn->trn", far_relative, jnp.stack(nearby), preferred_element_type=jnp.float32
+        near_back = back_project(residual_half.T[None], tiles, 0)
+        picked_t = jnp.einsum(
+            "td,drn->tnr", far_relative, jnp.stack(nearby), preferred_element_type=jnp.float32
         ).astype(jnp.bfloat16)
-        back_t = near_back + jnp.einsum(
-            "trn,trv->nv", picked, tiles[1:], preferred_element_type=jnp.float32
-        )
+        back_t = near_back + back_project(picked_t, tiles, 1)
         back_own = scatter_angle(back_t.reshape(groups, share_width, voxels))
         volume = volume + voxel_scale * back_own.reshape(share_width, slab_depth, height)
         volume = smooth_share(

time: 319 us -> 340 us (1.066)
  Pallas kernels: 102 us -> 163 us
  matrix products: 74.7 us -> 19.4 us
  local copies, waits for them, and re-layouts: 24.9 us -> 35 us
  other arithmetic: 12.3 us -> 21.2 us
  waiting for transfers between devices: 13.8 us -> 9.12 us
    pallas_call x0 -> x12, Pallas kernels: none -> 62.8 us  [the longest x6 31.9 us: back_project(): pl.pallas_call(_back_kernel, grid=(count, ray_count // rows), in_specs=[p...]
    dot_general x15 -> x3, matrix products: 59.6 us -> 1.46 us  [shards(): jnp.einsum('td,drn->tnr', far_relative, jnp.stack(nearby), preferred_elem...]
    add x0 -> x3, other arithmetic: none -> 9.48 us  [shards(): back_t = near_back + back_project(picked_t, tiles, 1)]
    ppermute x27, waiting for transfers between devices: 13.8 us -> 9.12 us  [from_behind(): lax.ppermute(value, axis, [(source, source + steps) for source in range(f...]
    reshape x0 -> x2, local copies, waits for them, and re-layouts: none -> 4.54 us  [shards(): gathered = gather_angle(own_half, groups).reshape(column_count, voxels)]
    pallas_call x0 -> x3, local copies, waits for them, and re-layouts: none -> 3.66 us  [project(): pl.pallas_call(_project_kernel, grid=(count, ray_count // rows), in_specs...]
    unnamed x73 -> x83, local copies, waits for them, and re-layouts: 13.7 us -> 12.4 us
  transfers between devices with their start and end apart: 27 -> 27, of which waited for: 9 -> 5; matrix products, arithmetic and copies ran while one was open for 20% -> 12% of each run, Pallas kernels for 9% -> 20%
where the time goes in v6:
time: 340 us; the launch traced here: 339 us
  Pallas kernels  163 us (48%)
  starting transfers between devices  88.4 us (26%)
  local copies, waits for them, and re-layouts  35 us (10%)
  other arithmetic  21.2 us (6%)
  matrix products  19.4 us (6%)
  waiting for transfers between devices  9.12 us (3%)
    ppermute x27, starting transfers between devices, from_behind(): lax.ppermute(value, axis, [(source, source + steps) for source in range(f...  88.4 us
    pallas_call x3, Pallas kernels, scatter_angle(): pl.pallas_call(functools.partial(_scatter_kernel, n_chip), out_shape=jax....  60.4 us
    pallas_call x6, Pallas kernels, back_project(): pl.pallas_call(_back_kernel, grid=(count, ray_count // rows), in_specs=[p...  31.9 us
    pallas_call x6, Pallas kernels, project(): pl.pallas_call(_project_kernel, grid=(count, ray_count // rows), in_specs...  30.9 us
    pallas_call x2, Pallas kernels, gather_angle(): pl.pallas_call(functools.partial(_gather_kernel, n_chip), out_shape=jax.S...  30.1 us
    unnamed x83, local copies, waits for them, and re-layouts  12.4 us
    pallas_call x1, Pallas kernels, sum_angle(): pl.pallas_call(functools.partial(_sum_kernel, groups), out_shape=jax.Shap...  9.61 us
    add x3, other arithmetic, shards(): back_t = near_back + back_project(picked_t, tiles, 1)  9.48 us
  transfers between devices with their start and end apart: 27, of which 5 were waited for; matrix products, arithmetic and copies ran while one was open for 12% of the time, Pallas kernels for 20%

profile of v6, /device:TPU:33, one launch (start us, length us, event | category | flops | bytes accessed | tf_op | source)
XLA Modules:
  0.0 338.6 jit_solution(5759013423093615427)
XLA Ops:
  2.2 8.1 %fusion.55 = bf16[1,3,512]{2,0,1:T(2,128)(2,1)S(1)} fusion(bf16[1,1,3,512,4096]{4,3,2,1,0:T(8,128)(2,1)} %param.10), kind=kOutput, calls=%fused_computation.118 | convolution fusion | flops 12582912 | bytes 12585984 | tf_op jit(solution)/shard_map/dot_general | solution.py:352
  11.0 4.8 %collective-permute-start.3 = (f32[512]{0:T(512)}, f32[512]{0:T(512)}, u32[]{:S(2)}, u32[]{:S(2)}) collective-permute-start(f32[512]{0:T(512)} %bitcast.17), channel_id=1, source_target_pairs={{0,16},{8,24},{16,32},{24,40},{32,48},{40,56},{48,64},{56,72},{64,... | collective-permute-start | bytes 6152 | tf_op jit(solution)/shard_map/ppermute | solution.py:22
  15.8 2.3 collective-permute-start.2
  18.9 2.6 collective-permute-start.7
  22.8 6.4 %shard_map.106 = bf16[2,512,128]{2,1,0:T(8,128)(2,1)} custom-call(bf16[3,512,4096]{2,1,0:T(8,128)(2,1)} %bitcast.242, bf16[4096,128]{1,0:T(8,128)(2,1)} %bitcast.261), custom_call_target="tpu_custom_call" | custom-call | flops 1073741824 | bytes 9437184 | tf_op jit(solution)/shard_map/pallas_call | solution.py:248
  29.2 1.4 fusion.43
  31.4 3.8 %collective-permute-start = (bf16[512,128]{0,1:T(8,128)(2,1)}, bf16[512,128]{0,1:T(8,128)(2,1)}, u32[]{:S(2)}, u32[]{:S(2)}) collective-permute-start(bf16[512,128]{0,1:T(8,128)(2,1)} %get-tuple-element.35), channel_id=1, source_target_pairs={{0,8},{8,16},{16,24},{24,32},{32,40},{40,48},{48,56},{56,64},{64,7... | collective-permute-start | bytes 393224 | tf_op jit(solution)/shard_map/ppermute | solution.py:22
  35.2 4.5 %collective-permute-start.1 = (bf16[512,128]{0,1:T(8,128)(2,1)}, bf16[512,128]{0,1:T(8,128)(2,1)}, u32[]{:S(2)}, u32[]{:S(2)}) collective-permute-start(bf16[512,128]{0,1:T(8,128)(2,1)} %get-tuple-element.36), channel_id=1, source_target_pairs={{0,16},{8,24},{16,32},{24,40},{32,48},{40,56},{48,64},{56,72},{64,... | collective-permute-start | bytes 393224 | tf_op jit(solution)/shard_map/ppermute | solution.py:22
  40.8 1.6 constant_dynamic-slice_fusion.3
  42.4 1.9 constant_dynamic-slice_fusion.4
  44.4 5.6 %fusion = f32[1,8,512]{2,0,1:T(1,128)S(1)} fusion(pred[1536,1,1]{0,1,2:T(4,128)(4,1)S(1)} %reshape.83, bf16[192,8,8,512]{3,2,1,0:T(8,128)(2,1)} %bitcast.243), kind=kOutput, calls=%fused_computation | convolution fusion | flops 12582912 | bytes 12600832 | tf_op jit(solution)/shard_map/dot_general | solution.py:360
  50.6 9.6 %shard_map.104 = f32[8,512]{1,0:T(8,128)} custom-call(f32[8,512]{1,0:T(8,128)} %bitcast.293), custom_call_target="tpu_custom_call" | custom-call | flops 32768 | bytes 262144 | tf_op jit(solution)/shard_map/pallas_call | solution.py:148
  62.3 2.0 constant_dynamic-slice_fusion.1
  64.3 3.9 %shard_map.105 = bf16[1,512,128]{2,1,0:T(8,128)(2,1)} custom-call(bf16[3,512,4096]{2,1,0:T(8,128)(2,1)} %bitcast.244, bf16[4096,128]{1,0:T(8,128)(2,1)} %bitcast.262), custom_call_target="tpu_custom_call" | custom-call | flops 536870912 | bytes 5242880 | tf_op jit(solution)/shard_map/pallas_call | solution.py:248
  69.0 2.2 copy.178
  71.2 1.6 copy.113
  74.6 1.6 copy.177
  78.4 3.2 collective-permute-start.5
  81.6 3.5 %collective-permute-start.4 = (bf16[512,128]{0,1:T(8,128)(2,1)S(1)}, bf16[512,128]{0,1:T(8,128)(2,1)S(1)}, u32[]{:S(2)}, u32[]{:S(2)}) collective-permute-start(bf16[512,128]{0,1:T(8,128)(2,1)S(1)} %fusion.4), channel_id=1, source_target_pairs={{8,0},{16,8},{24,16},{32,24},{40,32},{48,40},{56,48},{64,56},{72,6... | collective-permute-start | bytes 393224 | tf_op jit(solution)/shard_map/ppermute | solution.py:22
  85.1 4.1 %shard_map.107 = f32[128,4096]{1,0:T(8,128)} custom-call(bf16[1,128,512]{2,1,0:T(8,128)(2,1)} %bitcast.282, bf16[3,512,4096]{2,1,0:T(8,128)(2,1)} %bitcast.245), custom_call_target="tpu_custom_call" | custom-call | flops 536870912 | bytes 6291456 | tf_op jit(solution)/shard_map/pallas_call | solution.py:276
  91.0 6.6 %shard_map.108 = f32[128,4096]{1,0:T(8,128)} custom-call(bf16[2,128,512]{2,1,0:T(8,128)(2,1)} %bitcast.275, bf16[3,512,4096]{2,1,0:T(8,128)(2,1)} %bitcast.246), custom_call_target="tpu_custom_call" | custom-call | flops 1073741824 | bytes 10485760 | tf_op jit(solution)/shard_map/pallas_call | solution.py:276
  97.6 3.2 add.175
  100.8 20.4 %shard_map.109 = f32[16,4096]{1,0:T(8,128)} custom-call(f32[8,16,4096]{2,1,0:T(8,128)} %bitcast.255, f32[8,16,4096]{2,1,0:T(8,128)} %bitcast.256), custom_call_target="tpu_custom_call" | custom-call | flops 1048576 | bytes 6291456 | tf_op jit(solution)/shard_map/pallas_call | solution.py:97
  122.3 2.6 collective-permute-start.10
  125.2 1.9 collective-permute-start.9
  127.1 5.3 %collective-permute-start.6 = (f32[16,512]{1,0:T(8,128)S(1)}, f32[16,512]{1,0:T(8,128)S(1)}, u32[]{:S(2)}, u32[]{:S(2)}) collective-permute-start(f32[16,512]{1,0:T(8,128)S(1)} %bitcast.295), channel_id=1, source_target_pairs={{8,0},{16,8},{24,16},{32,24},{40,32},{48,40},{56,48},{64,56},{72,6... | collective-permute-start | bytes 98312 | tf_op jit(solution)/shard_map/ppermute | solution.py:22
  132.4 1.9 collective-permute-start.8
  134.4 5.3 %collective-permute-done.8 = f32[16,512]{1,0:T(8,128)S(1)} collective-permute-done((f32[16,512]{1,0:T(8,128)S(1)}, f32[16,512]{1,0:T(8,128)S(1)}, u32[]{:S(2)}, u32[]{:S(2)}) %collective-permute-start.8) | collective-permute-done | bytes 32800 | tf_op jit(solution)/shard_map/ppermute | solution.py:22
  141.8 15.4 %shard_map.110 = bf16[8,16,4096]{2,1,0:T(8,128)(2,1)} custom-call(bf16[16,4096]{1,0:T(8,128)(2,1)} %bitcast.285), custom_call_target="tpu_custom_call" | custom-call | bytes 2097152 | tf_op jit(solution)/shard_map/pallas_call | solution.py:219
  157.2 2.3 copy.128
  159.5 6.4 %shard_map.112 = bf16[2,512,128]{2,1,0:T(8,128)(2,1)} custom-call(bf16[3,512,4096]{2,1,0:T(8,128)(2,1)} %bitcast.247, bf16[4096,128]{1,0:T(8,128)(2,1)} %bitcast.263), custom_call_target="tpu_custom_call" | custom-call | flops 1073741824 | bytes 9437184 | tf_op jit(solution)/shard_map/pallas_call | solution.py:248
  165.9 1.4 fusion.41
  167.5 1.9 collective-permute-start.11
  169.4 3.0 collective-permute-start.12
  172.4 3.9 %shard_map.111 = bf16[1,512,128]{2,1,0:T(8,128)(2,1)} custom-call(bf16[3,512,4096]{2,1,0:T(8,128)(2,1)} %bitcast.248, bf16[4096,128]{1,0:T(8,128)(2,1)} %bitcast.264), custom_call_target="tpu_custom_call" | custom-call | flops 536870912 | bytes 5242880 | tf_op jit(solution)/shard_map/pallas_call | solution.py:248
  177.4 1.5 collective-permute-done.12
  178.9 3.4 collective-permute-start.14
  182.3 4.6 %collective-permute-start.13 = (bf16[512,128]{0,1:T(8,128)(2,1)S(1)}, bf16[512,128]{0,1:T(8,128)(2,1)S(1)}, u32[]{:S(2)}, u32[]{:S(2)}) collective-permute-start(bf16[512,128]{0,1:T(8,128)(2,1)S(1)} %fusion.6), channel_id=1, source_target_pairs={{8,0},{16,8},{24,16},{32,24},{40,32},{48,40},{56,48},{64,56},{72,6... | collective-permute-start | bytes 393224 | tf_op jit(solution)/shard_map/ppermute | solution.py:22
  187.5 4.0 %shard_map.113 = f32[128,4096]{1,0:T(8,128)} custom-call(bf16[1,128,512]{2,1,0:T(8,128)(2,1)} %bitcast.283, bf16[3,512,4096]{2,1,0:T(8,128)(2,1)} %bitcast.249), custom_call_target="tpu_custom_call" | custom-call | flops 536870912 | bytes 6291456 | tf_op jit(solution)/shard_map/pallas_call | solution.py:276
  193.1 6.6 %shard_map.114 = f32[128,4096]{1,0:T(8,128)} custom-call(bf16[2,128,512]{2,1,0:T(8,128)(2,1)} %bitcast.276, bf16[3,512,4096]{2,1,0:T(8,128)(2,1)} %bitcast.250), custom_call_target="tpu_custom_call" | custom-call | flops 1073741824 | bytes 10485760 | tf_op jit(solution)/shard_map/pallas_call | solution.py:276
  199.7 3.2 add.193
  202.8 20.0 %shard_map.115 = f32[16,4096]{1,0:T(8,128)} custom-call(f32[8,16,4096]{2,1,0:T(8,128)} %bitcast.257, f32[8,16,4096]{2,1,0:T(8,128)} %bitcast.258), custom_call_target="tpu_custom_call" | custom-call | flops 1048576 | bytes 6291456 | tf_op jit(solution)/shard_map/pallas_call | solution.py:97
  224.4 2.6 collective-permute-start.18
  227.0 1.9 collective-permute-start.17
  228.9 2.4 collective-permute-start.16
  231.4 5.2 %collective-permute-start.15 = (f32[16,512]{1,0:T(8,128)S(1)}, f32[16,512]{1,0:T(8,128)S(1)}, u32[]{:S(2)}, u32[]{:S(2)}) collective-permute-start(f32[16,512]{1,0:T(8,128)S(1)} %get-tuple-element.22), channel_id=1, source_target_pairs={{8,0},{16,8},{24,16},{32,24},{40,32},{48,40},{56,48},{64,56},{72,6... | collective-permute-start | bytes 98312 | tf_op jit(solution)/shard_map/ppermute | solution.py:22
  239.0 14.6 %shard_map.116 = bf16[8,16,4096]{2,1,0:T(8,128)(2,1)} custom-call(bf16[16,4096]{1,0:T(8,128)(2,1)} %bitcast.286), custom_call_target="tpu_custom_call" | custom-call | bytes 2097152 | tf_op jit(solution)/shard_map/pallas_call | solution.py:219
  253.7 2.3 copy.142
  255.9 6.4 %shard_map.118 = bf16[2,512,128]{2,1,0:T(8,128)(2,1)} custom-call(bf16[3,512,4096]{2,1,0:T(8,128)(2,1)} %bitcast.251, bf16[4096,128]{1,0:T(8,128)(2,1)} %bitcast.265), custom_call_target="tpu_custom_call" | custom-call | flops 1073741824 | bytes 9437184 | tf_op jit(solution)/shard_map/pallas_call | solution.py:248
  262.4 1.4 fusion.39
  263.9 2.2 collective-permute-start.19
  266.1 7.3 %collective-permute-start.20 = (bf16[512,128]{0,1:T(8,128)(2,1)S(1)}, bf16[512,128]{0,1:T(8,128)(2,1)S(1)}, u32[]{:S(2)}, u32[]{:S(2)}) collective-permute-start(bf16[512,128]{0,1:T(8,128)(2,1)S(1)} %get-tuple-element.18), channel_id=1, source_target_pairs={{0,16},{8,24},{16,32},{24,40},{32,48},{40,56},{48,64},{56,72},{64,... | collective-permute-start | bytes 393224 | tf_op jit(solution)/shard_map/ppermute | solution.py:22
  273.5 3.9 %shard_map.117 = bf16[1,512,128]{2,1,0:T(8,128)(2,1)} custom-call(bf16[3,512,4096]{2,1,0:T(8,128)(2,1)} %bitcast.252, bf16[4096,128]{1,0:T(8,128)(2,1)} %bitcast.266), custom_call_target="tpu_custom_call" | custom-call | flops 536870912 | bytes 5242880 | tf_op jit(solution)/shard_map/pallas_call | solution.py:248
  278.5 2.7 collective-permute-start.22
  281.2 2.6 collective-permute-start.21
  284.6 4.0 %shard_map.119 = f32[128,4096]{1,0:T(8,128)} custom-call(bf16[1,128,512]{2,1,0:T(8,128)(2,1)} %bitcast.281, bf16[3,512,4096]{2,1,0:T(8,128)(2,1)} %bitcast.253), custom_call_target="tpu_custom_call" | custom-call | flops 536870912 | bytes 6291456 | tf_op jit(solution)/shard_map/pallas_call | solution.py:276
  290.3 6.6 %shard_map.120 = f32[128,4096]{1,0:T(8,128)} custom-call(bf16[2,128,512]{2,1,0:T(8,128)(2,1)} %bitcast.277, bf16[3,512,4096]{2,1,0:T(8,128)(2,1)} %bitcast.254), custom_call_target="tpu_custom_call" | custom-call | flops 1073741824 | bytes 10485760 | tf_op jit(solution)/shard_map/pallas_call | solution.py:276
  296.8 3.2 add.205
  300.0 20.0 %shard_map.121 = f32[16,4096]{1,0:T(8,128)} custom-call(f32[8,16,4096]{2,1,0:T(8,128)} %bitcast.259, f32[8,16,4096]{2,1,0:T(8,128)} %bitcast.260), custom_call_target="tpu_custom_call" | custom-call | flops 1048576 | bytes 6291456 | tf_op jit(solution)/shard_map/pallas_call | solution.py:97
  321.9 2.6 collective-permute-start.26
  324.6 2.6 collective-permute-start.24
  327.3 4.7 %collective-permute-start.23 = (f32[16,512]{1,0:T(8,128)S(1)}, f32[16,512]{1,0:T(8,128)S(1)}, u32[]{:S(2)}, u32[]{:S(2)}) collective-permute-start(f32[16,512]{1,0:T(8,128)S(1)} %get-tuple-element.13), channel_id=1, source_target_pairs={{8,0},{16,8},{24,16},{32,24},{40,32},{48,40},{56,48},{64,56},{72,6... | collective-permute-start | bytes 98312 | tf_op jit(solution)/shard_map/ppermute | solution.py:22
  332.1 2.3 collective-permute-start.25
  335.3 1.8 collective-permute-done.25
  (194 shorter events, 33.3 us)
Async XLA Ops:
  2.2 16.0 %slice-start = ((bf16[8,512,128]{2,1,0:T(8,128)(2,1)}), bf16[1,512,128]{2,1,0:T(8,128)(2,1)S(1)}, s32[]{:S(2)}) async-start(bf16[8,512,128]{2,1,0:T(8,128)(2,1)} %param.15), calls=%async_computation | async-start | bytes 262144 | tf_op jit(solution)/shard_map/slice | solution.py:364
  2.2 19.4 %copy-start.3 = (f32[8,512,128]{2,1,0:T(8,128)S(1)}, f32[8,512,128]{2,1,0:T(8,128)}, u32[]{:S(2)}) copy-start(f32[8,512,128]{2,1,0:T(8,128)} %param.9) | copy-start | bytes 6291460
  11.0 65.6 %collective-permute-start.3 = (f32[512]{0:T(512)}, f32[512]{0:T(512)}, u32[]{:S(2)}, u32[]{:S(2)}) collective-permute-start(f32[512]{0:T(512)} %bitcast.17), channel_id=1, source_target_pairs={{0,16},{8,24},{16,32},{24,40},{32,48},{40,56},{48,64},{56,72},{64,... | collective-permute-start | bytes 6152 | tf_op jit(solution)/shard_map/ppermute | solution.py:22
  15.8 60.8 %collective-permute-start.2 = (f32[512]{0:T(512)}, f32[512]{0:T(512)}, u32[]{:S(2)}, u32[]{:S(2)}) collective-permute-start(f32[512]{0:T(512)} %bitcast.16), channel_id=1, source_target_pairs={{0,8},{8,16},{16,24},{24,32},{32,40},{40,48},{48,56},{56,64},{64,7... | collective-permute-start | bytes 6152 | tf_op jit(solution)/shard_map/ppermute | solution.py:22
  18.9 115.5 %collective-permute-start.7 = (bf16[512,128]{0,1:T(8,128)(2,1)}, bf16[512,128]{0,1:T(8,128)(2,1)}, u32[]{:S(2)}, u32[]{:S(2)}) collective-permute-start(bf16[512,128]{0,1:T(8,128)(2,1)} %bitcast.27), channel_id=1, source_target_pairs={{0,8},{8,16},{16,24},{24,32},{32,40},{40,48},{48,56},{56,64},{64,7... | collective-permute-start | bytes 393224 | tf_op jit(solution)/shard_map/ppermute | solution.py:22
  21.6 7.6 %copy-start.30 = (pred[2,2,1]{0,1,2:T(4,128)(4,1)}, pred[2,2,1]{0,1,2:T(4,128)(4,1)S(1)}, u32[]{:S(2)}) copy-start(pred[2,2,1]{0,1,2:T(4,128)(4,1)S(1)} %slice_bitcast_fusion.15) | copy-start | bytes 16
  31.4 45.9 %collective-permute-start = (bf16[512,128]{0,1:T(8,128)(2,1)}, bf16[512,128]{0,1:T(8,128)(2,1)}, u32[]{:S(2)}, u32[]{:S(2)}) collective-permute-start(bf16[512,128]{0,1:T(8,128)(2,1)} %get-tuple-element.35), channel_id=1, source_target_pairs={{0,8},{8,16},{16,24},{24,32},{32,40},{40,48},{48,56},{56,64},{64,7... | collective-permute-start | bytes 393224 | tf_op jit(solution)/shard_map/ppermute | solution.py:22
  35.2 42.1 %collective-permute-start.1 = (bf16[512,128]{0,1:T(8,128)(2,1)}, bf16[512,128]{0,1:T(8,128)(2,1)}, u32[]{:S(2)}, u32[]{:S(2)}) collective-permute-start(bf16[512,128]{0,1:T(8,128)(2,1)} %get-tuple-element.36), channel_id=1, source_target_pairs={{0,16},{8,24},{16,32},{24,40},{32,48},{40,56},{48,64},{56,72},{64,... | collective-permute-start | bytes 393224 | tf_op jit(solution)/shard_map/ppermute | solution.py:22
  44.4 16.6 %copy-start.5 = (bf16[8,512,128]{2,1,0:T(8,128)(2,1)S(1)}, bf16[8,512,128]{2,1,0:T(8,128)(2,1)}, u32[]{:S(2)}) copy-start(bf16[8,512,128]{2,1,0:T(8,128)(2,1)} %param.17) | copy-start | bytes 3145732
  50.0 12.3 %copy-start.9 = (bf16[8,512,128]{2,1,0:T(8,128)(2,1)S(1)}, bf16[8,512,128]{2,1,0:T(8,128)(2,1)}, u32[]{:S(2)}) copy-start(bf16[8,512,128]{2,1,0:T(8,128)(2,1)} %param.16) | copy-start | bytes 3145732
  64.3 3.9 %copy-start.17 = (bf16[1,1,512,128]{3,2,1,0:T(8,128)(2,1)S(1)}, bf16[1,1,512,128]{3,2,1,0:T(8,128)(2,1)}, u32[]{:S(2)}) copy-start(bf16[1,1,512,128]{3,2,1,0:T(8,128)(2,1)} %param.14) | copy-start | bytes 393220
  68.2 5.0 %copy-start.4 = (f32[8,512,16]{2,1,0:T(8,128)S(1)}, f32[8,512,16]{2,1,0:T(8,128)}, u32[]{:S(2)}) copy-start(f32[8,512,16]{2,1,0:T(8,128)} %constant_dynamic-slice_fusion.4) | copy-start | bytes 786436
  73.2 3.0 copy-start.6
  74.6 2.0 copy-start.22
  74.6 2.8 copy-start.7
  74.6 2.8 copy-start.14
  77.3 101.5 %copy-start.18 = (f32[512]{0:T(512)}, f32[512]{0:T(512)S(1)}, u32[]{:S(2)}) copy-start(f32[512]{0:T(512)S(1)} %add_divide_fusion) | copy-start | bytes 6148
  78.4 6.7 %copy-start.12 = (bf16[512,128]{0,1:T(8,128)(2,1)}, bf16[512,128]{0,1:T(8,128)(2,1)S(1)}, u32[]{:S(2)}) copy-start(bf16[512,128]{0,1:T(8,128)(2,1)S(1)} %fusion.4) | copy-start | bytes 393220
  78.4 10.8 %collective-permute-start.5 = (bf16[512,128]{0,1:T(8,128)(2,1)S(1)}, bf16[512,128]{0,1:T(8,128)(2,1)S(1)}, u32[]{:S(2)}, u32[]{:S(2)}) collective-permute-start(bf16[512,128]{0,1:T(8,128)(2,1)S(1)} %fusion.4), channel_id=1, source_target_pairs={{16,0},{24,8},{32,16},{40,24},{48,32},{56,40},{64,48},{72,56},{80,... | collective-permute-start | bytes 393224 | tf_op jit(solution)/shard_map/ppermute | solution.py:22
  81.6 7.9 %collective-permute-start.4 = (bf16[512,128]{0,1:T(8,128)(2,1)S(1)}, bf16[512,128]{0,1:T(8,128)(2,1)S(1)}, u32[]{:S(2)}, u32[]{:S(2)}) collective-permute-start(bf16[512,128]{0,1:T(8,128)(2,1)S(1)} %fusion.4), channel_id=1, source_target_pairs={{8,0},{16,8},{24,16},{32,24},{40,32},{48,40},{56,48},{64,56},{72,6... | collective-permute-start | bytes 393224 | tf_op jit(solution)/shard_map/ppermute | solution.py:22
  85.1 55.5 %copy-start.26 = (pred[8]{0:T(512)(128)(4,1)}, pred[8]{0:T(512)(128)(4,1)S(1)}, u32[]{:S(2)}) copy-start(pred[8]{0:T(512)(128)(4,1)S(1)} %add_compare_fusion.1) | copy-start | bytes 28
  85.1 4.6 %copy-start.31 = (pred[2,2,1]{0,1,2:T(4,128)(4,1)S(1)}, pred[2,2,1]{0,1,2:T(4,128)(4,1)}, u32[]{:S(2)}) copy-start(pred[2,2,1]{0,1,2:T(4,128)(4,1)} %copy-done.30) | copy-start | bytes 16
  91.0 6.6 %copy-start.1 = (f32[128,4096]{1,0:T(8,128)S(1)}, f32[128,4096]{1,0:T(8,128)}, u32[]{:S(2)}) copy-start(f32[128,4096]{1,0:T(8,128)} %shard_map.107) | copy-start | bytes 6291460
  100.8 21.5 %copy-start.10 = (f32[8,512,16]{1,0,2:T(8,128)S(1)}, f32[8,512,16]{1,0,2:T(8,128)}, u32[]{:S(2)}) copy-start(f32[8,512,16]{1,0,2:T(8,128)} %copy.171) | copy-start | bytes 786436
  121.1 13.2 %copy-start.15 = (bf16[8,512,1]{1,0,2:T(8,128)(2,1)S(1)}, bf16[8,512,1]{1,0,2:T(8,128)(2,1)}, u32[]{:S(2)}) copy-start(bf16[8,512,1]{1,0,2:T(8,128)(2,1)} %copy.178) | copy-start | bytes 24580
  121.1 19.4 %copy-start.23 = (pred[16]{0:T(512)(128)(4,1)S(1)}, pred[16]{0:T(512)(128)(4,1)}, u32[]{:S(2)}) copy-start(pred[16]{0:T(512)(128)(4,1)} %add_compare_fusion) | copy-start | bytes 52
  121.2 19.4 %copy-start.29 = (pred[512]{0:T(512)(128)(4,1)S(1)}, pred[512]{0:T(512)(128)(4,1)}, u32[]{:S(2)}) copy-start(pred[512]{0:T(512)(128)(4,1)} %iota_compare_fusion) | copy-start | bytes 1540
  122.3 12.0 %collective-permute-start.10 = (f32[8,512]{1,0:T(8,128)S(1)}, f32[8,512]{1,0:T(8,128)S(1)}, u32[]{:S(2)}, u32[]{:S(2)}) collective-permute-start(f32[8,512]{1,0:T(8,128)S(1)} %get-tuple-element.33), channel_id=1, source_target_pairs={{0,1},{1,2},{2,3},{3,4},{4,5},{5,6},{6,7},{8,9},{9,10},{10,11},{11... | collective-permute-start | bytes 49160 | tf_op jit(solution)/shard_map/ppermute | solution.py:22
  125.2 15.4 %collective-permute-start.9 = (f32[8,512]{1,0:T(8,128)S(1)}, f32[8,512]{1,0:T(8,128)S(1)}, u32[]{:S(2)}, u32[]{:S(2)}) collective-permute-start(f32[8,512]{1,0:T(8,128)S(1)} %get-tuple-element.34), channel_id=1, source_target_pairs={{1,0},{2,1},{3,2},{4,3},{5,4},{6,5},{7,6},{9,8},{10,9},{11,10},{12... | collective-permute-start | bytes 49160 | tf_op jit(solution)/shard_map/ppermute | solution.py:22
  127.1 13.4 %collective-permute-start.6 = (f32[16,512]{1,0:T(8,128)S(1)}, f32[16,512]{1,0:T(8,128)S(1)}, u32[]{:S(2)}, u32[]{:S(2)}) collective-permute-start(f32[16,512]{1,0:T(8,128)S(1)} %bitcast.295), channel_id=1, source_target_pairs={{8,0},{16,8},{24,16},{32,24},{40,32},{48,40},{56,48},{64,56},{72,6... | collective-permute-start | bytes 98312 | tf_op jit(solution)/shard_map/ppermute | solution.py:22
  132.4 7.3 %collective-permute-start.8 = (f32[16,512]{1,0:T(8,128)S(1)}, f32[16,512]{1,0:T(8,128)S(1)}, u32[]{:S(2)}, u32[]{:S(2)}) collective-permute-start(f32[16,512]{1,0:T(8,128)S(1)} %bitcast.296), channel_id=1, source_target_pairs={{0,8},{8,16},{16,24},{24,32},{32,40},{40,48},{48,56},{56,64},{64,7... | collective-permute-start | bytes 98312 | tf_op jit(solution)/shard_map/ppermute | solution.py:22
  167.5 9.9 %collective-permute-start.11 = (bf16[512,128]{0,1:T(8,128)(2,1)S(1)}, bf16[512,128]{0,1:T(8,128)(2,1)S(1)}, u32[]{:S(2)}, u32[]{:S(2)}) collective-permute-start(bf16[512,128]{0,1:T(8,128)(2,1)S(1)} %get-tuple-element.26), channel_id=1, source_target_pairs={{0,8},{8,16},{16,24},{24,32},{32,40},{40,48},{48,56},{56,64},{64,7... | collective-permute-start | bytes 393224 | tf_op jit(solution)/shard_map/ppermute | solution.py:22
  169.4 9.4 %copy-start.8 = (bf16[1,1,512,128]{2,3,1,0:T(8,128)(2,1)S(1)}, bf16[1,1,512,128]{2,3,1,0:T(8,128)(2,1)}, u32[]{:S(2)}) copy-start(bf16[1,1,512,128]{2,3,1,0:T(8,128)(2,1)} %copy.112) | copy-start | bytes 393220
  169.4 9.4 %collective-permute-start.12 = (bf16[512,128]{0,1:T(8,128)(2,1)S(1)}, bf16[512,128]{0,1:T(8,128)(2,1)S(1)}, u32[]{:S(2)}, u32[]{:S(2)}) collective-permute-start(bf16[512,128]{0,1:T(8,128)(2,1)S(1)} %get-tuple-element.27), channel_id=1, source_target_pairs={{0,16},{8,24},{16,32},{24,40},{32,48},{40,56},{48,64},{56,72},{64,... | collective-permute-start | bytes 393224 | tf_op jit(solution)/shard_map/ppermute | solution.py:22
  178.9 8.5 %copy-start.13 = (bf16[512,128]{0,1:T(8,128)(2,1)}, bf16[512,128]{0,1:T(8,128)(2,1)S(1)}, u32[]{:S(2)}) copy-start(bf16[512,128]{0,1:T(8,128)(2,1)S(1)} %fusion.6) | copy-start | bytes 393220
  178.9 12.6 %collective-permute-start.14 = (bf16[512,128]{0,1:T(8,128)(2,1)S(1)}, bf16[512,128]{0,1:T(8,128)(2,1)S(1)}, u32[]{:S(2)}, u32[]{:S(2)}) collective-permute-start(bf16[512,128]{0,1:T(8,128)(2,1)S(1)} %fusion.6), channel_id=1, source_target_pairs={{16,0},{24,8},{32,16},{40,24},{48,32},{56,40},{64,48},{72,56},{80,... | collective-permute-start | bytes 393224 | tf_op jit(solution)/shard_map/ppermute | solution.py:22
  182.3 9.2 %collective-permute-start.13 = (bf16[512,128]{0,1:T(8,128)(2,1)S(1)}, bf16[512,128]{0,1:T(8,128)(2,1)S(1)}, u32[]{:S(2)}, u32[]{:S(2)}) collective-permute-start(bf16[512,128]{0,1:T(8,128)(2,1)S(1)} %fusion.6), channel_id=1, source_target_pairs={{8,0},{16,8},{24,16},{32,24},{40,32},{48,40},{56,48},{64,56},{72,6... | collective-permute-start | bytes 393224 | tf_op jit(solution)/shard_map/ppermute | solution.py:22
  187.5 4.3 %copy-start.32 = (pred[2,2,1]{0,1,2:T(4,128)(4,1)S(1)}, pred[2,2,1]{0,1,2:T(4,128)(4,1)}, u32[]{:S(2)}) copy-start(pred[2,2,1]{0,1,2:T(4,128)(4,1)} %copy-done.30) | copy-start | bytes 16
  193.1 6.6 %copy-start.2 = (f32[128,4096]{1,0:T(8,128)S(1)}, f32[128,4096]{1,0:T(8,128)}, u32[]{:S(2)}) copy-start(f32[128,4096]{1,0:T(8,128)} %shard_map.113) | copy-start | bytes 6291460
  222.9 14.7 %copy-start.20 = (f32[512]{0:T(512)S(1)}, f32[512]{0:T(512)}, u32[]{:S(2)}) copy-start(f32[512]{0:T(512)} %fusion.59) | copy-start | bytes 6148
  222.9 14.7 %copy-start.24 = (pred[16]{0:T(512)(128)(4,1)S(1)}, pred[16]{0:T(512)(128)(4,1)}, u32[]{:S(2)}) copy-start(pred[16]{0:T(512)(128)(4,1)} %add_compare_fusion) | copy-start | bytes 52
  222.9 14.7 %copy-start.27 = (pred[8]{0:T(512)(128)(4,1)S(1)}, pred[8]{0:T(512)(128)(4,1)}, u32[]{:S(2)}) copy-start(pred[8]{0:T(512)(128)(4,1)} %copy-done.26) | copy-start | bytes 28
  224.4 12.1 %collective-permute-start.18 = (f32[8,512]{1,0:T(8,128)S(1)}, f32[8,512]{1,0:T(8,128)S(1)}, u32[]{:S(2)}, u32[]{:S(2)}) collective-permute-start(f32[8,512]{1,0:T(8,128)S(1)} %get-tuple-element.19), channel_id=1, source_target_pairs={{0,1},{1,2},{2,3},{3,4},{4,5},{5,6},{6,7},{8,9},{9,10},{10,11},{11... | collective-permute-start | bytes 49160 | tf_op jit(solution)/shard_map/ppermute | solution.py:22
  227.0 10.6 %collective-permute-start.17 = (f32[8,512]{1,0:T(8,128)S(1)}, f32[8,512]{1,0:T(8,128)S(1)}, u32[]{:S(2)}, u32[]{:S(2)}) collective-permute-start(f32[8,512]{1,0:T(8,128)S(1)} %get-tuple-element.20), channel_id=1, source_target_pairs={{1,0},{2,1},{3,2},{4,3},{5,4},{6,5},{7,6},{9,8},{10,9},{11,10},{12... | collective-permute-start | bytes 49160 | tf_op jit(solution)/shard_map/ppermute | solution.py:22
  228.9 7.7 %collective-permute-start.16 = (f32[16,512]{1,0:T(8,128)S(1)}, f32[16,512]{1,0:T(8,128)S(1)}, u32[]{:S(2)}, u32[]{:S(2)}) collective-permute-start(f32[16,512]{1,0:T(8,128)S(1)} %get-tuple-element.21), channel_id=1, source_target_pairs={{0,8},{8,16},{16,24},{24,32},{32,40},{40,48},{48,56},{56,64},{64,7... | collective-permute-start | bytes 98312 | tf_op jit(solution)/shard_map/ppermute | solution.py:22
  231.4 6.2 %collective-permute-start.15 = (f32[16,512]{1,0:T(8,128)S(1)}, f32[16,512]{1,0:T(8,128)S(1)}, u32[]{:S(2)}, u32[]{:S(2)}) collective-permute-start(f32[16,512]{1,0:T(8,128)S(1)} %get-tuple-element.22), channel_id=1, source_target_pairs={{8,0},{16,8},{24,16},{32,24},{40,32},{48,40},{56,48},{64,56},{72,6... | collective-permute-start | bytes 98312 | tf_op jit(solution)/shard_map/ppermute | solution.py:22
  255.9 6.4 %copy-start.33 = (pred[2,2,1]{0,1,2:T(4,128)(4,1)S(1)}, pred[2,2,1]{0,1,2:T(4,128)(4,1)}, u32[]{:S(2)}) copy-start(pred[2,2,1]{0,1,2:T(4,128)(4,1)} %copy-done.30) | copy-start | bytes 16
  263.9 14.5 %collective-permute-start.19 = (bf16[512,128]{0,1:T(8,128)(2,1)S(1)}, bf16[512,128]{0,1:T(8,128)(2,1)S(1)}, u32[]{:S(2)}, u32[]{:S(2)}) collective-permute-start(bf16[512,128]{0,1:T(8,128)(2,1)S(1)} %get-tuple-element.17), channel_id=1, source_target_pairs={{0,8},{8,16},{16,24},{24,32},{32,40},{40,48},{48,56},{56,64},{64,7... | collective-permute-start | bytes 393224 | tf_op jit(solution)/shard_map/ppermute | solution.py:22
  266.1 12.3 %copy-start.19 = (f32[512]{0:T(512)S(1)}, f32[512]{0:T(512)}, u32[]{:S(2)}) copy-start(f32[512]{0:T(512)} %copy-done.18) | copy-start | bytes 6148
  266.1 12.2 %collective-permute-start.20 = (bf16[512,128]{0,1:T(8,128)(2,1)S(1)}, bf16[512,128]{0,1:T(8,128)(2,1)S(1)}, u32[]{:S(2)}, u32[]{:S(2)}) collective-permute-start(bf16[512,128]{0,1:T(8,128)(2,1)S(1)} %get-tuple-element.18), channel_id=1, source_target_pairs={{0,16},{8,24},{16,32},{24,40},{32,48},{40,56},{48,64},{56,72},{64,... | collective-permute-start | bytes 393224 | tf_op jit(solution)/shard_map/ppermute | solution.py:22
  278.5 6.1 %copy-start.11 = (bf16[512,128]{0,1:T(8,128)(2,1)}, bf16[512,128]{0,1:T(8,128)(2,1)S(1)}, u32[]{:S(2)}) copy-start(bf16[512,128]{0,1:T(8,128)(2,1)S(1)} %get-tuple-element.11) | copy-start | bytes 393220
  278.5 10.2 %collective-permute-start.22 = (bf16[512,128]{0,1:T(8,128)(2,1)S(1)}, bf16[512,128]{0,1:T(8,128)(2,1)S(1)}, u32[]{:S(2)}, u32[]{:S(2)}) collective-permute-start(bf16[512,128]{0,1:T(8,128)(2,1)S(1)} %get-tuple-element.11), channel_id=1, source_target_pairs={{16,0},{24,8},{32,16},{40,24},{48,32},{56,40},{64,48},{72,56},{80,... | collective-permute-start | bytes 393224 | tf_op jit(solution)/shard_map/ppermute | solution.py:22
  281.2 7.5 %collective-permute-start.21 = (bf16[512,128]{0,1:T(8,128)(2,1)S(1)}, bf16[512,128]{0,1:T(8,128)(2,1)S(1)}, u32[]{:S(2)}, u32[]{:S(2)}) collective-permute-start(bf16[512,128]{0,1:T(8,128)(2,1)S(1)} %get-tuple-element.11), channel_id=1, source_target_pairs={{8,0},{16,8},{24,16},{32,24},{40,32},{48,40},{56,48},{64,56},{72,6... | collective-permute-start | bytes 393224 | tf_op jit(solution)/shard_map/ppermute | solution.py:22
  290.2 6.6 %copy-start = (f32[128,4096]{1,0:T(8,128)S(1)}, f32[128,4096]{1,0:T(8,128)}, u32[]{:S(2)}) copy-start(f32[128,4096]{1,0:T(8,128)} %shard_map.119) | copy-start | bytes 6291460
  320.0 14.4 %copy-start.16 = (bf16[8,512,1]{1,0,2:T(8,128)(2,1)S(1)}, bf16[8,512,1]{1,0,2:T(8,128)(2,1)}, u32[]{:S(2)}) copy-start(bf16[8,512,1]{1,0,2:T(8,128)(2,1)} %copy.178) | copy-start | bytes 24580
  321.1 16.0 %copy-start.21 = (f32[512]{0:T(512)S(1)}, f32[512]{0:T(512)}, u32[]{:S(2)}) copy-start(f32[512]{0:T(512)} %fusion.59) | copy-start | bytes 6148
  321.1 16.0 %copy-start.25 = (pred[16]{0:T(512)(128)(4,1)S(1)}, pred[16]{0:T(512)(128)(4,1)}, u32[]{:S(2)}) copy-start(pred[16]{0:T(512)(128)(4,1)} %add_compare_fusion) | copy-start | bytes 52
  321.1 16.0 %copy-start.28 = (pred[8]{0:T(512)(128)(4,1)S(1)}, pred[8]{0:T(512)(128)(4,1)}, u32[]{:S(2)}) copy-start(pred[8]{0:T(512)(128)(4,1)} %copy-done.26) | copy-start | bytes 28
  321.9 12.5 %collective-permute-start.26 = (f32[8,512]{1,0:T(8,128)S(1)}, f32[8,512]{1,0:T(8,128)S(1)}, u32[]{:S(2)}, u32[]{:S(2)}) collective-permute-start(f32[8,512]{1,0:T(8,128)S(1)} %bitcast.301), channel_id=1, source_target_pairs={{0,1},{1,2},{2,3},{3,4},{4,5},{5,6},{6,7},{8,9},{9,10},{10,11},{11... | collective-permute-start | bytes 49160 | tf_op jit(solution)/shard_map/ppermute | solution.py:22
  324.6 9.8 %collective-permute-start.24 = (f32[16,512]{1,0:T(8,128)S(1)}, f32[16,512]{1,0:T(8,128)S(1)}, u32[]{:S(2)}, u32[]{:S(2)}) collective-permute-start(f32[16,512]{1,0:T(8,128)S(1)} %get-tuple-element.12), channel_id=1, source_target_pairs={{0,8},{8,16},{16,24},{24,32},{32,40},{40,48},{48,56},{56,64},{64,7... | collective-permute-start | bytes 98312 | tf_op jit(solution)/shard_map/ppermute | solution.py:22
  327.3 7.9 %collective-permute-start.23 = (f32[16,512]{1,0:T(8,128)S(1)}, f32[16,512]{1,0:T(8,128)S(1)}, u32[]{:S(2)}, u32[]{:S(2)}) collective-permute-start(f32[16,512]{1,0:T(8,128)S(1)} %get-tuple-element.13), channel_id=1, source_target_pairs={{8,0},{16,8},{24,16},{32,24},{40,32},{48,40},{56,48},{64,56},{72,6... | collective-permute-start | bytes 98312 | tf_op jit(solution)/shard_map/ppermute | solution.py:22
  332.1 5.1 %collective-permute-start.25 = (f32[8,512]{1,0:T(8,128)S(1)}, f32[8,512]{1,0:T(8,128)S(1)}, u32[]{:S(2)}, u32[]{:S(2)}) collective-permute-start(f32[8,512]{1,0:T(8,128)S(1)} %slice_bitcast_fusion.10), channel_id=1, source_target_pairs={{1,0},{2,1},{3,2},{4,3},{5,4},{6,5},{7,6},{9,8},{10,9},{11,10},{12... | collective-permute-start | bytes 49160 | tf_op jit(solution)/shard_map/ppermute | solution.py:22

commit v7 on v5

--- a/solution.py
+++ b/solution.py
@@ -44,10 +44,26 @@
     pl.semaphore_wait(barrier, n_chip)
 
 
-def _scatter_kernel(n_chip, part_ref, half_ref, out_ref, got_pair, got_ring, chip_sum,
-                    send_a, recv_a, send_b, recv_b):
+def _scatter_kernel(n_chip, with_extra, *refs):
+    if with_extra:
+        (part_ref, half_ref, extra_ref, out_ref, extra_out, got_pair, got_ring, chip_sum,
+         send_a, recv_a, send_b, recv_b, extra_pair, extra_ring, extra_chip,
+         send_c, recv_c) = refs
+    else:
+        (part_ref, half_ref, out_ref, got_pair, got_ring, chip_sum,
+         send_a, recv_a, send_b, recv_b) = refs
     slab, here, chip, core, partner = _where_am_i()
     _greet(slab, chip, core, partner, n_chip)
+    if with_extra:
+        extra_copy = pltpu.make_async_remote_copy(
+            src_ref=extra_ref,
+            dst_ref=extra_pair,
+            send_sem=send_c.at[0],
+            recv_sem=recv_c.at[0],
+            device_id=(slab, partner),
+            device_id_type=MESH_ID,
+        )
+        extra_copy.start()
     order = list(range(1, n_chip)) + [0]
     pair = []
     for i, d in enumerate(order):
@@ -62,6 +78,22 @@
         )
         copy.start()
         pair.append(copy)
+    extra_sends = []
+    if with_extra:
+        extra_copy.wait()
+        extra_chip[...] = extra_ref[...] + extra_pair[...]
+        for d in range(1, n_chip):
+            dest = (chip + d) % n_chip
+            copy = pltpu.make_async_remote_copy(
+                src_ref=extra_chip,
+                dst_ref=extra_ring.at[d],
+                send_sem=send_c.at[d],
+                recv_sem=recv_c.at[d],
+                device_id=(slab, 2 * dest + core),
+                device_id_type=MESH_ID,
+            )
+            copy.start()
+            extra_sends.append(copy)
     ring = []
     for i, d in enumerate(order[:-1]):
         dest = (chip + d) % n_chip
@@ -88,32 +120,56 @@
     for d in range(1, n_chip):
         total = total + got_ring[d].astype(jnp.float32)
     out_ref[...] = total
-
-
-def scatter_angle(part):
+    if with_extra:
+        for copy in extra_sends:
+            copy.wait()
+        extra_total = extra_chip[...]
+        for d in range(1, n_chip):
+            extra_total = extra_total + extra_ring[d]
+        extra_out[...] = extra_total
+
+
+def scatter_angle(part, extra=None):
     blocks, rows, cols = part.shape
     n_chip = blocks // 2
     link = part.dtype
-    return pl.pallas_call(
-        functools.partial(_scatter_kernel, n_chip),
-        out_shape=jax.ShapeDtypeStruct((rows, cols), jnp.float32),
-        in_specs=[pl.BlockSpec(memory_space=pltpu.VMEM)] * 2,
-        out_specs=pl.BlockSpec(memory_space=pltpu.VMEM),
-        scratch_shapes=[
-            pltpu.VMEM((n_chip, rows, cols), link),
-            pltpu.VMEM((n_chip, rows, cols), link),
-            pltpu.VMEM((n_chip, rows, cols), link),
-            pltpu.SemaphoreType.DMA((n_chip,)),
-            pltpu.SemaphoreType.DMA((n_chip,)),
-            pltpu.SemaphoreType.DMA((n_chip,)),
-            pltpu.SemaphoreType.DMA((n_chip,)),
-        ],
-        compiler_params=pltpu.CompilerParams(collective_id=0, has_side_effects=True),
+    with_extra = extra is not None
+    scratch = [
+        pltpu.VMEM((n_chip, rows, cols), link),
+        pltpu.VMEM((n_chip, rows, cols), link),
+        pltpu.VMEM((n_chip, rows, cols), link),
+        pltpu.SemaphoreType.DMA((n_chip,)),
+        pltpu.SemaphoreType.DMA((n_chip,)),
+        pltpu.SemaphoreType.DMA((n_chip,)),
+        pltpu.SemaphoreType.DMA((n_chip,)),
+    ]
+    operands = [part, part.astype(link)]
+    out_shape = [jax.ShapeDtypeStruct((rows, cols), jnp.float32)]
+    if with_extra:
+        scratch += [
+            pltpu.VMEM(extra.shape, extra.dtype),
+            pltpu.VMEM((n_chip,) + extra.shape, extra.dtype),
+            pltpu.VMEM(extra.shape, extra.dtype),
+            pltpu.SemaphoreType.DMA((n_chip,)),
+            pltpu.SemaphoreType.DMA((n_chip,)),
+        ]
+        operands.append(extra)
+        out_shape.append(jax.ShapeDtypeStruct(extra.shape, extra.dtype))
+    result = pl.pallas_call(
+        functools.partial(_scatter_kernel, n_chip, with_extra),
+        out_shape=tuple(out_shape),
+        in_specs=[pl.BlockSpec(memory_space=pltpu.VMEM)] * len(operands),
+        out_specs=tuple(pl.BlockSpec(memory_space=pltpu.VMEM) for _ in out_shape),
+        scratch_shapes=scratch,
+        compiler_params=pltpu.CompilerParams(
+            collective_id=5 if with_extra else 0, has_side_effects=True
+        ),
         cost_estimate=pl.CostEstimate(
             flops=2 * blocks * rows * cols, bytes_accessed=4 * 3 * blocks * rows * cols,
             transcendentals=0,
         ),
-    )(part, part.astype(link))
+    )(*operands)
+    return result if with_extra else result[0]
 
 
 def _sum_kernel(groups, part_ref, out_ref, got, send_sem, recv_sem):
@@ -304,9 +360,7 @@
         ray_total = ray_total + from_behind(ray_sends[distance], "slab", distance)
     live_rows = jnp.repeat(live_slots, ray_count).astype(jnp.bfloat16)
     voxel_local = jnp.dot(live_rows, flat_tiles, preferred_element_type=jnp.float32)
-    voxel_total = sum_angle(voxel_local.reshape(slab_depth, height), lax.axis_size("angle"))
     ray_scale = 1.0 / ray_total
-    voxel_scale = (1.0 / voxel_total).reshape(1, slab_depth, height)
     lower_all = from_behind(weight_z[slab_depth - 1], "slab", 1)
     z_first = slab_pos * slab_depth
     z_total = slab_depth * lax.axis_size("slab")
@@ -374,7 +428,14 @@
         back_t = near_back + jnp.einsum(
             "trn,trv->nv", picked, tiles[1:], preferred_element_type=jnp.float32
         )
-        back_own = scatter_angle(back_t.reshape(groups, share_width, voxels))
+        if iteration == 0:
+            back_own, voxel_total = scatter_angle(
+                back_t.reshape(groups, share_width, voxels),
+                voxel_local.reshape(slab_depth, height),
+            )
+            voxel_scale = (1.0 / voxel_total).reshape(1, slab_depth, height)
+        else:
+            back_own = scatter_angle(back_t.reshape(groups, share_width, voxels))
         volume = volume + voxel_scale * back_own.reshape(share_width, slab_depth, height)
         volume = smooth_share(
             volume,

time: 319 us -> 308 us (0.966)
  Pallas kernels: 102 us -> 95.2 us
    pallas_call x4 -> x3, Pallas kernels: 71.8 us -> 65.2 us  [scatter_angle(): pl.pallas_call(functools.partial(_scatter_kernel, n_chip, with_extra), ou...]
    unnamed x73 -> x33, local copies, waits for them, and re-layouts: 13.7 us -> 11.9 us
  transfers between devices with their start and end apart: 27 -> 27, of which waited for: 9 -> 9; matrix products, arithmetic and copies ran while one was open for 20% -> 20% of each run, Pallas kernels for 9% -> 8%
where the time goes in v7:
time: 308 us; the launch traced here: 306 us
  Pallas kernels  95.2 us (31%)
  starting transfers between devices  86 us (28%)
  matrix products  74.9 us (24%)
  local copies, waits for them, and re-layouts  24.6 us (8%)
  waiting for transfers between devices  13.5 us (4%)
  other arithmetic  9.4 us (3%)
    ppermute x27, starting transfers between devices, from_behind(): lax.ppermute(value, axis, [(source, source + steps) for source in range(f...  86 us
    pallas_call x3, Pallas kernels, scatter_angle(): pl.pallas_call(functools.partial(_scatter_kernel, n_chip, with_extra), ou...  65.2 us
    pallas_call x2, Pallas kernels, gather_angle(): pl.pallas_call(functools.partial(_gather_kernel, n_chip), out_shape=jax.S...  29.9 us
    dot_general x3, matrix products, shards(): jnp.einsum('trn,trv->nv', picked, tiles[1:], preferred_element_type=jnp.f...  18 us
    ppermute x27, waiting for transfers between devices, from_behind(): lax.ppermute(value, axis, [(source, source + steps) for source in range(f...  13.5 us
    dot_general x2, matrix products, shards(): jnp.einsum('trv,nv->trn', tiles[1:], gathered, preferred_element_type=jnp...  13.4 us
    unnamed x33, local copies, waits for them, and re-layouts  11.9 us
    dot_general x3, matrix products, shards(): jnp.einsum('rn,rv->nv', residual_half, tiles[0], preferred_element_type=j...  8.79 us
  transfers between devices with their start and end apart: 27, of which 9 were waited for; matrix products, arithmetic and copies ran while one was open for 20% of the time, Pallas kernels for 8%

profile of v7, /device:TPU:33, one launch (start us, length us, event | category | flops | bytes accessed | tf_op | source)
XLA Modules:
  0.0 306.0 jit_solution(7195080388953614850)
XLA Ops:
  2.3 7.9 %fusion.3 = bf16[1,3,512]{2,0,1:T(2,128)(2,1)S(1)} fusion(bf16[1,1,3,512,4096]{4,3,2,1,0:T(8,128)(2,1)} %param.10), kind=kOutput, calls=%fused_computation.3 | convolution fusion | flops 12582912 | bytes 12585984 | tf_op jit(solution)/shard_map/dot_general | solution.py:354
  10.4 4.8 %collective-permute-start.3 = (f32[512]{0:T(512)S(1)}, f32[512]{0:T(512)S(1)}, u32[]{:S(2)}, u32[]{:S(2)}) collective-permute-start(f32[512]{0:T(512)S(1)} %bitcast.337), channel_id=1, source_target_pairs={{0,16},{8,24},{16,32},{24,40},{32,48},{40,56},{48,64},{56,72},{64,... | collective-permute-start | bytes 6152 | tf_op jit(solution)/shard_map/ppermute | solution.py:22
  15.2 2.3 collective-permute-start.2
  18.3 2.6 collective-permute-start.7
  21.1 1.0 copy-done.6
  22.1 5.7 %fusion.15 = bf16[2,512,128]{2,1,0:T(8,128)(2,1)S(1)} fusion(bf16[4096,128,1]{1,0,2:T(8,128)(2,1)S(1)} %bitcast.308, bf16[1,1,3,512,4096]{4,3,2,1,0:T(8,128)(2,1)} %param.10), kind=kOutput, calls=%fused_computation.15 | convolution fusion | flops 1073741824 | bytes 9699328 | tf_op jit(solution)/shard_map/trv,vn->trn/dot_general | solution.py:391
  29.1 3.8 %collective-permute-start = (bf16[512,128]{1,0:T(8,128)(2,1)}, bf16[512,128]{1,0:T(8,128)(2,1)}, u32[]{:S(2)}, u32[]{:S(2)}) collective-permute-start(bf16[512,128]{1,0:T(8,128)(2,1)} %get-tuple-element.33), channel_id=1, source_target_pairs={{0,8},{8,16},{16,24},{24,32},{32,40},{40,48},{48,56},{56,64},{64,7... | collective-permute-start | bytes 393224 | tf_op jit(solution)/shard_map/ppermute | solution.py:22
  32.9 4.5 %collective-permute-start.1 = (bf16[512,128]{1,0:T(8,128)(2,1)}, bf16[512,128]{1,0:T(8,128)(2,1)}, u32[]{:S(2)}, u32[]{:S(2)}) collective-permute-start(bf16[512,128]{1,0:T(8,128)(2,1)} %get-tuple-element.34), channel_id=1, source_target_pairs={{0,16},{8,24},{16,32},{24,40},{32,48},{40,56},{48,64},{56,72},{64,... | collective-permute-start | bytes 393224 | tf_op jit(solution)/shard_map/ppermute | solution.py:22
  37.4 2.5 constant_dynamic-slice_fusion.3
  40.0 1.9 constant_dynamic-slice_fusion.4
  42.0 4.5 %fusion.65 = bf16[512,128]{1,0:T(8,128)(2,1)} fusion(bf16[4096,128]{1,0:T(8,128)(2,1)} %bitcast.309, bf16[1,1,3,512,4096]{4,3,2,1,0:T(8,128)(2,1)} %param.10), kind=kOutput, calls=%fused_computation.49 | convolution fusion | flops 536936448 | bytes 5373952 | tf_op jit(solution)/shard_map/rv,vn->rn/dot_general | solution.py:406
  46.5 1.3 constant_dynamic-slice_fusion
  47.8 2.0 constant_dynamic-slice_fusion.1
  49.9 5.7 %fusion = f32[1,8,512]{2,0,1:T(1,128)S(1)} fusion(pred[1536,1,1]{0,1,2:T(4,128)(4,1)S(1)} %reshape.82, bf16[192,8,8,512]{3,2,1,0:T(8,128)(2,1)} %bitcast.295), kind=kOutput, calls=%fused_computation | convolution fusion | flops 12582912 | bytes 12600832 | tf_op jit(solution)/shard_map/dot_general | solution.py:362
  56.2 1.6 copy.99
  58.8 1.6 copy.98
  60.4 1.6 copy.97
  62.0 1.2 fusion.81
  63.2 3.2 %collective-permute-start.5 = (bf16[512,128]{1,0:T(8,128)(2,1)S(1)}, bf16[512,128]{1,0:T(8,128)(2,1)S(1)}, u32[]{:S(2)}, u32[]{:S(2)}) collective-permute-start(bf16[512,128]{1,0:T(8,128)(2,1)S(1)} %fusion.81), channel_id=1, source_target_pairs={{16,0},{24,8},{32,16},{40,24},{48,32},{56,40},{64,48},{72,56},{80,... | collective-permute-start | bytes 393224 | tf_op jit(solution)/shard_map/ppermute | solution.py:22
  66.3 3.5 %collective-permute-start.4 = (bf16[512,128]{1,0:T(8,128)(2,1)S(1)}, bf16[512,128]{1,0:T(8,128)(2,1)S(1)}, u32[]{:S(2)}, u32[]{:S(2)}) collective-permute-start(bf16[512,128]{1,0:T(8,128)(2,1)S(1)} %fusion.81), channel_id=1, source_target_pairs={{8,0},{16,8},{24,16},{32,24},{40,32},{48,40},{56,48},{64,56},{72,6... | collective-permute-start | bytes 393224 | tf_op jit(solution)/shard_map/ppermute | solution.py:22
  69.8 2.9 fusion.43
  74.2 6.0 %fusion.32 = f32[128,4096]{1,0:T(8,128)} fusion(f32[128,4096]{1,0:T(8,128)S(1)} %fusion.43, bf16[1,1,3,512,4096]{4,3,2,1,0:T(8,128)(2,1)} %param.10, bf16[2,512,128]{1,2,0:T(8,128)(2,1)S(1)} %copy.80), kind=kOutput, calls=%fused_computation.22 | convolution fusion | flops 1074266112 | bytes 12845056 | tf_op jit(solution)/shard_map/trn,trv->nv/dot_general | solution.py:428
  80.2 23.4 %shard_map.104 = (f32[16,4096]{1,0:T(8,128)}, f32[8,512]{1,0:T(8,128)}) custom-call(f32[8,16,4096]{2,1,0:T(8,128)} %bitcast.296, f32[8,16,4096]{2,1,0:T(8,128)} %bitcast.297, f32[8,512]{1,0:T(8,128)} %bitcast.326), custom_call_target="tpu_custom_call" | custom-call | flops 1048576 | bytes 6291456 | tf_op jit(solution)/shard_map/pallas_call | solution.py:158
  104.3 1.1 copy.102
  105.4 2.1 collective-permute-start.10
  107.8 2.2 collective-permute-start.9
  110.0 5.2 %collective-permute-start.6 = (f32[16,512]{1,0:T(8,128)S(1)}, f32[16,512]{1,0:T(8,128)S(1)}, u32[]{:S(2)}, u32[]{:S(2)}) collective-permute-start(f32[16,512]{1,0:T(8,128)S(1)} %bitcast.328), channel_id=1, source_target_pairs={{8,0},{16,8},{24,16},{32,24},{40,32},{48,40},{56,48},{64,56},{72,6... | collective-permute-start | bytes 98312 | tf_op jit(solution)/shard_map/ppermute | solution.py:22
  115.2 1.9 collective-permute-start.8
  117.2 5.3 %collective-permute-done.8 = f32[16,512]{1,0:T(8,128)S(1)} collective-permute-done((f32[16,512]{1,0:T(8,128)S(1)}, f32[16,512]{1,0:T(8,128)S(1)}, u32[]{:S(2)}, u32[]{:S(2)}) %collective-permute-start.8) | collective-permute-done | bytes 32800 | tf_op jit(solution)/shard_map/ppermute | solution.py:22
  124.5 15.4 %shard_map.105 = bf16[8,16,4096]{2,1,0:T(8,128)(2,1)} custom-call(bf16[16,4096]{1,0:T(8,128)(2,1)} %bitcast.317), custom_call_target="tpu_custom_call" | custom-call | bytes 2097152 | tf_op jit(solution)/shard_map/pallas_call | solution.py:275
  140.0 6.7 %fusion.59 = bf16[128,2,512]{2,0,1:T(8,128)(2,1)S(1)} fusion(bf16[128,4096,1]{1,0,2:T(8,128)(2,1)} %bitcast.312, bf16[1,1,3,512,4096]{4,3,2,1,0:T(8,128)(2,1)} %param.10), kind=kOutput, calls=%fused_computation.47 | convolution fusion | flops 1073872896 | bytes 9699328 | tf_op jit(solution)/shard_map/trv,nv->trn/dot_general | solution.py:395
  147.4 1.9 collective-permute-start.11
  149.3 2.7 collective-permute-start.12
  152.0 3.4 %fusion.77 = bf16[512,128]{1,0:T(8,128)(2,1)S(1)} fusion(bf16[128,4096]{1,0:T(8,128)(2,1)S(1)} %bitcast.313, bf16[1,1,3,512,4096]{4,3,2,1,0:T(8,128)(2,1)} %param.10), kind=kOutput, calls=%fused_computation.53 | convolution fusion | flops 536936448 | bytes 5373952 | tf_op jit(solution)/shard_map/rv,nv->rn/dot_general | solution.py:410
  156.4 2.3 collective-permute-done.12
  158.8 1.9 collective-permute-start.14
  160.7 4.5 %collective-permute-start.13 = (bf16[512,128]{1,0:T(8,128)(2,1)S(1)}, bf16[512,128]{1,0:T(8,128)(2,1)S(1)}, u32[]{:S(2)}, u32[]{:S(2)}) collective-permute-start(bf16[512,128]{1,0:T(8,128)(2,1)S(1)} %fusion.83), channel_id=1, source_target_pairs={{8,0},{16,8},{24,16},{32,24},{40,32},{48,40},{56,48},{64,56},{72,6... | collective-permute-start | bytes 393224 | tf_op jit(solution)/shard_map/ppermute | solution.py:22
  165.2 2.9 fusion.39
  168.2 1.3 collective-permute-done.13
  170.3 6.0 %fusion.29 = f32[128,4096]{1,0:T(8,128)} fusion(f32[128,4096]{1,0:T(8,128)S(1)} %fusion.39, bf16[1,1,3,512,4096]{4,3,2,1,0:T(8,128)(2,1)} %param.10, bf16[2,512,128]{1,2,0:T(8,128)(2,1)S(1)} %copy.86), kind=kOutput, calls=%fused_computation.21 | convolution fusion | flops 1074266112 | bytes 12845056 | tf_op jit(solution)/shard_map/trn,trv->nv/dot_general | solution.py:428
  176.3 20.4 %shard_map.106 = f32[16,4096]{1,0:T(8,128)} custom-call(f32[8,16,4096]{2,1,0:T(8,128)} %bitcast.298, f32[8,16,4096]{2,1,0:T(8,128)} %bitcast.299), custom_call_target="tpu_custom_call" | custom-call | flops 1048576 | bytes 6291456 | tf_op jit(solution)/shard_map/pallas_call | solution.py:158
  196.7 1.1 copy.104
  198.3 2.2 collective-permute-start.18
  200.5 2.1 collective-permute-start.17
  202.6 2.8 collective-permute-start.16
  205.4 4.6 %collective-permute-start.15 = (f32[16,512]{1,0:T(8,128)S(1)}, f32[16,512]{1,0:T(8,128)S(1)}, u32[]{:S(2)}, u32[]{:S(2)}) collective-permute-start(f32[16,512]{1,0:T(8,128)S(1)} %get-tuple-element.20), channel_id=1, source_target_pairs={{8,0},{16,8},{24,16},{32,24},{40,32},{48,40},{56,48},{64,56},{72,6... | collective-permute-start | bytes 98312 | tf_op jit(solution)/shard_map/ppermute | solution.py:22
  212.6 14.5 %shard_map.107 = bf16[8,16,4096]{2,1,0:T(8,128)(2,1)} custom-call(bf16[16,4096]{1,0:T(8,128)(2,1)} %bitcast.318), custom_call_target="tpu_custom_call" | custom-call | bytes 2097152 | tf_op jit(solution)/shard_map/pallas_call | solution.py:275
  227.1 6.7 %fusion.62 = bf16[128,2,512]{2,0,1:T(8,128)(2,1)S(1)} fusion(bf16[128,4096,1]{1,0,2:T(8,128)(2,1)} %bitcast.314, bf16[1,1,3,512,4096]{4,3,2,1,0:T(8,128)(2,1)} %param.10), kind=kOutput, calls=%fused_computation.48 | convolution fusion | flops 1073872896 | bytes 9699328 | tf_op jit(solution)/shard_map/trv,nv->trn/dot_general | solution.py:395
  234.5 3.4 %collective-permute-start.19 = (bf16[512,128]{1,0:T(8,128)(2,1)S(1)}, bf16[512,128]{1,0:T(8,128)(2,1)S(1)}, u32[]{:S(2)}, u32[]{:S(2)}) collective-permute-start(bf16[512,128]{1,0:T(8,128)(2,1)S(1)} %get-tuple-element.15), channel_id=1, source_target_pairs={{0,8},{8,16},{16,24},{24,32},{32,40},{40,48},{48,56},{56,64},{64,7... | collective-permute-start | bytes 393224 | tf_op jit(solution)/shard_map/ppermute | solution.py:22
  238.0 5.9 %collective-permute-start.20 = (bf16[512,128]{1,0:T(8,128)(2,1)S(1)}, bf16[512,128]{1,0:T(8,128)(2,1)S(1)}, u32[]{:S(2)}, u32[]{:S(2)}) collective-permute-start(bf16[512,128]{1,0:T(8,128)(2,1)S(1)} %get-tuple-element.16), channel_id=1, source_target_pairs={{0,16},{8,24},{16,32},{24,40},{32,48},{40,56},{48,64},{56,72},{64,... | collective-permute-start | bytes 393224 | tf_op jit(solution)/shard_map/ppermute | solution.py:22
  243.8 3.4 %fusion.74 = bf16[512,128]{1,0:T(8,128)(2,1)S(1)} fusion(bf16[128,4096]{1,0:T(8,128)(2,1)S(1)} %bitcast.315, bf16[1,1,3,512,4096]{4,3,2,1,0:T(8,128)(2,1)} %param.10), kind=kOutput, calls=%fused_computation.52 | convolution fusion | flops 536936448 | bytes 5373952 | tf_op jit(solution)/shard_map/rv,nv->rn/dot_general | solution.py:410
  248.9 3.7 %collective-permute-start.22 = (bf16[512,128]{1,0:T(8,128)(2,1)S(1)}, bf16[512,128]{1,0:T(8,128)(2,1)S(1)}, u32[]{:S(2)}, u32[]{:S(2)}) collective-permute-start(bf16[512,128]{1,0:T(8,128)(2,1)S(1)} %get-tuple-element.9), channel_id=1, source_target_pairs={{16,0},{24,8},{32,16},{40,24},{48,32},{56,40},{64,48},{72,56},{80,... | collective-permute-start | bytes 393224 | tf_op jit(solution)/shard_map/ppermute | solution.py:22
  252.5 1.9 collective-permute-start.21
  254.5 2.9 fusion.35
  258.3 1.3 fusion.121
  259.6 1.1 copy.90
  260.7 6.0 %fusion.26 = f32[128,4096]{1,0:T(8,128)} fusion(f32[128,4096]{1,0:T(8,128)S(1)} %fusion.35, bf16[1,1,3,512,4096]{4,3,2,1,0:T(8,128)(2,1)} %param.10, bf16[2,512,128]{1,2,0:T(8,128)(2,1)S(1)} %copy.90), kind=kOutput, calls=%fused_computation.20 | convolution fusion | flops 1074266112 | bytes 12845056 | tf_op jit(solution)/shard_map/trn,trv->nv/dot_general | solution.py:428
  266.7 21.5 %shard_map.108 = f32[16,4096]{1,0:T(8,128)} custom-call(f32[8,16,4096]{2,1,0:T(8,128)} %bitcast.300, f32[8,16,4096]{2,1,0:T(8,128)} %bitcast.301), custom_call_target="tpu_custom_call" | custom-call | flops 1048576 | bytes 6291456 | tf_op jit(solution)/shard_map/pallas_call | solution.py:158
  288.2 1.1 copy.105
  290.0 1.9 collective-permute-start.26
  292.1 3.2 %collective-permute-start.24 = (f32[16,512]{1,0:T(8,128)S(1)}, f32[16,512]{1,0:T(8,128)S(1)}, u32[]{:S(2)}, u32[]{:S(2)}) collective-permute-start(f32[16,512]{1,0:T(8,128)S(1)} %get-tuple-element.10), channel_id=1, source_target_pairs={{0,8},{8,16},{16,24},{24,32},{32,40},{40,48},{48,56},{56,64},{64,7... | collective-permute-start | bytes 98312 | tf_op jit(solution)/shard_map/ppermute | solution.py:22
  295.3 4.2 %collective-permute-start.23 = (f32[16,512]{1,0:T(8,128)S(1)}, f32[16,512]{1,0:T(8,128)S(1)}, u32[]{:S(2)}, u32[]{:S(2)}) collective-permute-start(f32[16,512]{1,0:T(8,128)S(1)} %get-tuple-element.11), channel_id=1, source_target_pairs={{8,0},{16,8},{24,16},{32,24},{40,32},{48,40},{56,48},{64,56},{72,6... | collective-permute-start | bytes 98312 | tf_op jit(solution)/shard_map/ppermute | solution.py:22
  299.5 3.0 collective-permute-start.25
  303.4 1.2 collective-permute-done.25
  (131 shorter events, 20.9 us)
Async XLA Ops:
  0.6 16.9 %slice-start = ((bf16[8,512,128]{2,1,0:T(8,128)(2,1)}), bf16[1,512,128]{2,1,0:T(8,128)(2,1)S(1)}, s32[]{:S(2)}) async-start(bf16[8,512,128]{2,1,0:T(8,128)(2,1)} %param.15), calls=%async_computation | async-start | bytes 262144 | tf_op jit(solution)/shard_map/slice | solution.py:364
  0.6 20.3 %copy-start = (f32[8,512,128]{2,1,0:T(8,128)S(1)}, f32[8,512,128]{2,1,0:T(8,128)}, u32[]{:S(2)}) copy-start(f32[8,512,128]{2,1,0:T(8,128)} %param.9) | copy-start | bytes 6291460
  10.4 51.6 %collective-permute-start.3 = (f32[512]{0:T(512)S(1)}, f32[512]{0:T(512)S(1)}, u32[]{:S(2)}, u32[]{:S(2)}) collective-permute-start(f32[512]{0:T(512)S(1)} %bitcast.337), channel_id=1, source_target_pairs={{0,16},{8,24},{16,32},{24,40},{32,48},{40,56},{48,64},{56,72},{64,... | collective-permute-start | bytes 6152 | tf_op jit(solution)/shard_map/ppermute | solution.py:22
  15.2 46.7 %collective-permute-start.2 = (f32[512]{0:T(512)S(1)}, f32[512]{0:T(512)S(1)}, u32[]{:S(2)}, u32[]{:S(2)}) collective-permute-start(f32[512]{0:T(512)S(1)} %bitcast.336), channel_id=1, source_target_pairs={{0,8},{8,16},{16,24},{24,32},{32,40},{40,48},{48,56},{56,64},{64,7... | collective-permute-start | bytes 6152 | tf_op jit(solution)/shard_map/ppermute | solution.py:22
  18.3 98.9 %collective-permute-start.7 = (bf16[512,128]{0,1:T(8,128)(2,1)}, bf16[512,128]{0,1:T(8,128)(2,1)}, u32[]{:S(2)}, u32[]{:S(2)}) collective-permute-start(bf16[512,128]{0,1:T(8,128)(2,1)} %bitcast.26), channel_id=1, source_target_pairs={{0,8},{8,16},{16,24},{24,32},{32,40},{40,48},{48,56},{56,64},{64,7... | collective-permute-start | bytes 393224 | tf_op jit(solution)/shard_map/ppermute | solution.py:22
  21.1 1.0 copy-start.6
  27.8 18.7 %copy-start.2 = (bf16[8,512,128]{2,1,0:T(8,128)(2,1)S(1)}, bf16[8,512,128]{2,1,0:T(8,128)(2,1)}, u32[]{:S(2)}) copy-start(bf16[8,512,128]{2,1,0:T(8,128)(2,1)} %param.17) | copy-start | bytes 3145732
  29.1 32.9 %collective-permute-start = (bf16[512,128]{1,0:T(8,128)(2,1)}, bf16[512,128]{1,0:T(8,128)(2,1)}, u32[]{:S(2)}, u32[]{:S(2)}) collective-permute-start(bf16[512,128]{1,0:T(8,128)(2,1)} %get-tuple-element.33), channel_id=1, source_target_pairs={{0,8},{8,16},{16,24},{24,32},{32,40},{40,48},{48,56},{56,64},{64,7... | collective-permute-start | bytes 393224 | tf_op jit(solution)/shard_map/ppermute | solution.py:22
  32.9 29.1 %collective-permute-start.1 = (bf16[512,128]{1,0:T(8,128)(2,1)}, bf16[512,128]{1,0:T(8,128)(2,1)}, u32[]{:S(2)}, u32[]{:S(2)}) collective-permute-start(bf16[512,128]{1,0:T(8,128)(2,1)} %get-tuple-element.34), channel_id=1, source_target_pairs={{0,16},{8,24},{16,32},{24,40},{32,48},{40,56},{48,64},{56,72},{64,... | collective-permute-start | bytes 393224 | tf_op jit(solution)/shard_map/ppermute | solution.py:22
  41.9 5.9 %copy-start.5 = (bf16[8,512,128]{2,1,0:T(8,128)(2,1)S(1)}, bf16[8,512,128]{2,1,0:T(8,128)(2,1)}, u32[]{:S(2)}) copy-start(bf16[8,512,128]{2,1,0:T(8,128)(2,1)} %param.16) | copy-start | bytes 3145732
  49.8 7.9 %copy-start.3 = (bf16[8,512,16]{2,1,0:T(8,128)(2,1)S(1)}, bf16[8,512,16]{2,1,0:T(8,128)(2,1)}, u32[]{:S(2)}) copy-start(bf16[8,512,16]{2,1,0:T(8,128)(2,1)} %constant_dynamic-slice_fusion.3) | copy-start | bytes 393220
  49.9 8.3 %copy-start.1 = (f32[8,512,16]{2,1,0:T(8,128)S(1)}, f32[8,512,16]{2,1,0:T(8,128)}, u32[]{:S(2)}) copy-start(f32[8,512,16]{2,1,0:T(8,128)} %constant_dynamic-slice_fusion.4) | copy-start | bytes 786436
  49.9 12.2 %copy-start.4 = (bf16[1,1,512,128]{3,2,1,0:T(8,128)(2,1)S(1)}, bf16[1,1,512,128]{3,2,1,0:T(8,128)(2,1)}, u32[]{:S(2)}) copy-start(bf16[1,1,512,128]{3,2,1,0:T(8,128)(2,1)} %param.14) | copy-start | bytes 393220
  63.2 9.6 %collective-permute-start.5 = (bf16[512,128]{1,0:T(8,128)(2,1)S(1)}, bf16[512,128]{1,0:T(8,128)(2,1)S(1)}, u32[]{:S(2)}, u32[]{:S(2)}) collective-permute-start(bf16[512,128]{1,0:T(8,128)(2,1)S(1)} %fusion.81), channel_id=1, source_target_pairs={{16,0},{24,8},{32,16},{40,24},{48,32},{56,40},{64,48},{72,56},{80,... | collective-permute-start | bytes 393224 | tf_op jit(solution)/shard_map/ppermute | solution.py:22
  66.3 7.0 %collective-permute-start.4 = (bf16[512,128]{1,0:T(8,128)(2,1)S(1)}, bf16[512,128]{1,0:T(8,128)(2,1)S(1)}, u32[]{:S(2)}, u32[]{:S(2)}) collective-permute-start(bf16[512,128]{1,0:T(8,128)(2,1)S(1)} %fusion.81), channel_id=1, source_target_pairs={{8,0},{16,8},{24,16},{32,24},{40,32},{48,40},{56,48},{64,56},{72,6... | collective-permute-start | bytes 393224 | tf_op jit(solution)/shard_map/ppermute | solution.py:22
  105.4 11.7 %collective-permute-start.10 = (f32[8,512]{1,0:T(8,128)S(1)}, f32[8,512]{1,0:T(8,128)S(1)}, u32[]{:S(2)}, u32[]{:S(2)}) collective-permute-start(f32[8,512]{1,0:T(8,128)S(1)} %get-tuple-element.31), channel_id=1, source_target_pairs={{0,1},{1,2},{2,3},{3,4},{4,5},{5,6},{6,7},{8,9},{9,10},{10,11},{11... | collective-permute-start | bytes 49160 | tf_op jit(solution)/shard_map/ppermute | solution.py:22
  107.8 15.5 %collective-permute-start.9 = (f32[8,512]{1,0:T(8,128)S(1)}, f32[8,512]{1,0:T(8,128)S(1)}, u32[]{:S(2)}, u32[]{:S(2)}) collective-permute-start(f32[8,512]{1,0:T(8,128)S(1)} %get-tuple-element.32), channel_id=1, source_target_pairs={{1,0},{2,1},{3,2},{4,3},{5,4},{6,5},{7,6},{9,8},{10,9},{11,10},{12... | collective-permute-start | bytes 49160 | tf_op jit(solution)/shard_map/ppermute | solution.py:22
  110.0 13.3 %collective-permute-start.6 = (f32[16,512]{1,0:T(8,128)S(1)}, f32[16,512]{1,0:T(8,128)S(1)}, u32[]{:S(2)}, u32[]{:S(2)}) collective-permute-start(f32[16,512]{1,0:T(8,128)S(1)} %bitcast.328), channel_id=1, source_target_pairs={{8,0},{16,8},{24,16},{32,24},{40,32},{48,40},{56,48},{64,56},{72,6... | collective-permute-start | bytes 98312 | tf_op jit(solution)/shard_map/ppermute | solution.py:22
  115.2 7.3 %collective-permute-start.8 = (f32[16,512]{1,0:T(8,128)S(1)}, f32[16,512]{1,0:T(8,128)S(1)}, u32[]{:S(2)}, u32[]{:S(2)}) collective-permute-start(f32[16,512]{1,0:T(8,128)S(1)} %bitcast.329), channel_id=1, source_target_pairs={{0,8},{8,16},{16,24},{24,32},{32,40},{40,48},{48,56},{56,64},{64,7... | collective-permute-start | bytes 98312 | tf_op jit(solution)/shard_map/ppermute | solution.py:22
  140.0 12.0 %copy-start.7 = (bf16[8,16,4096]{2,1,0:T(8,128)(2,1)S(1)}, bf16[8,16,4096]{2,1,0:T(8,128)(2,1)}, u32[]{:S(2)}) copy-start(bf16[8,16,4096]{2,1,0:T(8,128)(2,1)} %shard_map.105) | copy-start | bytes 3145732
  147.4 9.0 %collective-permute-start.11 = (bf16[512,128]{1,0:T(8,128)(2,1)S(1)}, bf16[512,128]{1,0:T(8,128)(2,1)S(1)}, u32[]{:S(2)}, u32[]{:S(2)}) collective-permute-start(bf16[512,128]{1,0:T(8,128)(2,1)S(1)} %get-tuple-element.24), channel_id=1, source_target_pairs={{0,8},{8,16},{16,24},{24,32},{32,40},{40,48},{48,56},{56,64},{64,7... | collective-permute-start | bytes 393224 | tf_op jit(solution)/shard_map/ppermute | solution.py:22
  149.3 9.3 %collective-permute-start.12 = (bf16[512,128]{1,0:T(8,128)(2,1)S(1)}, bf16[512,128]{1,0:T(8,128)(2,1)S(1)}, u32[]{:S(2)}, u32[]{:S(2)}) collective-permute-start(bf16[512,128]{1,0:T(8,128)(2,1)S(1)} %get-tuple-element.25), channel_id=1, source_target_pairs={{0,16},{8,24},{16,32},{24,40},{32,48},{40,56},{48,64},{56,72},{64,... | collective-permute-start | bytes 393224 | tf_op jit(solution)/shard_map/ppermute | solution.py:22
  158.8 9.4 %collective-permute-start.14 = (bf16[512,128]{1,0:T(8,128)(2,1)S(1)}, bf16[512,128]{1,0:T(8,128)(2,1)S(1)}, u32[]{:S(2)}, u32[]{:S(2)}) collective-permute-start(bf16[512,128]{1,0:T(8,128)(2,1)S(1)} %fusion.83), channel_id=1, source_target_pairs={{16,0},{24,8},{32,16},{40,24},{48,32},{56,40},{64,48},{72,56},{80,... | collective-permute-start | bytes 393224 | tf_op jit(solution)/shard_map/ppermute | solution.py:22
  160.7 8.8 %collective-permute-start.13 = (bf16[512,128]{1,0:T(8,128)(2,1)S(1)}, bf16[512,128]{1,0:T(8,128)(2,1)S(1)}, u32[]{:S(2)}, u32[]{:S(2)}) collective-permute-start(bf16[512,128]{1,0:T(8,128)(2,1)S(1)} %fusion.83), channel_id=1, source_target_pairs={{8,0},{16,8},{24,16},{32,24},{40,32},{48,40},{56,48},{64,56},{72,6... | collective-permute-start | bytes 393224 | tf_op jit(solution)/shard_map/ppermute | solution.py:22
  198.3 11.8 %collective-permute-start.18 = (f32[8,512]{1,0:T(8,128)S(1)}, f32[8,512]{1,0:T(8,128)S(1)}, u32[]{:S(2)}, u32[]{:S(2)}) collective-permute-start(f32[8,512]{1,0:T(8,128)S(1)} %get-tuple-element.17), channel_id=1, source_target_pairs={{0,1},{1,2},{2,3},{3,4},{4,5},{5,6},{6,7},{8,9},{9,10},{10,11},{11... | collective-permute-start | bytes 49160 | tf_op jit(solution)/shard_map/ppermute | solution.py:22
  200.5 10.7 %collective-permute-start.17 = (f32[8,512]{1,0:T(8,128)S(1)}, f32[8,512]{1,0:T(8,128)S(1)}, u32[]{:S(2)}, u32[]{:S(2)}) collective-permute-start(f32[8,512]{1,0:T(8,128)S(1)} %get-tuple-element.18), channel_id=1, source_target_pairs={{1,0},{2,1},{3,2},{4,3},{5,4},{6,5},{7,6},{9,8},{10,9},{11,10},{12... | collective-permute-start | bytes 49160 | tf_op jit(solution)/shard_map/ppermute | solution.py:22
  202.6 7.4 %collective-permute-start.16 = (f32[16,512]{1,0:T(8,128)S(1)}, f32[16,512]{1,0:T(8,128)S(1)}, u32[]{:S(2)}, u32[]{:S(2)}) collective-permute-start(f32[16,512]{1,0:T(8,128)S(1)} %get-tuple-element.19), channel_id=1, source_target_pairs={{0,8},{8,16},{16,24},{24,32},{32,40},{40,48},{48,56},{56,64},{64,7... | collective-permute-start | bytes 98312 | tf_op jit(solution)/shard_map/ppermute | solution.py:22
  205.4 5.7 %collective-permute-start.15 = (f32[16,512]{1,0:T(8,128)S(1)}, f32[16,512]{1,0:T(8,128)S(1)}, u32[]{:S(2)}, u32[]{:S(2)}) collective-permute-start(f32[16,512]{1,0:T(8,128)S(1)} %get-tuple-element.20), channel_id=1, source_target_pairs={{8,0},{16,8},{24,16},{32,24},{40,32},{48,40},{56,48},{64,56},{72,6... | collective-permute-start | bytes 98312 | tf_op jit(solution)/shard_map/ppermute | solution.py:22
  227.1 16.8 %copy-start.8 = (bf16[8,16,4096]{2,1,0:T(8,128)(2,1)S(1)}, bf16[8,16,4096]{2,1,0:T(8,128)(2,1)}, u32[]{:S(2)}) copy-start(bf16[8,16,4096]{2,1,0:T(8,128)(2,1)} %shard_map.107) | copy-start | bytes 3145732
  234.5 12.8 %collective-permute-start.19 = (bf16[512,128]{1,0:T(8,128)(2,1)S(1)}, bf16[512,128]{1,0:T(8,128)(2,1)S(1)}, u32[]{:S(2)}, u32[]{:S(2)}) collective-permute-start(bf16[512,128]{1,0:T(8,128)(2,1)S(1)} %get-tuple-element.15), channel_id=1, source_target_pairs={{0,8},{8,16},{16,24},{24,32},{32,40},{40,48},{48,56},{56,64},{64,7... | collective-permute-start | bytes 393224 | tf_op jit(solution)/shard_map/ppermute | solution.py:22
  238.0 10.1 %collective-permute-start.20 = (bf16[512,128]{1,0:T(8,128)(2,1)S(1)}, bf16[512,128]{1,0:T(8,128)(2,1)S(1)}, u32[]{:S(2)}, u32[]{:S(2)}) collective-permute-start(bf16[512,128]{1,0:T(8,128)(2,1)S(1)} %get-tuple-element.16), channel_id=1, source_target_pairs={{0,16},{8,24},{16,32},{24,40},{32,48},{40,56},{48,64},{56,72},{64,... | collective-permute-start | bytes 393224 | tf_op jit(solution)/shard_map/ppermute | solution.py:22
  248.9 8.5 %collective-permute-start.22 = (bf16[512,128]{1,0:T(8,128)(2,1)S(1)}, bf16[512,128]{1,0:T(8,128)(2,1)S(1)}, u32[]{:S(2)}, u32[]{:S(2)}) collective-permute-start(bf16[512,128]{1,0:T(8,128)(2,1)S(1)} %get-tuple-element.9), channel_id=1, source_target_pairs={{16,0},{24,8},{32,16},{40,24},{48,32},{56,40},{64,48},{72,56},{80,... | collective-permute-start | bytes 393224 | tf_op jit(solution)/shard_map/ppermute | solution.py:22
  252.5 5.7 %collective-permute-start.21 = (bf16[512,128]{1,0:T(8,128)(2,1)S(1)}, bf16[512,128]{1,0:T(8,128)(2,1)S(1)}, u32[]{:S(2)}, u32[]{:S(2)}) collective-permute-start(bf16[512,128]{1,0:T(8,128)(2,1)S(1)} %get-tuple-element.9), channel_id=1, source_target_pairs={{8,0},{16,8},{24,16},{32,24},{40,32},{48,40},{56,48},{64,56},{72,6... | collective-permute-start | bytes 393224 | tf_op jit(solution)/shard_map/ppermute | solution.py:22
  290.0 12.5 %collective-permute-start.26 = (f32[8,512]{1,0:T(8,128)S(1)}, f32[8,512]{1,0:T(8,128)S(1)}, u32[]{:S(2)}, u32[]{:S(2)}) collective-permute-start(f32[8,512]{1,0:T(8,128)S(1)} %bitcast.334), channel_id=1, source_target_pairs={{0,1},{1,2},{2,3},{3,4},{4,5},{5,6},{6,7},{8,9},{9,10},{10,11},{11... | collective-permute-start | bytes 49160 | tf_op jit(solution)/shard_map/ppermute | solution.py:22
  292.1 10.4 %collective-permute-start.24 = (f32[16,512]{1,0:T(8,128)S(1)}, f32[16,512]{1,0:T(8,128)S(1)}, u32[]{:S(2)}, u32[]{:S(2)}) collective-permute-start(f32[16,512]{1,0:T(8,128)S(1)} %get-tuple-element.10), channel_id=1, source_target_pairs={{0,8},{8,16},{16,24},{24,32},{32,40},{40,48},{48,56},{56,64},{64,7... | collective-permute-start | bytes 98312 | tf_op jit(solution)/shard_map/ppermute | solution.py:22
  295.3 8.0 %collective-permute-start.23 = (f32[16,512]{1,0:T(8,128)S(1)}, f32[16,512]{1,0:T(8,128)S(1)}, u32[]{:S(2)}, u32[]{:S(2)}) collective-permute-start(f32[16,512]{1,0:T(8,128)S(1)} %get-tuple-element.11), channel_id=1, source_target_pairs={{8,0},{16,8},{24,16},{32,24},{40,32},{48,40},{56,48},{64,56},{72,6... | collective-permute-start | bytes 98312 | tf_op jit(solution)/shard_map/ppermute | solution.py:22
  299.5 5.1 %collective-permute-start.25 = (f32[8,512]{1,0:T(8,128)S(1)}, f32[8,512]{1,0:T(8,128)S(1)}, u32[]{:S(2)}, u32[]{:S(2)}) collective-permute-start(f32[8,512]{1,0:T(8,128)S(1)} %slice_bitcast_fusion.10), channel_id=1, source_target_pairs={{1,0},{2,1},{3,2},{4,3},{5,4},{6,5},{7,6},{9,8},{10,9},{11,10},{12... | collective-permute-start | bytes 49160 | tf_op jit(solution)/shard_map/ppermute | solution.py:22

commit v8 on v7

--- a/solution.py
+++ b/solution.py
@@ -371,10 +371,10 @@
 
     def share_of(array):
         part = lax.dynamic_slice_in_dim(array, share_first, share_width, array.ndim - 1)
-        return jnp.moveaxis(part, -1, 0).astype(jnp.float32)
+        return jnp.moveaxis(part, -1, 0)
 
     measured = sino[0, 0].astype(jnp.float32)
-    volume = share_of(volume0)
+    volume = share_of(volume0).astype(jnp.float32)
     local_z = share_of(weight_z)
     local_y = share_of(weight_y)
     local_x = share_of(weight_x)

time: 308 us -> 308 us (level)
  no operation moved by 1% of the time
where the time goes in v8:
time: 308 us; the launch traced here: 306 us
  Pallas kernels  95.2 us (31%)
  starting transfers between devices  86 us (28%)
  matrix products  74.9 us (24%)
  local copies, waits for them, and re-layouts  24.6 us (8%)
  waiting for transfers between devices  13.5 us (4%)
  other arithmetic  9.4 us (3%)
    ppermute x27, starting transfers between devices, from_behind(): lax.ppermute(value, axis, [(source, source + steps) for source in range(f...  86 us
    pallas_call x3, Pallas kernels, scatter_angle(): pl.pallas_call(functools.partial(_scatter_kernel, n_chip, with_extra), ou...  65.2 us
    pallas_call x2, Pallas kernels, gather_angle(): pl.pallas_call(functools.partial(_gather_kernel, n_chip), out_shape=jax.S...  29.9 us
    dot_general x3, matrix products, shards(): jnp.einsum('trn,trv->nv', picked, tiles[1:], preferred_element_type=jnp.f...  18 us
    ppermute x27, waiting for transfers between devices, from_behind(): lax.ppermute(value, axis, [(source, source + steps) for source in range(f...  13.5 us
    dot_general x2, matrix products, shards(): jnp.einsum('trv,nv->trn', tiles[1:], gathered, preferred_element_type=jnp...  13.4 us
    unnamed x33, local copies, waits for them, and re-layouts  11.9 us
    dot_general x3, matrix products, shards(): jnp.einsum('rn,rv->nv', residual_half, tiles[0], preferred_element_type=j...  8.79 us
  transfers between devices with their start and end apart: 27, of which 9 were waited for; matrix products, arithmetic and copies ran while one was open for 20% of the time, Pallas kernels for 8%

profile of v8, /device:TPU:33, one launch (start us, length us, event | category | flops | bytes accessed | tf_op | source)
XLA Modules:
  0.0 306.0 jit_solution(7195080388953614850)
XLA Ops:
  2.3 7.9 %fusion.3 = bf16[1,3,512]{2,0,1:T(2,128)(2,1)S(1)} fusion(bf16[1,1,3,512,4096]{4,3,2,1,0:T(8,128)(2,1)} %param.10), kind=kOutput, calls=%fused_computation.3 | convolution fusion | flops 12582912 | bytes 12585984 | tf_op jit(solution)/shard_map/dot_general | solution.py:354
  10.4 4.8 %collective-permute-start.3 = (f32[512]{0:T(512)S(1)}, f32[512]{0:T(512)S(1)}, u32[]{:S(2)}, u32[]{:S(2)}) collective-permute-start(f32[512]{0:T(512)S(1)} %bitcast.337), channel_id=1, source_target_pairs={{0,16},{8,24},{16,32},{24,40},{32,48},{40,56},{48,64},{56,72},{64,... | collective-permute-start | bytes 6152 | tf_op jit(solution)/shard_map/ppermute | solution.py:22
  15.2 2.3 collective-permute-start.2
  18.3 2.6 collective-permute-start.7
  21.1 1.0 copy-done.6
  22.1 5.7 %fusion.15 = bf16[2,512,128]{2,1,0:T(8,128)(2,1)S(1)} fusion(bf16[4096,128,1]{1,0,2:T(8,128)(2,1)S(1)} %bitcast.308, bf16[1,1,3,512,4096]{4,3,2,1,0:T(8,128)(2,1)} %param.10), kind=kOutput, calls=%fused_computation.15 | convolution fusion | flops 1073741824 | bytes 9699328 | tf_op jit(solution)/shard_map/trv,vn->trn/dot_general | solution.py:391
  29.1 3.8 %collective-permute-start = (bf16[512,128]{1,0:T(8,128)(2,1)}, bf16[512,128]{1,0:T(8,128)(2,1)}, u32[]{:S(2)}, u32[]{:S(2)}) collective-permute-start(bf16[512,128]{1,0:T(8,128)(2,1)} %get-tuple-element.33), channel_id=1, source_target_pairs={{0,8},{8,16},{16,24},{24,32},{32,40},{40,48},{48,56},{56,64},{64,7... | collective-permute-start | bytes 393224 | tf_op jit(solution)/shard_map/ppermute | solution.py:22
  32.9 4.5 %collective-permute-start.1 = (bf16[512,128]{1,0:T(8,128)(2,1)}, bf16[512,128]{1,0:T(8,128)(2,1)}, u32[]{:S(2)}, u32[]{:S(2)}) collective-permute-start(bf16[512,128]{1,0:T(8,128)(2,1)} %get-tuple-element.34), channel_id=1, source_target_pairs={{0,16},{8,24},{16,32},{24,40},{32,48},{40,56},{48,64},{56,72},{64,... | collective-permute-start | bytes 393224 | tf_op jit(solution)/shard_map/ppermute | solution.py:22
  37.4 2.5 constant_dynamic-slice_fusion.3
  40.0 1.9 constant_dynamic-slice_fusion.4
  42.0 4.5 %fusion.65 = bf16[512,128]{1,0:T(8,128)(2,1)} fusion(bf16[4096,128]{1,0:T(8,128)(2,1)} %bitcast.309, bf16[1,1,3,512,4096]{4,3,2,1,0:T(8,128)(2,1)} %param.10), kind=kOutput, calls=%fused_computation.49 | convolution fusion | flops 536936448 | bytes 5373952 | tf_op jit(solution)/shard_map/rv,vn->rn/dot_general | solution.py:406
  46.5 1.3 constant_dynamic-slice_fusion
  47.8 2.0 constant_dynamic-slice_fusion.1
  49.9 5.7 %fusion = f32[1,8,512]{2,0,1:T(1,128)S(1)} fusion(pred[1536,1,1]{0,1,2:T(4,128)(4,1)S(1)} %reshape.82, bf16[192,8,8,512]{3,2,1,0:T(8,128)(2,1)} %bitcast.295), kind=kOutput, calls=%fused_computation | convolution fusion | flops 12582912 | bytes 12600832 | tf_op jit(solution)/shard_map/dot_general | solution.py:362
  56.2 1.6 copy.99
  58.8 1.6 copy.98
  60.4 1.6 copy.97
  62.0 1.2 fusion.81
  63.2 3.2 %collective-permute-start.5 = (bf16[512,128]{1,0:T(8,128)(2,1)S(1)}, bf16[512,128]{1,0:T(8,128)(2,1)S(1)}, u32[]{:S(2)}, u32[]{:S(2)}) collective-permute-start(bf16[512,128]{1,0:T(8,128)(2,1)S(1)} %fusion.81), channel_id=1, source_target_pairs={{16,0},{24,8},{32,16},{40,24},{48,32},{56,40},{64,48},{72,56},{80,... | collective-permute-start | bytes 393224 | tf_op jit(solution)/shard_map/ppermute | solution.py:22
  66.3 3.5 %collective-permute-start.4 = (bf16[512,128]{1,0:T(8,128)(2,1)S(1)}, bf16[512,128]{1,0:T(8,128)(2,1)S(1)}, u32[]{:S(2)}, u32[]{:S(2)}) collective-permute-start(bf16[512,128]{1,0:T(8,128)(2,1)S(1)} %fusion.81), channel_id=1, source_target_pairs={{8,0},{16,8},{24,16},{32,24},{40,32},{48,40},{56,48},{64,56},{72,6... | collective-permute-start | bytes 393224 | tf_op jit(solution)/shard_map/ppermute | solution.py:22
  69.8 2.9 fusion.43
  74.2 6.0 %fusion.32 = f32[128,4096]{1,0:T(8,128)} fusion(f32[128,4096]{1,0:T(8,128)S(1)} %fusion.43, bf16[1,1,3,512,4096]{4,3,2,1,0:T(8,128)(2,1)} %param.10, bf16[2,512,128]{1,2,0:T(8,128)(2,1)S(1)} %copy.80), kind=kOutput, calls=%fused_computation.22 | convolution fusion | flops 1074266112 | bytes 12845056 | tf_op jit(solution)/shard_map/trn,trv->nv/dot_general | solution.py:428
  80.2 23.4 %shard_map.104 = (f32[16,4096]{1,0:T(8,128)}, f32[8,512]{1,0:T(8,128)}) custom-call(f32[8,16,4096]{2,1,0:T(8,128)} %bitcast.296, f32[8,16,4096]{2,1,0:T(8,128)} %bitcast.297, f32[8,512]{1,0:T(8,128)} %bitcast.326), custom_call_target="tpu_custom_call" | custom-call | flops 1048576 | bytes 6291456 | tf_op jit(solution)/shard_map/pallas_call | solution.py:158
  104.3 1.1 copy.102
  105.4 2.1 collective-permute-start.10
  107.8 2.2 collective-permute-start.9
  110.0 5.2 %collective-permute-start.6 = (f32[16,512]{1,0:T(8,128)S(1)}, f32[16,512]{1,0:T(8,128)S(1)}, u32[]{:S(2)}, u32[]{:S(2)}) collective-permute-start(f32[16,512]{1,0:T(8,128)S(1)} %bitcast.328), channel_id=1, source_target_pairs={{8,0},{16,8},{24,16},{32,24},{40,32},{48,40},{56,48},{64,56},{72,6... | collective-permute-start | bytes 98312 | tf_op jit(solution)/shard_map/ppermute | solution.py:22
  115.2 1.9 collective-permute-start.8
  117.2 5.3 %collective-permute-done.8 = f32[16,512]{1,0:T(8,128)S(1)} collective-permute-done((f32[16,512]{1,0:T(8,128)S(1)}, f32[16,512]{1,0:T(8,128)S(1)}, u32[]{:S(2)}, u32[]{:S(2)}) %collective-permute-start.8) | collective-permute-done | bytes 32800 | tf_op jit(solution)/shard_map/ppermute | solution.py:22
  124.5 15.4 %shard_map.105 = bf16[8,16,4096]{2,1,0:T(8,128)(2,1)} custom-call(bf16[16,4096]{1,0:T(8,128)(2,1)} %bitcast.317), custom_call_target="tpu_custom_call" | custom-call | bytes 2097152 | tf_op jit(solution)/shard_map/pallas_call | solution.py:275
  140.0 6.7 %fusion.59 = bf16[128,2,512]{2,0,1:T(8,128)(2,1)S(1)} fusion(bf16[128,4096,1]{1,0,2:T(8,128)(2,1)} %bitcast.312, bf16[1,1,3,512,4096]{4,3,2,1,0:T(8,128)(2,1)} %param.10), kind=kOutput, calls=%fused_computation.47 | convolution fusion | flops 1073872896 | bytes 9699328 | tf_op jit(solution)/shard_map/trv,nv->trn/dot_general | solution.py:395
  147.4 1.9 collective-permute-start.11
  149.3 2.7 collective-permute-start.12
  152.0 3.4 %fusion.77 = bf16[512,128]{1,0:T(8,128)(2,1)S(1)} fusion(bf16[128,4096]{1,0:T(8,128)(2,1)S(1)} %bitcast.313, bf16[1,1,3,512,4096]{4,3,2,1,0:T(8,128)(2,1)} %param.10), kind=kOutput, calls=%fused_computation.53 | convolution fusion | flops 536936448 | bytes 5373952 | tf_op jit(solution)/shard_map/rv,nv->rn/dot_general | solution.py:410
  156.4 2.3 collective-permute-done.12
  158.8 1.9 collective-permute-start.14
  160.7 4.5 %collective-permute-start.13 = (bf16[512,128]{1,0:T(8,128)(2,1)S(1)}, bf16[512,128]{1,0:T(8,128)(2,1)S(1)}, u32[]{:S(2)}, u32[]{:S(2)}) collective-permute-start(bf16[512,128]{1,0:T(8,128)(2,1)S(1)} %fusion.83), channel_id=1, source_target_pairs={{8,0},{16,8},{24,16},{32,24},{40,32},{48,40},{56,48},{64,56},{72,6... | collective-permute-start | bytes 393224 | tf_op jit(solution)/shard_map/ppermute | solution.py:22
  165.2 2.9 fusion.39
  168.2 1.3 collective-permute-done.13
  170.3 6.0 %fusion.29 = f32[128,4096]{1,0:T(8,128)} fusion(f32[128,4096]{1,0:T(8,128)S(1)} %fusion.39, bf16[1,1,3,512,4096]{4,3,2,1,0:T(8,128)(2,1)} %param.10, bf16[2,512,128]{1,2,0:T(8,128)(2,1)S(1)} %copy.86), kind=kOutput, calls=%fused_computation.21 | convolution fusion | flops 1074266112 | bytes 12845056 | tf_op jit(solution)/shard_map/trn,trv->nv/dot_general | solution.py:428
  176.3 20.4 %shard_map.106 = f32[16,4096]{1,0:T(8,128)} custom-call(f32[8,16,4096]{2,1,0:T(8,128)} %bitcast.298, f32[8,16,4096]{2,1,0:T(8,128)} %bitcast.299), custom_call_target="tpu_custom_call" | custom-call | flops 1048576 | bytes 6291456 | tf_op jit(solution)/shard_map/pallas_call | solution.py:158
  196.7 1.1 copy.104
  198.3 2.2 collective-permute-start.18
  200.5 2.1 collective-permute-start.17
  202.6 2.8 collective-permute-start.16
  205.4 4.6 %collective-permute-start.15 = (f32[16,512]{1,0:T(8,128)S(1)}, f32[16,512]{1,0:T(8,128)S(1)}, u32[]{:S(2)}, u32[]{:S(2)}) collective-permute-start(f32[16,512]{1,0:T(8,128)S(1)} %get-tuple-element.20), channel_id=1, source_target_pairs={{8,0},{16,8},{24,16},{32,24},{40,32},{48,40},{56,48},{64,56},{72,6... | collective-permute-start | bytes 98312 | tf_op jit(solution)/shard_map/ppermute | solution.py:22
  212.6 14.5 %shard_map.107 = bf16[8,16,4096]{2,1,0:T(8,128)(2,1)} custom-call(bf16[16,4096]{1,0:T(8,128)(2,1)} %bitcast.318), custom_call_target="tpu_custom_call" | custom-call | bytes 2097152 | tf_op jit(solution)/shard_map/pallas_call | solution.py:275
  227.1 6.7 %fusion.62 = bf16[128,2,512]{2,0,1:T(8,128)(2,1)S(1)} fusion(bf16[128,4096,1]{1,0,2:T(8,128)(2,1)} %bitcast.314, bf16[1,1,3,512,4096]{4,3,2,1,0:T(8,128)(2,1)} %param.10), kind=kOutput, calls=%fused_computation.48 | convolution fusion | flops 1073872896 | bytes 9699328 | tf_op jit(solution)/shard_map/trv,nv->trn/dot_general | solution.py:395
  234.5 3.4 %collective-permute-start.19 = (bf16[512,128]{1,0:T(8,128)(2,1)S(1)}, bf16[512,128]{1,0:T(8,128)(2,1)S(1)}, u32[]{:S(2)}, u32[]{:S(2)}) collective-permute-start(bf16[512,128]{1,0:T(8,128)(2,1)S(1)} %get-tuple-element.15), channel_id=1, source_target_pairs={{0,8},{8,16},{16,24},{24,32},{32,40},{40,48},{48,56},{56,64},{64,7... | collective-permute-start | bytes 393224 | tf_op jit(solution)/shard_map/ppermute | solution.py:22
  238.0 5.9 %collective-permute-start.20 = (bf16[512,128]{1,0:T(8,128)(2,1)S(1)}, bf16[512,128]{1,0:T(8,128)(2,1)S(1)}, u32[]{:S(2)}, u32[]{:S(2)}) collective-permute-start(bf16[512,128]{1,0:T(8,128)(2,1)S(1)} %get-tuple-element.16), channel_id=1, source_target_pairs={{0,16},{8,24},{16,32},{24,40},{32,48},{40,56},{48,64},{56,72},{64,... | collective-permute-start | bytes 393224 | tf_op jit(solution)/shard_map/ppermute | solution.py:22
  243.8 3.4 %fusion.74 = bf16[512,128]{1,0:T(8,128)(2,1)S(1)} fusion(bf16[128,4096]{1,0:T(8,128)(2,1)S(1)} %bitcast.315, bf16[1,1,3,512,4096]{4,3,2,1,0:T(8,128)(2,1)} %param.10), kind=kOutput, calls=%fused_computation.52 | convolution fusion | flops 536936448 | bytes 5373952 | tf_op jit(solution)/shard_map/rv,nv->rn/dot_general | solution.py:410
  248.9 3.7 %collective-permute-start.22 = (bf16[512,128]{1,0:T(8,128)(2,1)S(1)}, bf16[512,128]{1,0:T(8,128)(2,1)S(1)}, u32[]{:S(2)}, u32[]{:S(2)}) collective-permute-start(bf16[512,128]{1,0:T(8,128)(2,1)S(1)} %get-tuple-element.9), channel_id=1, source_target_pairs={{16,0},{24,8},{32,16},{40,24},{48,32},{56,40},{64,48},{72,56},{80,... | collective-permute-start | bytes 393224 | tf_op jit(solution)/shard_map/ppermute | solution.py:22
  252.5 1.9 collective-permute-start.21
  254.5 2.9 fusion.35
  258.3 1.3 fusion.121
  259.6 1.1 copy.90
  260.7 6.0 %fusion.26 = f32[128,4096]{1,0:T(8,128)} fusion(f32[128,4096]{1,0:T(8,128)S(1)} %fusion.35, bf16[1,1,3,512,4096]{4,3,2,1,0:T(8,128)(2,1)} %param.10, bf16[2,512,128]{1,2,0:T(8,128)(2,1)S(1)} %copy.90), kind=kOutput, calls=%fused_computation.20 | convolution fusion | flops 1074266112 | bytes 12845056 | tf_op jit(solution)/shard_map/trn,trv->nv/dot_general | solution.py:428
  266.7 21.5 %shard_map.108 = f32[16,4096]{1,0:T(8,128)} custom-call(f32[8,16,4096]{2,1,0:T(8,128)} %bitcast.300, f32[8,16,4096]{2,1,0:T(8,128)} %bitcast.301), custom_call_target="tpu_custom_call" | custom-call | flops 1048576 | bytes 6291456 | tf_op jit(solution)/shard_map/pallas_call | solution.py:158
  288.2 1.1 copy.105
  290.0 1.9 collective-permute-start.26
  292.1 3.2 %collective-permute-start.24 = (f32[16,512]{1,0:T(8,128)S(1)}, f32[16,512]{1,0:T(8,128)S(1)}, u32[]{:S(2)}, u32[]{:S(2)}) collective-permute-start(f32[16,512]{1,0:T(8,128)S(1)} %get-tuple-element.10), channel_id=1, source_target_pairs={{0,8},{8,16},{16,24},{24,32},{32,40},{40,48},{48,56},{56,64},{64,7... | collective-permute-start | bytes 98312 | tf_op jit(solution)/shard_map/ppermute | solution.py:22
  295.3 4.2 %collective-permute-start.23 = (f32[16,512]{1,0:T(8,128)S(1)}, f32[16,512]{1,0:T(8,128)S(1)}, u32[]{:S(2)}, u32[]{:S(2)}) collective-permute-start(f32[16,512]{1,0:T(8,128)S(1)} %get-tuple-element.11), channel_id=1, source_target_pairs={{8,0},{16,8},{24,16},{32,24},{40,32},{48,40},{56,48},{64,56},{72,6... | collective-permute-start | bytes 98312 | tf_op jit(solution)/shard_map/ppermute | solution.py:22
  299.5 3.0 collective-permute-start.25
  303.4 1.2 collective-permute-done.25
  (131 shorter events, 20.9 us)
Async XLA Ops:
  0.6 16.9 %slice-start = ((bf16[8,512,128]{2,1,0:T(8,128)(2,1)}), bf16[1,512,128]{2,1,0:T(8,128)(2,1)S(1)}, s32[]{:S(2)}) async-start(bf16[8,512,128]{2,1,0:T(8,128)(2,1)} %param.15), calls=%async_computation | async-start | bytes 262144 | tf_op jit(solution)/shard_map/slice | solution.py:364
  0.6 20.3 %copy-start = (f32[8,512,128]{2,1,0:T(8,128)S(1)}, f32[8,512,128]{2,1,0:T(8,128)}, u32[]{:S(2)}) copy-start(f32[8,512,128]{2,1,0:T(8,128)} %param.9) | copy-start | bytes 6291460
  10.4 51.6 %collective-permute-start.3 = (f32[512]{0:T(512)S(1)}, f32[512]{0:T(512)S(1)}, u32[]{:S(2)}, u32[]{:S(2)}) collective-permute-start(f32[512]{0:T(512)S(1)} %bitcast.337), channel_id=1, source_target_pairs={{0,16},{8,24},{16,32},{24,40},{32,48},{40,56},{48,64},{56,72},{64,... | collective-permute-start | bytes 6152 | tf_op jit(solution)/shard_map/ppermute | solution.py:22
  15.2 46.7 %collective-permute-start.2 = (f32[512]{0:T(512)S(1)}, f32[512]{0:T(512)S(1)}, u32[]{:S(2)}, u32[]{:S(2)}) collective-permute-start(f32[512]{0:T(512)S(1)} %bitcast.336), channel_id=1, source_target_pairs={{0,8},{8,16},{16,24},{24,32},{32,40},{40,48},{48,56},{56,64},{64,7... | collective-permute-start | bytes 6152 | tf_op jit(solution)/shard_map/ppermute | solution.py:22
  18.3 98.9 %collective-permute-start.7 = (bf16[512,128]{0,1:T(8,128)(2,1)}, bf16[512,128]{0,1:T(8,128)(2,1)}, u32[]{:S(2)}, u32[]{:S(2)}) collective-permute-start(bf16[512,128]{0,1:T(8,128)(2,1)} %bitcast.26), channel_id=1, source_target_pairs={{0,8},{8,16},{16,24},{24,32},{32,40},{40,48},{48,56},{56,64},{64,7... | collective-permute-start | bytes 393224 | tf_op jit(solution)/shard_map/ppermute | solution.py:22
  21.1 1.0 copy-start.6
  27.8 18.7 %copy-start.2 = (bf16[8,512,128]{2,1,0:T(8,128)(2,1)S(1)}, bf16[8,512,128]{2,1,0:T(8,128)(2,1)}, u32[]{:S(2)}) copy-start(bf16[8,512,128]{2,1,0:T(8,128)(2,1)} %param.17) | copy-start | bytes 3145732
  29.1 32.9 %collective-permute-start = (bf16[512,128]{1,0:T(8,128)(2,1)}, bf16[512,128]{1,0:T(8,128)(2,1)}, u32[]{:S(2)}, u32[]{:S(2)}) collective-permute-start(bf16[512,128]{1,0:T(8,128)(2,1)} %get-tuple-element.33), channel_id=1, source_target_pairs={{0,8},{8,16},{16,24},{24,32},{32,40},{40,48},{48,56},{56,64},{64,7... | collective-permute-start | bytes 393224 | tf_op jit(solution)/shard_map/ppermute | solution.py:22
  32.9 29.1 %collective-permute-start.1 = (bf16[512,128]{1,0:T(8,128)(2,1)}, bf16[512,128]{1,0:T(8,128)(2,1)}, u32[]{:S(2)}, u32[]{:S(2)}) collective-permute-start(bf16[512,128]{1,0:T(8,128)(2,1)} %get-tuple-element.34), channel_id=1, source_target_pairs={{0,16},{8,24},{16,32},{24,40},{32,48},{40,56},{48,64},{56,72},{64,... | collective-permute-start | bytes 393224 | tf_op jit(solution)/shard_map/ppermute | solution.py:22
  41.9 5.9 %copy-start.5 = (bf16[8,512,128]{2,1,0:T(8,128)(2,1)S(1)}, bf16[8,512,128]{2,1,0:T(8,128)(2,1)}, u32[]{:S(2)}) copy-start(bf16[8,512,128]{2,1,0:T(8,128)(2,1)} %param.16) | copy-start | bytes 3145732
  49.8 7.9 %copy-start.3 = (bf16[8,512,16]{2,1,0:T(8,128)(2,1)S(1)}, bf16[8,512,16]{2,1,0:T(8,128)(2,1)}, u32[]{:S(2)}) copy-start(bf16[8,512,16]{2,1,0:T(8,128)(2,1)} %constant_dynamic-slice_fusion.3) | copy-start | bytes 393220
  49.9 8.3 %copy-start.1 = (f32[8,512,16]{2,1,0:T(8,128)S(1)}, f32[8,512,16]{2,1,0:T(8,128)}, u32[]{:S(2)}) copy-start(f32[8,512,16]{2,1,0:T(8,128)} %constant_dynamic-slice_fusion.4) | copy-start | bytes 786436
  49.9 12.2 %copy-start.4 = (bf16[1,1,512,128]{3,2,1,0:T(8,128)(2,1)S(1)}, bf16[1,1,512,128]{3,2,1,0:T(8,128)(2,1)}, u32[]{:S(2)}) copy-start(bf16[1,1,512,128]{3,2,1,0:T(8,128)(2,1)} %param.14) | copy-start | bytes 393220
  63.2 9.6 %collective-permute-start.5 = (bf16[512,128]{1,0:T(8,128)(2,1)S(1)}, bf16[512,128]{1,0:T(8,128)(2,1)S(1)}, u32[]{:S(2)}, u32[]{:S(2)}) collective-permute-start(bf16[512,128]{1,0:T(8,128)(2,1)S(1)} %fusion.81), channel_id=1, source_target_pairs={{16,0},{24,8},{32,16},{40,24},{48,32},{56,40},{64,48},{72,56},{80,... | collective-permute-start | bytes 393224 | tf_op jit(solution)/shard_map/ppermute | solution.py:22
  66.3 7.0 %collective-permute-start.4 = (bf16[512,128]{1,0:T(8,128)(2,1)S(1)}, bf16[512,128]{1,0:T(8,128)(2,1)S(1)}, u32[]{:S(2)}, u32[]{:S(2)}) collective-permute-start(bf16[512,128]{1,0:T(8,128)(2,1)S(1)} %fusion.81), channel_id=1, source_target_pairs={{8,0},{16,8},{24,16},{32,24},{40,32},{48,40},{56,48},{64,56},{72,6... | collective-permute-start | bytes 393224 | tf_op jit(solution)/shard_map/ppermute | solution.py:22
  105.4 11.7 %collective-permute-start.10 = (f32[8,512]{1,0:T(8,128)S(1)}, f32[8,512]{1,0:T(8,128)S(1)}, u32[]{:S(2)}, u32[]{:S(2)}) collective-permute-start(f32[8,512]{1,0:T(8,128)S(1)} %get-tuple-element.31), channel_id=1, source_target_pairs={{0,1},{1,2},{2,3},{3,4},{4,5},{5,6},{6,7},{8,9},{9,10},{10,11},{11... | collective-permute-start | bytes 49160 | tf_op jit(solution)/shard_map/ppermute | solution.py:22
  107.8 15.5 %collective-permute-start.9 = (f32[8,512]{1,0:T(8,128)S(1)}, f32[8,512]{1,0:T(8,128)S(1)}, u32[]{:S(2)}, u32[]{:S(2)}) collective-permute-start(f32[8,512]{1,0:T(8,128)S(1)} %get-tuple-element.32), channel_id=1, source_target_pairs={{1,0},{2,1},{3,2},{4,3},{5,4},{6,5},{7,6},{9,8},{10,9},{11,10},{12... | collective-permute-start | bytes 49160 | tf_op jit(solution)/shard_map/ppermute | solution.py:22
  110.0 13.3 %collective-permute-start.6 = (f32[16,512]{1,0:T(8,128)S(1)}, f32[16,512]{1,0:T(8,128)S(1)}, u32[]{:S(2)}, u32[]{:S(2)}) collective-permute-start(f32[16,512]{1,0:T(8,128)S(1)} %bitcast.328), channel_id=1, source_target_pairs={{8,0},{16,8},{24,16},{32,24},{40,32},{48,40},{56,48},{64,56},{72,6... | collective-permute-start | bytes 98312 | tf_op jit(solution)/shard_map/ppermute | solution.py:22
  115.2 7.3 %collective-permute-start.8 = (f32[16,512]{1,0:T(8,128)S(1)}, f32[16,512]{1,0:T(8,128)S(1)}, u32[]{:S(2)}, u32[]{:S(2)}) collective-permute-start(f32[16,512]{1,0:T(8,128)S(1)} %bitcast.329), channel_id=1, source_target_pairs={{0,8},{8,16},{16,24},{24,32},{32,40},{40,48},{48,56},{56,64},{64,7... | collective-permute-start | bytes 98312 | tf_op jit(solution)/shard_map/ppermute | solution.py:22
  140.0 12.0 %copy-start.7 = (bf16[8,16,4096]{2,1,0:T(8,128)(2,1)S(1)}, bf16[8,16,4096]{2,1,0:T(8,128)(2,1)}, u32[]{:S(2)}) copy-start(bf16[8,16,4096]{2,1,0:T(8,128)(2,1)} %shard_map.105) | copy-start | bytes 3145732
  147.4 9.0 %collective-permute-start.11 = (bf16[512,128]{1,0:T(8,128)(2,1)S(1)}, bf16[512,128]{1,0:T(8,128)(2,1)S(1)}, u32[]{:S(2)}, u32[]{:S(2)}) collective-permute-start(bf16[512,128]{1,0:T(8,128)(2,1)S(1)} %get-tuple-element.24), channel_id=1, source_target_pairs={{0,8},{8,16},{16,24},{24,32},{32,40},{40,48},{48,56},{56,64},{64,7... | collective-permute-start | bytes 393224 | tf_op jit(solution)/shard_map/ppermute | solution.py:22
  149.3 9.3 %collective-permute-start.12 = (bf16[512,128]{1,0:T(8,128)(2,1)S(1)}, bf16[512,128]{1,0:T(8,128)(2,1)S(1)}, u32[]{:S(2)}, u32[]{:S(2)}) collective-permute-start(bf16[512,128]{1,0:T(8,128)(2,1)S(1)} %get-tuple-element.25), channel_id=1, source_target_pairs={{0,16},{8,24},{16,32},{24,40},{32,48},{40,56},{48,64},{56,72},{64,... | collective-permute-start | bytes 393224 | tf_op jit(solution)/shard_map/ppermute | solution.py:22
  158.8 9.4 %collective-permute-start.14 = (bf16[512,128]{1,0:T(8,128)(2,1)S(1)}, bf16[512,128]{1,0:T(8,128)(2,1)S(1)}, u32[]{:S(2)}, u32[]{:S(2)}) collective-permute-start(bf16[512,128]{1,0:T(8,128)(2,1)S(1)} %fusion.83), channel_id=1, source_target_pairs={{16,0},{24,8},{32,16},{40,24},{48,32},{56,40},{64,48},{72,56},{80,... | collective-permute-start | bytes 393224 | tf_op jit(solution)/shard_map/ppermute | solution.py:22
  160.7 8.8 %collective-permute-start.13 = (bf16[512,128]{1,0:T(8,128)(2,1)S(1)}, bf16[512,128]{1,0:T(8,128)(2,1)S(1)}, u32[]{:S(2)}, u32[]{:S(2)}) collective-permute-start(bf16[512,128]{1,0:T(8,128)(2,1)S(1)} %fusion.83), channel_id=1, source_target_pairs={{8,0},{16,8},{24,16},{32,24},{40,32},{48,40},{56,48},{64,56},{72,6... | collective-permute-start | bytes 393224 | tf_op jit(solution)/shard_map/ppermute | solution.py:22
  198.3 11.8 %collective-permute-start.18 = (f32[8,512]{1,0:T(8,128)S(1)}, f32[8,512]{1,0:T(8,128)S(1)}, u32[]{:S(2)}, u32[]{:S(2)}) collective-permute-start(f32[8,512]{1,0:T(8,128)S(1)} %get-tuple-element.17), channel_id=1, source_target_pairs={{0,1},{1,2},{2,3},{3,4},{4,5},{5,6},{6,7},{8,9},{9,10},{10,11},{11... | collective-permute-start | bytes 49160 | tf_op jit(solution)/shard_map/ppermute | solution.py:22
  200.5 10.7 %collective-permute-start.17 = (f32[8,512]{1,0:T(8,128)S(1)}, f32[8,512]{1,0:T(8,128)S(1)}, u32[]{:S(2)}, u32[]{:S(2)}) collective-permute-start(f32[8,512]{1,0:T(8,128)S(1)} %get-tuple-element.18), channel_id=1, source_target_pairs={{1,0},{2,1},{3,2},{4,3},{5,4},{6,5},{7,6},{9,8},{10,9},{11,10},{12... | collective-permute-start | bytes 49160 | tf_op jit(solution)/shard_map/ppermute | solution.py:22
  202.6 7.4 %collective-permute-start.16 = (f32[16,512]{1,0:T(8,128)S(1)}, f32[16,512]{1,0:T(8,128)S(1)}, u32[]{:S(2)}, u32[]{:S(2)}) collective-permute-start(f32[16,512]{1,0:T(8,128)S(1)} %get-tuple-element.19), channel_id=1, source_target_pairs={{0,8},{8,16},{16,24},{24,32},{32,40},{40,48},{48,56},{56,64},{64,7... | collective-permute-start | bytes 98312 | tf_op jit(solution)/shard_map/ppermute | solution.py:22
  205.4 5.7 %collective-permute-start.15 = (f32[16,512]{1,0:T(8,128)S(1)}, f32[16,512]{1,0:T(8,128)S(1)}, u32[]{:S(2)}, u32[]{:S(2)}) collective-permute-start(f32[16,512]{1,0:T(8,128)S(1)} %get-tuple-element.20), channel_id=1, source_target_pairs={{8,0},{16,8},{24,16},{32,24},{40,32},{48,40},{56,48},{64,56},{72,6... | collective-permute-start | bytes 98312 | tf_op jit(solution)/shard_map/ppermute | solution.py:22
  227.1 16.8 %copy-start.8 = (bf16[8,16,4096]{2,1,0:T(8,128)(2,1)S(1)}, bf16[8,16,4096]{2,1,0:T(8,128)(2,1)}, u32[]{:S(2)}) copy-start(bf16[8,16,4096]{2,1,0:T(8,128)(2,1)} %shard_map.107) | copy-start | bytes 3145732
  234.5 12.8 %collective-permute-start.19 = (bf16[512,128]{1,0:T(8,128)(2,1)S(1)}, bf16[512,128]{1,0:T(8,128)(2,1)S(1)}, u32[]{:S(2)}, u32[]{:S(2)}) collective-permute-start(bf16[512,128]{1,0:T(8,128)(2,1)S(1)} %get-tuple-element.15), channel_id=1, source_target_pairs={{0,8},{8,16},{16,24},{24,32},{32,40},{40,48},{48,56},{56,64},{64,7... | collective-permute-start | bytes 393224 | tf_op jit(solution)/shard_map/ppermute | solution.py:22
  238.0 10.1 %collective-permute-start.20 = (bf16[512,128]{1,0:T(8,128)(2,1)S(1)}, bf16[512,128]{1,0:T(8,128)(2,1)S(1)}, u32[]{:S(2)}, u32[]{:S(2)}) collective-permute-start(bf16[512,128]{1,0:T(8,128)(2,1)S(1)} %get-tuple-element.16), channel_id=1, source_target_pairs={{0,16},{8,24},{16,32},{24,40},{32,48},{40,56},{48,64},{56,72},{64,... | collective-permute-start | bytes 393224 | tf_op jit(solution)/shard_map/ppermute | solution.py:22
  248.9 8.5 %collective-permute-start.22 = (bf16[512,128]{1,0:T(8,128)(2,1)S(1)}, bf16[512,128]{1,0:T(8,128)(2,1)S(1)}, u32[]{:S(2)}, u32[]{:S(2)}) collective-permute-start(bf16[512,128]{1,0:T(8,128)(2,1)S(1)} %get-tuple-element.9), channel_id=1, source_target_pairs={{16,0},{24,8},{32,16},{40,24},{48,32},{56,40},{64,48},{72,56},{80,... | collective-permute-start | bytes 393224 | tf_op jit(solution)/shard_map/ppermute | solution.py:22
  252.5 5.7 %collective-permute-start.21 = (bf16[512,128]{1,0:T(8,128)(2,1)S(1)}, bf16[512,128]{1,0:T(8,128)(2,1)S(1)}, u32[]{:S(2)}, u32[]{:S(2)}) collective-permute-start(bf16[512,128]{1,0:T(8,128)(2,1)S(1)} %get-tuple-element.9), channel_id=1, source_target_pairs={{8,0},{16,8},{24,16},{32,24},{40,32},{48,40},{56,48},{64,56},{72,6... | collective-permute-start | bytes 393224 | tf_op jit(solution)/shard_map/ppermute | solution.py:22
  290.0 12.5 %collective-permute-start.26 = (f32[8,512]{1,0:T(8,128)S(1)}, f32[8,512]{1,0:T(8,128)S(1)}, u32[]{:S(2)}, u32[]{:S(2)}) collective-permute-start(f32[8,512]{1,0:T(8,128)S(1)} %bitcast.334), channel_id=1, source_target_pairs={{0,1},{1,2},{2,3},{3,4},{4,5},{5,6},{6,7},{8,9},{9,10},{10,11},{11... | collective-permute-start | bytes 49160 | tf_op jit(solution)/shard_map/ppermute | solution.py:22
  292.1 10.4 %collective-permute-start.24 = (f32[16,512]{1,0:T(8,128)S(1)}, f32[16,512]{1,0:T(8,128)S(1)}, u32[]{:S(2)}, u32[]{:S(2)}) collective-permute-start(f32[16,512]{1,0:T(8,128)S(1)} %get-tuple-element.10), channel_id=1, source_target_pairs={{0,8},{8,16},{16,24},{24,32},{32,40},{40,48},{48,56},{56,64},{64,7... | collective-permute-start | bytes 98312 | tf_op jit(solution)/shard_map/ppermute | solution.py:22
  295.3 8.0 %collective-permute-start.23 = (f32[16,512]{1,0:T(8,128)S(1)}, f32[16,512]{1,0:T(8,128)S(1)}, u32[]{:S(2)}, u32[]{:S(2)}) collective-permute-start(f32[16,512]{1,0:T(8,128)S(1)} %get-tuple-element.11), channel_id=1, source_target_pairs={{8,0},{16,8},{24,16},{32,24},{40,32},{48,40},{56,48},{64,56},{72,6... | collective-permute-start | bytes 98312 | tf_op jit(solution)/shard_map/ppermute | solution.py:22
  299.5 5.1 %collective-permute-start.25 = (f32[8,512]{1,0:T(8,128)S(1)}, f32[8,512]{1,0:T(8,128)S(1)}, u32[]{:S(2)}, u32[]{:S(2)}) collective-permute-start(f32[8,512]{1,0:T(8,128)S(1)} %slice_bitcast_fusion.10), channel_id=1, source_target_pairs={{1,0},{2,1},{3,2},{4,3},{5,4},{6,5},{7,6},{9,8},{10,9},{11,10},{12... | collective-permute-start | bytes 49160 | tf_op jit(solution)/shard_map/ppermute | solution.py:22

commit v9 on v8

--- a/solution.py
+++ b/solution.py
@@ -374,11 +374,6 @@
         return jnp.moveaxis(part, -1, 0)
 
     measured = sino[0, 0].astype(jnp.float32)
-    volume = share_of(volume0).astype(jnp.float32)
-    local_z = share_of(weight_z)
-    local_y = share_of(weight_y)
-    local_x = share_of(weight_x)
-    lower_rim = share_of(lower_all)
     left_index = jnp.maximum(share_first - 1, 0)
     left_rim = lax.dynamic_index_in_dim(weight_x, left_index, 2, keepdims=False).astype(
         jnp.float32
@@ -416,6 +411,15 @@
             projected = projected + arrived[distance - 1].astype(jnp.float32)
         residual = (measured - projected) * ray_scale[:, None]
         residual_half = residual.astype(jnp.bfloat16)
+        if iteration == 0:
+            residual_half, late = lax.optimization_barrier(
+                (residual_half, (volume0, weight_z, weight_y, weight_x, lower_all))
+            )
+            volume = share_of(late[0]).astype(jnp.float32)
+            local_z = share_of(late[1])
+            local_y = share_of(late[2])
+            local_x = share_of(late[3])
+            lower_rim = share_of(late[4])
         nearby = [
             from_behind(residual_half, "slab", -distance) for distance in range(1, slot_count)
         ]

time: 308 us -> 306 us (level)
  other arithmetic: 9.4 us -> 18.5 us
  starting transfers between devices: 86 us -> 79.8 us
  matrix products: 74.9 us -> 70 us
  waiting for transfers between devices: 13.5 us -> 17.6 us
  local copies, waits for them, and re-layouts: 24.6 us -> 20.6 us
    optimization_barrier x0 -> x4, local copies, waits for them, and re-layouts: none -> 10.2 us  [shards(): lax.optimization_barrier((residual_half, (volume0, weight_z, weight_y, we...]
    dynamic_slice x3 -> x0, local copies, waits for them, and re-layouts: 6.5 us -> none  [share_of(): lax.dynamic_slice_in_dim(array, share_first, share_width, array.ndim - 1)]
    unnamed x33 -> x37, local copies, waits for them, and re-layouts: 11.9 us -> 5.55 us
    ppermute x27, starting transfers between devices: 86 us -> 79.8 us  [from_behind(): lax.ppermute(value, axis, [(source, source + steps) for source in range(f...]
    ppermute x27, waiting for transfers between devices: 13.5 us -> 17.6 us  [from_behind(): lax.ppermute(value, axis, [(source, source + steps) for source in range(f...]
    dot_general x1, matrix products: 5.7 us -> 2.33 us  [shards(): jnp.einsum('trv,vn->trn', tiles[1:], flat_volume, preferred_element_type=...]
    mul x3, other arithmetic: 0.88 us -> 3.98 us  [smooth_share(): face_flux = weight_z * limiter(upper - volume) * inside]
  transfers between devices with their start and end apart: 27 -> 27, of which waited for: 9 -> 9; matrix products, arithmetic and copies ran while one was open for 20% -> 16% of each run, Pallas kernels for 8% -> 0%
where the time goes in v9:
time: 306 us; the launch traced here: 304 us
  Pallas kernels  94.9 us (31%)
  starting transfers between devices  79.8 us (26%)
  matrix products  70 us (23%)
  local copies, waits for them, and re-layouts  20.6 us (7%)
  other arithmetic  18.5 us (6%)
  waiting for transfers between devices  17.6 us (6%)
    ppermute x27, starting transfers between devices, from_behind(): lax.ppermute(value, axis, [(source, source + steps) for source in range(f...  79.8 us
    pallas_call x3, Pallas kernels, scatter_angle(): pl.pallas_call(functools.partial(_scatter_kernel, n_chip, with_extra), ou...  66.2 us
    pallas_call x2, Pallas kernels, gather_angle(): pl.pallas_call(functools.partial(_gather_kernel, n_chip), out_shape=jax.S...  28.7 us
    ppermute x27, waiting for transfers between devices, from_behind(): lax.ppermute(value, axis, [(source, source + steps) for source in range(f...  17.6 us
    dot_general x3, matrix products, shards(): jnp.einsum('trn,trv->nv', picked, tiles[1:], preferred_element_type=jnp.f...  16.7 us
    dot_general x2, matrix products, shards(): jnp.einsum('trv,nv->trn', tiles[1:], gathered, preferred_element_type=jnp...  13.4 us
    optimization_barrier x4, local copies, waits for them, and re-layouts, shards(): lax.optimization_barrier((residual_half, (volume0, weight_z, weight_y, we...  10.2 us
    dot_general x3, matrix products, shards(): jnp.einsum('rn,rv->nv', residual_half, tiles[0], preferred_element_type=j...  8.8 us
  transfers between devices with their start and end apart: 27, of which 9 were waited for; matrix products, arithmetic and copies ran while one was open for 16% of the time, Pallas kernels for 0%

profile of v9, /device:TPU:33, one launch (start us, length us, event | category | flops | bytes accessed | tf_op | source)
XLA Modules:
  0.0 303.9 jit_solution(935143525964847578)
XLA Ops:
  1.5 1.3 select_reduce_fusion
  2.7 8.3 %fusion.3 = bf16[1,3,512]{2,0,1:T(2,128)(2,1)S(1)} fusion(bf16[1,1,3,512,4096]{4,3,2,1,0:T(8,128)(2,1)} %param.10), kind=kOutput, calls=%fused_computation.3 | convolution fusion | flops 12582912 | bytes 12585984 | tf_op jit(solution)/shard_map/dot_general | solution.py:354
  11.7 3.2 %collective-permute-start.2 = (f32[512]{0:T(512)}, f32[512]{0:T(512)}, u32[]{:S(2)}, u32[]{:S(2)}) collective-permute-start(f32[512]{0:T(512)} %bitcast.14), channel_id=1, source_target_pairs={{0,8},{8,16},{16,24},{24,32},{32,40},{40,48},{48,56},{56,64},{64,7... | collective-permute-start | bytes 6152 | tf_op jit(solution)/shard_map/ppermute | solution.py:22
  14.9 4.5 %collective-permute-start.3 = (f32[512]{0:T(512)}, f32[512]{0:T(512)}, u32[]{:S(2)}, u32[]{:S(2)}) collective-permute-start(f32[512]{0:T(512)} %bitcast.15), channel_id=1, source_target_pairs={{0,16},{8,24},{16,32},{24,40},{32,48},{40,56},{48,64},{56,72},{64,... | collective-permute-start | bytes 6152 | tf_op jit(solution)/shard_map/ppermute | solution.py:22
  19.7 2.3 fusion.15
  23.2 2.6 collective-permute-start
  25.8 4.8 %collective-permute-start.1 = (bf16[512,128]{1,0:T(8,128)(2,1)S(1)}, bf16[512,128]{1,0:T(8,128)(2,1)}, u32[]{:S(2)}, u32[]{:S(2)}) collective-permute-start(bf16[512,128]{1,0:T(8,128)(2,1)S(1)} %get-tuple-element.46), channel_id=1, source_target_pairs={{0,16},{8,24},{16,32},{24,40},{32,48},{40,56},{48,64},{56,72},{64,... | collective-permute-start | bytes 393224 | tf_op jit(solution)/shard_map/ppermute | solution.py:22
  31.4 2.9 collective-permute-start.4
  34.9 4.2 %fusion.62 = bf16[512,128]{1,0:T(8,128)(2,1)} fusion(bf16[4096,128]{1,0:T(8,128)(2,1)S(1)} %bitcast.305, bf16[1,1,3,512,4096]{4,3,2,1,0:T(8,128)(2,1)} %param.10), kind=kOutput, calls=%fused_computation.48 | convolution fusion | flops 536936448 | bytes 5373952 | tf_op jit(solution)/shard_map/rv,vn->rn/dot_general | solution.py:401
  39.7 5.5 %fusion = f32[1,8,512]{2,0,1:T(1,128)S(1)} fusion(pred[1536,1,1]{0,1,2:T(4,128)(4,1)S(1)} %reshape.82, bf16[192,8,8,512]{3,2,1,0:T(8,128)(2,1)} %bitcast.291), kind=kOutput, calls=%fused_computation | convolution fusion | flops 12582912 | bytes 12600832 | tf_op jit(solution)/shard_map/dot_general | solution.py:362
  48.9 4.5 %collective-permute-start.5 = (bf16[512,128]{1,0:T(8,128)(2,1)S(1)}, bf16[512,128]{1,0:T(8,128)(2,1)S(1)}, u32[]{:S(2)}, u32[]{:S(2)}) collective-permute-start(bf16[512,128]{1,0:T(8,128)(2,1)S(1)} %fusion.78), channel_id=1, source_target_pairs={{8,0},{16,8},{24,16},{32,24},{40,32},{48,40},{56,48},{64,56},{72,6... | collective-permute-start | bytes 393224 | tf_op jit(solution)/shard_map/ppermute | solution.py:22
  53.4 2.1 collective-permute-start.6
  55.5 2.9 fusion.40
  58.4 3.2 %copy.46 = f32[8,512,128]{1,0,2:T(8,128)} copy(f32[8,512,128]{2,1,0:T(8,128)} %param.9) | data formatting | bytes 4194304 | tf_op jit(solution)/shard_map/optimization_barrier | solution.py:415
  61.6 2.7 copy.47
  64.2 2.7 copy.51
  66.9 1.7 copy.52
  69.6 1.2 fusion.122
  71.0 4.6 %fusion.17 = f32[128,4096]{1,0:T(8,128)S(1)} fusion(bf16[1,1,3,512,4096]{4,3,2,1,0:T(8,128)(2,1)} %param.10, bf16[2,512,128]{1,2,0:T(8,128)(2,1)S(1)} %copy.80), kind=kOutput, calls=%fused_computation.17 | convolution fusion | flops 1073741824 | bytes 10747904 | tf_op jit(solution)/shard_map/trn,trv->nv/dot_general | solution.py:432
  75.6 1.6 add.175
  77.3 23.1 %shard_map.104 = (f32[16,4096]{1,0:T(8,128)}, f32[8,512]{1,0:T(8,128)}) custom-call(f32[8,16,4096]{2,1,0:T(8,128)} %bitcast.292, f32[8,16,4096]{2,1,0:T(8,128)} %bitcast.293, f32[8,512]{1,0:T(8,128)} %bitcast.321), custom_call_target="tpu_custom_call" | custom-call | flops 1048576 | bytes 6291456 | tf_op jit(solution)/shard_map/pallas_call | solution.py:158
  101.1 1.1 copy.98
  103.3 2.1 collective-permute-start.10
  105.6 2.5 collective-permute-start.8
  108.2 4.9 %collective-permute-start.7 = (f32[16,512]{1,0:T(8,128)S(1)}, f32[16,512]{1,0:T(8,128)S(1)}, u32[]{:S(2)}, u32[]{:S(2)}) collective-permute-start(f32[16,512]{1,0:T(8,128)S(1)} %bitcast.322), channel_id=1, source_target_pairs={{8,0},{16,8},{24,16},{32,24},{40,32},{48,40},{56,48},{64,56},{72,6... | collective-permute-start | bytes 98312 | tf_op jit(solution)/shard_map/ppermute | solution.py:22
  113.1 2.8 collective-permute-start.9
  116.7 1.4 collective-permute-done.9
  118.1 1.3 fusion.104
  120.4 14.4 %shard_map.105 = bf16[8,16,4096]{2,1,0:T(8,128)(2,1)} custom-call(bf16[16,4096]{1,0:T(8,128)(2,1)} %bitcast.313), custom_call_target="tpu_custom_call" | custom-call | bytes 2097152 | tf_op jit(solution)/shard_map/pallas_call | solution.py:275
  134.8 6.7 %fusion.56 = bf16[128,2,512]{2,0,1:T(8,128)(2,1)S(1)} fusion(bf16[128,4096,1]{1,0,2:T(8,128)(2,1)} %bitcast.308, bf16[1,1,3,512,4096]{4,3,2,1,0:T(8,128)(2,1)} %param.10), kind=kOutput, calls=%fused_computation.46 | convolution fusion | flops 1073872896 | bytes 9699328 | tf_op jit(solution)/shard_map/trv,nv->trn/dot_general | solution.py:390
  142.2 1.9 collective-permute-start.11
  144.2 4.0 %collective-permute-start.12 = (bf16[512,128]{1,0:T(8,128)(2,1)S(1)}, bf16[512,128]{1,0:T(8,128)(2,1)S(1)}, u32[]{:S(2)}, u32[]{:S(2)}) collective-permute-start(bf16[512,128]{1,0:T(8,128)(2,1)S(1)} %get-tuple-element.37), channel_id=1, source_target_pairs={{0,16},{8,24},{16,32},{24,40},{32,48},{40,56},{48,64},{56,72},{64,... | collective-permute-start | bytes 393224 | tf_op jit(solution)/shard_map/ppermute | solution.py:22
  148.2 3.4 %fusion.74 = bf16[512,128]{1,0:T(8,128)(2,1)S(1)} fusion(bf16[128,4096]{1,0:T(8,128)(2,1)S(1)} %bitcast.309, bf16[1,1,3,512,4096]{4,3,2,1,0:T(8,128)(2,1)} %param.10), kind=kOutput, calls=%fused_computation.52 | convolution fusion | flops 536936448 | bytes 5373952 | tf_op jit(solution)/shard_map/rv,nv->rn/dot_general | solution.py:405
  151.7 1.8 collective-permute-done.12
  153.6 4.2 %collective-permute-start.13 = (bf16[512,128]{1,0:T(8,128)(2,1)S(1)}, bf16[512,128]{1,0:T(8,128)(2,1)S(1)}, u32[]{:S(2)}, u32[]{:S(2)}) collective-permute-start(bf16[512,128]{1,0:T(8,128)(2,1)S(1)} %fusion.80), channel_id=1, source_target_pairs={{8,0},{16,8},{24,16},{32,24},{40,32},{48,40},{56,48},{64,56},{72,6... | collective-permute-start | bytes 393224 | tf_op jit(solution)/shard_map/ppermute | solution.py:22
  157.8 2.1 collective-permute-start.14
  160.0 2.9 fusion.36
  162.9 2.1 collective-permute-done.14
  165.8 6.0 %fusion.29 = f32[128,4096]{1,0:T(8,128)} fusion(f32[128,4096]{1,0:T(8,128)S(1)} %fusion.36, bf16[1,1,3,512,4096]{4,3,2,1,0:T(8,128)(2,1)} %param.10, bf16[2,512,128]{1,2,0:T(8,128)(2,1)S(1)} %copy.86), kind=kOutput, calls=%fused_computation.21 | convolution fusion | flops 1074266112 | bytes 12845056 | tf_op jit(solution)/shard_map/trn,trv->nv/dot_general | solution.py:432
  171.8 21.6 %shard_map.106 = f32[16,4096]{1,0:T(8,128)} custom-call(f32[8,16,4096]{2,1,0:T(8,128)} %bitcast.294, f32[8,16,4096]{2,1,0:T(8,128)} %bitcast.295), custom_call_target="tpu_custom_call" | custom-call | flops 1048576 | bytes 6291456 | tf_op jit(solution)/shard_map/pallas_call | solution.py:158
  194.8 2.7 collective-permute-start.18
  197.7 3.1 %collective-permute-start.15 = (f32[16,512]{1,0:T(8,128)S(1)}, f32[16,512]{1,0:T(8,128)S(1)}, u32[]{:S(2)}, u32[]{:S(2)}) collective-permute-start(f32[16,512]{1,0:T(8,128)S(1)} %get-tuple-element.32), channel_id=1, source_target_pairs={{8,0},{16,8},{24,16},{32,24},{40,32},{48,40},{56,48},{64,56},{72,6... | collective-permute-start | bytes 98312 | tf_op jit(solution)/shard_map/ppermute | solution.py:22
  200.9 1.9 collective-permute-start.17
  202.8 2.2 collective-permute-start.16
  205.9 1.3 fusion.105
  207.3 2.6 collective-permute-done.16
  211.7 14.3 %shard_map.107 = bf16[8,16,4096]{2,1,0:T(8,128)(2,1)} custom-call(bf16[16,4096]{1,0:T(8,128)(2,1)} %bitcast.314), custom_call_target="tpu_custom_call" | custom-call | bytes 2097152 | tf_op jit(solution)/shard_map/pallas_call | solution.py:275
  226.1 6.7 %fusion.59 = bf16[128,2,512]{2,0,1:T(8,128)(2,1)S(1)} fusion(bf16[128,4096,1]{1,0,2:T(8,128)(2,1)} %bitcast.310, bf16[1,1,3,512,4096]{4,3,2,1,0:T(8,128)(2,1)} %param.10), kind=kOutput, calls=%fused_computation.47 | convolution fusion | flops 1073872896 | bytes 9699328 | tf_op jit(solution)/shard_map/trv,nv->trn/dot_general | solution.py:390
  233.5 1.9 collective-permute-start.19
  235.4 2.7 collective-permute-start.20
  238.2 3.4 %fusion.71 = bf16[512,128]{1,0:T(8,128)(2,1)S(1)} fusion(bf16[128,4096]{1,0:T(8,128)(2,1)S(1)} %bitcast.311, bf16[1,1,3,512,4096]{4,3,2,1,0:T(8,128)(2,1)} %param.10), kind=kOutput, calls=%fused_computation.51 | convolution fusion | flops 536936448 | bytes 5373952 | tf_op jit(solution)/shard_map/rv,nv->rn/dot_general | solution.py:405
  242.5 2.3 collective-permute-done.20
  245.6 4.2 %collective-permute-start.21 = (bf16[512,128]{1,0:T(8,128)(2,1)S(1)}, bf16[512,128]{1,0:T(8,128)(2,1)S(1)}, u32[]{:S(2)}, u32[]{:S(2)}) collective-permute-start(bf16[512,128]{1,0:T(8,128)(2,1)S(1)} %get-tuple-element.21), channel_id=1, source_target_pairs={{8,0},{16,8},{24,16},{32,24},{40,32},{48,40},{56,48},{64,56},{72,6... | collective-permute-start | bytes 393224 | tf_op jit(solution)/shard_map/ppermute | solution.py:22
  249.8 2.2 collective-permute-start.22
  252.0 2.9 fusion.32
  254.9 2.1 collective-permute-done.22
  257.8 6.0 %fusion.26 = f32[128,4096]{1,0:T(8,128)} fusion(f32[128,4096]{1,0:T(8,128)S(1)} %fusion.32, bf16[1,1,3,512,4096]{4,3,2,1,0:T(8,128)(2,1)} %param.10, bf16[2,512,128]{1,2,0:T(8,128)(2,1)S(1)} %copy.90), kind=kOutput, calls=%fused_computation.20 | convolution fusion | flops 1074266112 | bytes 12845056 | tf_op jit(solution)/shard_map/trn,trv->nv/dot_general | solution.py:432
  263.8 21.5 %shard_map.108 = f32[16,4096]{1,0:T(8,128)} custom-call(f32[8,16,4096]{2,1,0:T(8,128)} %bitcast.296, f32[8,16,4096]{2,1,0:T(8,128)} %bitcast.297), custom_call_target="tpu_custom_call" | custom-call | flops 1048576 | bytes 6291456 | tf_op jit(solution)/shard_map/pallas_call | solution.py:158
  287.1 1.9 collective-permute-start.26
  289.2 2.4 collective-permute-start.25
  291.6 3.1 %collective-permute-start.23 = (f32[16,512]{1,0:T(8,128)S(1)}, f32[16,512]{1,0:T(8,128)S(1)}, u32[]{:S(2)}, u32[]{:S(2)}) collective-permute-start(f32[16,512]{1,0:T(8,128)S(1)} %get-tuple-element.23), channel_id=1, source_target_pairs={{8,0},{16,8},{24,16},{32,24},{40,32},{48,40},{56,48},{64,56},{72,6... | collective-permute-start | bytes 98312 | tf_op jit(solution)/shard_map/ppermute | solution.py:22
  294.8 2.2 collective-permute-start.24
  297.0 1.4 fusion.106
  298.4 3.6 %collective-permute-done.24 = f32[16,512]{1,0:T(8,128)S(1)} collective-permute-done((f32[16,512]{1,0:T(8,128)S(1)}, f32[16,512]{1,0:T(8,128)S(1)}, u32[]{:S(2)}, u32[]{:S(2)}) %collective-permute-start.24) | collective-permute-done | bytes 32800 | tf_op jit(solution)/shard_map/ppermute | solution.py:22
  (137 shorter events, 25.4 us)
Async XLA Ops:
  0.6 18.9 %copy-start.1 = (f32[8,512,128]{2,1,0:T(8,128)S(1)}, f32[8,512,128]{2,1,0:T(8,128)}, u32[]{:S(2)}) copy-start(f32[8,512,128]{2,1,0:T(8,128)} %param.9) | copy-start | bytes 6291460
  0.6 19.0 %copy-start = (bf16[1,1,3,512,4096]{4,3,2,1,0:T(8,128)(2,1)S(1)}, bf16[1,1,3,512,4096]{4,3,2,1,0:T(8,128)(2,1)}, u32[]{:S(2)}) copy-start(bf16[1,1,3,512,4096]{4,3,2,1,0:T(8,128)(2,1)} %param.10) | copy-start | bytes 37748740
  2.7 19.3 %copy-start.11 = (pred[3,3]{0,1:T(4,128)(4,1)}, pred[3,3]{0,1:T(4,128)(4,1)S(1)}, u32[]{:S(2)}) copy-start(pred[3,3]{0,1:T(4,128)(4,1)S(1)} %fusion.136) | copy-start | bytes 31
  11.7 35.3 %collective-permute-start.2 = (f32[512]{0:T(512)}, f32[512]{0:T(512)}, u32[]{:S(2)}, u32[]{:S(2)}) collective-permute-start(f32[512]{0:T(512)} %bitcast.14), channel_id=1, source_target_pairs={{0,8},{8,16},{16,24},{24,32},{32,40},{40,48},{48,56},{56,64},{64,7... | collective-permute-start | bytes 6152 | tf_op jit(solution)/shard_map/ppermute | solution.py:22
  14.9 32.1 %collective-permute-start.3 = (f32[512]{0:T(512)}, f32[512]{0:T(512)}, u32[]{:S(2)}, u32[]{:S(2)}) collective-permute-start(f32[512]{0:T(512)} %bitcast.15), channel_id=1, source_target_pairs={{0,16},{8,24},{16,32},{24,40},{32,48},{40,56},{48,64},{56,72},{64,... | collective-permute-start | bytes 6152 | tf_op jit(solution)/shard_map/ppermute | solution.py:22
  19.7 11.0 %slice-start = ((bf16[8,512,128]{2,1,0:T(8,128)(2,1)}), bf16[1,512,128]{2,1,0:T(8,128)(2,1)S(1)}, s32[]{:S(2)}) async-start(bf16[8,512,128]{2,1,0:T(8,128)(2,1)} %param.15), calls=%async_computation | async-start | bytes 262144 | tf_op jit(solution)/shard_map/slice | solution.py:364
  23.2 24.5 %collective-permute-start = (bf16[512,128]{1,0:T(8,128)(2,1)}, bf16[512,128]{1,0:T(8,128)(2,1)S(1)}, u32[]{:S(2)}, u32[]{:S(2)}) collective-permute-start(bf16[512,128]{1,0:T(8,128)(2,1)} %get-tuple-element.45), channel_id=1, source_target_pairs={{0,8},{8,16},{16,24},{24,32},{32,40},{40,48},{48,56},{56,64},{64,7... | collective-permute-start | bytes 393224 | tf_op jit(solution)/shard_map/ppermute | solution.py:22
  25.8 22.0 %collective-permute-start.1 = (bf16[512,128]{1,0:T(8,128)(2,1)S(1)}, bf16[512,128]{1,0:T(8,128)(2,1)}, u32[]{:S(2)}, u32[]{:S(2)}) collective-permute-start(bf16[512,128]{1,0:T(8,128)(2,1)S(1)} %get-tuple-element.46), channel_id=1, source_target_pairs={{0,16},{8,24},{16,32},{24,40},{32,48},{40,56},{48,64},{56,72},{64,... | collective-permute-start | bytes 393224 | tf_op jit(solution)/shard_map/ppermute | solution.py:22
  31.4 17.4 %collective-permute-start.4 = (bf16[512,128]{0,1:T(8,128)(2,1)}, bf16[512,128]{0,1:T(8,128)(2,1)}, u32[]{:S(2)}, u32[]{:S(2)}) collective-permute-start(bf16[512,128]{0,1:T(8,128)(2,1)} %bitcast.16), channel_id=1, source_target_pairs={{0,8},{8,16},{16,24},{24,32},{32,40},{40,48},{48,56},{56,64},{64,7... | collective-permute-start | bytes 393224 | tf_op jit(solution)/shard_map/ppermute | solution.py:22
  34.9 10.4 %copy-start.2 = (bf16[8,512,128]{2,1,0:T(8,128)(2,1)S(1)}, bf16[8,512,128]{2,1,0:T(8,128)(2,1)}, u32[]{:S(2)}) copy-start(bf16[8,512,128]{2,1,0:T(8,128)(2,1)} %param.17) | copy-start | bytes 3145732
  39.1 8.0 %copy-start.7 = (f32[1,512]{1,0:T(1,128)S(1)}, f32[1,512]{1,0:T(1,128)}, u32[]{:S(2)}) copy-start(f32[1,512]{1,0:T(1,128)} %get-tuple-element.49) | copy-start | bytes 6148
  39.1 8.7 %copy-start.3 = (bf16[1,1,512,128]{3,2,1,0:T(8,128)(2,1)S(1)}, bf16[1,1,512,128]{3,2,1,0:T(8,128)(2,1)}, u32[]{:S(2)}) copy-start(bf16[1,1,512,128]{3,2,1,0:T(8,128)(2,1)} %param.14) | copy-start | bytes 393220
  39.1 8.7 %copy-start.6 = (bf16[512,128]{1,0:T(8,128)(2,1)S(1)}, bf16[512,128]{1,0:T(8,128)(2,1)}, u32[]{:S(2)}) copy-start(bf16[512,128]{1,0:T(8,128)(2,1)} %fusion.62) | copy-start | bytes 393220
  48.9 19.8 %collective-permute-start.5 = (bf16[512,128]{1,0:T(8,128)(2,1)S(1)}, bf16[512,128]{1,0:T(8,128)(2,1)S(1)}, u32[]{:S(2)}, u32[]{:S(2)}) collective-permute-start(bf16[512,128]{1,0:T(8,128)(2,1)S(1)} %fusion.78), channel_id=1, source_target_pairs={{8,0},{16,8},{24,16},{32,24},{40,32},{48,40},{56,48},{64,56},{72,6... | collective-permute-start | bytes 393224 | tf_op jit(solution)/shard_map/ppermute | solution.py:22
  53.4 15.3 %collective-permute-start.6 = (bf16[512,128]{1,0:T(8,128)(2,1)S(1)}, bf16[512,128]{1,0:T(8,128)(2,1)}, u32[]{:S(2)}, u32[]{:S(2)}) collective-permute-start(bf16[512,128]{1,0:T(8,128)(2,1)S(1)} %fusion.78), channel_id=1, source_target_pairs={{16,0},{24,8},{32,16},{40,24},{48,32},{56,40},{64,48},{72,56},{80,... | collective-permute-start | bytes 393224 | tf_op jit(solution)/shard_map/ppermute | solution.py:22
  75.6 42.5 %copy-start.8 = (pred[16]{0:T(512)(128)(4,1)S(1)}, pred[16]{0:T(512)(128)(4,1)}, u32[]{:S(2)}) copy-start(pred[16]{0:T(512)(128)(4,1)} %add_compare_fusion) | copy-start | bytes 52
  75.6 42.5 %copy-start.9 = (pred[8]{0:T(512)(128)(4,1)S(1)}, pred[8]{0:T(512)(128)(4,1)}, u32[]{:S(2)}) copy-start(pred[8]{0:T(512)(128)(4,1)} %add_compare_fusion.1) | copy-start | bytes 28
  75.6 42.5 %copy-start.10 = (pred[512]{0:T(512)(128)(4,1)S(1)}, pred[512]{0:T(512)(128)(4,1)}, u32[]{:S(2)}) copy-start(pred[512]{0:T(512)(128)(4,1)} %iota_compare_fusion) | copy-start | bytes 1540
  103.3 12.6 %collective-permute-start.10 = (f32[8,512]{1,0:T(8,128)S(1)}, f32[8,512]{1,0:T(8,128)S(1)}, u32[]{:S(2)}, u32[]{:S(2)}) collective-permute-start(f32[8,512]{1,0:T(8,128)S(1)} %get-tuple-element.43), channel_id=1, source_target_pairs={{0,1},{1,2},{2,3},{3,4},{4,5},{5,6},{6,7},{8,9},{9,10},{10,11},{11... | collective-permute-start | bytes 49160 | tf_op jit(solution)/shard_map/ppermute | solution.py:22
  105.6 10.2 %collective-permute-start.8 = (f32[16,512]{1,0:T(8,128)S(1)}, f32[16,512]{1,0:T(8,128)S(1)}, u32[]{:S(2)}, u32[]{:S(2)}) collective-permute-start(f32[16,512]{1,0:T(8,128)S(1)} %bitcast.323), channel_id=1, source_target_pairs={{0,8},{8,16},{16,24},{24,32},{32,40},{40,48},{48,56},{56,64},{64,7... | collective-permute-start | bytes 98312 | tf_op jit(solution)/shard_map/ppermute | solution.py:22
  108.2 8.5 %collective-permute-start.7 = (f32[16,512]{1,0:T(8,128)S(1)}, f32[16,512]{1,0:T(8,128)S(1)}, u32[]{:S(2)}, u32[]{:S(2)}) collective-permute-start(f32[16,512]{1,0:T(8,128)S(1)} %bitcast.322), channel_id=1, source_target_pairs={{8,0},{16,8},{24,16},{32,24},{40,32},{48,40},{56,48},{64,56},{72,6... | collective-permute-start | bytes 98312 | tf_op jit(solution)/shard_map/ppermute | solution.py:22
  113.1 5.1 %collective-permute-start.9 = (f32[8,512]{1,0:T(8,128)S(1)}, f32[8,512]{1,0:T(8,128)S(1)}, u32[]{:S(2)}, u32[]{:S(2)}) collective-permute-start(f32[8,512]{1,0:T(8,128)S(1)} %get-tuple-element.44), channel_id=1, source_target_pairs={{1,0},{2,1},{3,2},{4,3},{5,4},{6,5},{7,6},{9,8},{10,9},{11,10},{12... | collective-permute-start | bytes 49160 | tf_op jit(solution)/shard_map/ppermute | solution.py:22
  119.5 22.2 %copy-start.12 = (pred[3,3]{0,1:T(4,128)(4,1)S(1)}, pred[3,3]{0,1:T(4,128)(4,1)}, u32[]{:S(2)}) copy-start(pred[3,3]{0,1:T(4,128)(4,1)} %copy-done.11) | copy-start | bytes 31
  134.8 13.4 %copy-start.4 = (bf16[8,16,4096]{2,1,0:T(8,128)(2,1)S(1)}, bf16[8,16,4096]{2,1,0:T(8,128)(2,1)}, u32[]{:S(2)}) copy-start(bf16[8,16,4096]{2,1,0:T(8,128)(2,1)} %shard_map.105) | copy-start | bytes 3145732
  142.2 9.4 %collective-permute-start.11 = (bf16[512,128]{1,0:T(8,128)(2,1)S(1)}, bf16[512,128]{1,0:T(8,128)(2,1)S(1)}, u32[]{:S(2)}, u32[]{:S(2)}) collective-permute-start(bf16[512,128]{1,0:T(8,128)(2,1)S(1)} %get-tuple-element.36), channel_id=1, source_target_pairs={{0,8},{8,16},{16,24},{24,32},{32,40},{40,48},{48,56},{56,64},{64,7... | collective-permute-start | bytes 393224 | tf_op jit(solution)/shard_map/ppermute | solution.py:22
  144.2 9.3 %collective-permute-start.12 = (bf16[512,128]{1,0:T(8,128)(2,1)S(1)}, bf16[512,128]{1,0:T(8,128)(2,1)S(1)}, u32[]{:S(2)}, u32[]{:S(2)}) collective-permute-start(bf16[512,128]{1,0:T(8,128)(2,1)S(1)} %get-tuple-element.37), channel_id=1, source_target_pairs={{0,16},{8,24},{16,32},{24,40},{32,48},{40,56},{48,64},{56,72},{64,... | collective-permute-start | bytes 393224 | tf_op jit(solution)/shard_map/ppermute | solution.py:22
  153.6 9.3 %collective-permute-start.13 = (bf16[512,128]{1,0:T(8,128)(2,1)S(1)}, bf16[512,128]{1,0:T(8,128)(2,1)S(1)}, u32[]{:S(2)}, u32[]{:S(2)}) collective-permute-start(bf16[512,128]{1,0:T(8,128)(2,1)S(1)} %fusion.80), channel_id=1, source_target_pairs={{8,0},{16,8},{24,16},{32,24},{40,32},{48,40},{56,48},{64,56},{72,6... | collective-permute-start | bytes 393224 | tf_op jit(solution)/shard_map/ppermute | solution.py:22
  157.8 7.2 %collective-permute-start.14 = (bf16[512,128]{1,0:T(8,128)(2,1)S(1)}, bf16[512,128]{1,0:T(8,128)(2,1)S(1)}, u32[]{:S(2)}, u32[]{:S(2)}) collective-permute-start(bf16[512,128]{1,0:T(8,128)(2,1)S(1)} %fusion.80), channel_id=1, source_target_pairs={{16,0},{24,8},{32,16},{40,24},{48,32},{56,40},{64,48},{72,56},{80,... | collective-permute-start | bytes 393224 | tf_op jit(solution)/shard_map/ppermute | solution.py:22
  194.8 10.2 %collective-permute-start.18 = (f32[8,512]{1,0:T(8,128)S(1)}, f32[8,512]{1,0:T(8,128)S(1)}, u32[]{:S(2)}, u32[]{:S(2)}) collective-permute-start(f32[8,512]{1,0:T(8,128)S(1)} %get-tuple-element.29), channel_id=1, source_target_pairs={{0,1},{1,2},{2,3},{3,4},{4,5},{5,6},{6,7},{8,9},{9,10},{10,11},{11... | collective-permute-start | bytes 49160 | tf_op jit(solution)/shard_map/ppermute | solution.py:22
  197.7 7.3 %collective-permute-start.15 = (f32[16,512]{1,0:T(8,128)S(1)}, f32[16,512]{1,0:T(8,128)S(1)}, u32[]{:S(2)}, u32[]{:S(2)}) collective-permute-start(f32[16,512]{1,0:T(8,128)S(1)} %get-tuple-element.32), channel_id=1, source_target_pairs={{8,0},{16,8},{24,16},{32,24},{40,32},{48,40},{56,48},{64,56},{72,6... | collective-permute-start | bytes 98312 | tf_op jit(solution)/shard_map/ppermute | solution.py:22
  200.9 5.1 %collective-permute-start.17 = (f32[8,512]{1,0:T(8,128)S(1)}, f32[8,512]{1,0:T(8,128)S(1)}, u32[]{:S(2)}, u32[]{:S(2)}) collective-permute-start(f32[8,512]{1,0:T(8,128)S(1)} %get-tuple-element.30), channel_id=1, source_target_pairs={{1,0},{2,1},{3,2},{4,3},{5,4},{6,5},{7,6},{9,8},{10,9},{11,10},{12... | collective-permute-start | bytes 49160 | tf_op jit(solution)/shard_map/ppermute | solution.py:22
  202.8 7.0 %collective-permute-start.16 = (f32[16,512]{1,0:T(8,128)S(1)}, f32[16,512]{1,0:T(8,128)S(1)}, u32[]{:S(2)}, u32[]{:S(2)}) collective-permute-start(f32[16,512]{1,0:T(8,128)S(1)} %get-tuple-element.31), channel_id=1, source_target_pairs={{0,8},{8,16},{16,24},{24,32},{32,40},{40,48},{48,56},{56,64},{64,7... | collective-permute-start | bytes 98312 | tf_op jit(solution)/shard_map/ppermute | solution.py:22
  226.1 12.1 %copy-start.5 = (bf16[8,16,4096]{2,1,0:T(8,128)(2,1)S(1)}, bf16[8,16,4096]{2,1,0:T(8,128)(2,1)}, u32[]{:S(2)}) copy-start(bf16[8,16,4096]{2,1,0:T(8,128)(2,1)} %shard_map.107) | copy-start | bytes 3145732
  233.5 9.0 %collective-permute-start.19 = (bf16[512,128]{1,0:T(8,128)(2,1)S(1)}, bf16[512,128]{1,0:T(8,128)(2,1)S(1)}, u32[]{:S(2)}, u32[]{:S(2)}) collective-permute-start(bf16[512,128]{1,0:T(8,128)(2,1)S(1)} %get-tuple-element.27), channel_id=1, source_target_pairs={{0,8},{8,16},{16,24},{24,32},{32,40},{40,48},{48,56},{56,64},{64,7... | collective-permute-start | bytes 393224 | tf_op jit(solution)/shard_map/ppermute | solution.py:22
  235.4 9.3 %collective-permute-start.20 = (bf16[512,128]{1,0:T(8,128)(2,1)S(1)}, bf16[512,128]{1,0:T(8,128)(2,1)S(1)}, u32[]{:S(2)}, u32[]{:S(2)}) collective-permute-start(bf16[512,128]{1,0:T(8,128)(2,1)S(1)} %get-tuple-element.28), channel_id=1, source_target_pairs={{0,16},{8,24},{16,32},{24,40},{32,48},{40,56},{48,64},{56,72},{64,... | collective-permute-start | bytes 393224 | tf_op jit(solution)/shard_map/ppermute | solution.py:22
  245.6 9.3 %collective-permute-start.21 = (bf16[512,128]{1,0:T(8,128)(2,1)S(1)}, bf16[512,128]{1,0:T(8,128)(2,1)S(1)}, u32[]{:S(2)}, u32[]{:S(2)}) collective-permute-start(bf16[512,128]{1,0:T(8,128)(2,1)S(1)} %get-tuple-element.21), channel_id=1, source_target_pairs={{8,0},{16,8},{24,16},{32,24},{40,32},{48,40},{56,48},{64,56},{72,6... | collective-permute-start | bytes 393224 | tf_op jit(solution)/shard_map/ppermute | solution.py:22
  249.8 7.2 %collective-permute-start.22 = (bf16[512,128]{1,0:T(8,128)(2,1)S(1)}, bf16[512,128]{1,0:T(8,128)(2,1)S(1)}, u32[]{:S(2)}, u32[]{:S(2)}) collective-permute-start(bf16[512,128]{1,0:T(8,128)(2,1)S(1)} %get-tuple-element.21), channel_id=1, source_target_pairs={{16,0},{24,8},{32,16},{40,24},{48,32},{56,40},{64,48},{72,56},{80,... | collective-permute-start | bytes 393224 | tf_op jit(solution)/shard_map/ppermute | solution.py:22
  287.1 9.8 %collective-permute-start.26 = (f32[8,512]{1,0:T(8,128)S(1)}, f32[8,512]{1,0:T(8,128)S(1)}, u32[]{:S(2)}, u32[]{:S(2)}) collective-permute-start(f32[8,512]{1,0:T(8,128)S(1)} %bitcast.329), channel_id=1, source_target_pairs={{0,1},{1,2},{2,3},{3,4},{4,5},{5,6},{6,7},{8,9},{9,10},{10,11},{11... | collective-permute-start | bytes 49160 | tf_op jit(solution)/shard_map/ppermute | solution.py:22
  289.2 7.8 %collective-permute-start.25 = (f32[8,512]{1,0:T(8,128)S(1)}, f32[8,512]{1,0:T(8,128)S(1)}, u32[]{:S(2)}, u32[]{:S(2)}) collective-permute-start(f32[8,512]{1,0:T(8,128)S(1)} %slice_bitcast_fusion.10), channel_id=1, source_target_pairs={{1,0},{2,1},{3,2},{4,3},{5,4},{6,5},{7,6},{9,8},{10,9},{11,10},{12... | collective-permute-start | bytes 49160 | tf_op jit(solution)/shard_map/ppermute | solution.py:22
  291.6 5.3 %collective-permute-start.23 = (f32[16,512]{1,0:T(8,128)S(1)}, f32[16,512]{1,0:T(8,128)S(1)}, u32[]{:S(2)}, u32[]{:S(2)}) collective-permute-start(f32[16,512]{1,0:T(8,128)S(1)} %get-tuple-element.23), channel_id=1, source_target_pairs={{8,0},{16,8},{24,16},{32,24},{40,32},{48,40},{56,48},{64,56},{72,6... | collective-permute-start | bytes 98312 | tf_op jit(solution)/shard_map/ppermute | solution.py:22
  294.8 7.3 %collective-permute-start.24 = (f32[16,512]{1,0:T(8,128)S(1)}, f32[16,512]{1,0:T(8,128)S(1)}, u32[]{:S(2)}, u32[]{:S(2)}) collective-permute-start(f32[16,512]{1,0:T(8,128)S(1)} %get-tuple-element.22), channel_id=1, source_target_pairs={{0,8},{8,16},{16,24},{24,32},{32,40},{40,48},{48,56},{56,64},{64,7... | collective-permute-start | bytes 98312 | tf_op jit(solution)/shard_map/ppermute | solution.py:22

commit v10 on v9

--- a/solution.py
+++ b/solution.py
@@ -375,9 +375,6 @@
 
     measured = sino[0, 0].astype(jnp.float32)
     left_index = jnp.maximum(share_first - 1, 0)
-    left_rim = lax.dynamic_index_in_dim(weight_x, left_index, 2, keepdims=False).astype(
-        jnp.float32
-    ) * (angle_pos > 0).astype(jnp.float32)
     gathered = None
     residual = jnp.zeros((ray_count, column_count), jnp.float32)
     for iteration in range(ITERS):
@@ -420,6 +417,9 @@
             local_y = share_of(late[2])
             local_x = share_of(late[3])
             lower_rim = share_of(late[4])
+            left_rim = lax.dynamic_index_in_dim(late[3], left_index, 2, keepdims=False).astype(
+                jnp.float32
+            ) * (angle_pos > 0).astype(jnp.float32)
         nearby = [
             from_behind(residual_half, "slab", -distance) for distance in range(1, slot_count)
         ]

time: 306 us -> 305 us (level)
  transfers between devices with their start and end apart: 27 -> 27, of which waited for: 9 -> 9; matrix products, arithmetic and copies ran while one was open for 16% -> 15% of each run, Pallas kernels for 0% -> 0%
where the time goes in v10:
time: 305 us; the launch traced here: 303 us
  Pallas kernels  95 us (31%)
  starting transfers between devices  79.8 us (26%)
  matrix products  69.6 us (23%)
  local copies, waits for them, and re-layouts  20.9 us (7%)
  other arithmetic  18.2 us (6%)
  waiting for transfers between devices  17 us (6%)
    ppermute x27, starting transfers between devices, from_behind(): lax.ppermute(value, axis, [(source, source + steps) for source in range(f...  79.8 us
    pallas_call x3, Pallas kernels, scatter_angle(): pl.pallas_call(functools.partial(_scatter_kernel, n_chip, with_extra), ou...  66.2 us
    pallas_call x2, Pallas kernels, gather_angle(): pl.pallas_call(functools.partial(_gather_kernel, n_chip), out_shape=jax.S...  28.8 us
    ppermute x27, waiting for transfers between devices, from_behind(): lax.ppermute(value, axis, [(source, source + steps) for source in range(f...  17 us
    dot_general x3, matrix products, shards(): jnp.einsum('trn,trv->nv', picked, tiles[1:], preferred_element_type=jnp.f...  16.9 us
    dot_general x2, matrix products, shards(): jnp.einsum('trv,nv->trn', tiles[1:], gathered, preferred_element_type=jnp...  13.4 us
    optimization_barrier x4, local copies, waits for them, and re-layouts, shards(): lax.optimization_barrier((residual_half, (volume0, weight_z, weight_y, we...  10.8 us
    dot_general x3, matrix products, shards(): jnp.einsum('rn,rv->nv', residual_half, tiles[0], preferred_element_type=j...  8.8 us
  transfers between devices with their start and end apart: 27, of which 9 were waited for; matrix products, arithmetic and copies ran while one was open for 15% of the time, Pallas kernels for 0%

profile of v10, /device:TPU:33, one launch (start us, length us, event | category | flops | bytes accessed | tf_op | source)
XLA Modules:
  0.0 303.0 jit_solution(7672820520940682766)
XLA Ops:
  1.5 1.3 select_reduce_fusion
  2.7 8.3 %fusion.3 = bf16[1,3,512]{2,0,1:T(2,128)(2,1)S(1)} fusion(bf16[1,1,3,512,4096]{4,3,2,1,0:T(8,128)(2,1)} %param.10), kind=kOutput, calls=%fused_computation.3 | convolution fusion | flops 12582912 | bytes 12585984 | tf_op jit(solution)/shard_map/dot_general | solution.py:354
  11.1 3.2 %collective-permute-start.2 = (f32[512]{0:T(512)S(1)}, f32[512]{0:T(512)S(1)}, u32[]{:S(2)}, u32[]{:S(2)}) collective-permute-start(f32[512]{0:T(512)S(1)} %bitcast.333), channel_id=1, source_target_pairs={{0,8},{8,16},{16,24},{24,32},{32,40},{40,48},{48,56},{56,64},{64,7... | collective-permute-start | bytes 6152 | tf_op jit(solution)/shard_map/ppermute | solution.py:22
  14.4 4.5 %collective-permute-start.3 = (f32[512]{0:T(512)S(1)}, f32[512]{0:T(512)S(1)}, u32[]{:S(2)}, u32[]{:S(2)}) collective-permute-start(f32[512]{0:T(512)S(1)} %bitcast.332), channel_id=1, source_target_pairs={{0,16},{8,24},{16,32},{24,40},{32,48},{40,56},{48,64},{56,72},{64,... | collective-permute-start | bytes 6152 | tf_op jit(solution)/shard_map/ppermute | solution.py:22
  19.1 2.3 fusion.15
  22.0 2.6 collective-permute-start
  24.6 4.8 %collective-permute-start.1 = (bf16[512,128]{1,0:T(8,128)(2,1)S(1)}, bf16[512,128]{1,0:T(8,128)(2,1)S(1)}, u32[]{:S(2)}, u32[]{:S(2)}) collective-permute-start(bf16[512,128]{1,0:T(8,128)(2,1)S(1)} %get-tuple-element.46), channel_id=1, source_target_pairs={{0,16},{8,24},{16,32},{24,40},{32,48},{40,56},{48,64},{56,72},{64,... | collective-permute-start | bytes 393224 | tf_op jit(solution)/shard_map/ppermute | solution.py:22
  29.6 2.9 collective-permute-start.4
  33.7 3.5 %fusion.62 = bf16[512,128]{1,0:T(8,128)(2,1)S(1)} fusion(bf16[4096,128]{1,0:T(8,128)(2,1)S(1)} %bitcast.305, bf16[1,1,3,512,4096]{4,3,2,1,0:T(8,128)(2,1)} %param.10), kind=kOutput, calls=%fused_computation.48 | convolution fusion | flops 536936448 | bytes 5373952 | tf_op jit(solution)/shard_map/rv,vn->rn/dot_general | solution.py:398
  37.8 5.5 %fusion = f32[1,8,512]{2,0,1:T(1,128)S(1)} fusion(pred[1536,1,1]{0,1,2:T(4,128)(4,1)S(1)} %reshape.82, bf16[192,8,8,512]{3,2,1,0:T(8,128)(2,1)} %bitcast.291), kind=kOutput, calls=%fused_computation | convolution fusion | flops 12582912 | bytes 12600832 | tf_op jit(solution)/shard_map/dot_general | solution.py:362
  44.7 4.5 %collective-permute-start.5 = (bf16[512,128]{1,0:T(8,128)(2,1)S(1)}, bf16[512,128]{1,0:T(8,128)(2,1)S(1)}, u32[]{:S(2)}, u32[]{:S(2)}) collective-permute-start(bf16[512,128]{1,0:T(8,128)(2,1)S(1)} %fusion.78), channel_id=1, source_target_pairs={{8,0},{16,8},{24,16},{32,24},{40,32},{48,40},{56,48},{64,56},{72,6... | collective-permute-start | bytes 393224 | tf_op jit(solution)/shard_map/ppermute | solution.py:22
  49.2 2.1 collective-permute-start.6
  51.3 2.9 fusion.40
  54.2 3.1 %copy.46 = f32[8,512,128]{1,0,2:T(8,128)} copy(f32[8,512,128]{2,1,0:T(8,128)} %param.9) | data formatting | bytes 4194304 | tf_op jit(solution)/shard_map/optimization_barrier | solution.py:412
  57.4 1.9 copy.52
  59.3 3.1 %copy.47 = bf16[8,512,128]{1,0,2:T(8,128)(2,1)} copy(bf16[8,512,128]{2,1,0:T(8,128)(2,1)} %param.15) | data formatting | bytes 2097152 | tf_op jit(solution)/shard_map/optimization_barrier | solution.py:412
  62.4 2.7 copy.51
  67.4 4.7 %fusion.17 = f32[128,4096]{1,0:T(8,128)S(1)} fusion(bf16[1,1,3,512,4096]{4,3,2,1,0:T(8,128)(2,1)} %param.10, bf16[2,512,128]{1,2,0:T(8,128)(2,1)} %copy.80), kind=kOutput, calls=%fused_computation.17 | convolution fusion | flops 1073741824 | bytes 10747904 | tf_op jit(solution)/shard_map/trn,trv->nv/dot_general | solution.py:432
  72.2 1.6 add.175
  73.9 23.1 %shard_map.104 = (f32[16,4096]{1,0:T(8,128)}, f32[8,512]{1,0:T(8,128)}) custom-call(f32[8,16,4096]{2,1,0:T(8,128)} %bitcast.292, f32[8,16,4096]{2,1,0:T(8,128)} %bitcast.293, f32[8,512]{1,0:T(8,128)} %bitcast.322), custom_call_target="tpu_custom_call" | custom-call | flops 1048576 | bytes 6291456 | tf_op jit(solution)/shard_map/pallas_call | solution.py:158
  99.8 2.1 collective-permute-start.10
  102.2 2.5 collective-permute-start.8
  104.7 4.9 %collective-permute-start.7 = (f32[16,512]{1,0:T(8,128)S(1)}, f32[16,512]{1,0:T(8,128)S(1)}, u32[]{:S(2)}, u32[]{:S(2)}) collective-permute-start(f32[16,512]{1,0:T(8,128)S(1)} %bitcast.323), channel_id=1, source_target_pairs={{8,0},{16,8},{24,16},{32,24},{40,32},{48,40},{56,48},{64,56},{72,6... | collective-permute-start | bytes 98312 | tf_op jit(solution)/shard_map/ppermute | solution.py:22
  109.6 2.8 collective-permute-start.9
  113.2 1.4 collective-permute-done.9
  114.7 1.2 fusion.104
  116.8 14.4 %shard_map.105 = bf16[8,16,4096]{2,1,0:T(8,128)(2,1)} custom-call(bf16[16,4096]{1,0:T(8,128)(2,1)} %bitcast.313), custom_call_target="tpu_custom_call" | custom-call | bytes 2097152 | tf_op jit(solution)/shard_map/pallas_call | solution.py:275
  131.3 6.7 %fusion.56 = bf16[128,2,512]{2,0,1:T(8,128)(2,1)S(1)} fusion(bf16[128,4096,1]{1,0,2:T(8,128)(2,1)} %bitcast.308, bf16[1,1,3,512,4096]{4,3,2,1,0:T(8,128)(2,1)} %param.10), kind=kOutput, calls=%fused_computation.46 | convolution fusion | flops 1073872896 | bytes 9699328 | tf_op jit(solution)/shard_map/trv,nv->trn/dot_general | solution.py:387
  138.8 1.9 collective-permute-start.11
  140.7 4.0 %collective-permute-start.12 = (bf16[512,128]{1,0:T(8,128)(2,1)S(1)}, bf16[512,128]{1,0:T(8,128)(2,1)S(1)}, u32[]{:S(2)}, u32[]{:S(2)}) collective-permute-start(bf16[512,128]{1,0:T(8,128)(2,1)S(1)} %get-tuple-element.37), channel_id=1, source_target_pairs={{0,16},{8,24},{16,32},{24,40},{32,48},{40,56},{48,64},{56,72},{64,... | collective-permute-start | bytes 393224 | tf_op jit(solution)/shard_map/ppermute | solution.py:22
  144.7 3.4 %fusion.74 = bf16[512,128]{1,0:T(8,128)(2,1)S(1)} fusion(bf16[128,4096]{1,0:T(8,128)(2,1)S(1)} %bitcast.309, bf16[1,1,3,512,4096]{4,3,2,1,0:T(8,128)(2,1)} %param.10), kind=kOutput, calls=%fused_computation.52 | convolution fusion | flops 536936448 | bytes 5373952 | tf_op jit(solution)/shard_map/rv,nv->rn/dot_general | solution.py:402
  148.2 1.8 collective-permute-done.12
  150.1 4.2 %collective-permute-start.13 = (bf16[512,128]{1,0:T(8,128)(2,1)S(1)}, bf16[512,128]{1,0:T(8,128)(2,1)S(1)}, u32[]{:S(2)}, u32[]{:S(2)}) collective-permute-start(bf16[512,128]{1,0:T(8,128)(2,1)S(1)} %fusion.80), channel_id=1, source_target_pairs={{8,0},{16,8},{24,16},{32,24},{40,32},{48,40},{56,48},{64,56},{72,6... | collective-permute-start | bytes 393224 | tf_op jit(solution)/shard_map/ppermute | solution.py:22
  154.3 2.1 collective-permute-start.14
  156.5 2.9 fusion.36
  159.4 2.1 collective-permute-done.14
  161.6 1.3 fusion.120
  162.9 1.8 copy.86
  164.7 6.1 %fusion.29 = f32[128,4096]{1,0:T(8,128)} fusion(f32[128,4096]{1,0:T(8,128)S(1)} %fusion.36, bf16[1,1,3,512,4096]{4,3,2,1,0:T(8,128)(2,1)} %param.10, bf16[2,512,128]{1,2,0:T(8,128)(2,1)} %copy.86), kind=kOutput, calls=%fused_computation.21 | convolution fusion | flops 1074266112 | bytes 12845056 | tf_op jit(solution)/shard_map/trn,trv->nv/dot_general | solution.py:432
  170.8 21.6 %shard_map.106 = f32[16,4096]{1,0:T(8,128)} custom-call(f32[8,16,4096]{2,1,0:T(8,128)} %bitcast.294, f32[8,16,4096]{2,1,0:T(8,128)} %bitcast.295), custom_call_target="tpu_custom_call" | custom-call | flops 1048576 | bytes 6291456 | tf_op jit(solution)/shard_map/pallas_call | solution.py:158
  193.8 2.7 collective-permute-start.18
  196.7 3.1 %collective-permute-start.15 = (f32[16,512]{1,0:T(8,128)S(1)}, f32[16,512]{1,0:T(8,128)S(1)}, u32[]{:S(2)}, u32[]{:S(2)}) collective-permute-start(f32[16,512]{1,0:T(8,128)S(1)} %get-tuple-element.32), channel_id=1, source_target_pairs={{8,0},{16,8},{24,16},{32,24},{40,32},{48,40},{56,48},{64,56},{72,6... | collective-permute-start | bytes 98312 | tf_op jit(solution)/shard_map/ppermute | solution.py:22
  199.9 1.9 collective-permute-start.17
  201.8 2.2 collective-permute-start.16
  204.9 1.2 fusion.105
  206.2 2.6 collective-permute-done.16
  210.7 14.3 %shard_map.107 = bf16[8,16,4096]{2,1,0:T(8,128)(2,1)} custom-call(bf16[16,4096]{1,0:T(8,128)(2,1)} %bitcast.314), custom_call_target="tpu_custom_call" | custom-call | bytes 2097152 | tf_op jit(solution)/shard_map/pallas_call | solution.py:275
  225.1 6.7 %fusion.59 = bf16[128,2,512]{2,0,1:T(8,128)(2,1)S(1)} fusion(bf16[128,4096,1]{1,0,2:T(8,128)(2,1)} %bitcast.310, bf16[1,1,3,512,4096]{4,3,2,1,0:T(8,128)(2,1)} %param.10), kind=kOutput, calls=%fused_computation.47 | convolution fusion | flops 1073872896 | bytes 9699328 | tf_op jit(solution)/shard_map/trv,nv->trn/dot_general | solution.py:387
  232.6 1.9 collective-permute-start.19
  234.5 2.7 collective-permute-start.20
  237.2 3.4 %fusion.71 = bf16[512,128]{1,0:T(8,128)(2,1)S(1)} fusion(bf16[128,4096]{1,0:T(8,128)(2,1)S(1)} %bitcast.311, bf16[1,1,3,512,4096]{4,3,2,1,0:T(8,128)(2,1)} %param.10), kind=kOutput, calls=%fused_computation.51 | convolution fusion | flops 536936448 | bytes 5373952 | tf_op jit(solution)/shard_map/rv,nv->rn/dot_general | solution.py:402
  241.5 2.3 collective-permute-done.20
  244.6 4.2 %collective-permute-start.21 = (bf16[512,128]{1,0:T(8,128)(2,1)S(1)}, bf16[512,128]{1,0:T(8,128)(2,1)S(1)}, u32[]{:S(2)}, u32[]{:S(2)}) collective-permute-start(bf16[512,128]{1,0:T(8,128)(2,1)S(1)} %get-tuple-element.21), channel_id=1, source_target_pairs={{8,0},{16,8},{24,16},{32,24},{40,32},{48,40},{56,48},{64,56},{72,6... | collective-permute-start | bytes 393224 | tf_op jit(solution)/shard_map/ppermute | solution.py:22
  248.8 2.2 collective-permute-start.22
  251.0 2.9 fusion.32
  254.0 2.1 collective-permute-done.22
  256.9 6.0 %fusion.26 = f32[128,4096]{1,0:T(8,128)} fusion(f32[128,4096]{1,0:T(8,128)S(1)} %fusion.32, bf16[1,1,3,512,4096]{4,3,2,1,0:T(8,128)(2,1)} %param.10, bf16[2,512,128]{1,2,0:T(8,128)(2,1)S(1)} %copy.90), kind=kOutput, calls=%fused_computation.20 | convolution fusion | flops 1074266112 | bytes 12845056 | tf_op jit(solution)/shard_map/trn,trv->nv/dot_general | solution.py:432
  262.9 21.5 %shard_map.108 = f32[16,4096]{1,0:T(8,128)} custom-call(f32[8,16,4096]{2,1,0:T(8,128)} %bitcast.296, f32[8,16,4096]{2,1,0:T(8,128)} %bitcast.297), custom_call_target="tpu_custom_call" | custom-call | flops 1048576 | bytes 6291456 | tf_op jit(solution)/shard_map/pallas_call | solution.py:158
  286.2 1.9 collective-permute-start.26
  288.3 2.4 collective-permute-start.25
  290.7 3.1 %collective-permute-start.23 = (f32[16,512]{1,0:T(8,128)S(1)}, f32[16,512]{1,0:T(8,128)S(1)}, u32[]{:S(2)}, u32[]{:S(2)}) collective-permute-start(f32[16,512]{1,0:T(8,128)S(1)} %get-tuple-element.23), channel_id=1, source_target_pairs={{8,0},{16,8},{24,16},{32,24},{40,32},{48,40},{56,48},{64,56},{72,6... | collective-permute-start | bytes 98312 | tf_op jit(solution)/shard_map/ppermute | solution.py:22
  293.9 2.2 collective-permute-start.24
  296.9 1.4 fusion.106
  298.3 2.9 collective-permute-done.24
  (149 shorter events, 24.3 us)
Async XLA Ops:
  0.6 18.3 %copy-start.1 = (f32[8,512,128]{2,1,0:T(8,128)S(1)}, f32[8,512,128]{2,1,0:T(8,128)}, u32[]{:S(2)}) copy-start(f32[8,512,128]{2,1,0:T(8,128)} %param.9) | copy-start | bytes 6291460
  0.6 18.4 %copy-start = (bf16[1,1,3,512,4096]{4,3,2,1,0:T(8,128)(2,1)S(1)}, bf16[1,1,3,512,4096]{4,3,2,1,0:T(8,128)(2,1)}, u32[]{:S(2)}) copy-start(bf16[1,1,3,512,4096]{4,3,2,1,0:T(8,128)(2,1)} %param.10) | copy-start | bytes 37748740
  2.7 63.2 %copy-start.16 = (pred[3,3]{0,1:T(4,128)(4,1)}, pred[3,3]{0,1:T(4,128)(4,1)S(1)}, u32[]{:S(2)}) copy-start(pred[3,3]{0,1:T(4,128)(4,1)S(1)} %fusion.136) | copy-start | bytes 31
  11.1 33.3 %collective-permute-start.2 = (f32[512]{0:T(512)S(1)}, f32[512]{0:T(512)S(1)}, u32[]{:S(2)}, u32[]{:S(2)}) collective-permute-start(f32[512]{0:T(512)S(1)} %bitcast.333), channel_id=1, source_target_pairs={{0,8},{8,16},{16,24},{24,32},{32,40},{40,48},{48,56},{56,64},{64,7... | collective-permute-start | bytes 6152 | tf_op jit(solution)/shard_map/ppermute | solution.py:22
  14.4 30.1 %collective-permute-start.3 = (f32[512]{0:T(512)S(1)}, f32[512]{0:T(512)S(1)}, u32[]{:S(2)}, u32[]{:S(2)}) collective-permute-start(f32[512]{0:T(512)S(1)} %bitcast.332), channel_id=1, source_target_pairs={{0,16},{8,24},{16,32},{24,40},{32,48},{40,56},{48,64},{56,72},{64,... | collective-permute-start | bytes 6152 | tf_op jit(solution)/shard_map/ppermute | solution.py:22
  19.1 10.4 %slice-start = ((bf16[8,512,128]{2,1,0:T(8,128)(2,1)}), bf16[1,512,128]{2,1,0:T(8,128)(2,1)S(1)}, s32[]{:S(2)}) async-start(bf16[8,512,128]{2,1,0:T(8,128)(2,1)} %param.15), calls=%async_computation | async-start | bytes 262144 | tf_op jit(solution)/shard_map/slice | solution.py:364
  22.0 22.5 %collective-permute-start = (bf16[512,128]{1,0:T(8,128)(2,1)S(1)}, bf16[512,128]{1,0:T(8,128)(2,1)S(1)}, u32[]{:S(2)}, u32[]{:S(2)}) collective-permute-start(bf16[512,128]{1,0:T(8,128)(2,1)S(1)} %get-tuple-element.45), channel_id=1, source_target_pairs={{0,8},{8,16},{16,24},{24,32},{32,40},{40,48},{48,56},{56,64},{64,7... | collective-permute-start | bytes 393224 | tf_op jit(solution)/shard_map/ppermute | solution.py:22
  24.6 19.9 %collective-permute-start.1 = (bf16[512,128]{1,0:T(8,128)(2,1)S(1)}, bf16[512,128]{1,0:T(8,128)(2,1)S(1)}, u32[]{:S(2)}, u32[]{:S(2)}) collective-permute-start(bf16[512,128]{1,0:T(8,128)(2,1)S(1)} %get-tuple-element.46), channel_id=1, source_target_pairs={{0,16},{8,24},{16,32},{24,40},{32,48},{40,56},{48,64},{56,72},{64,... | collective-permute-start | bytes 393224 | tf_op jit(solution)/shard_map/ppermute | solution.py:22
  29.6 15.1 %collective-permute-start.4 = (bf16[512,128]{0,1:T(8,128)(2,1)S(1)}, bf16[512,128]{0,1:T(8,128)(2,1)S(1)}, u32[]{:S(2)}, u32[]{:S(2)}) collective-permute-start(bf16[512,128]{0,1:T(8,128)(2,1)S(1)} %bitcast.316), channel_id=1, source_target_pairs={{0,8},{8,16},{16,24},{24,32},{32,40},{40,48},{48,56},{56,64},{64,7... | collective-permute-start | bytes 393224 | tf_op jit(solution)/shard_map/ppermute | solution.py:22
  33.7 10.9 %copy-start.3 = (bf16[1,1,512,128]{3,2,1,0:T(8,128)(2,1)S(1)}, bf16[1,1,512,128]{3,2,1,0:T(8,128)(2,1)}, u32[]{:S(2)}) copy-start(bf16[1,1,512,128]{3,2,1,0:T(8,128)(2,1)} %param.14) | copy-start | bytes 393220
  44.5 9.7 %copy-start.6 = (f32[512]{0:T(512)}, f32[512]{0:T(512)S(1)}, u32[]{:S(2)}) copy-start(f32[512]{0:T(512)S(1)} %add_divide_fusion) | copy-start | bytes 6148
  44.7 9.6 %copy-start.9 = (bf16[512,128]{0,1:T(8,128)(2,1)}, bf16[512,128]{0,1:T(8,128)(2,1)S(1)}, u32[]{:S(2)}) copy-start(bf16[512,128]{0,1:T(8,128)(2,1)S(1)} %collective-permute-done.4) | copy-start | bytes 393220
  44.7 20.3 %collective-permute-start.5 = (bf16[512,128]{1,0:T(8,128)(2,1)S(1)}, bf16[512,128]{1,0:T(8,128)(2,1)S(1)}, u32[]{:S(2)}, u32[]{:S(2)}) collective-permute-start(bf16[512,128]{1,0:T(8,128)(2,1)S(1)} %fusion.78), channel_id=1, source_target_pairs={{8,0},{16,8},{24,16},{32,24},{40,32},{48,40},{56,48},{64,56},{72,6... | collective-permute-start | bytes 393224 | tf_op jit(solution)/shard_map/ppermute | solution.py:22
  49.2 15.9 %collective-permute-start.6 = (bf16[512,128]{1,0:T(8,128)(2,1)S(1)}, bf16[512,128]{1,0:T(8,128)(2,1)}, u32[]{:S(2)}, u32[]{:S(2)}) collective-permute-start(bf16[512,128]{1,0:T(8,128)(2,1)S(1)} %fusion.78), channel_id=1, source_target_pairs={{16,0},{24,8},{32,16},{40,24},{48,32},{56,40},{64,48},{72,56},{80,... | collective-permute-start | bytes 393224 | tf_op jit(solution)/shard_map/ppermute | solution.py:22
  59.3 145.7 %copy-start.2 = (bf16[8,512,128]{1,0,2:T(8,128)(2,1)}, bf16[8,512,128]{1,0,2:T(8,128)(2,1)S(1)}, u32[]{:S(2)}) copy-start(bf16[8,512,128]{1,0,2:T(8,128)(2,1)S(1)} %copy.52) | copy-start | bytes 3145732
  72.2 42.5 %copy-start.11 = (pred[16]{0:T(512)(128)(4,1)S(1)}, pred[16]{0:T(512)(128)(4,1)}, u32[]{:S(2)}) copy-start(pred[16]{0:T(512)(128)(4,1)} %add_compare_fusion) | copy-start | bytes 52
  72.2 42.5 %copy-start.13 = (pred[8]{0:T(512)(128)(4,1)S(1)}, pred[8]{0:T(512)(128)(4,1)}, u32[]{:S(2)}) copy-start(pred[8]{0:T(512)(128)(4,1)} %add_compare_fusion.1) | copy-start | bytes 28
  72.2 42.4 %copy-start.15 = (pred[512]{0:T(512)(128)(4,1)S(1)}, pred[512]{0:T(512)(128)(4,1)}, u32[]{:S(2)}) copy-start(pred[512]{0:T(512)(128)(4,1)} %iota_compare_fusion) | copy-start | bytes 1540
  99.8 12.6 %collective-permute-start.10 = (f32[8,512]{1,0:T(8,128)S(1)}, f32[8,512]{1,0:T(8,128)S(1)}, u32[]{:S(2)}, u32[]{:S(2)}) collective-permute-start(f32[8,512]{1,0:T(8,128)S(1)} %get-tuple-element.43), channel_id=1, source_target_pairs={{0,1},{1,2},{2,3},{3,4},{4,5},{5,6},{6,7},{8,9},{9,10},{10,11},{11... | collective-permute-start | bytes 49160 | tf_op jit(solution)/shard_map/ppermute | solution.py:22
  102.2 10.2 %collective-permute-start.8 = (f32[16,512]{1,0:T(8,128)S(1)}, f32[16,512]{1,0:T(8,128)S(1)}, u32[]{:S(2)}, u32[]{:S(2)}) collective-permute-start(f32[16,512]{1,0:T(8,128)S(1)} %bitcast.324), channel_id=1, source_target_pairs={{0,8},{8,16},{16,24},{24,32},{32,40},{40,48},{48,56},{56,64},{64,7... | collective-permute-start | bytes 98312 | tf_op jit(solution)/shard_map/ppermute | solution.py:22
  104.7 8.5 %collective-permute-start.7 = (f32[16,512]{1,0:T(8,128)S(1)}, f32[16,512]{1,0:T(8,128)S(1)}, u32[]{:S(2)}, u32[]{:S(2)}) collective-permute-start(f32[16,512]{1,0:T(8,128)S(1)} %bitcast.323), channel_id=1, source_target_pairs={{8,0},{16,8},{24,16},{32,24},{40,32},{48,40},{56,48},{64,56},{72,6... | collective-permute-start | bytes 98312 | tf_op jit(solution)/shard_map/ppermute | solution.py:22
  109.6 5.1 %collective-permute-start.9 = (f32[8,512]{1,0:T(8,128)S(1)}, f32[8,512]{1,0:T(8,128)S(1)}, u32[]{:S(2)}, u32[]{:S(2)}) collective-permute-start(f32[8,512]{1,0:T(8,128)S(1)} %get-tuple-element.44), channel_id=1, source_target_pairs={{1,0},{2,1},{3,2},{4,3},{5,4},{6,5},{7,6},{9,8},{10,9},{11,10},{12... | collective-permute-start | bytes 49160 | tf_op jit(solution)/shard_map/ppermute | solution.py:22
  115.9 22.2 %copy-start.17 = (pred[3,3]{0,1:T(4,128)(4,1)S(1)}, pred[3,3]{0,1:T(4,128)(4,1)}, u32[]{:S(2)}) copy-start(pred[3,3]{0,1:T(4,128)(4,1)} %copy-done.16) | copy-start | bytes 31
  131.3 13.5 %copy-start.4 = (bf16[8,16,4096]{2,1,0:T(8,128)(2,1)S(1)}, bf16[8,16,4096]{2,1,0:T(8,128)(2,1)}, u32[]{:S(2)}) copy-start(bf16[8,16,4096]{2,1,0:T(8,128)(2,1)} %shard_map.105) | copy-start | bytes 3145732
  131.3 18.7 %copy-start.7 = (f32[512]{0:T(512)S(1)}, f32[512]{0:T(512)}, u32[]{:S(2)}) copy-start(f32[512]{0:T(512)} %copy-done.6) | copy-start | bytes 6148
  138.2 23.4 %copy-start.18 = (pred[3,3]{0,1:T(4,128)(4,1)S(1)}, pred[3,3]{0,1:T(4,128)(4,1)}, u32[]{:S(2)}) copy-start(pred[3,3]{0,1:T(4,128)(4,1)} %copy-done.16) | copy-start | bytes 31
  138.8 9.4 %collective-permute-start.11 = (bf16[512,128]{1,0:T(8,128)(2,1)S(1)}, bf16[512,128]{1,0:T(8,128)(2,1)S(1)}, u32[]{:S(2)}, u32[]{:S(2)}) collective-permute-start(bf16[512,128]{1,0:T(8,128)(2,1)S(1)} %get-tuple-element.36), channel_id=1, source_target_pairs={{0,8},{8,16},{16,24},{24,32},{32,40},{40,48},{48,56},{56,64},{64,7... | collective-permute-start | bytes 393224 | tf_op jit(solution)/shard_map/ppermute | solution.py:22
  140.7 9.3 %collective-permute-start.12 = (bf16[512,128]{1,0:T(8,128)(2,1)S(1)}, bf16[512,128]{1,0:T(8,128)(2,1)S(1)}, u32[]{:S(2)}, u32[]{:S(2)}) collective-permute-start(bf16[512,128]{1,0:T(8,128)(2,1)S(1)} %get-tuple-element.37), channel_id=1, source_target_pairs={{0,16},{8,24},{16,32},{24,40},{32,48},{40,56},{48,64},{56,72},{64,... | collective-permute-start | bytes 393224 | tf_op jit(solution)/shard_map/ppermute | solution.py:22
  150.1 9.3 %collective-permute-start.13 = (bf16[512,128]{1,0:T(8,128)(2,1)S(1)}, bf16[512,128]{1,0:T(8,128)(2,1)S(1)}, u32[]{:S(2)}, u32[]{:S(2)}) collective-permute-start(bf16[512,128]{1,0:T(8,128)(2,1)S(1)} %fusion.80), channel_id=1, source_target_pairs={{8,0},{16,8},{24,16},{32,24},{40,32},{48,40},{56,48},{64,56},{72,6... | collective-permute-start | bytes 393224 | tf_op jit(solution)/shard_map/ppermute | solution.py:22
  154.3 7.2 %collective-permute-start.14 = (bf16[512,128]{1,0:T(8,128)(2,1)S(1)}, bf16[512,128]{1,0:T(8,128)(2,1)S(1)}, u32[]{:S(2)}, u32[]{:S(2)}) collective-permute-start(bf16[512,128]{1,0:T(8,128)(2,1)S(1)} %fusion.80), channel_id=1, source_target_pairs={{16,0},{24,8},{32,16},{40,24},{48,32},{56,40},{64,48},{72,56},{80,... | collective-permute-start | bytes 393224 | tf_op jit(solution)/shard_map/ppermute | solution.py:22
  193.8 10.2 %collective-permute-start.18 = (f32[8,512]{1,0:T(8,128)S(1)}, f32[8,512]{1,0:T(8,128)S(1)}, u32[]{:S(2)}, u32[]{:S(2)}) collective-permute-start(f32[8,512]{1,0:T(8,128)S(1)} %get-tuple-element.29), channel_id=1, source_target_pairs={{0,1},{1,2},{2,3},{3,4},{4,5},{5,6},{6,7},{8,9},{9,10},{10,11},{11... | collective-permute-start | bytes 49160 | tf_op jit(solution)/shard_map/ppermute | solution.py:22
  196.7 7.3 %collective-permute-start.15 = (f32[16,512]{1,0:T(8,128)S(1)}, f32[16,512]{1,0:T(8,128)S(1)}, u32[]{:S(2)}, u32[]{:S(2)}) collective-permute-start(f32[16,512]{1,0:T(8,128)S(1)} %get-tuple-element.32), channel_id=1, source_target_pairs={{8,0},{16,8},{24,16},{32,24},{40,32},{48,40},{56,48},{64,56},{72,6... | collective-permute-start | bytes 98312 | tf_op jit(solution)/shard_map/ppermute | solution.py:22
  199.9 5.1 %collective-permute-start.17 = (f32[8,512]{1,0:T(8,128)S(1)}, f32[8,512]{1,0:T(8,128)S(1)}, u32[]{:S(2)}, u32[]{:S(2)}) collective-permute-start(f32[8,512]{1,0:T(8,128)S(1)} %get-tuple-element.30), channel_id=1, source_target_pairs={{1,0},{2,1},{3,2},{4,3},{5,4},{6,5},{7,6},{9,8},{10,9},{11,10},{12... | collective-permute-start | bytes 49160 | tf_op jit(solution)/shard_map/ppermute | solution.py:22
  201.8 7.0 %collective-permute-start.16 = (f32[16,512]{1,0:T(8,128)S(1)}, f32[16,512]{1,0:T(8,128)S(1)}, u32[]{:S(2)}, u32[]{:S(2)}) collective-permute-start(f32[16,512]{1,0:T(8,128)S(1)} %get-tuple-element.31), channel_id=1, source_target_pairs={{0,8},{8,16},{16,24},{24,32},{32,40},{40,48},{48,56},{56,64},{64,7... | collective-permute-start | bytes 98312 | tf_op jit(solution)/shard_map/ppermute | solution.py:22
  209.6 22.4 %copy-start.19 = (pred[3,3]{0,1:T(4,128)(4,1)S(1)}, pred[3,3]{0,1:T(4,128)(4,1)}, u32[]{:S(2)}) copy-start(pred[3,3]{0,1:T(4,128)(4,1)} %copy-done.16) | copy-start | bytes 31
  225.1 12.1 %copy-start.5 = (bf16[8,16,4096]{2,1,0:T(8,128)(2,1)S(1)}, bf16[8,16,4096]{2,1,0:T(8,128)(2,1)}, u32[]{:S(2)}) copy-start(bf16[8,16,4096]{2,1,0:T(8,128)(2,1)} %shard_map.107) | copy-start | bytes 3145732
  225.1 18.7 %copy-start.8 = (f32[512]{0:T(512)S(1)}, f32[512]{0:T(512)}, u32[]{:S(2)}) copy-start(f32[512]{0:T(512)} %copy-done.6) | copy-start | bytes 6148
  232.6 9.0 %collective-permute-start.19 = (bf16[512,128]{1,0:T(8,128)(2,1)S(1)}, bf16[512,128]{1,0:T(8,128)(2,1)S(1)}, u32[]{:S(2)}, u32[]{:S(2)}) collective-permute-start(bf16[512,128]{1,0:T(8,128)(2,1)S(1)} %get-tuple-element.27), channel_id=1, source_target_pairs={{0,8},{8,16},{16,24},{24,32},{32,40},{40,48},{48,56},{56,64},{64,7... | collective-permute-start | bytes 393224 | tf_op jit(solution)/shard_map/ppermute | solution.py:22
  234.5 9.3 %collective-permute-start.20 = (bf16[512,128]{1,0:T(8,128)(2,1)S(1)}, bf16[512,128]{1,0:T(8,128)(2,1)S(1)}, u32[]{:S(2)}, u32[]{:S(2)}) collective-permute-start(bf16[512,128]{1,0:T(8,128)(2,1)S(1)} %get-tuple-element.28), channel_id=1, source_target_pairs={{0,16},{8,24},{16,32},{24,40},{32,48},{40,56},{48,64},{56,72},{64,... | collective-permute-start | bytes 393224 | tf_op jit(solution)/shard_map/ppermute | solution.py:22
  244.6 9.3 %collective-permute-start.21 = (bf16[512,128]{1,0:T(8,128)(2,1)S(1)}, bf16[512,128]{1,0:T(8,128)(2,1)S(1)}, u32[]{:S(2)}, u32[]{:S(2)}) collective-permute-start(bf16[512,128]{1,0:T(8,128)(2,1)S(1)} %get-tuple-element.21), channel_id=1, source_target_pairs={{8,0},{16,8},{24,16},{32,24},{40,32},{48,40},{56,48},{64,56},{72,6... | collective-permute-start | bytes 393224 | tf_op jit(solution)/shard_map/ppermute | solution.py:22
  248.8 7.2 %collective-permute-start.22 = (bf16[512,128]{1,0:T(8,128)(2,1)S(1)}, bf16[512,128]{1,0:T(8,128)(2,1)S(1)}, u32[]{:S(2)}, u32[]{:S(2)}) collective-permute-start(bf16[512,128]{1,0:T(8,128)(2,1)S(1)} %get-tuple-element.21), channel_id=1, source_target_pairs={{16,0},{24,8},{32,16},{40,24},{48,32},{56,40},{64,48},{72,56},{80,... | collective-permute-start | bytes 393224 | tf_op jit(solution)/shard_map/ppermute | solution.py:22
  256.8 40.0 %copy-start.10 = (f32[512]{0:T(512)S(1)}, f32[512]{0:T(512)}, u32[]{:S(2)}) copy-start(f32[512]{0:T(512)} %fusion.137) | copy-start | bytes 6148
  256.9 40.0 %copy-start.12 = (pred[16]{0:T(512)(128)(4,1)S(1)}, pred[16]{0:T(512)(128)(4,1)}, u32[]{:S(2)}) copy-start(pred[16]{0:T(512)(128)(4,1)} %add_compare_fusion) | copy-start | bytes 52
  256.9 40.0 %copy-start.14 = (pred[8]{0:T(512)(128)(4,1)S(1)}, pred[8]{0:T(512)(128)(4,1)}, u32[]{:S(2)}) copy-start(pred[8]{0:T(512)(128)(4,1)} %add_compare_fusion.1) | copy-start | bytes 28
  286.2 9.8 %collective-permute-start.26 = (f32[8,512]{1,0:T(8,128)S(1)}, f32[8,512]{1,0:T(8,128)S(1)}, u32[]{:S(2)}, u32[]{:S(2)}) collective-permute-start(f32[8,512]{1,0:T(8,128)S(1)} %bitcast.330), channel_id=1, source_target_pairs={{0,1},{1,2},{2,3},{3,4},{4,5},{5,6},{6,7},{8,9},{9,10},{10,11},{11... | collective-permute-start | bytes 49160 | tf_op jit(solution)/shard_map/ppermute | solution.py:22
  288.3 8.5 %collective-permute-start.25 = (f32[8,512]{1,0:T(8,128)S(1)}, f32[8,512]{1,0:T(8,128)S(1)}, u32[]{:S(2)}, u32[]{:S(2)}) collective-permute-start(f32[8,512]{1,0:T(8,128)S(1)} %slice_bitcast_fusion.10), channel_id=1, source_target_pairs={{1,0},{2,1},{3,2},{4,3},{5,4},{6,5},{7,6},{9,8},{10,9},{11,10},{12... | collective-permute-start | bytes 49160 | tf_op jit(solution)/shard_map/ppermute | solution.py:22
  290.7 6.0 %collective-permute-start.23 = (f32[16,512]{1,0:T(8,128)S(1)}, f32[16,512]{1,0:T(8,128)S(1)}, u32[]{:S(2)}, u32[]{:S(2)}) collective-permute-start(f32[16,512]{1,0:T(8,128)S(1)} %get-tuple-element.23), channel_id=1, source_target_pairs={{8,0},{16,8},{24,16},{32,24},{40,32},{48,40},{56,48},{64,56},{72,6... | collective-permute-start | bytes 98312 | tf_op jit(solution)/shard_map/ppermute | solution.py:22
  293.9 7.3 %collective-permute-start.24 = (f32[16,512]{1,0:T(8,128)S(1)}, f32[16,512]{1,0:T(8,128)S(1)}, u32[]{:S(2)}, u32[]{:S(2)}) collective-permute-start(f32[16,512]{1,0:T(8,128)S(1)} %get-tuple-element.22), channel_id=1, source_target_pairs={{0,8},{8,16},{16,24},{24,32},{32,40},{40,48},{48,56},{56,64},{64,7... | collective-permute-start | bytes 98312 | tf_op jit(solution)/shard_map/ppermute | solution.py:22
